TPU v7x, 32 devices: a whole 2x2x4 slice. The times are simulated.
32 devices in a mesh: groups: 2 (over y), ctx: 4 (over z), head: 2 (over x), rep: 2 (over core).
Axes of the slice: x: 2, y: 2, z: 4, core: 2. Of those that a mesh axis runs over, the one named last changes fastest.
Arguments:
- queries: bfloat16 [1024, 5120], P(('groups', 'ctx'), 'head'), parts along dimension 0, may hold values from -50 to 50
- key_vectors: bfloat16 [1024, 5120], P(('groups', 'ctx'), 'head'), parts along dimension 0, may hold values from -5 to 5
- values: bfloat16 [1024, 5120], P(('groups', 'ctx'), 'head'), parts along dimension 0, may hold values from -6 to 6
- learn_rates: float32 [8, 1024], P('head', ('groups', 'ctx')), parts along dimension 1, may hold values from 0.02 to 0.2
- fast_weights: float32 [16, 3, 640, 640], P(('groups', 'head'), None, ('ctx', 'rep')), parts along dimension 0, may hold values from -0.25 to 0.25
- momentum: float32 [16, 3, 640, 640], P(('groups', 'head'), None, ('ctx', 'rep')), parts along dimension 0, may hold values from -0.25 to 0.25
Outputs:
- layer_output: bfloat16 [1024, 5120], P(('groups', 'ctx'), ('head', 'rep')), parts along dimension 0
- fast_updated: float32 [16, 3, 640, 640], P(('groups', 'head'), None, ('ctx', 'rep')), parts along dimension 0
There are 2 independent parts, one for each index of `groups`. A program takes and returns all parts, laid end to end along the dimension named above; each array names one. Nothing has to cross between parts.
All inputs are finite; a program needn't handle non-finite values.
Results may differ from a plain program's by a relative error of at most 0.038.
Values may be sent and summed in bfloat16 or wider, within the bound.
No kernel may reach another device: no remote copies, remote signals or barrier semaphores. Data moves between devices by JAX's collectives and lax.ppermute only.
A program may use at most 64 MiB of HBM per device.

v0:
```python
import functools

import jax
import jax.numpy as jnp
from jax import lax
from jax.experimental import pallas as pl
from jax.experimental.pallas import tpu as pltpu
from jax.sharding import PartitionSpec as P


epsilon = 1e-06
momentum_decay = 0.9
NT = (((1,), (1,)), ((), ()))


def passed_along(value, axis, steps):
    count = lax.axis_size(axis)
    initial, last = (max(0, -steps), min(count, count - steps))
    return lax.ppermute(value, axis, [(source, source + steps) for source in range(initial, last)])


def ring(value, axis, steps=1):
    count = lax.axis_size(axis)
    return lax.ppermute(value, axis, [(source, (source + steps) % count) for source in range(count)])


def unit_rows(tensor):
    widened = tensor.astype(jnp.float32)
    factor = lax.rsqrt(jnp.mean(widened * widened, axis=-1, keepdims=True) + epsilon)
    return (widened * factor).astype(jnp.bfloat16)


def swiglu_apply(inputs, weights):
    gate = jnp.einsum("thd,hrd->htr", inputs, weights[:, 0], preferred_element_type=jnp.float32)
    upward = jnp.einsum("thd,hrd->htr", inputs, weights[:, 1], preferred_element_type=jnp.float32)
    hidden = (jax.nn.silu(gate) * upward).astype(jnp.bfloat16)
    return jnp.einsum("htr,hrd->htd", hidden, weights[:, 2], preferred_element_type=jnp.float32)


def window_attention(query_own, key_own, value_own, key_prior, value_prior, first_block):
    tok_rows = query_own.shape[0]
    per_rep = query_own.shape[1]
    width = query_own.shape[2]
    block_rows = min(tok_rows, 512)
    block_count = tok_rows // block_rows
    key_window = jnp.concatenate([key_prior, key_own], axis=0)
    value_window = jnp.concatenate([value_prior, value_own], axis=0)
    score_scale = width ** (-0.5)
    position = jnp.arange(2 * tok_rows)
    valid = jnp.logical_or(position >= tok_rows, jnp.logical_not(first_block))
    query_blocks = query_own.reshape(block_count, block_rows, per_rep, width)

    def one_block(query_block):
        scores = (
            jnp.einsum("tad,sad->ats", query_block, key_window, preferred_element_type=jnp.float32)
            * score_scale
        )
        scores = jnp.where(valid[None, None, :], scores, -jnp.inf)
        peak = jnp.max(scores, axis=-1, keepdims=True)
        weights = jnp.exp(scores - peak)
        probs = (weights / jnp.sum(weights, axis=-1, keepdims=True)).astype(jnp.bfloat16)
        return jnp.einsum("ats,sad->tad", probs, value_window, preferred_element_type=jnp.float32)

    return lax.map(one_block, query_blocks).reshape(tok_rows, per_rep, width)


def weights_travel(queries, key_vectors, values, learn_rates, fast_weights, momentum):
    tok_rows = queries.shape[0]
    head_count = fast_weights.shape[0]
    width = fast_weights.shape[3]
    rep_count = lax.axis_size("rep")
    per_rep = head_count // rep_count
    rep_index = lax.axis_index("rep")
    ctx_index = lax.axis_index("ctx")
    total_tokens = tok_rows * lax.axis_size("ctx")
    query_heads = queries.reshape(tok_rows, head_count, width)
    key_heads = key_vectors.reshape(tok_rows, head_count, width)
    value_heads = values.reshape(tok_rows, head_count, width)
    query_unit = unit_rows(query_heads)
    key_unit = unit_rows(key_heads)
    token_scale = float(total_tokens) ** (-0.5)
    cotangent = (
        -(learn_rates.T[:, :, None] * token_scale) * value_heads.astype(jnp.float32)
    ).astype(jnp.bfloat16)
    weight_rows = lax.all_gather(fast_weights.astype(jnp.bfloat16), "ctx", axis=2, tiled=True)
    gate = jnp.einsum(
        "thd,hrd->htr", key_unit, weight_rows[:, 0], preferred_element_type=jnp.float32
    )
    upward = jnp.einsum(
        "thd,hrd->htr", key_unit, weight_rows[:, 1], preferred_element_type=jnp.float32
    )
    back = jnp.einsum(
        "thd,hrd->htr", cotangent, weight_rows[:, 2], preferred_element_type=jnp.float32
    )
    sigma = jax.nn.sigmoid(gate)
    activated = jax.nn.silu(gate)
    hidden = (activated * upward).astype(jnp.bfloat16)
    gate_back = (back * upward * sigma * (1.0 + gate * (1.0 - sigma))).astype(jnp.bfloat16)
    up_back = (back * activated).astype(jnp.bfloat16)
    grad_gate = jnp.einsum("htr,thd->hrd", gate_back, key_unit, preferred_element_type=jnp.float32)
    grad_up = jnp.einsum("htr,thd->hrd", up_back, key_unit, preferred_element_type=jnp.float32)
    grad_down = jnp.einsum("htr,thd->hrd", hidden, cotangent, preferred_element_type=jnp.float32)
    gradient = jnp.stack([grad_gate, grad_up, grad_down], axis=1)
    share = lax.psum_scatter(
        gradient.astype(jnp.bfloat16), "ctx", scatter_dimension=2, tiled=True
    ).astype(jnp.float32)
    fast_updated = fast_weights - (momentum_decay * momentum + share)
    new_rows = lax.all_gather(fast_updated.astype(jnp.bfloat16), "ctx", axis=2, tiled=True)
    own_start = rep_index * per_rep
    partial_out = swiglu_apply(query_unit, new_rows)
    traded = lax.all_to_all(
        partial_out.astype(jnp.bfloat16), "rep", split_axis=0, concat_axis=0, tiled=True
    ).astype(partial_out.dtype)
    fast_out = jnp.sum(traded.reshape(rep_count, per_rep, tok_rows, width), axis=0)
    attend_query = lax.dynamic_slice_in_dim(query_heads, own_start, per_rep, 1)
    attend_key = lax.dynamic_slice_in_dim(key_heads, own_start, per_rep, 1)
    attend_value = lax.dynamic_slice_in_dim(value_heads, own_start, per_rep, 1)
    key_prior, value_prior = passed_along((attend_key, attend_value), "ctx", 1)
    attended = window_attention(
        attend_query, attend_key, attend_value, key_prior, value_prior, ctx_index == 0
    )
    combined = attended + jnp.transpose(fast_out, (1, 0, 2))
    layer_output = combined.astype(jnp.bfloat16).reshape(tok_rows, per_rep * width)
    return (layer_output, fast_updated)


def cotangent_body(token_scale, rep, values, rates, out_raw, out):
    heads = rates.shape[0] // 2
    rows, columns = out.shape
    width = columns // heads
    for h in range(heads):
        rate = -(rates[pl.ds(rep[0] * heads + h, 1), :] * token_scale)
        rate = jnp.transpose(jnp.broadcast_to(rate, (rows, rows)))[:, :1]
        part = values[:, h * width : (h + 1) * width]
        out_raw[:, h * width : (h + 1) * width] = part
        out[:, h * width : (h + 1) * width] = (rate * part.astype(jnp.float32)).astype(jnp.bfloat16)


def cotangent_step(token_scale, rep, values, rates):
    rows, columns = values.shape[0], values.shape[1] // 2
    made = jax.ShapeDtypeStruct((rows, columns), jnp.bfloat16)
    whole = pl.BlockSpec((rows, columns), lambda i, rep: (0, 0))
    return pl.pallas_call(
        functools.partial(cotangent_body, token_scale),
        out_shape=(made, made),
        grid_spec=pltpu.PrefetchScalarGridSpec(
            num_scalar_prefetch=1,
            grid=(1,),
            in_specs=[
                pl.BlockSpec((rows, columns), lambda i, rep: (0, rep[0])),
                pl.BlockSpec(rates.shape, lambda i, rep: (0, 0)),
            ],
            out_specs=(whole, whole),
        ),
        compiler_params=pltpu.CompilerParams(vmem_limit_bytes=8 << 20),
        cost_estimate=pl.CostEstimate(
            flops=2 * rows * columns, bytes_accessed=6 * rows * columns, transcendentals=0
        ),
        name="cotangent_step",
    )(rep, values, rates)


def gradient_body(slots, *refs):
    keys, cots = refs[:slots], refs[slots : 2 * slots]
    low_own, low_par, base_own, base_par, new_own, new_par, new_low, unit, cot, low = refs[2 * slots :]
    rows = keys[0].shape[0]
    hid = low_own.shape[2]
    for s in range(slots):
        here = pl.ds(s * rows, rows)
        unit[here, :] = unit_rows(keys[s][...])
        cot[here, :] = cots[s][...]
    for m in range(3):
        low[pl.ds(2 * m * hid, hid), :] = low_own[0, m]
        low[pl.ds((2 * m + 1) * hid, hid), :] = low_par[0, m]
    fed = lax.dot_general(low[: 4 * hid, :], unit[...], NT, preferred_element_type=jnp.float32)
    gate, upward = fed[: 2 * hid], fed[2 * hid :]
    back = lax.dot_general(low[4 * hid :, :], cot[...], NT, preferred_element_type=jnp.float32)
    sigma = jax.nn.sigmoid(gate)
    activated = gate * sigma
    hidden = (activated * upward).astype(jnp.bfloat16)
    gate_back = (back * upward * sigma * (1.0 + gate * (1.0 - sigma))).astype(jnp.bfloat16)
    up_back = (back * activated).astype(jnp.bfloat16)
    for m, (left, right) in enumerate(((gate_back, unit), (up_back, unit), (hidden, cot))):
        grad = jnp.dot(left, right[...], preferred_element_type=jnp.float32)
        fresh_own = base_own[0, m] - grad[:hid]
        fresh_par = base_par[0, m] - grad[hid:]
        new_own[0, m] = fresh_own
        new_par[0, m] = fresh_par
        new_low[0, pl.ds(2 * m * hid, hid), :] = fresh_own.astype(jnp.bfloat16)
        new_low[0, pl.ds((2 * m + 1) * hid, hid), :] = fresh_par.astype(jnp.bfloat16)


def gradient_step(keys, cots, low_own, low_par, base_own, base_par):
    slots = len(keys)
    rows = keys[0].shape[0]
    heads, _, hid, width = low_own.shape
    token_spec = pl.BlockSpec((rows, width), lambda h: (0, h))
    weight_spec = pl.BlockSpec((1, 3, hid, width), lambda h: (h, 0, 0, 0))
    low_spec = pl.BlockSpec((1, 6 * hid, width), lambda h: (h, 0, 0))
    fresh = pltpu.HBM(low_own.shape, jnp.float32)
    return pl.pallas_call(
        functools.partial(gradient_body, slots),
        out_shape=(fresh, fresh, jax.ShapeDtypeStruct((heads, 6 * hid, width), jnp.bfloat16)),
        grid=(heads,),
        in_specs=[token_spec] * (2 * slots) + [weight_spec] * 4,
        out_specs=(weight_spec, weight_spec, low_spec),
        scratch_shapes=[
            pltpu.VMEM((slots * rows, width), jnp.bfloat16),
            pltpu.VMEM((slots * rows, width), jnp.bfloat16),
            pltpu.VMEM((6 * hid, width), jnp.bfloat16),
        ],
        compiler_params=pltpu.CompilerParams(vmem_limit_bytes=24 << 20),
        cost_estimate=pl.CostEstimate(
            flops=24 * heads * slots * rows * hid * width,
            bytes_accessed=48 * heads * hid * width,
            transcendentals=0,
        ),
        name="gradient_step",
    )(*keys, *cots, low_own, low_par, base_own, base_par)


def apply_body(query, low, *refs):
    heads, total, width = low.shape
    more, outs = refs[:-heads], refs[-heads:]
    hid = total // 6
    for h in range(heads):
        columns = slice(h * width, (h + 1) * width)
        unit = unit_rows(query[:, columns])
        gate = lax.dot_general(unit, low[h, : 2 * hid, :], NT, preferred_element_type=jnp.float32)
        upward = lax.dot_general(
            unit, low[h, 2 * hid : 4 * hid, :], NT, preferred_element_type=jnp.float32
        )
        hidden = (gate * jax.nn.sigmoid(gate) * upward).astype(jnp.bfloat16)
        made = jnp.dot(hidden, low[h, 4 * hid :, :], preferred_element_type=jnp.float32)
        if more:
            made = made + more[0][:, columns]
        outs[h][...] = made.astype(outs[h].dtype)


def apply_step(query, low, dtype, *more):
    heads, total, width = low.shape
    rows = query.shape[0]
    return pl.pallas_call(
        apply_body,
        out_shape=tuple(jax.ShapeDtypeStruct((rows, width), dtype) for _ in range(heads)),
        compiler_params=pltpu.CompilerParams(vmem_limit_bytes=8 << 20),
        cost_estimate=pl.CostEstimate(
            flops=2 * rows * heads * total * width,
            bytes_accessed=2 * heads * total * width,
            transcendentals=0,
        ),
        name="apply_step",
    )(query, low, *more)


def attend_body(heads, token_scale, first, query, key_own, key_prior, value_own, cot_prior, rate_prior, out):
    width = query.shape[1] // heads
    allowed = jnp.where(first[0] != 0, -jnp.inf, 0.0).astype(jnp.float32)
    for h in range(heads):
        columns = slice(h * width, (h + 1) * width)
        part = query[:, columns]
        near = lax.dot_general(part, key_own[:, columns], NT, preferred_element_type=jnp.float32)
        far = lax.dot_general(part, key_prior[:, columns], NT, preferred_element_type=jnp.float32)
        near = near * width ** (-0.5)
        far = far * width ** (-0.5) + allowed
        peak = jnp.maximum(
            jnp.max(near, axis=-1, keepdims=True), jnp.max(far, axis=-1, keepdims=True)
        )
        near = jnp.exp(near - peak)
        far = jnp.exp(far - peak)
        total = jnp.sum(near, axis=-1, keepdims=True) + jnp.sum(far, axis=-1, keepdims=True)
        rate = -(rate_prior[h] * token_scale)
        near = (near / total).astype(jnp.bfloat16)
        far = (far / total / rate).astype(jnp.bfloat16)
        out[:, columns] = jnp.dot(
            near, value_own[:, columns], preferred_element_type=jnp.float32
        ) + jnp.dot(far, cot_prior[:, columns], preferred_element_type=jnp.float32)


def attend_step(token_scale, first, query, key_own, key_prior, value_own, cot_prior, rate_prior):
    rows, columns = query.shape
    return pl.pallas_call(
        functools.partial(attend_body, rate_prior.shape[0], token_scale),
        out_shape=jax.ShapeDtypeStruct(query.shape, jnp.float32),
        in_specs=[pl.BlockSpec(memory_space=pltpu.SMEM)] + [pl.BlockSpec()] * 6,
        out_specs=pl.BlockSpec(),
        compiler_params=pltpu.CompilerParams(vmem_limit_bytes=8 << 20),
        cost_estimate=pl.CostEstimate(
            flops=8 * rows * rows * columns, bytes_accessed=14 * rows * columns, transcendentals=0
        ),
        name="attend_step",
    )(first, query, key_own, key_prior, value_own, cot_prior, rate_prior)


def tokens_travel(queries, key_vectors, values, learn_rates, fast_weights, momentum):
    width = fast_weights.shape[3]
    slots = lax.axis_size("ctx")
    per_rep = fast_weights.shape[0] // 2
    rep_index = lax.axis_index("rep")
    start = rep_index * per_rep
    away = per_rep - start
    token_scale = float(slots * queries.shape[0]) ** (-0.5)

    def own_columns(tensor):
        return lax.dynamic_slice_in_dim(tensor, start * width, per_rep * width, 1)

    def own(tensor):
        return lax.dynamic_slice_in_dim(tensor, start, per_rep, 0)

    def other(tensor):
        return lax.dynamic_slice_in_dim(tensor, away, per_rep, 0)

    def hop(value, axis="ctx"):
        return ring(value, axis)

    value_own, cot = cotangent_step(token_scale, rep_index.reshape(1), values, learn_rates)
    keys, cots, asked = [own_columns(key_vectors)], [cot], [own_columns(queries)]
    for _ in range(1, slots):
        keys.append(hop(keys[-1]))
        cots.append(hop(cots[-1]))
    rate_prior = hop(own(learn_rates)[:, None, :])
    base = fast_weights - momentum_decay * momentum
    low = fast_weights.astype(jnp.bfloat16)
    low_par = hop(other(low), "rep")
    base_par = hop(other(base), "rep")
    for _ in range(1, slots):
        asked.append(hop(asked[-1]))
    first = (lax.axis_index("ctx") == 0).astype(jnp.int32).reshape(1)
    attended = attend_step(
        token_scale, first, asked[0], keys[0], keys[1], value_own, cots[1], rate_prior
    )
    own_low, own_base = own(low), own(base)
    new_own, new_par, new_low = gradient_step(
        keys, cots, own_low, low_par, own_base, base_par
    )
    heads = range(per_rep)
    moving = []
    for step in range(1, slots):
        if step == 1:
            sent = apply_step(asked[step], new_low, jnp.bfloat16)
        else:
            made = apply_step(asked[step], new_low, jnp.float32)
            sent = [
                (made[h] + moving[h].astype(jnp.float32)).astype(jnp.bfloat16) for h in heads
            ]
        moving = [hop(sent[h]) for h in heads]
    kept = apply_step(asked[0], new_low, jnp.float32, attended)
    layer_output = jnp.concatenate(
        [(kept[h] + moving[h].astype(jnp.float32)).astype(jnp.bfloat16) for h in heads], axis=1
    )
    returned = hop(new_par, "rep")
    fast_updated = jnp.where(
        rep_index == 0,
        jnp.concatenate([new_own, returned], axis=0),
        jnp.concatenate([returned, new_own], axis=0),
    )
    return (layer_output, fast_updated)


def on_device(queries, key_vectors, values, learn_rates, fast_weights, momentum):
    slots = lax.axis_size("ctx")
    fits = (
        lax.axis_size("rep") == 2
        and 2 <= slots <= 8
        and fast_weights.shape[0] % 2 == 0
        and fast_weights.shape[2] % 16 == 0
        and queries.shape[0] == 128
    )
    program = tokens_travel if fits else weights_travel
    return program(queries, key_vectors, values, learn_rates, fast_weights, momentum)


def solution(mesh):
    return jax.shard_map(
        on_device,
        mesh=mesh,
        in_specs=(
            P(("groups", "ctx"), "head"),
            P(("groups", "ctx"), "head"),
            P(("groups", "ctx"), "head"),
            P("head", ("groups", "ctx")),
            P(("groups", "head"), None, ("ctx", "rep"), None),
            P(("groups", "head"), None, ("ctx", "rep"), None),
        ),
        out_specs=(
            P(("groups", "ctx"), ("head", "rep")),
            P(("groups", "head"), None, ("ctx", "rep"), None),
        ),
        check_vma=False,
    )
```

profile of v0, /device:TPU:0, one launch (start us, length us, event | category | flops | bytes accessed | tf_op | source)
XLA Modules:
  0.0 114.7 jit_solution(3793652435651340223)
XLA Ops:
  0.6 0.0 copy-start
  0.7 4.7 %multiply_subtract_fusion = (f32[4,3,80,640]{3,2,1,0:T(8,128)S(1)}, bf16[4,3,80,640]{3,2,1,0:T(8,128)(2,1)}) fusion(f32[4,3,80,640]{3,2,1,0:T(8,128)} %param.10, f32[4,3,80,640]{3,2,1,0:T(8,128)} %param.11), kind=kLoop, calls=%fused_computation.1 | loop fusion | flops 1843200 | bytes 8601600 | tf_op jit(solution)/shard_map/sub | solution.py:322
  5.3 1.2 %constant_dynamic-slice_fusion.1 = (f32[2,3,80,640]{3,2,1,0:T(8,128)}, f32[2,3,80,640]{3,2,1,0:T(8,128)S(1)}) fusion(f32[4,3,80,640]{3,2,1,0:T(8,128)S(1)} %get-tuple-element.30, s32[]{:T(128)S(6)} %select_n.23, s32[]{:T(128)S(6)} %select_n.22), kind=kLoop, calls=%fused_computation.10 | loop fusion | bytes 4915208 | tf_op jit(solution)/shard_map/dynamic_slice | solution.py:311
  6.5 0.5 collective-permute-start.7
  7.0 0.0 copy-done
  7.1 2.6 %collective-permute-start = (bf16[128,1280]{1,0:T(8,128)(2,1)S(1)}, bf16[128,1280]{1,0:T(8,128)(2,1)S(1)}, u32[]{:S(2)}, u32[]{:S(2)}) collective-permute-start(bf16[128,1280]{1,0:T(8,128)(2,1)S(1)} %constant_dynamic-slice_fusion.5.refs_0_.key_own), channel_id=1, source_target_pairs={{0,4},{4,8},{8,12},{12,0},{1,5},{5,9},{9,13},{13,1},{2,6},{6,10},{... | collective-permute-start | bytes 983048 | tf_op jit(solution)/shard_map/ppermute | solution.py:24
  9.7 0.0 copy-done.7
  9.7 0.0 copy-done.10
  9.7 0.2 cotangent_step.1
  9.9 0.0 copy-start.8
  9.9 1.6 %collective-permute-start.3 = (bf16[128,1280]{1,0:T(8,128)(2,1)S(1)}, bf16[128,1280]{1,0:T(8,128)(2,1)S(1)}, u32[]{:S(2)}, u32[]{:S(2)}) collective-permute-start(bf16[128,1280]{1,0:T(8,128)(2,1)S(1)} %get-tuple-element.15.refs_4_), channel_id=1, source_target_pairs={{0,4},{4,8},{8,12},{12,0},{1,5},{5,9},{9,13},{13,1},{2,6},{6,10},{... | collective-permute-start | bytes 983048 | tf_op jit(solution)/shard_map/ppermute | solution.py:24
  11.5 0.0 copy-done.13
  11.6 0.0 copy-start.1
  11.6 1.6 %collective-permute-start.9 = (bf16[128,1280]{1,0:T(8,128)(2,1)S(1)}, bf16[128,1280]{1,0:T(8,128)(2,1)S(1)}, u32[]{:S(2)}, u32[]{:S(2)}) collective-permute-start(bf16[128,1280]{1,0:T(8,128)(2,1)S(1)} %constant_dynamic-slice_fusion.6.query), channel_id=1, source_target_pairs={{0,4},{4,8},{8,12},{12,0},{1,5},{5,9},{9,13},{13,1},{2,6},{6,10},{... | collective-permute-start | bytes 983048 | tf_op jit(solution)/shard_map/ppermute | solution.py:24
  13.2 7.1 %collective-permute-done.refs_1_.key_prior = bf16[128,1280]{1,0:T(8,128)(2,1)S(1)} collective-permute-done((bf16[128,1280]{1,0:T(8,128)(2,1)S(1)}, bf16[128,1280]{1,0:T(8,128)(2,1)S(1)}, u32[]{:S(2)}, u32[]{:S(2)}) %collective-permute-start) | collective-permute-done | bytes 327712 | tf_op jit(solution)/shard_map/ppermute | solution.py:24
  20.3 0.0 collective-permute-start.1
  20.3 7.0 %collective-permute-done.3.refs_5_.cot_prior = bf16[128,1280]{1,0:T(8,128)(2,1)S(1)} collective-permute-done((bf16[128,1280]{1,0:T(8,128)(2,1)S(1)}, bf16[128,1280]{1,0:T(8,128)(2,1)S(1)}, u32[]{:S(2)}, u32[]{:S(2)}) %collective-permute-start.3) | collective-permute-done | bytes 327712 | tf_op jit(solution)/shard_map/ppermute | solution.py:24
  27.3 0.0 collective-permute-start.4
  27.3 0.2 constant_dynamic-slice_fusion.3
  27.5 0.1 collective-permute-start.6
  27.5 6.8 %collective-permute-done.9.query = bf16[128,1280]{1,0:T(8,128)(2,1)S(1)} collective-permute-done((bf16[128,1280]{1,0:T(8,128)(2,1)S(1)}, bf16[128,1280]{1,0:T(8,128)(2,1)S(1)}, u32[]{:S(2)}, u32[]{:S(2)}) %collective-permute-start.9) | collective-permute-done | bytes 327712 | tf_op jit(solution)/shard_map/ppermute | solution.py:24
  34.3 0.0 collective-permute-start.10
  34.3 7.0 %collective-permute-done.1.refs_2_ = bf16[128,1280]{1,0:T(8,128)(2,1)S(1)} collective-permute-done((bf16[128,1280]{1,0:T(8,128)(2,1)S(1)}, bf16[128,1280]{1,0:T(8,128)(2,1)S(1)}, u32[]{:S(2)}, u32[]{:S(2)}) %collective-permute-start.1) | collective-permute-done | bytes 327712 | tf_op jit(solution)/shard_map/ppermute | solution.py:24
  41.3 0.0 collective-permute-start.2
  41.3 7.0 %collective-permute-done.4.refs_6_ = bf16[128,1280]{1,0:T(8,128)(2,1)S(1)} collective-permute-done((bf16[128,1280]{1,0:T(8,128)(2,1)S(1)}, bf16[128,1280]{1,0:T(8,128)(2,1)S(1)}, u32[]{:S(2)}, u32[]{:S(2)}) %collective-permute-start.4) | collective-permute-done | bytes 327712 | tf_op jit(solution)/shard_map/ppermute | solution.py:24
  48.4 0.0 collective-permute-start.5
  48.4 7.1 %collective-permute-done.10.query = bf16[128,1280]{1,0:T(8,128)(2,1)} collective-permute-done((bf16[128,1280]{1,0:T(8,128)(2,1)S(1)}, bf16[128,1280]{1,0:T(8,128)(2,1)}, u32[]{:S(2)}, u32[]{:S(2)}) %collective-permute-start.10) | collective-permute-done | bytes 327712 | tf_op jit(solution)/shard_map/ppermute | solution.py:24
  55.5 0.0 collective-permute-start.11
  55.5 0.0 collective-permute-done.6.refs_9_
  55.5 6.9 %collective-permute-done.2.refs_3_ = bf16[128,1280]{1,0:T(8,128)(2,1)S(1)} collective-permute-done((bf16[128,1280]{1,0:T(8,128)(2,1)S(1)}, bf16[128,1280]{1,0:T(8,128)(2,1)S(1)}, u32[]{:S(2)}, u32[]{:S(2)}) %collective-permute-start.2) | collective-permute-done | bytes 327712 | tf_op jit(solution)/shard_map/ppermute | solution.py:24
  62.4 7.0 %collective-permute-done.5.refs_7_ = bf16[128,1280]{1,0:T(8,128)(2,1)S(1)} collective-permute-done((bf16[128,1280]{1,0:T(8,128)(2,1)S(1)}, bf16[128,1280]{1,0:T(8,128)(2,1)S(1)}, u32[]{:S(2)}, u32[]{:S(2)}) %collective-permute-start.5) | collective-permute-done | bytes 327712 | tf_op jit(solution)/shard_map/ppermute | solution.py:24
  69.4 0.0 collective-permute-done.7.refs_11_
  69.4 4.8 %gradient_step.1 = (f32[2,3,80,640]{3,2,1,0:T(8,128)}, f32[2,3,80,640]{3,2,1,0:T(8,128)}, bf16[2,480,640]{2,1,0:T(8,128)(2,1)S(1)}) custom-call(bf16[128,1280]{1,0:T(8,128)(2,1)S(1)} %constant_dynamic-slice_fusion.5.refs_0_.key_own, bf16[128,1280]{1,0:T(8,128)(2,1)S(1)} %collective-permute-done.refs_1_.key_prior, ...), custom_call_target="tpu_custom_call" | custom-call | flops 1258291200 | bytes 4915200 | tf_op jit(solution)/shard_map/gradient_step/pallas_call | solution.py:201
  74.3 0.0 copy-done.3
  74.3 0.9 apply_step.7
  75.1 0.1 collective-permute-start.12
  75.2 1.5 %collective-permute-start.8 = (f32[2,1,128]{2,1,0:T(1,128)S(1)}, f32[2,1,128]{2,1,0:T(1,128)S(1)}, u32[]{:S(2)}, u32[]{:S(2)}) collective-permute-start(f32[2,1,128]{2,1,0:T(1,128)S(1)} %bitcast.3), channel_id=1, source_target_pairs={{0,4},{4,8},{8,12},{12,0},{1,5},{5,9},{9,13},{13,1},{2,6},{6,10},{... | collective-permute-start | bytes 3080 | tf_op jit(solution)/shard_map/ppermute | solution.py:24
  76.8 6.1 %collective-permute-done.8.rate_prior = f32[2,1,128]{2,1,0:T(1,128)S(1)} collective-permute-done((f32[2,1,128]{2,1,0:T(1,128)S(1)}, f32[2,1,128]{2,1,0:T(1,128)S(1)}, u32[]{:S(2)}, u32[]{:S(2)}) %collective-permute-start.8) | collective-permute-done | bytes 1056 | tf_op jit(solution)/shard_map/ppermute | solution.py:24
  82.9 1.0 copy-done.2
  83.9 1.0 copy-done.4
  84.8 1.0 copy-done.6
  85.8 1.0 copy-done.9
  86.8 1.2 %attend_step.1.refs_0_ = f32[128,1280]{1,0:T(8,128)S(1)} custom-call(s32[1]{0:T(128)} %bitcast.1.first, bf16[128,1280]{1,0:T(8,128)(2,1)S(1)} %copy-done.2, bf16[128,1280]{1,0:T(8,128)(2,1)S(1)} %constant_dynamic-slice_fusion.5.refs_0_.key_own, bf16[128,1280]{1,0:T(8,128)(2,1)S(1)} %copy-done.4, bf16[128,1280]{1,0:T(8,128)(2,1)S(1)} %copy-done.9, ...), custom_call_target="tpu_custom_call" | custom-call | flops 167772160 | bytes 2293760 | tf_op jit(solution)/shard_map/attend_step/pallas_call | solution.py:282
  87.9 0.1 collective-permute-start.18
  88.0 0.1 collective-permute-start.15
  88.1 0.9 apply_step.4
  89.0 1.8 %apply_step.6 = (f32[128,640]{1,0:T(8,128)S(1)}, f32[128,640]{1,0:T(8,128)S(1)}) custom-call(bf16[128,1280]{1,0:T(8,128)(2,1)} %collective-permute-done.10.query, bf16[2,480,640]{2,1,0:T(8,128)(2,1)S(1)} %get-tuple-element.16.low), custom_call_target="tpu_custom_call" | custom-call | flops 157286400 | bytes 1228800 | tf_op jit(solution)/shard_map/apply_step/pallas_call | solution.py:243
  90.8 0.0 collective-permute-done.11.query
  90.8 1.8 %apply_step.5 = (f32[128,640]{1,0:T(8,128)S(1)}, f32[128,640]{1,0:T(8,128)S(1)}) custom-call(bf16[128,1280]{1,0:T(8,128)(2,1)} %collective-permute-done.11.query, bf16[2,480,640]{2,1,0:T(8,128)(2,1)S(1)} %get-tuple-element.16.low), custom_call_target="tpu_custom_call" | custom-call | flops 157286400 | bytes 1228800 | tf_op jit(solution)/shard_map/apply_step/pallas_call | solution.py:243
  92.6 0.0 copy-start.12
  92.6 0.0 collective-permute-done.12
  92.7 0.1 collective-permute-start.13
  92.7 3.7 %collective-permute-done.15 = bf16[128,640]{1,0:T(8,128)(2,1)S(1)} collective-permute-done((bf16[128,640]{1,0:T(8,128)(2,1)S(1)}, bf16[128,640]{1,0:T(8,128)(2,1)S(1)}, u32[]{:S(2)}, u32[]{:S(2)}) %collective-permute-start.15) | collective-permute-done | bytes 163872 | tf_op jit(solution)/shard_map/ppermute | solution.py:24
  96.5 0.1 collective-permute-start.16
  96.5 5.1 %collective-permute-done.13 = bf16[128,640]{1,0:T(8,128)(2,1)S(1)} collective-permute-done((bf16[128,640]{1,0:T(8,128)(2,1)S(1)}, bf16[128,640]{1,0:T(8,128)(2,1)S(1)}, u32[]{:S(2)}, u32[]{:S(2)}) %collective-permute-start.13) | collective-permute-done | bytes 163872 | tf_op jit(solution)/shard_map/ppermute | solution.py:24
  101.6 0.1 collective-permute-start.14
  101.7 2.9 %collective-permute-done.16 = bf16[128,640]{1,0:T(8,128)(2,1)S(1)} collective-permute-done((bf16[128,640]{1,0:T(8,128)(2,1)S(1)}, bf16[128,640]{1,0:T(8,128)(2,1)S(1)}, u32[]{:S(2)}, u32[]{:S(2)}) %collective-permute-start.16) | collective-permute-done | bytes 163872 | tf_op jit(solution)/shard_map/ppermute | solution.py:24
  104.6 0.1 collective-permute-start.17
  104.7 4.6 %collective-permute-done.14 = bf16[128,640]{1,0:T(8,128)(2,1)S(1)} collective-permute-done((bf16[128,640]{1,0:T(8,128)(2,1)S(1)}, bf16[128,640]{1,0:T(8,128)(2,1)S(1)}, u32[]{:S(2)}, u32[]{:S(2)}) %collective-permute-start.14) | collective-permute-done | bytes 163872 | tf_op jit(solution)/shard_map/ppermute | solution.py:24
  109.3 3.0 %collective-permute-done.17 = bf16[128,640]{1,0:T(8,128)(2,1)S(1)} collective-permute-done((bf16[128,640]{1,0:T(8,128)(2,1)S(1)}, bf16[128,640]{1,0:T(8,128)(2,1)S(1)}, u32[]{:S(2)}, u32[]{:S(2)}) %collective-permute-start.17) | collective-permute-done | bytes 163872 | tf_op jit(solution)/shard_map/ppermute | solution.py:24
  112.4 0.8 pad_maximum_fusion
  113.1 0.0 collective-permute-done.18
  113.1 0.0 copy-done.12
  113.1 1.6 %maximum_select_fusion = f32[4,3,80,640]{3,2,1,0:T(8,128)} fusion(f32[2,3,80,640]{3,2,1,0:T(8,128)S(1)} %collective-permute-done.18, f32[2,3,80,640]{3,2,1,0:T(8,128)S(1)} %copy-done.12, pred[]{:T(512)S(6)} %eq.7), kind=kLoop, calls=%fused_computation | loop fusion | flops 1843200 | bytes 4915201 | tf_op jit(solution)/shard_map/jit(_where)/select_n | solution.py:352
  (23 shorter events, 0.3 us)
Async XLA Ops:
  0.6 6.4 %copy-start = (bf16[128,2560]{1,0:T(8,128)(2,1)S(1)}, bf16[128,2560]{1,0:T(8,128)(2,1)}, u32[]{:S(2)}) copy-start(bf16[128,2560]{1,0:T(8,128)(2,1)} %param.7) | copy-start | bytes 1966084
  5.3 4.4 %copy-start.7 = (bf16[128,2560]{1,0:T(8,128)(2,1)S(1)}, bf16[128,2560]{1,0:T(8,128)(2,1)}, u32[]{:S(2)}) copy-start(bf16[128,2560]{1,0:T(8,128)(2,1)} %values.1) | copy-start | bytes 1966084
  5.3 4.4 %copy-start.10 = (f32[4,128]{1,0:T(4,128)S(1)}, f32[4,128]{1,0:T(4,128)}, u32[]{:S(2)}) copy-start(f32[4,128]{1,0:T(4,128)} %rates.1) | copy-start | bytes 6148
  5.3 6.2 %copy-start.13 = (bf16[128,2560]{1,0:T(8,128)(2,1)S(1)}, bf16[128,2560]{1,0:T(8,128)(2,1)}, u32[]{:S(2)}) copy-start(bf16[128,2560]{1,0:T(8,128)(2,1)} %param.6) | copy-start | bytes 1966084
  6.5 62.9 %collective-permute-start.7 = (f32[2,3,80,640]{3,2,1,0:T(8,128)}, f32[2,3,80,640]{3,2,1,0:T(8,128)}, u32[]{:S(2)}, u32[]{:S(2)}) collective-permute-start(f32[2,3,80,640]{3,2,1,0:T(8,128)} %get-tuple-element.28), channel_id=1, source_target_pairs={{0,1},{1,0},{2,3},{3,2},{4,5},{5,4},{6,7},{7,6},{8,9},{9,8},{10,11... | collective-permute-start | bytes 3686408 | tf_op jit(solution)/shard_map/ppermute | solution.py:24
  7.0 20.3 %copy-start.11 = (bf16[4,3,80,640]{3,2,1,0:T(8,128)(2,1)S(1)}, bf16[4,3,80,640]{3,2,1,0:T(8,128)(2,1)}, u32[]{:S(2)}) copy-start(bf16[4,3,80,640]{3,2,1,0:T(8,128)(2,1)} %get-tuple-element.31) | copy-start | bytes 3686404
  7.1 13.2 %collective-permute-start = (bf16[128,1280]{1,0:T(8,128)(2,1)S(1)}, bf16[128,1280]{1,0:T(8,128)(2,1)S(1)}, u32[]{:S(2)}, u32[]{:S(2)}) collective-permute-start(bf16[128,1280]{1,0:T(8,128)(2,1)S(1)} %constant_dynamic-slice_fusion.5.refs_0_.key_own), channel_id=1, source_target_pairs={{0,4},{4,8},{8,12},{12,0},{1,5},{5,9},{9,13},{13,1},{2,6},{6,10},{... | collective-permute-start | bytes 983048 | tf_op jit(solution)/shard_map/ppermute | solution.py:24
  9.9 59.5 %copy-start.8 = (bf16[128,1280]{1,0:T(8,128)(2,1)}, bf16[128,1280]{1,0:T(8,128)(2,1)S(1)}, u32[]{:S(2)}) copy-start(bf16[128,1280]{1,0:T(8,128)(2,1)S(1)} %get-tuple-element.17.value_own) | copy-start | bytes 983044
  9.9 17.4 %collective-permute-start.3 = (bf16[128,1280]{1,0:T(8,128)(2,1)S(1)}, bf16[128,1280]{1,0:T(8,128)(2,1)S(1)}, u32[]{:S(2)}, u32[]{:S(2)}) collective-permute-start(bf16[128,1280]{1,0:T(8,128)(2,1)S(1)} %get-tuple-element.15.refs_4_), channel_id=1, source_target_pairs={{0,4},{4,8},{8,12},{12,0},{1,5},{5,9},{9,13},{13,1},{2,6},{6,10},{... | collective-permute-start | bytes 983048 | tf_op jit(solution)/shard_map/ppermute | solution.py:24
  11.6 57.9 %copy-start.1 = (bf16[128,1280]{1,0:T(8,128)(2,1)}, bf16[128,1280]{1,0:T(8,128)(2,1)S(1)}, u32[]{:S(2)}) copy-start(bf16[128,1280]{1,0:T(8,128)(2,1)S(1)} %constant_dynamic-slice_fusion.6.query) | copy-start | bytes 983044
  11.6 22.7 %collective-permute-start.9 = (bf16[128,1280]{1,0:T(8,128)(2,1)S(1)}, bf16[128,1280]{1,0:T(8,128)(2,1)S(1)}, u32[]{:S(2)}, u32[]{:S(2)}) collective-permute-start(bf16[128,1280]{1,0:T(8,128)(2,1)S(1)} %constant_dynamic-slice_fusion.6.query), channel_id=1, source_target_pairs={{0,4},{4,8},{8,12},{12,0},{1,5},{5,9},{9,13},{13,1},{2,6},{6,10},{... | collective-permute-start | bytes 983048 | tf_op jit(solution)/shard_map/ppermute | solution.py:24
  20.3 54.0 %copy-start.3 = (bf16[128,1280]{1,0:T(8,128)(2,1)}, bf16[128,1280]{1,0:T(8,128)(2,1)S(1)}, u32[]{:S(2)}) copy-start(bf16[128,1280]{1,0:T(8,128)(2,1)S(1)} %collective-permute-done.refs_1_.key_prior) | copy-start | bytes 983044
  20.3 21.1 %collective-permute-start.1 = (bf16[128,1280]{1,0:T(8,128)(2,1)S(1)}, bf16[128,1280]{1,0:T(8,128)(2,1)S(1)}, u32[]{:S(2)}, u32[]{:S(2)}) collective-permute-start(bf16[128,1280]{1,0:T(8,128)(2,1)S(1)} %collective-permute-done.refs_1_.key_prior), channel_id=1, source_target_pairs={{0,4},{4,8},{8,12},{12,0},{1,5},{5,9},{9,13},{13,1},{2,6},{6,10},{... | collective-permute-start | bytes 983048 | tf_op jit(solution)/shard_map/ppermute | solution.py:24
  27.3 47.0 %copy-start.5 = (bf16[128,1280]{1,0:T(8,128)(2,1)}, bf16[128,1280]{1,0:T(8,128)(2,1)S(1)}, u32[]{:S(2)}) copy-start(bf16[128,1280]{1,0:T(8,128)(2,1)S(1)} %collective-permute-done.3.refs_5_.cot_prior) | copy-start | bytes 983044
  27.3 21.1 %collective-permute-start.4 = (bf16[128,1280]{1,0:T(8,128)(2,1)S(1)}, bf16[128,1280]{1,0:T(8,128)(2,1)S(1)}, u32[]{:S(2)}, u32[]{:S(2)}) collective-permute-start(bf16[128,1280]{1,0:T(8,128)(2,1)S(1)} %collective-permute-done.3.refs_5_.cot_prior), channel_id=1, source_target_pairs={{0,4},{4,8},{8,12},{12,0},{1,5},{5,9},{9,13},{13,1},{2,6},{6,10},{... | collective-permute-start | bytes 983048 | tf_op jit(solution)/shard_map/ppermute | solution.py:24
  27.5 28.0 %collective-permute-start.6 = (bf16[2,3,80,640]{3,2,1,0:T(8,128)(2,1)S(1)}, bf16[2,3,80,640]{3,2,1,0:T(8,128)(2,1)S(1)}, u32[]{:S(2)}, u32[]{:S(2)}) collective-permute-start(bf16[2,3,80,640]{3,2,1,0:T(8,128)(2,1)S(1)} %get-tuple-element.32), channel_id=1, source_target_pairs={{0,1},{1,0},{2,3},{3,2},{4,5},{5,4},{6,7},{7,6},{8,9},{9,8},{10,11... | collective-permute-start | bytes 1843208 | tf_op jit(solution)/shard_map/ppermute | solution.py:24
  34.3 21.2 %collective-permute-start.10 = (bf16[128,1280]{1,0:T(8,128)(2,1)S(1)}, bf16[128,1280]{1,0:T(8,128)(2,1)}, u32[]{:S(2)}, u32[]{:S(2)}) collective-permute-start(bf16[128,1280]{1,0:T(8,128)(2,1)S(1)} %collective-permute-done.9.query), channel_id=1, source_target_pairs={{0,4},{4,8},{8,12},{12,0},{1,5},{5,9},{9,13},{13,1},{2,6},{6,10},{... | collective-permute-start | bytes 983048 | tf_op jit(solution)/shard_map/ppermute | solution.py:24
  41.3 21.1 %collective-permute-start.2 = (bf16[128,1280]{1,0:T(8,128)(2,1)S(1)}, bf16[128,1280]{1,0:T(8,128)(2,1)S(1)}, u32[]{:S(2)}, u32[]{:S(2)}) collective-permute-start(bf16[128,1280]{1,0:T(8,128)(2,1)S(1)} %collective-permute-done.1.refs_2_), channel_id=1, source_target_pairs={{0,4},{4,8},{8,12},{12,0},{1,5},{5,9},{9,13},{13,1},{2,6},{6,10},{... | collective-permute-start | bytes 983048 | tf_op jit(solution)/shard_map/ppermute | solution.py:24
  48.4 21.1 %collective-permute-start.5 = (bf16[128,1280]{1,0:T(8,128)(2,1)S(1)}, bf16[128,1280]{1,0:T(8,128)(2,1)S(1)}, u32[]{:S(2)}, u32[]{:S(2)}) collective-permute-start(bf16[128,1280]{1,0:T(8,128)(2,1)S(1)} %collective-permute-done.4.refs_6_), channel_id=1, source_target_pairs={{0,4},{4,8},{8,12},{12,0},{1,5},{5,9},{9,13},{13,1},{2,6},{6,10},{... | collective-permute-start | bytes 983048 | tf_op jit(solution)/shard_map/ppermute | solution.py:24
  55.5 35.3 %collective-permute-start.11 = (bf16[128,1280]{1,0:T(8,128)(2,1)}, bf16[128,1280]{1,0:T(8,128)(2,1)}, u32[]{:S(2)}, u32[]{:S(2)}) collective-permute-start(bf16[128,1280]{1,0:T(8,128)(2,1)} %collective-permute-done.10.query), channel_id=1, source_target_pairs={{0,4},{4,8},{8,12},{12,0},{1,5},{5,9},{9,13},{13,1},{2,6},{6,10},{... | collective-permute-start | bytes 983048 | tf_op jit(solution)/shard_map/ppermute | solution.py:24
  75.1 17.5 %collective-permute-start.12 = (bf16[128,640]{1,0:T(8,128)(2,1)S(1)}, bf16[128,640]{1,0:T(8,128)(2,1)S(1)}, u32[]{:S(2)}, u32[]{:S(2)}) collective-permute-start(bf16[128,640]{1,0:T(8,128)(2,1)S(1)} %get-tuple-element.21), channel_id=1, source_target_pairs={{0,4},{4,8},{8,12},{12,0},{1,5},{5,9},{9,13},{13,1},{2,6},{6,10},{... | collective-permute-start | bytes 491528 | tf_op jit(solution)/shard_map/ppermute | solution.py:24
  75.2 7.7 %collective-permute-start.8 = (f32[2,1,128]{2,1,0:T(1,128)S(1)}, f32[2,1,128]{2,1,0:T(1,128)S(1)}, u32[]{:S(2)}, u32[]{:S(2)}) collective-permute-start(f32[2,1,128]{2,1,0:T(1,128)S(1)} %bitcast.3), channel_id=1, source_target_pairs={{0,4},{4,8},{8,12},{12,0},{1,5},{5,9},{9,13},{13,1},{2,6},{6,10},{... | collective-permute-start | bytes 3080 | tf_op jit(solution)/shard_map/ppermute | solution.py:24
  82.9 1.0 copy-start.2
  83.9 1.0 copy-start.4
  84.8 1.0 copy-start.6
  85.8 1.0 copy-start.9
  87.9 25.2 %collective-permute-start.18 = (f32[2,3,80,640]{3,2,1,0:T(8,128)}, f32[2,3,80,640]{3,2,1,0:T(8,128)S(1)}, u32[]{:S(2)}, u32[]{:S(2)}) collective-permute-start(f32[2,3,80,640]{3,2,1,0:T(8,128)} %get-tuple-element.27), channel_id=1, source_target_pairs={{0,1},{1,0},{2,3},{3,2},{4,5},{5,4},{6,7},{7,6},{8,9},{9,8},{10,11... | collective-permute-start | bytes 3686408 | tf_op jit(solution)/shard_map/ppermute | solution.py:24
  88.0 8.4 %collective-permute-start.15 = (bf16[128,640]{1,0:T(8,128)(2,1)S(1)}, bf16[128,640]{1,0:T(8,128)(2,1)S(1)}, u32[]{:S(2)}, u32[]{:S(2)}) collective-permute-start(bf16[128,640]{1,0:T(8,128)(2,1)S(1)} %get-tuple-element.25), channel_id=1, source_target_pairs={{0,4},{4,8},{8,12},{12,0},{1,5},{5,9},{9,13},{13,1},{2,6},{6,10},{... | collective-permute-start | bytes 491528 | tf_op jit(solution)/shard_map/ppermute | solution.py:24
  92.6 20.5 %copy-start.12 = (f32[2,3,80,640]{3,2,1,0:T(8,128)S(1)}, f32[2,3,80,640]{3,2,1,0:T(8,128)}, u32[]{:S(2)}) copy-start(f32[2,3,80,640]{3,2,1,0:T(8,128)} %get-tuple-element.26) | copy-start | bytes 3686404
  92.7 8.9 %collective-permute-start.13 = (bf16[128,640]{1,0:T(8,128)(2,1)S(1)}, bf16[128,640]{1,0:T(8,128)(2,1)S(1)}, u32[]{:S(2)}, u32[]{:S(2)}) collective-permute-start(bf16[128,640]{1,0:T(8,128)(2,1)S(1)} %add_convert_fusion.5), channel_id=1, source_target_pairs={{0,4},{4,8},{8,12},{12,0},{1,5},{5,9},{9,13},{13,1},{2,6},{6,10},{... | collective-permute-start | bytes 491528 | tf_op jit(solution)/shard_map/ppermute | solution.py:24
  96.5 8.1 %collective-permute-start.16 = (bf16[128,640]{1,0:T(8,128)(2,1)S(1)}, bf16[128,640]{1,0:T(8,128)(2,1)S(1)}, u32[]{:S(2)}, u32[]{:S(2)}) collective-permute-start(bf16[128,640]{1,0:T(8,128)(2,1)S(1)} %add_convert_fusion.2), channel_id=1, source_target_pairs={{0,4},{4,8},{8,12},{12,0},{1,5},{5,9},{9,13},{13,1},{2,6},{6,10},{... | collective-permute-start | bytes 491528 | tf_op jit(solution)/shard_map/ppermute | solution.py:24
  101.6 7.6 %collective-permute-start.14 = (bf16[128,640]{1,0:T(8,128)(2,1)S(1)}, bf16[128,640]{1,0:T(8,128)(2,1)S(1)}, u32[]{:S(2)}, u32[]{:S(2)}) collective-permute-start(bf16[128,640]{1,0:T(8,128)(2,1)S(1)} %add_convert_fusion.4), channel_id=1, source_target_pairs={{0,4},{4,8},{8,12},{12,0},{1,5},{5,9},{9,13},{13,1},{2,6},{6,10},{... | collective-permute-start | bytes 491528 | tf_op jit(solution)/shard_map/ppermute | solution.py:24
  104.6 7.7 %collective-permute-start.17 = (bf16[128,640]{1,0:T(8,128)(2,1)S(1)}, bf16[128,640]{1,0:T(8,128)(2,1)S(1)}, u32[]{:S(2)}, u32[]{:S(2)}) collective-permute-start(bf16[128,640]{1,0:T(8,128)(2,1)S(1)} %add_convert_fusion.1), channel_id=1, source_target_pairs={{0,4},{4,8},{8,12},{12,0},{1,5},{5,9},{9,13},{13,1},{2,6},{6,10},{... | collective-permute-start | bytes 491528 | tf_op jit(solution)/shard_map/ppermute | solution.py:24
where the time goes:
time: 115 us
  waiting for transfers between devices  81.3 us (71%)
  Pallas kernels  11.5 us (10%)
  starting transfers between devices  8.43 us (7%)
  other arithmetic  7.2 us (6%)
  local copies, waits for them, and re-layouts  5.36 us (5%)
    ppermute x19, waiting for transfers between devices, ring(): lax.ppermute(value, axis, [(source, (source + steps) % count) for source...  81.3 us
    ppermute x19, starting transfers between devices, ring(): lax.ppermute(value, axis, [(source, (source + steps) % count) for source...  8.43 us
    pallas_call x4, Pallas kernels, apply_step(): pl.pallas_call(apply_body, out_shape=tuple((jax.ShapeDtypeStruct((rows, w...  5.36 us
    pallas_call x1, Pallas kernels, gradient_step(): pl.pallas_call(functools.partial(gradient_body, slots), out_shape=(fresh,...  4.83 us
    sub x1, other arithmetic, tokens_travel(): base = fast_weights - momentum_decay * momentum  4.66 us
    unnamed x28, local copies, waits for them, and re-layouts  3.94 us
  transfers between devices with their start and end apart: 19, of which 14 were waited for; matrix products, arithmetic and copies ran while one was open for 1% of the time, Pallas kernels for 10%

commit v1 on v0

--- a/solution.py
+++ b/solution.py
@@ -124,6 +124,10 @@
     return (layer_output, fast_updated)
 
 
+def in_hbm(value):
+    return pltpu.with_memory_space_constraint(value, pltpu.HBM)
+
+
 def cotangent_body(token_scale, rep, values, rates, out_raw, out):
     heads = rates.shape[0] // 2
     rows, columns = out.shape
@@ -157,20 +161,49 @@
             flops=2 * rows * columns, bytes_accessed=6 * rows * columns, transcendentals=0
         ),
         name="cotangent_step",
-    )(rep, values, rates)
-
-
-def gradient_body(slots, *refs):
+    )(rep, in_hbm(values), in_hbm(rates))
+
+
+def other_body(rep, weights, momentum, low, base):
+    current = weights[...]
+    low[...] = current.astype(jnp.bfloat16)
+    base[...] = current - momentum_decay * momentum[...]
+
+
+def other_step(rep, weights, momentum):
+    heads = weights.shape[0] // 2
+    block = (1,) + weights.shape[1:]
+    made = (heads,) + weights.shape[1:]
+    taken = pl.BlockSpec(block, lambda h, rep: ((1 - rep[0]) * heads + h, 0, 0, 0))
+    given = pl.BlockSpec(block, lambda h, rep: (h, 0, 0, 0))
+    return pl.pallas_call(
+        other_body,
+        out_shape=(pltpu.HBM(made, jnp.bfloat16), pltpu.HBM(made, jnp.float32)),
+        grid_spec=pltpu.PrefetchScalarGridSpec(
+            num_scalar_prefetch=1,
+            grid=(heads,),
+            in_specs=[taken, taken],
+            out_specs=(given, given),
+        ),
+        compiler_params=pltpu.CompilerParams(vmem_limit_bytes=12 << 20),
+        cost_estimate=pl.CostEstimate(
+            flops=weights.size, bytes_accessed=7 * weights.size, transcendentals=0
+        ),
+        name="other_step",
+    )(rep, in_hbm(weights), in_hbm(momentum))
+
+
+def gradient_body(slots, rep, *refs):
     keys, cots = refs[:slots], refs[slots : 2 * slots]
-    low_own, low_par, base_own, base_par, new_own, new_par, new_low, unit, cot, low = refs[2 * slots :]
+    weights, momentum, low_par, base_par, new_own, new_par, new_low, unit, cot, low = refs[2 * slots :]
     rows = keys[0].shape[0]
-    hid = low_own.shape[2]
+    hid = weights.shape[2]
     for s in range(slots):
         here = pl.ds(s * rows, rows)
         unit[here, :] = unit_rows(keys[s][...])
         cot[here, :] = cots[s][...]
     for m in range(3):
-        low[pl.ds(2 * m * hid, hid), :] = low_own[0, m]
+        low[pl.ds(2 * m * hid, hid), :] = weights[0, m].astype(jnp.bfloat16)
         low[pl.ds((2 * m + 1) * hid, hid), :] = low_par[0, m]
     fed = lax.dot_general(low[: 4 * hid, :], unit[...], NT, preferred_element_type=jnp.float32)
     gate, upward = fed[: 2 * hid], fed[2 * hid :]
@@ -182,7 +215,7 @@
     up_back = (back * activated).astype(jnp.bfloat16)
     for m, (left, right) in enumerate(((gate_back, unit), (up_back, unit), (hidden, cot))):
         grad = jnp.dot(left, right[...], preferred_element_type=jnp.float32)
-        fresh_own = base_own[0, m] - grad[:hid]
+        fresh_own = weights[0, m] - (momentum_decay * momentum[0, m] + grad[:hid])
         fresh_par = base_par[0, m] - grad[hid:]
         new_own[0, m] = fresh_own
         new_par[0, m] = fresh_par
@@ -190,25 +223,29 @@
         new_low[0, pl.ds((2 * m + 1) * hid, hid), :] = fresh_par.astype(jnp.bfloat16)
 
 
-def gradient_step(keys, cots, low_own, low_par, base_own, base_par):
+def gradient_step(rep, keys, cots, weights, momentum, low_par, base_par):
     slots = len(keys)
     rows = keys[0].shape[0]
-    heads, _, hid, width = low_own.shape
-    token_spec = pl.BlockSpec((rows, width), lambda h: (0, h))
-    weight_spec = pl.BlockSpec((1, 3, hid, width), lambda h: (h, 0, 0, 0))
-    low_spec = pl.BlockSpec((1, 6 * hid, width), lambda h: (h, 0, 0))
-    fresh = pltpu.HBM(low_own.shape, jnp.float32)
+    heads, _, hid, width = low_par.shape
+    token_spec = pl.BlockSpec((rows, width), lambda h, rep: (0, h))
+    own_spec = pl.BlockSpec((1, 3, hid, width), lambda h, rep: (rep[0] * heads + h, 0, 0, 0))
+    weight_spec = pl.BlockSpec((1, 3, hid, width), lambda h, rep: (h, 0, 0, 0))
+    low_spec = pl.BlockSpec((1, 6 * hid, width), lambda h, rep: (h, 0, 0))
+    fresh = pltpu.HBM(low_par.shape, jnp.float32)
     return pl.pallas_call(
         functools.partial(gradient_body, slots),
         out_shape=(fresh, fresh, jax.ShapeDtypeStruct((heads, 6 * hid, width), jnp.bfloat16)),
-        grid=(heads,),
-        in_specs=[token_spec] * (2 * slots) + [weight_spec] * 4,
-        out_specs=(weight_spec, weight_spec, low_spec),
-        scratch_shapes=[
-            pltpu.VMEM((slots * rows, width), jnp.bfloat16),
-            pltpu.VMEM((slots * rows, width), jnp.bfloat16),
-            pltpu.VMEM((6 * hid, width), jnp.bfloat16),
-        ],
+        grid_spec=pltpu.PrefetchScalarGridSpec(
+            num_scalar_prefetch=1,
+            grid=(heads,),
+            in_specs=[token_spec] * (2 * slots) + [own_spec] * 2 + [weight_spec] * 2,
+            out_specs=(weight_spec, weight_spec, low_spec),
+            scratch_shapes=[
+                pltpu.VMEM((slots * rows, width), jnp.bfloat16),
+                pltpu.VMEM((slots * rows, width), jnp.bfloat16),
+                pltpu.VMEM((6 * hid, width), jnp.bfloat16),
+            ],
+        ),
         compiler_params=pltpu.CompilerParams(vmem_limit_bytes=24 << 20),
         cost_estimate=pl.CostEstimate(
             flops=24 * heads * slots * rows * hid * width,
@@ -216,49 +253,50 @@
             transcendentals=0,
         ),
         name="gradient_step",
-    )(*keys, *cots, low_own, low_par, base_own, base_par)
+    )(rep, *map(in_hbm, (*keys, *cots, weights, momentum, low_par, base_par)))
 
 
 def apply_body(query, low, *refs):
-    heads, total, width = low.shape
-    more, outs = refs[:-heads], refs[-heads:]
-    hid = total // 6
-    for h in range(heads):
-        columns = slice(h * width, (h + 1) * width)
-        unit = unit_rows(query[:, columns])
-        gate = lax.dot_general(unit, low[h, : 2 * hid, :], NT, preferred_element_type=jnp.float32)
-        upward = lax.dot_general(
-            unit, low[h, 2 * hid : 4 * hid, :], NT, preferred_element_type=jnp.float32
-        )
-        hidden = (gate * jax.nn.sigmoid(gate) * upward).astype(jnp.bfloat16)
-        made = jnp.dot(hidden, low[h, 4 * hid :, :], preferred_element_type=jnp.float32)
-        if more:
-            made = made + more[0][:, columns]
-        outs[h][...] = made.astype(outs[h].dtype)
-
-
-def apply_step(query, low, dtype, *more):
-    heads, total, width = low.shape
-    rows = query.shape[0]
+    hid = low.shape[1] // 6
+    unit = unit_rows(query[...])
+    gate = lax.dot_general(unit, low[0, : 2 * hid, :], NT, preferred_element_type=jnp.float32)
+    upward = lax.dot_general(
+        unit, low[0, 2 * hid : 4 * hid, :], NT, preferred_element_type=jnp.float32
+    )
+    hidden = (gate * jax.nn.sigmoid(gate) * upward).astype(jnp.bfloat16)
+    made = jnp.dot(hidden, low[0, 4 * hid :, :], preferred_element_type=jnp.float32)
+    if len(refs) > 1:
+        made = made + refs[0][...]
+    refs[-1][...] = made.astype(refs[-1].dtype)
+
+
+def apply_step(head, query, low, dtype, *more):
+    rows, width = query.shape
+    total = low.shape[1]
+    whole = pl.BlockSpec((rows, width), lambda i: (0, 0))
     return pl.pallas_call(
         apply_body,
-        out_shape=tuple(jax.ShapeDtypeStruct((rows, width), dtype) for _ in range(heads)),
+        out_shape=jax.ShapeDtypeStruct((rows, width), dtype),
+        grid=(1,),
+        in_specs=[whole, pl.BlockSpec((1, total, width), lambda i: (head, 0, 0))]
+        + [whole] * len(more),
+        out_specs=whole,
         compiler_params=pltpu.CompilerParams(vmem_limit_bytes=8 << 20),
         cost_estimate=pl.CostEstimate(
-            flops=2 * rows * heads * total * width,
-            bytes_accessed=2 * heads * total * width,
-            transcendentals=0,
+            flops=2 * rows * total * width, bytes_accessed=2 * total * width, transcendentals=0
         ),
         name="apply_step",
     )(query, low, *more)
 
 
-def attend_body(heads, token_scale, first, query, key_own, key_prior, value_own, cot_prior, rate_prior, out):
-    width = query.shape[1] // heads
+def attend_body(token_scale, first, key_own, key_prior, value_own, cot_prior, rate_prior, *refs):
+    heads = len(refs) // 2
+    asked, outs = refs[:heads], refs[heads:]
+    width = asked[0].shape[1]
     allowed = jnp.where(first[0] != 0, -jnp.inf, 0.0).astype(jnp.float32)
     for h in range(heads):
         columns = slice(h * width, (h + 1) * width)
-        part = query[:, columns]
+        part = asked[h][...]
         near = lax.dot_general(part, key_own[:, columns], NT, preferred_element_type=jnp.float32)
         far = lax.dot_general(part, key_prior[:, columns], NT, preferred_element_type=jnp.float32)
         near = near * width ** (-0.5)
@@ -272,24 +310,24 @@
         rate = -(rate_prior[h] * token_scale)
         near = (near / total).astype(jnp.bfloat16)
         far = (far / total / rate).astype(jnp.bfloat16)
-        out[:, columns] = jnp.dot(
+        outs[h][...] = jnp.dot(
             near, value_own[:, columns], preferred_element_type=jnp.float32
         ) + jnp.dot(far, cot_prior[:, columns], preferred_element_type=jnp.float32)
 
 
-def attend_step(token_scale, first, query, key_own, key_prior, value_own, cot_prior, rate_prior):
-    rows, columns = query.shape
+def attend_step(token_scale, first, key_own, key_prior, value_own, cot_prior, rate_prior, asked):
+    rows, columns = key_own.shape
+    made = tuple(jax.ShapeDtypeStruct(query.shape, jnp.float32) for query in asked)
     return pl.pallas_call(
-        functools.partial(attend_body, rate_prior.shape[0], token_scale),
-        out_shape=jax.ShapeDtypeStruct(query.shape, jnp.float32),
-        in_specs=[pl.BlockSpec(memory_space=pltpu.SMEM)] + [pl.BlockSpec()] * 6,
-        out_specs=pl.BlockSpec(),
+        functools.partial(attend_body, token_scale),
+        out_shape=made,
+        in_specs=[pl.BlockSpec(memory_space=pltpu.SMEM)] + [pl.BlockSpec()] * (5 + len(asked)),
         compiler_params=pltpu.CompilerParams(vmem_limit_bytes=8 << 20),
         cost_estimate=pl.CostEstimate(
             flops=8 * rows * rows * columns, bytes_accessed=14 * rows * columns, transcendentals=0
         ),
         name="attend_step",
-    )(first, query, key_own, key_prior, value_own, cot_prior, rate_prior)
+    )(first, *map(in_hbm, (key_own, key_prior, value_own, cot_prior)), rate_prior, *asked)
 
 
 def tokens_travel(queries, key_vectors, values, learn_rates, fast_weights, momentum):
@@ -298,53 +336,48 @@
     per_rep = fast_weights.shape[0] // 2
     rep_index = lax.axis_index("rep")
     start = rep_index * per_rep
-    away = per_rep - start
     token_scale = float(slots * queries.shape[0]) ** (-0.5)
 
     def own_columns(tensor):
         return lax.dynamic_slice_in_dim(tensor, start * width, per_rep * width, 1)
 
-    def own(tensor):
-        return lax.dynamic_slice_in_dim(tensor, start, per_rep, 0)
-
-    def other(tensor):
-        return lax.dynamic_slice_in_dim(tensor, away, per_rep, 0)
-
     def hop(value, axis="ctx"):
         return ring(value, axis)
 
-    value_own, cot = cotangent_step(token_scale, rep_index.reshape(1), values, learn_rates)
-    keys, cots, asked = [own_columns(key_vectors)], [cot], [own_columns(queries)]
+    rep = rep_index.reshape(1)
+    value_own, cot = cotangent_step(token_scale, rep, values, learn_rates)
+    heads = range(per_rep)
+    keys, cots = [own_columns(key_vectors)], [cot]
+    asked = [[lax.dynamic_slice_in_dim(queries, (start + h) * width, width, 1) for h in heads]]
     for _ in range(1, slots):
         keys.append(hop(keys[-1]))
         cots.append(hop(cots[-1]))
-    rate_prior = hop(own(learn_rates)[:, None, :])
-    base = fast_weights - momentum_decay * momentum
-    low = fast_weights.astype(jnp.bfloat16)
-    low_par = hop(other(low), "rep")
-    base_par = hop(other(base), "rep")
+    rate_prior = hop(lax.dynamic_slice_in_dim(learn_rates, start, per_rep, 0)[:, None, :])
+    low_other, base_other = other_step(rep, fast_weights, momentum)
+    low_par = hop(low_other, "rep")
+    base_par = hop(base_other, "rep")
     for _ in range(1, slots):
-        asked.append(hop(asked[-1]))
+        asked.append([hop(asked[-1][h]) for h in heads])
     first = (lax.axis_index("ctx") == 0).astype(jnp.int32).reshape(1)
     attended = attend_step(
-        token_scale, first, asked[0], keys[0], keys[1], value_own, cots[1], rate_prior
-    )
-    own_low, own_base = own(low), own(base)
+        token_scale, first, keys[0], keys[1], value_own, cots[1], rate_prior, asked[0]
+    )
     new_own, new_par, new_low = gradient_step(
-        keys, cots, own_low, low_par, own_base, base_par
-    )
-    heads = range(per_rep)
+        rep, keys, cots, fast_weights, momentum, low_par, base_par
+    )
     moving = []
     for step in range(1, slots):
         if step == 1:
-            sent = apply_step(asked[step], new_low, jnp.bfloat16)
+            sent = [apply_step(h, asked[step][h], new_low, jnp.bfloat16) for h in heads]
         else:
-            made = apply_step(asked[step], new_low, jnp.float32)
+            made = [apply_step(h, asked[step][h], new_low, jnp.float32) for h in heads]
             sent = [
                 (made[h] + moving[h].astype(jnp.float32)).astype(jnp.bfloat16) for h in heads
             ]
         moving = [hop(sent[h]) for h in heads]
-    kept = apply_step(asked[0], new_low, jnp.float32, attended)
+    kept = []
+    for h in heads:
+        kept.append(apply_step(h, asked[0][h], new_low, jnp.float32, attended[h]))
     layer_output = jnp.concatenate(
         [(kept[h] + moving[h].astype(jnp.float32)).astype(jnp.bfloat16) for h in heads], axis=1
     )

time: 115 us -> 113 us (0.983)
  starting transfers between devices: 8.43 us -> 18.4 us
  waiting for transfers between devices: 81.3 us -> 74.1 us
  other arithmetic: 7.2 us -> 2.58 us
  Pallas kernels: 11.5 us -> 16.1 us
  local copies, waits for them, and re-layouts: 5.36 us -> 1.09 us
    ppermute x19 -> x22, starting transfers between devices: 8.43 us -> 18.4 us  [ring(): lax.ppermute(value, axis, [(source, (source + steps) % count) for source...]
    ppermute x19 -> x22, waiting for transfers between devices: 81.3 us -> 74.1 us  [ring(): lax.ppermute(value, axis, [(source, (source + steps) % count) for source...]
    sub x1 -> x0, other arithmetic: 4.66 us -> none  [tokens_travel(): base = fast_weights - momentum_decay * momentum]
    unnamed x28 -> x16, local copies, waits for them, and re-layouts: 3.94 us -> 0.04 us
    pallas_call x5 -> x10, Pallas kernels: 6.51 us -> 9.21 us  [the longest x8 4.05 us: apply_step(): pl.pallas_call(apply_body, out_shape=jax.ShapeDtypeStruct((rows, width),...]
  transfers between devices with their start and end apart: 19 -> 22, of which waited for: 14 -> 12; matrix products, arithmetic and copies ran while one was open for 1% -> 2% of each run, Pallas kernels for 10% -> 12%
where the time goes in v1:
time: 113 us
  waiting for transfers between devices  74.1 us (66%)
  starting transfers between devices  18.4 us (16%)
  Pallas kernels  16.1 us (14%)
  other arithmetic  2.58 us (2%)
    ppermute x22, waiting for transfers between devices, ring(): lax.ppermute(value, axis, [(source, (source + steps) % count) for source...  74.1 us
    ppermute x22, starting transfers between devices, ring(): lax.ppermute(value, axis, [(source, (source + steps) % count) for source...  18.4 us
    pallas_call x1, Pallas kernels, gradient_step(): pl.pallas_call(functools.partial(gradient_body, slots), out_shape=(fresh,...  5.75 us
    pallas_call x8, Pallas kernels, apply_step(): pl.pallas_call(apply_body, out_shape=jax.ShapeDtypeStruct((rows, width),...  4.05 us
    pallas_call x1, Pallas kernels, other_step(): pl.pallas_call(other_body, out_shape=(pltpu.HBM(made, jnp.bfloat16), pltp...  2.74 us
    pallas_call x1, Pallas kernels, attend_step(): pl.pallas_call(functools.partial(attend_body, token_scale), out_shape=mad...  2.41 us
  transfers between devices with their start and end apart: 22, of which 12 were waited for; matrix products, arithmetic and copies ran while one was open for 2% of the time, Pallas kernels for 12%

profile of v1, /device:TPU:0, one launch (start us, length us, event | category | flops | bytes accessed | tf_op | source)
XLA Modules:
  0.0 113.2 jit_solution(17078947521188736443)
XLA Ops:
  0.6 0.0 copy-start
  0.6 2.7 %other_step.1 = (bf16[2,3,80,640]{3,2,1,0:T(8,128)(2,1)}, f32[2,3,80,640]{3,2,1,0:T(8,128)}) custom-call(s32[1]{0:T(128)} %bitcast.rep, f32[4,3,80,640]{3,2,1,0:T(8,128)} %refs_8_.1, f32[4,3,80,640]{3,2,1,0:T(8,128)} %refs_9_.1), custom_call_target="tpu_custom_call" | custom-call | flops 614400 | bytes 4300800 | tf_op jit(solution)/shard_map/other_step/pallas_call | solution.py:179
  3.4 0.5 collective-permute-start.7
  3.9 0.0 copy-done
  3.9 0.0 copy-start.3
  3.9 2.6 %collective-permute-start = (bf16[128,1280]{1,0:T(8,128)(2,1)S(1)}, bf16[128,1280]{1,0:T(8,128)(2,1)S(1)}, u32[]{:S(2)}, u32[]{:S(2)}) collective-permute-start(bf16[128,1280]{1,0:T(8,128)(2,1)S(1)} %constant_dynamic-slice_fusion.2.refs_0_.key_own), channel_id=1, source_target_pairs={{0,4},{4,8},{8,12},{12,0},{1,5},{5,9},{9,13},{13,1},{2,6},{6,10},{... | collective-permute-start | bytes 983048 | tf_op jit(solution)/shard_map/ppermute | solution.py:24
  6.6 1.2 %cotangent_step.1 = (bf16[128,1280]{1,0:T(8,128)(2,1)S(1)}, bf16[128,1280]{1,0:T(8,128)(2,1)S(1)}) custom-call(s32[1]{0:T(128)} %bitcast.rep, bf16[128,2560]{1,0:T(8,128)(2,1)} %values.1, f32[4,128]{1,0:T(4,128)} %rates.1), custom_call_target="tpu_custom_call" | custom-call | flops 327680 | bytes 983040 | tf_op jit(solution)/shard_map/cotangent_step/pallas_call | solution.py:147
  7.7 0.0 copy-start.2
  7.7 1.6 %collective-permute-start.3 = (bf16[128,1280]{1,0:T(8,128)(2,1)S(1)}, bf16[128,1280]{1,0:T(8,128)(2,1)S(1)}, u32[]{:S(2)}, u32[]{:S(2)}) collective-permute-start(bf16[128,1280]{1,0:T(8,128)(2,1)S(1)} %get-tuple-element.11.refs_4_), channel_id=1, source_target_pairs={{0,4},{4,8},{8,12},{12,0},{1,5},{5,9},{9,13},{13,1},{2,6},{6,10},{... | collective-permute-start | bytes 983048 | tf_op jit(solution)/shard_map/ppermute | solution.py:24
  9.4 1.0 constant_dynamic-slice_fusion.3
  10.4 1.6 %collective-permute-start.9 = (bf16[128,640]{1,0:T(8,128)(2,1)S(1)}, bf16[128,640]{1,0:T(8,128)(2,1)S(1)}, u32[]{:S(2)}, u32[]{:S(2)}) collective-permute-start(bf16[128,640]{1,0:T(8,128)(2,1)S(1)} %get-tuple-element.20.refs_0_.query), channel_id=1, source_target_pairs={{0,4},{4,8},{8,12},{12,0},{1,5},{5,9},{9,13},{13,1},{2,6},{6,10},{... | collective-permute-start | bytes 491528 | tf_op jit(solution)/shard_map/ppermute | solution.py:24
  12.0 5.1 %collective-permute-done.refs_1_.key_prior = bf16[128,1280]{1,0:T(8,128)(2,1)S(1)} collective-permute-done((bf16[128,1280]{1,0:T(8,128)(2,1)S(1)}, bf16[128,1280]{1,0:T(8,128)(2,1)S(1)}, u32[]{:S(2)}, u32[]{:S(2)}) %collective-permute-start) | collective-permute-done | bytes 327712 | tf_op jit(solution)/shard_map/ppermute | solution.py:24
  17.1 0.0 collective-permute-start.1
  17.1 7.0 %collective-permute-done.3.refs_5_.cot_prior = bf16[128,1280]{1,0:T(8,128)(2,1)S(1)} collective-permute-done((bf16[128,1280]{1,0:T(8,128)(2,1)S(1)}, bf16[128,1280]{1,0:T(8,128)(2,1)S(1)}, u32[]{:S(2)}, u32[]{:S(2)}) %collective-permute-start.3) | collective-permute-done | bytes 327712 | tf_op jit(solution)/shard_map/ppermute | solution.py:24
  24.2 0.0 collective-permute-start.4
  24.2 0.0 collective-permute-start.6
  24.2 3.5 %collective-permute-done.9.query = bf16[128,640]{1,0:T(8,128)(2,1)S(1)} collective-permute-done((bf16[128,640]{1,0:T(8,128)(2,1)S(1)}, bf16[128,640]{1,0:T(8,128)(2,1)S(1)}, u32[]{:S(2)}, u32[]{:S(2)}) %collective-permute-start.9) | collective-permute-done | bytes 163872 | tf_op jit(solution)/shard_map/ppermute | solution.py:24
  27.7 0.0 collective-permute-start.15
  27.7 17.4 %collective-permute-done.15.query = bf16[128,640]{1,0:T(8,128)(2,1)S(1)} collective-permute-done((bf16[128,640]{1,0:T(8,128)(2,1)S(1)}, bf16[128,640]{1,0:T(8,128)(2,1)S(1)}, u32[]{:S(2)}, u32[]{:S(2)}) %collective-permute-start.15) | collective-permute-done | bytes 163872 | tf_op jit(solution)/shard_map/ppermute | solution.py:24
  45.0 0.0 collective-permute-start.10
  45.0 0.0 collective-permute-done.1.refs_2_
  45.0 1.3 %collective-permute-start.2 = (bf16[128,1280]{1,0:T(8,128)(2,1)}, bf16[128,1280]{1,0:T(8,128)(2,1)}, u32[]{:S(2)}, u32[]{:S(2)}) collective-permute-start(bf16[128,1280]{1,0:T(8,128)(2,1)} %collective-permute-done.1.refs_2_), channel_id=1, source_target_pairs={{0,4},{4,8},{8,12},{12,0},{1,5},{5,9},{9,13},{13,1},{2,6},{6,10},{... | collective-permute-start | bytes 983048 | tf_op jit(solution)/shard_map/ppermute | solution.py:24
  46.3 0.0 collective-permute-done.4.refs_6_
  46.3 1.6 %collective-permute-start.5 = (bf16[128,1280]{1,0:T(8,128)(2,1)}, bf16[128,1280]{1,0:T(8,128)(2,1)}, u32[]{:S(2)}, u32[]{:S(2)}) collective-permute-start(bf16[128,1280]{1,0:T(8,128)(2,1)} %collective-permute-done.4.refs_6_), channel_id=1, source_target_pairs={{0,4},{4,8},{8,12},{12,0},{1,5},{5,9},{9,13},{13,1},{2,6},{6,10},{... | collective-permute-start | bytes 983048 | tf_op jit(solution)/shard_map/ppermute | solution.py:24
  47.9 6.0 %collective-permute-done.10.query = bf16[128,640]{1,0:T(8,128)(2,1)S(1)} collective-permute-done((bf16[128,640]{1,0:T(8,128)(2,1)S(1)}, bf16[128,640]{1,0:T(8,128)(2,1)S(1)}, u32[]{:S(2)}, u32[]{:S(2)}) %collective-permute-start.10) | collective-permute-done | bytes 163872 | tf_op jit(solution)/shard_map/ppermute | solution.py:24
  53.9 0.0 collective-permute-start.16
  53.9 16.5 %collective-permute-done.16.query = bf16[128,640]{1,0:T(8,128)(2,1)S(1)} collective-permute-done((bf16[128,640]{1,0:T(8,128)(2,1)S(1)}, bf16[128,640]{1,0:T(8,128)(2,1)S(1)}, u32[]{:S(2)}, u32[]{:S(2)}) %collective-permute-start.16) | collective-permute-done | bytes 163872 | tf_op jit(solution)/shard_map/ppermute | solution.py:24
  70.4 0.0 collective-permute-start.11
  70.4 0.0 collective-permute-done.6.refs_10_
  70.4 0.0 collective-permute-start.17
  70.4 0.0 collective-permute-done.2.refs_3_
  70.4 0.0 collective-permute-done.5.refs_7_
  70.5 0.0 collective-permute-done.7.refs_11_
  70.5 5.8 %gradient_step.1 = (f32[2,3,80,640]{3,2,1,0:T(8,128)}, f32[2,3,80,640]{3,2,1,0:T(8,128)}, bf16[2,480,640]{2,1,0:T(8,128)(2,1)S(1)}) custom-call(s32[1]{0:T(128)} %bitcast.rep, bf16[128,1280]{1,0:T(8,128)(2,1)} %copy-done.3, bf16[128,1280]{1,0:T(8,128)(2,1)} %copy-done.4, bf16[128,1280]{1,0:T(8,128)(2,1)} %collective-permute-done.1.refs_2_, ...), custom_call_target="tpu_custom_call" | custom-call | flops 1258291200 | bytes 4915200 | tf_op jit(solution)/shard_map/gradient_step/pallas_call | solution.py:235
  76.3 0.5 apply_step.11
  76.8 0.8 collective-permute-start.12
  77.6 4.2 %collective-permute-start.8 = (f32[2,1,128]{2,1,0:T(1,128)S(1)}, f32[2,1,128]{2,1,0:T(1,128)S(1)}, u32[]{:S(2)}, u32[]{:S(2)}) collective-permute-start(f32[2,1,128]{2,1,0:T(1,128)S(1)} %bitcast.3), channel_id=1, source_target_pairs={{0,4},{4,8},{8,12},{12,0},{1,5},{5,9},{9,13},{13,1},{2,6},{6,10},{... | collective-permute-start | bytes 3080 | tf_op jit(solution)/shard_map/ppermute | solution.py:24
  81.8 2.7 %collective-permute-done.8.rate_prior = f32[2,1,128]{2,1,0:T(1,128)S(1)} collective-permute-done((f32[2,1,128]{2,1,0:T(1,128)S(1)}, f32[2,1,128]{2,1,0:T(1,128)S(1)}, u32[]{:S(2)}, u32[]{:S(2)}) %collective-permute-start.8) | collective-permute-done | bytes 1056 | tf_op jit(solution)/shard_map/ppermute | solution.py:24
  84.5 2.4 %attend_step.1 = (f32[128,640]{1,0:T(8,128)S(1)}, f32[128,640]{1,0:T(8,128)S(1)}) custom-call(s32[1]{0:T(128)} %bitcast.1.first, bf16[128,1280]{1,0:T(8,128)(2,1)} %copy-done.3, bf16[128,1280]{1,0:T(8,128)(2,1)} %copy-done.4, bf16[128,1280]{1,0:T(8,128)(2,1)} %copy-done.2, bf16[128,1280]{1,0:T(8,128)(2,1)} %copy-done.5, ...), custom_call_target="tpu_custom_call" | custom-call | flops 167772160 | bytes 2293760 | tf_op jit(solution)/shard_map/attend_step/pallas_call | solution.py:321
  86.9 0.1 collective-permute-start.21
  87.0 0.5 apply_step.15
  87.5 1.0 collective-permute-start.18
  88.4 0.5 apply_step.8
  88.9 0.5 apply_step.12
  89.5 0.5 apply_step.10
  90.0 0.5 apply_step.14
  90.5 0.0 collective-permute-done.11.query
  90.5 0.5 apply_step.9
  91.0 0.0 collective-permute-done.17.query
  91.0 0.5 apply_step.13
  91.5 0.0 copy-start.6
  91.5 0.0 collective-permute-done.12
  91.6 1.8 %collective-permute-start.13 = (bf16[128,640]{1,0:T(8,128)(2,1)S(1)}, bf16[128,640]{1,0:T(8,128)(2,1)S(1)}, u32[]{:S(2)}, u32[]{:S(2)}) collective-permute-start(bf16[128,640]{1,0:T(8,128)(2,1)S(1)} %add_convert_fusion.5), channel_id=1, source_target_pairs={{0,4},{4,8},{8,12},{12,0},{1,5},{5,9},{9,13},{13,1},{2,6},{6,10},{... | collective-permute-start | bytes 491528 | tf_op jit(solution)/shard_map/ppermute | solution.py:24
  93.4 2.5 %collective-permute-done.18 = bf16[128,640]{1,0:T(8,128)(2,1)S(1)} collective-permute-done((bf16[128,640]{1,0:T(8,128)(2,1)S(1)}, bf16[128,640]{1,0:T(8,128)(2,1)S(1)}, u32[]{:S(2)}, u32[]{:S(2)}) %collective-permute-start.18) | collective-permute-done | bytes 163872 | tf_op jit(solution)/shard_map/ppermute | solution.py:24
  96.0 0.1 collective-permute-start.19
  96.0 3.7 %collective-permute-done.13 = bf16[128,640]{1,0:T(8,128)(2,1)S(1)} collective-permute-done((bf16[128,640]{1,0:T(8,128)(2,1)S(1)}, bf16[128,640]{1,0:T(8,128)(2,1)S(1)}, u32[]{:S(2)}, u32[]{:S(2)}) %collective-permute-start.13) | collective-permute-done | bytes 163872 | tf_op jit(solution)/shard_map/ppermute | solution.py:24
  99.8 0.8 collective-permute-start.14
  100.6 3.0 %collective-permute-done.19 = bf16[128,640]{1,0:T(8,128)(2,1)S(1)} collective-permute-done((bf16[128,640]{1,0:T(8,128)(2,1)S(1)}, bf16[128,640]{1,0:T(8,128)(2,1)S(1)}, u32[]{:S(2)}, u32[]{:S(2)}) %collective-permute-start.19) | collective-permute-done | bytes 163872 | tf_op jit(solution)/shard_map/ppermute | solution.py:24
  103.6 0.5 collective-permute-start.20
  104.1 3.4 %collective-permute-done.14 = bf16[128,640]{1,0:T(8,128)(2,1)S(1)} collective-permute-done((bf16[128,640]{1,0:T(8,128)(2,1)S(1)}, bf16[128,640]{1,0:T(8,128)(2,1)S(1)}, u32[]{:S(2)}, u32[]{:S(2)}) %collective-permute-start.14) | collective-permute-done | bytes 163872 | tf_op jit(solution)/shard_map/ppermute | solution.py:24
  107.5 3.3 %collective-permute-done.20 = bf16[128,640]{1,0:T(8,128)(2,1)S(1)} collective-permute-done((bf16[128,640]{1,0:T(8,128)(2,1)S(1)}, bf16[128,640]{1,0:T(8,128)(2,1)S(1)}, u32[]{:S(2)}, u32[]{:S(2)}) %collective-permute-start.20) | collective-permute-done | bytes 163872 | tf_op jit(solution)/shard_map/ppermute | solution.py:24
  110.8 0.8 pad_maximum_fusion
  111.5 0.0 collective-permute-done.21
  111.6 1.6 %maximum_select_fusion = f32[4,3,80,640]{3,2,1,0:T(8,128)} fusion(f32[2,3,80,640]{3,2,1,0:T(8,128)S(1)} %collective-permute-done.21, f32[2,3,80,640]{3,2,1,0:T(8,128)S(1)} %copy-done.6, pred[]{:T(512)S(6)} %eq.7), kind=kLoop, calls=%fused_computation | loop fusion | flops 1843200 | bytes 4915201 | tf_op jit(solution)/shard_map/jit(_where)/select_n | solution.py:385
  (19 shorter events, 0.3 us)
Async XLA Ops:
  0.6 3.3 %copy-start = (bf16[128,2560]{1,0:T(8,128)(2,1)S(1)}, bf16[128,2560]{1,0:T(8,128)(2,1)}, u32[]{:S(2)}) copy-start(bf16[128,2560]{1,0:T(8,128)(2,1)} %param.7) | copy-start | bytes 1966084
  3.4 67.1 %collective-permute-start.7 = (f32[2,3,80,640]{3,2,1,0:T(8,128)}, f32[2,3,80,640]{3,2,1,0:T(8,128)}, u32[]{:S(2)}, u32[]{:S(2)}) collective-permute-start(f32[2,3,80,640]{3,2,1,0:T(8,128)} %get-tuple-element.13), channel_id=1, source_target_pairs={{0,1},{1,0},{2,3},{3,2},{4,5},{5,4},{6,7},{7,6},{8,9},{9,8},{10,11... | collective-permute-start | bytes 3686408 | tf_op jit(solution)/shard_map/ppermute | solution.py:24
  3.9 66.5 %copy-start.3 = (bf16[128,1280]{1,0:T(8,128)(2,1)}, bf16[128,1280]{1,0:T(8,128)(2,1)S(1)}, u32[]{:S(2)}) copy-start(bf16[128,1280]{1,0:T(8,128)(2,1)S(1)} %constant_dynamic-slice_fusion.2.refs_0_.key_own) | copy-start | bytes 983044
  3.9 13.2 %collective-permute-start = (bf16[128,1280]{1,0:T(8,128)(2,1)S(1)}, bf16[128,1280]{1,0:T(8,128)(2,1)S(1)}, u32[]{:S(2)}, u32[]{:S(2)}) collective-permute-start(bf16[128,1280]{1,0:T(8,128)(2,1)S(1)} %constant_dynamic-slice_fusion.2.refs_0_.key_own), channel_id=1, source_target_pairs={{0,4},{4,8},{8,12},{12,0},{1,5},{5,9},{9,13},{13,1},{2,6},{6,10},{... | collective-permute-start | bytes 983048 | tf_op jit(solution)/shard_map/ppermute | solution.py:24
  7.7 62.7 %copy-start.2 = (bf16[128,1280]{1,0:T(8,128)(2,1)}, bf16[128,1280]{1,0:T(8,128)(2,1)S(1)}, u32[]{:S(2)}) copy-start(bf16[128,1280]{1,0:T(8,128)(2,1)S(1)} %get-tuple-element.15.value_own) | copy-start | bytes 983044
  7.7 62.8 %copy-start.1 = (bf16[128,1280]{1,0:T(8,128)(2,1)}, bf16[128,1280]{1,0:T(8,128)(2,1)S(1)}, u32[]{:S(2)}) copy-start(bf16[128,1280]{1,0:T(8,128)(2,1)S(1)} %get-tuple-element.11.refs_4_) | copy-start | bytes 983044
  7.7 16.4 %collective-permute-start.3 = (bf16[128,1280]{1,0:T(8,128)(2,1)S(1)}, bf16[128,1280]{1,0:T(8,128)(2,1)S(1)}, u32[]{:S(2)}, u32[]{:S(2)}) collective-permute-start(bf16[128,1280]{1,0:T(8,128)(2,1)S(1)} %get-tuple-element.11.refs_4_), channel_id=1, source_target_pairs={{0,4},{4,8},{8,12},{12,0},{1,5},{5,9},{9,13},{13,1},{2,6},{6,10},{... | collective-permute-start | bytes 983048 | tf_op jit(solution)/shard_map/ppermute | solution.py:24
  10.4 17.3 %collective-permute-start.9 = (bf16[128,640]{1,0:T(8,128)(2,1)S(1)}, bf16[128,640]{1,0:T(8,128)(2,1)S(1)}, u32[]{:S(2)}, u32[]{:S(2)}) collective-permute-start(bf16[128,640]{1,0:T(8,128)(2,1)S(1)} %get-tuple-element.20.refs_0_.query), channel_id=1, source_target_pairs={{0,4},{4,8},{8,12},{12,0},{1,5},{5,9},{9,13},{13,1},{2,6},{6,10},{... | collective-permute-start | bytes 491528 | tf_op jit(solution)/shard_map/ppermute | solution.py:24
  17.1 53.3 %copy-start.4 = (bf16[128,1280]{1,0:T(8,128)(2,1)}, bf16[128,1280]{1,0:T(8,128)(2,1)S(1)}, u32[]{:S(2)}) copy-start(bf16[128,1280]{1,0:T(8,128)(2,1)S(1)} %collective-permute-done.refs_1_.key_prior) | copy-start | bytes 983044
  17.1 27.9 %collective-permute-start.1 = (bf16[128,1280]{1,0:T(8,128)(2,1)S(1)}, bf16[128,1280]{1,0:T(8,128)(2,1)}, u32[]{:S(2)}, u32[]{:S(2)}) collective-permute-start(bf16[128,1280]{1,0:T(8,128)(2,1)S(1)} %collective-permute-done.refs_1_.key_prior), channel_id=1, source_target_pairs={{0,4},{4,8},{8,12},{12,0},{1,5},{5,9},{9,13},{13,1},{2,6},{6,10},{... | collective-permute-start | bytes 983048 | tf_op jit(solution)/shard_map/ppermute | solution.py:24
  24.2 23.8 %copy-start.5 = (bf16[128,1280]{1,0:T(8,128)(2,1)}, bf16[128,1280]{1,0:T(8,128)(2,1)S(1)}, u32[]{:S(2)}) copy-start(bf16[128,1280]{1,0:T(8,128)(2,1)S(1)} %collective-permute-done.3.refs_5_.cot_prior) | copy-start | bytes 983044
  24.2 22.2 %collective-permute-start.4 = (bf16[128,1280]{1,0:T(8,128)(2,1)S(1)}, bf16[128,1280]{1,0:T(8,128)(2,1)}, u32[]{:S(2)}, u32[]{:S(2)}) collective-permute-start(bf16[128,1280]{1,0:T(8,128)(2,1)S(1)} %collective-permute-done.3.refs_5_.cot_prior), channel_id=1, source_target_pairs={{0,4},{4,8},{8,12},{12,0},{1,5},{5,9},{9,13},{13,1},{2,6},{6,10},{... | collective-permute-start | bytes 983048 | tf_op jit(solution)/shard_map/ppermute | solution.py:24
  24.2 46.3 %collective-permute-start.6 = (bf16[2,3,80,640]{3,2,1,0:T(8,128)(2,1)}, bf16[2,3,80,640]{3,2,1,0:T(8,128)(2,1)}, u32[]{:S(2)}, u32[]{:S(2)}) collective-permute-start(bf16[2,3,80,640]{3,2,1,0:T(8,128)(2,1)} %get-tuple-element.12), channel_id=1, source_target_pairs={{0,1},{1,0},{2,3},{3,2},{4,5},{5,4},{6,7},{7,6},{8,9},{9,8},{10,11... | collective-permute-start | bytes 1843208 | tf_op jit(solution)/shard_map/ppermute | solution.py:24
  27.7 17.4 %collective-permute-start.15 = (bf16[128,640]{1,0:T(8,128)(2,1)S(1)}, bf16[128,640]{1,0:T(8,128)(2,1)S(1)}, u32[]{:S(2)}, u32[]{:S(2)}) collective-permute-start(bf16[128,640]{1,0:T(8,128)(2,1)S(1)} %get-tuple-element.21.refs_1_.query), channel_id=1, source_target_pairs={{0,4},{4,8},{8,12},{12,0},{1,5},{5,9},{9,13},{13,1},{2,6},{6,10},{... | collective-permute-start | bytes 491528 | tf_op jit(solution)/shard_map/ppermute | solution.py:24
  45.0 8.9 %collective-permute-start.10 = (bf16[128,640]{1,0:T(8,128)(2,1)S(1)}, bf16[128,640]{1,0:T(8,128)(2,1)S(1)}, u32[]{:S(2)}, u32[]{:S(2)}) collective-permute-start(bf16[128,640]{1,0:T(8,128)(2,1)S(1)} %collective-permute-done.9.query), channel_id=1, source_target_pairs={{0,4},{4,8},{8,12},{12,0},{1,5},{5,9},{9,13},{13,1},{2,6},{6,10},{... | collective-permute-start | bytes 491528 | tf_op jit(solution)/shard_map/ppermute | solution.py:24
  45.0 25.4 %collective-permute-start.2 = (bf16[128,1280]{1,0:T(8,128)(2,1)}, bf16[128,1280]{1,0:T(8,128)(2,1)}, u32[]{:S(2)}, u32[]{:S(2)}) collective-permute-start(bf16[128,1280]{1,0:T(8,128)(2,1)} %collective-permute-done.1.refs_2_), channel_id=1, source_target_pairs={{0,4},{4,8},{8,12},{12,0},{1,5},{5,9},{9,13},{13,1},{2,6},{6,10},{... | collective-permute-start | bytes 983048 | tf_op jit(solution)/shard_map/ppermute | solution.py:24
  46.3 24.1 %collective-permute-start.5 = (bf16[128,1280]{1,0:T(8,128)(2,1)}, bf16[128,1280]{1,0:T(8,128)(2,1)}, u32[]{:S(2)}, u32[]{:S(2)}) collective-permute-start(bf16[128,1280]{1,0:T(8,128)(2,1)} %collective-permute-done.4.refs_6_), channel_id=1, source_target_pairs={{0,4},{4,8},{8,12},{12,0},{1,5},{5,9},{9,13},{13,1},{2,6},{6,10},{... | collective-permute-start | bytes 983048 | tf_op jit(solution)/shard_map/ppermute | solution.py:24
  53.9 16.5 %collective-permute-start.16 = (bf16[128,640]{1,0:T(8,128)(2,1)S(1)}, bf16[128,640]{1,0:T(8,128)(2,1)S(1)}, u32[]{:S(2)}, u32[]{:S(2)}) collective-permute-start(bf16[128,640]{1,0:T(8,128)(2,1)S(1)} %collective-permute-done.15.query), channel_id=1, source_target_pairs={{0,4},{4,8},{8,12},{12,0},{1,5},{5,9},{9,13},{13,1},{2,6},{6,10},{... | collective-permute-start | bytes 491528 | tf_op jit(solution)/shard_map/ppermute | solution.py:24
  53.9 23.7 %copy-start.7 = (f32[4,128]{1,0:T(4,128)S(1)}, f32[4,128]{1,0:T(4,128)}, u32[]{:S(2)}) copy-start(f32[4,128]{1,0:T(4,128)} %rates.1) | copy-start | bytes 6148
  70.4 20.1 %collective-permute-start.11 = (bf16[128,640]{1,0:T(8,128)(2,1)S(1)}, bf16[128,640]{1,0:T(8,128)(2,1)S(1)}, u32[]{:S(2)}, u32[]{:S(2)}) collective-permute-start(bf16[128,640]{1,0:T(8,128)(2,1)S(1)} %collective-permute-done.10.query), channel_id=1, source_target_pairs={{0,4},{4,8},{8,12},{12,0},{1,5},{5,9},{9,13},{13,1},{2,6},{6,10},{... | collective-permute-start | bytes 491528 | tf_op jit(solution)/shard_map/ppermute | solution.py:24
  70.4 20.6 %collective-permute-start.17 = (bf16[128,640]{1,0:T(8,128)(2,1)S(1)}, bf16[128,640]{1,0:T(8,128)(2,1)S(1)}, u32[]{:S(2)}, u32[]{:S(2)}) collective-permute-start(bf16[128,640]{1,0:T(8,128)(2,1)S(1)} %collective-permute-done.16.query), channel_id=1, source_target_pairs={{0,4},{4,8},{8,12},{12,0},{1,5},{5,9},{9,13},{13,1},{2,6},{6,10},{... | collective-permute-start | bytes 491528 | tf_op jit(solution)/shard_map/ppermute | solution.py:24
  76.8 14.8 %collective-permute-start.12 = (bf16[128,640]{1,0:T(8,128)(2,1)S(1)}, bf16[128,640]{1,0:T(8,128)(2,1)S(1)}, u32[]{:S(2)}, u32[]{:S(2)}) collective-permute-start(bf16[128,640]{1,0:T(8,128)(2,1)S(1)} %apply_step.11), channel_id=1, source_target_pairs={{0,4},{4,8},{8,12},{12,0},{1,5},{5,9},{9,13},{13,1},{2,6},{6,10},{... | collective-permute-start | bytes 491528 | tf_op jit(solution)/shard_map/ppermute | solution.py:24
  77.6 6.9 %collective-permute-start.8 = (f32[2,1,128]{2,1,0:T(1,128)S(1)}, f32[2,1,128]{2,1,0:T(1,128)S(1)}, u32[]{:S(2)}, u32[]{:S(2)}) collective-permute-start(f32[2,1,128]{2,1,0:T(1,128)S(1)} %bitcast.3), channel_id=1, source_target_pairs={{0,4},{4,8},{8,12},{12,0},{1,5},{5,9},{9,13},{13,1},{2,6},{6,10},{... | collective-permute-start | bytes 3080 | tf_op jit(solution)/shard_map/ppermute | solution.py:24
  86.9 24.7 %collective-permute-start.21 = (f32[2,3,80,640]{3,2,1,0:T(8,128)}, f32[2,3,80,640]{3,2,1,0:T(8,128)S(1)}, u32[]{:S(2)}, u32[]{:S(2)}) collective-permute-start(f32[2,3,80,640]{3,2,1,0:T(8,128)} %get-tuple-element.19), channel_id=1, source_target_pairs={{0,1},{1,0},{2,3},{3,2},{4,5},{5,4},{6,7},{7,6},{8,9},{9,8},{10,11... | collective-permute-start | bytes 3686408 | tf_op jit(solution)/shard_map/ppermute | solution.py:24
  87.5 8.4 %collective-permute-start.18 = (bf16[128,640]{1,0:T(8,128)(2,1)S(1)}, bf16[128,640]{1,0:T(8,128)(2,1)S(1)}, u32[]{:S(2)}, u32[]{:S(2)}) collective-permute-start(bf16[128,640]{1,0:T(8,128)(2,1)S(1)} %apply_step.15), channel_id=1, source_target_pairs={{0,4},{4,8},{8,12},{12,0},{1,5},{5,9},{9,13},{13,1},{2,6},{6,10},{... | collective-permute-start | bytes 491528 | tf_op jit(solution)/shard_map/ppermute | solution.py:24
  91.5 20.0 %copy-start.6 = (f32[2,3,80,640]{3,2,1,0:T(8,128)S(1)}, f32[2,3,80,640]{3,2,1,0:T(8,128)}, u32[]{:S(2)}) copy-start(f32[2,3,80,640]{3,2,1,0:T(8,128)} %get-tuple-element.18) | copy-start | bytes 3686404
  91.6 8.2 %collective-permute-start.13 = (bf16[128,640]{1,0:T(8,128)(2,1)S(1)}, bf16[128,640]{1,0:T(8,128)(2,1)S(1)}, u32[]{:S(2)}, u32[]{:S(2)}) collective-permute-start(bf16[128,640]{1,0:T(8,128)(2,1)S(1)} %add_convert_fusion.5), channel_id=1, source_target_pairs={{0,4},{4,8},{8,12},{12,0},{1,5},{5,9},{9,13},{13,1},{2,6},{6,10},{... | collective-permute-start | bytes 491528 | tf_op jit(solution)/shard_map/ppermute | solution.py:24
  96.0 7.6 %collective-permute-start.19 = (bf16[128,640]{1,0:T(8,128)(2,1)S(1)}, bf16[128,640]{1,0:T(8,128)(2,1)S(1)}, u32[]{:S(2)}, u32[]{:S(2)}) collective-permute-start(bf16[128,640]{1,0:T(8,128)(2,1)S(1)} %add_convert_fusion.2), channel_id=1, source_target_pairs={{0,4},{4,8},{8,12},{12,0},{1,5},{5,9},{9,13},{13,1},{2,6},{6,10},{... | collective-permute-start | bytes 491528 | tf_op jit(solution)/shard_map/ppermute | solution.py:24
  99.8 7.6 %collective-permute-start.14 = (bf16[128,640]{1,0:T(8,128)(2,1)S(1)}, bf16[128,640]{1,0:T(8,128)(2,1)S(1)}, u32[]{:S(2)}, u32[]{:S(2)}) collective-permute-start(bf16[128,640]{1,0:T(8,128)(2,1)S(1)} %add_convert_fusion.4), channel_id=1, source_target_pairs={{0,4},{4,8},{8,12},{12,0},{1,5},{5,9},{9,13},{13,1},{2,6},{6,10},{... | collective-permute-start | bytes 491528 | tf_op jit(solution)/shard_map/ppermute | solution.py:24
  103.6 7.2 %collective-permute-start.20 = (bf16[128,640]{1,0:T(8,128)(2,1)S(1)}, bf16[128,640]{1,0:T(8,128)(2,1)S(1)}, u32[]{:S(2)}, u32[]{:S(2)}) collective-permute-start(bf16[128,640]{1,0:T(8,128)(2,1)S(1)} %add_convert_fusion.1), channel_id=1, source_target_pairs={{0,4},{4,8},{8,12},{12,0},{1,5},{5,9},{9,13},{13,1},{2,6},{6,10},{... | collective-permute-start | bytes 491528 | tf_op jit(solution)/shard_map/ppermute | solution.py:24

commit v2 on v1

--- a/solution.py
+++ b/solution.py
@@ -126,6 +126,30 @@
 
 def in_hbm(value):
     return pltpu.with_memory_space_constraint(value, pltpu.HBM)
+
+
+def columns_body(rep, whole, out, semaphore):
+    columns = out.shape[1]
+    taken = whole.at[:, pl.ds(pl.multiple_of(rep[0] * columns, columns), columns)]
+    copy = pltpu.make_async_copy(taken, out, semaphore)
+    copy.start()
+    copy.wait()
+
+
+def columns_step(rep, whole):
+    rows, columns = whole.shape[0], whole.shape[1] // 2
+    return pl.pallas_call(
+        columns_body,
+        out_shape=jax.ShapeDtypeStruct((rows, columns), whole.dtype),
+        in_specs=[pl.BlockSpec(memory_space=pltpu.SMEM), pl.BlockSpec(memory_space=pl.ANY)],
+        out_specs=pl.BlockSpec(memory_space=pltpu.VMEM),
+        scratch_shapes=[pltpu.SemaphoreType.DMA],
+        compiler_params=pltpu.CompilerParams(vmem_limit_bytes=4 << 20),
+        cost_estimate=pl.CostEstimate(
+            flops=0, bytes_accessed=4 * rows * columns, transcendentals=0
+        ),
+        name="columns_step",
+    )(rep, in_hbm(whole))
 
 
 def cotangent_body(token_scale, rep, values, rates, out_raw, out):
@@ -223,23 +247,25 @@
         new_low[0, pl.ds((2 * m + 1) * hid, hid), :] = fresh_par.astype(jnp.bfloat16)
 
 
-def gradient_step(rep, keys, cots, weights, momentum, low_par, base_par):
+def gradient_step(head, rep, keys, cots, weights, momentum, low_par, base_par):
     slots = len(keys)
     rows = keys[0].shape[0]
     heads, _, hid, width = low_par.shape
-    token_spec = pl.BlockSpec((rows, width), lambda h, rep: (0, h))
-    own_spec = pl.BlockSpec((1, 3, hid, width), lambda h, rep: (rep[0] * heads + h, 0, 0, 0))
-    weight_spec = pl.BlockSpec((1, 3, hid, width), lambda h, rep: (h, 0, 0, 0))
-    low_spec = pl.BlockSpec((1, 6 * hid, width), lambda h, rep: (h, 0, 0))
-    fresh = pltpu.HBM(low_par.shape, jnp.float32)
+    block = (1, 3, hid, width)
+    token_spec = pl.BlockSpec((rows, width), lambda i, rep: (0, head))
+    own_spec = pl.BlockSpec(block, lambda i, rep: (rep[0] * heads + head, 0, 0, 0))
+    par_spec = pl.BlockSpec(block, lambda i, rep: (head, 0, 0, 0))
+    new_spec = pl.BlockSpec(block, lambda i, rep: (0, 0, 0, 0))
+    low_spec = pl.BlockSpec((1, 6 * hid, width), lambda i, rep: (0, 0, 0))
+    fresh = pltpu.HBM(block, jnp.float32)
     return pl.pallas_call(
         functools.partial(gradient_body, slots),
-        out_shape=(fresh, fresh, jax.ShapeDtypeStruct((heads, 6 * hid, width), jnp.bfloat16)),
+        out_shape=(fresh, fresh, jax.ShapeDtypeStruct((1, 6 * hid, width), jnp.bfloat16)),
         grid_spec=pltpu.PrefetchScalarGridSpec(
             num_scalar_prefetch=1,
-            grid=(heads,),
-            in_specs=[token_spec] * (2 * slots) + [own_spec] * 2 + [weight_spec] * 2,
-            out_specs=(weight_spec, weight_spec, low_spec),
+            grid=(1,),
+            in_specs=[token_spec] * (2 * slots) + [own_spec] * 2 + [par_spec] * 2,
+            out_specs=(new_spec, new_spec, low_spec),
             scratch_shapes=[
                 pltpu.VMEM((slots * rows, width), jnp.bfloat16),
                 pltpu.VMEM((slots * rows, width), jnp.bfloat16),
@@ -248,12 +274,12 @@
         ),
         compiler_params=pltpu.CompilerParams(vmem_limit_bytes=24 << 20),
         cost_estimate=pl.CostEstimate(
-            flops=24 * heads * slots * rows * hid * width,
-            bytes_accessed=48 * heads * hid * width,
+            flops=24 * slots * rows * hid * width,
+            bytes_accessed=48 * hid * width,
             transcendentals=0,
         ),
         name="gradient_step",
-    )(rep, *map(in_hbm, (*keys, *cots, weights, momentum, low_par, base_par)))
+    )(rep, *map(in_hbm, (*keys, *cots, weights, momentum)), low_par, base_par)
 
 
 def apply_body(query, low, *refs):
@@ -270,7 +296,7 @@
     refs[-1][...] = made.astype(refs[-1].dtype)
 
 
-def apply_step(head, query, low, dtype, *more):
+def apply_step(query, low, dtype, *more):
     rows, width = query.shape
     total = low.shape[1]
     whole = pl.BlockSpec((rows, width), lambda i: (0, 0))
@@ -278,7 +304,7 @@
         apply_body,
         out_shape=jax.ShapeDtypeStruct((rows, width), dtype),
         grid=(1,),
-        in_specs=[whole, pl.BlockSpec((1, total, width), lambda i: (head, 0, 0))]
+        in_specs=[whole, pl.BlockSpec((1, total, width), lambda i: (0, 0, 0))]
         + [whole] * len(more),
         out_specs=whole,
         compiler_params=pltpu.CompilerParams(vmem_limit_bytes=8 << 20),
@@ -287,6 +313,29 @@
         ),
         name="apply_step",
     )(query, low, *more)
+
+
+def output_body(kept, moved, *refs):
+    refs[-1][...] = (kept[...] + moved[...].astype(jnp.float32)).astype(jnp.bfloat16)
+
+
+def output_step(head, heads, kept, moved, before):
+    rows, width = kept.shape
+    whole = pl.BlockSpec((rows, width), lambda i: (0, 0))
+    more = () if before is None else (before,)
+    return pl.pallas_call(
+        output_body,
+        out_shape=pltpu.HBM((rows, heads * width), jnp.bfloat16),
+        grid=(1,),
+        in_specs=[whole, whole] + [pl.BlockSpec(memory_space=pl.ANY)] * len(more),
+        out_specs=pl.BlockSpec((rows, width), lambda i: (0, head)),
+        input_output_aliases={2: 0} if more else {},
+        compiler_params=pltpu.CompilerParams(vmem_limit_bytes=4 << 20),
+        cost_estimate=pl.CostEstimate(
+            flops=rows * width, bytes_accessed=8 * rows * width, transcendentals=0
+        ),
+        name="output_step",
+    )(kept, moved, *more)
 
 
 def attend_body(token_scale, first, key_own, key_prior, value_own, cot_prior, rate_prior, *refs):
@@ -338,16 +387,13 @@
     start = rep_index * per_rep
     token_scale = float(slots * queries.shape[0]) ** (-0.5)
 
-    def own_columns(tensor):
-        return lax.dynamic_slice_in_dim(tensor, start * width, per_rep * width, 1)
-
     def hop(value, axis="ctx"):
         return ring(value, axis)
 
     rep = rep_index.reshape(1)
     value_own, cot = cotangent_step(token_scale, rep, values, learn_rates)
     heads = range(per_rep)
-    keys, cots = [own_columns(key_vectors)], [cot]
+    keys, cots = [columns_step(rep, key_vectors)], [cot]
     asked = [[lax.dynamic_slice_in_dim(queries, (start + h) * width, width, 1) for h in heads]]
     for _ in range(1, slots):
         keys.append(hop(keys[-1]))
@@ -362,30 +408,30 @@
     attended = attend_step(
         token_scale, first, keys[0], keys[1], value_own, cots[1], rate_prior, asked[0]
     )
-    new_own, new_par, new_low = gradient_step(
-        rep, keys, cots, fast_weights, momentum, low_par, base_par
-    )
+    fresh = []
+    for h in heads:
+        fresh.append(gradient_step(h, rep, keys, cots, fast_weights, momentum, low_par, base_par))
+    lows = [new[2] for new in fresh]
     moving = []
     for step in range(1, slots):
         if step == 1:
-            sent = [apply_step(h, asked[step][h], new_low, jnp.bfloat16) for h in heads]
+            sent = [apply_step(asked[step][h], lows[h], jnp.bfloat16) for h in heads]
         else:
-            made = [apply_step(h, asked[step][h], new_low, jnp.float32) for h in heads]
+            made = [apply_step(asked[step][h], lows[h], jnp.float32) for h in heads]
             sent = [
                 (made[h] + moving[h].astype(jnp.float32)).astype(jnp.bfloat16) for h in heads
             ]
         moving = [hop(sent[h]) for h in heads]
-    kept = []
+    layer_output = None
     for h in heads:
-        kept.append(apply_step(h, asked[0][h], new_low, jnp.float32, attended[h]))
-    layer_output = jnp.concatenate(
-        [(kept[h] + moving[h].astype(jnp.float32)).astype(jnp.bfloat16) for h in heads], axis=1
-    )
-    returned = hop(new_par, "rep")
+        kept = apply_step(asked[0][h], lows[h], jnp.float32, attended[h])
+        layer_output = output_step(h, per_rep, kept, moving[h], layer_output)
+    returned = [hop(fresh[h][1], "rep") for h in heads]
+    owned = [new[0] for new in fresh]
     fast_updated = jnp.where(
         rep_index == 0,
-        jnp.concatenate([new_own, returned], axis=0),
-        jnp.concatenate([returned, new_own], axis=0),
+        jnp.concatenate([*owned, *returned], axis=0),
+        jnp.concatenate([*returned, *owned], axis=0),
     )
     return (layer_output, fast_updated)
 

time: 113 us -> 118 us (1.044)
  Pallas kernels: 16.1 us -> 20.9 us
  waiting for transfers between devices: 74.1 us -> 70.1 us
  starting transfers between devices: 18.4 us -> 20.1 us
    ppermute x22 -> x23, waiting for transfers between devices: 74.1 us -> 70.1 us  [ring(): lax.ppermute(value, axis, [(source, (source + steps) % count) for source...]
    pallas_call x1 -> x2, Pallas kernels: 5.75 us -> 8.15 us  [gradient_step(): pl.pallas_call(functools.partial(gradient_body, slots), out_shape=(fresh,...]
    pallas_call x0 -> x3, Pallas kernels: none -> 2.38 us  [the longest x2 1.4 us: output_step(): pl.pallas_call(output_body, out_shape=pltpu.HBM((rows, heads * width), jn...]
    select_n x1, other arithmetic: 1.6 us -> 3.38 us  [tokens_travel(): jnp.where(rep_index == 0, jnp.concatenate([*owned, *returned], axis=0), j...]
    ppermute x22 -> x23, starting transfers between devices: 18.4 us -> 20.1 us  [ring(): lax.ppermute(value, axis, [(source, (source + steps) % count) for source...]
  transfers between devices with their start and end apart: 22 -> 23, of which waited for: 12 -> 10; matrix products, arithmetic and copies ran while one was open for 2% -> 1% of each run, Pallas kernels for 12% -> 15%
where the time goes in v2:
time: 118 us; the launch traced here: 117 us
  waiting for transfers between devices  70.1 us (59%)
  Pallas kernels  20.9 us (18%)
  starting transfers between devices  20.1 us (17%)
  other arithmetic  3.51 us (3%)
  local copies, waits for them, and re-layouts  1.83 us (2%)
    ppermute x23, waiting for transfers between devices, ring(): lax.ppermute(value, axis, [(source, (source + steps) % count) for source...  70.1 us
    ppermute x23, starting transfers between devices, ring(): lax.ppermute(value, axis, [(source, (source + steps) % count) for source...  20.1 us
    pallas_call x2, Pallas kernels, gradient_step(): pl.pallas_call(functools.partial(gradient_body, slots), out_shape=(fresh,...  8.15 us
    pallas_call x8, Pallas kernels, apply_step(): pl.pallas_call(apply_body, out_shape=jax.ShapeDtypeStruct((rows, width),...  4.07 us
    select_n x1, other arithmetic, tokens_travel(): jnp.where(rep_index == 0, jnp.concatenate([*owned, *returned], axis=0), j...  3.38 us
    pallas_call x1, Pallas kernels, other_step(): pl.pallas_call(other_body, out_shape=(pltpu.HBM(made, jnp.bfloat16), pltp...  2.69 us
    pallas_call x1, Pallas kernels, attend_step(): pl.pallas_call(functools.partial(attend_body, token_scale), out_shape=mad...  2.41 us
  transfers between devices with their start and end apart: 23, of which 10 were waited for; matrix products, arithmetic and copies ran while one was open for 1% of the time, Pallas kernels for 15%

profile of v2, /device:TPU:0, one launch (start us, length us, event | category | flops | bytes accessed | tf_op | source)
XLA Modules:
  0.0 117.3 jit_solution(11491943632742513809)
XLA Ops:
  0.6 2.7 %other_step.1 = (bf16[2,3,80,640]{3,2,1,0:T(8,128)(2,1)}, f32[2,3,80,640]{3,2,1,0:T(8,128)}) custom-call(s32[1]{0:T(128)} %bitcast.rep, f32[4,3,80,640]{3,2,1,0:T(8,128)} %refs_8_.3, f32[4,3,80,640]{3,2,1,0:T(8,128)} %refs_9_.3), custom_call_target="tpu_custom_call" | custom-call | flops 614400 | bytes 4300800 | tf_op jit(solution)/shard_map/other_step/pallas_call | solution.py:203
  3.3 0.5 collective-permute-start.7
  3.8 1.2 cotangent_step.1
  5.0 2.6 %collective-permute-start.3 = (bf16[128,1280]{1,0:T(8,128)(2,1)S(1)}, bf16[128,1280]{1,0:T(8,128)(2,1)S(1)}, u32[]{:S(2)}, u32[]{:S(2)}) collective-permute-start(bf16[128,1280]{1,0:T(8,128)(2,1)S(1)} %get-tuple-element.14.refs_4_), channel_id=1, source_target_pairs={{0,4},{4,8},{8,12},{12,0},{1,5},{5,9},{9,13},{13,1},{2,6},{6,10},{... | collective-permute-start | bytes 983048 | tf_op jit(solution)/shard_map/ppermute | solution.py:24
  7.6 1.0 columns_step.1.refs_0_.key_own
  8.6 0.0 copy-start
  8.6 1.6 %collective-permute-start = (bf16[128,1280]{1,0:T(8,128)(2,1)S(1)}, bf16[128,1280]{1,0:T(8,128)(2,1)S(1)}, u32[]{:S(2)}, u32[]{:S(2)}) collective-permute-start(bf16[128,1280]{1,0:T(8,128)(2,1)S(1)} %columns_step.1.refs_0_.key_own), channel_id=1, source_target_pairs={{0,4},{4,8},{8,12},{12,0},{1,5},{5,9},{9,13},{13,1},{2,6},{6,10},{... | collective-permute-start | bytes 983048 | tf_op jit(solution)/shard_map/ppermute | solution.py:24
  10.3 1.0 constant_dynamic-slice_fusion
  11.3 1.6 %collective-permute-start.15 = (bf16[128,640]{1,0:T(8,128)(2,1)S(1)}, bf16[128,640]{1,0:T(8,128)(2,1)S(1)}, u32[]{:S(2)}, u32[]{:S(2)}) collective-permute-start(bf16[128,640]{1,0:T(8,128)(2,1)S(1)} %get-tuple-element.26.refs_0_.query), channel_id=1, source_target_pairs={{0,4},{4,8},{8,12},{12,0},{1,5},{5,9},{9,13},{13,1},{2,6},{6,10},{... | collective-permute-start | bytes 491528 | tf_op jit(solution)/shard_map/ppermute | solution.py:24
  12.9 5.3 %collective-permute-done.3.refs_5_.cot_prior = bf16[128,1280]{1,0:T(8,128)(2,1)S(1)} collective-permute-done((bf16[128,1280]{1,0:T(8,128)(2,1)S(1)}, bf16[128,1280]{1,0:T(8,128)(2,1)S(1)}, u32[]{:S(2)}, u32[]{:S(2)}) %collective-permute-start.3) | collective-permute-done | bytes 327712 | tf_op jit(solution)/shard_map/ppermute | solution.py:24
  18.2 0.0 collective-permute-start.4
  18.2 7.0 %collective-permute-done.refs_1_.key_prior = bf16[128,1280]{1,0:T(8,128)(2,1)S(1)} collective-permute-done((bf16[128,1280]{1,0:T(8,128)(2,1)S(1)}, bf16[128,1280]{1,0:T(8,128)(2,1)S(1)}, u32[]{:S(2)}, u32[]{:S(2)}) %collective-permute-start) | collective-permute-done | bytes 327712 | tf_op jit(solution)/shard_map/ppermute | solution.py:24
  25.2 0.0 collective-permute-start.1
  25.2 0.0 collective-permute-start.6
  25.2 3.5 %collective-permute-done.15.query = bf16[128,640]{1,0:T(8,128)(2,1)S(1)} collective-permute-done((bf16[128,640]{1,0:T(8,128)(2,1)S(1)}, bf16[128,640]{1,0:T(8,128)(2,1)S(1)}, u32[]{:S(2)}, u32[]{:S(2)}) %collective-permute-start.15) | collective-permute-done | bytes 163872 | tf_op jit(solution)/shard_map/ppermute | solution.py:24
  28.7 0.0 collective-permute-start.9
  28.8 17.4 %collective-permute-done.9.query = bf16[128,640]{1,0:T(8,128)(2,1)S(1)} collective-permute-done((bf16[128,640]{1,0:T(8,128)(2,1)S(1)}, bf16[128,640]{1,0:T(8,128)(2,1)S(1)}, u32[]{:S(2)}, u32[]{:S(2)}) %collective-permute-start.9) | collective-permute-done | bytes 163872 | tf_op jit(solution)/shard_map/ppermute | solution.py:24
  46.1 0.0 collective-permute-start.16
  46.1 0.0 collective-permute-done.4.refs_6_
  46.1 1.3 %collective-permute-start.5 = (bf16[128,1280]{1,0:T(8,128)(2,1)S(1)}, bf16[128,1280]{1,0:T(8,128)(2,1)S(1)}, u32[]{:S(2)}, u32[]{:S(2)}) collective-permute-start(bf16[128,1280]{1,0:T(8,128)(2,1)S(1)} %collective-permute-done.4.refs_6_), channel_id=1, source_target_pairs={{0,4},{4,8},{8,12},{12,0},{1,5},{5,9},{9,13},{13,1},{2,6},{6,10},{... | collective-permute-start | bytes 983048 | tf_op jit(solution)/shard_map/ppermute | solution.py:24
  47.4 0.0 collective-permute-done.1.refs_2_
  47.4 1.6 %collective-permute-start.2 = (bf16[128,1280]{1,0:T(8,128)(2,1)S(1)}, bf16[128,1280]{1,0:T(8,128)(2,1)S(1)}, u32[]{:S(2)}, u32[]{:S(2)}) collective-permute-start(bf16[128,1280]{1,0:T(8,128)(2,1)S(1)} %collective-permute-done.1.refs_2_), channel_id=1, source_target_pairs={{0,4},{4,8},{8,12},{12,0},{1,5},{5,9},{9,13},{13,1},{2,6},{6,10},{... | collective-permute-start | bytes 983048 | tf_op jit(solution)/shard_map/ppermute | solution.py:24
  49.0 6.0 %collective-permute-done.16.query = bf16[128,640]{1,0:T(8,128)(2,1)S(1)} collective-permute-done((bf16[128,640]{1,0:T(8,128)(2,1)S(1)}, bf16[128,640]{1,0:T(8,128)(2,1)S(1)}, u32[]{:S(2)}, u32[]{:S(2)}) %collective-permute-start.16) | collective-permute-done | bytes 163872 | tf_op jit(solution)/shard_map/ppermute | solution.py:24
  55.0 0.0 collective-permute-start.10
  55.0 16.5 %collective-permute-done.10.query = bf16[128,640]{1,0:T(8,128)(2,1)S(1)} collective-permute-done((bf16[128,640]{1,0:T(8,128)(2,1)S(1)}, bf16[128,640]{1,0:T(8,128)(2,1)S(1)}, u32[]{:S(2)}, u32[]{:S(2)}) %collective-permute-start.10) | collective-permute-done | bytes 163872 | tf_op jit(solution)/shard_map/ppermute | solution.py:24
  71.5 0.0 collective-permute-start.17
  71.5 0.0 collective-permute-done.6.refs_10_
  71.5 0.0 collective-permute-start.11
  71.5 0.0 collective-permute-done.5.refs_7_
  71.5 0.0 collective-permute-done.2.refs_3_
  71.6 0.6 copy-done.7
  72.3 0.1 copy-done.8
  72.4 4.1 %gradient_step.3 = (f32[1,3,80,640]{3,2,1,0:T(8,128)}, f32[1,3,80,640]{3,2,1,0:T(8,128)}, bf16[1,480,640]{2,1,0:T(8,128)(2,1)S(1)}) custom-call(s32[1]{0:T(128)} %bitcast.rep, bf16[128,1280]{1,0:T(8,128)(2,1)} %copy-done, bf16[128,1280]{1,0:T(8,128)(2,1)} %copy-done.4, bf16[128,1280]{1,0:T(8,128)(2,1)} %copy-done.6, bf16[128,1280]{1,0:T(8,128)(2,1)} %copy-done.8, ...), custom_call_target="tpu_custom_call" | custom-call | flops 629145600 | bytes 2457600 | tf_op jit(solution)/shard_map/gradient_step/pallas_call | solution.py:261
  76.5 0.5 apply_step.15
  77.0 0.8 collective-permute-start.18
  77.8 0.0 collective-permute-start.21
  77.8 4.1 %gradient_step.2 = (f32[1,3,80,640]{3,2,1,0:T(8,128)}, f32[1,3,80,640]{3,2,1,0:T(8,128)}, bf16[1,480,640]{2,1,0:T(8,128)(2,1)S(1)}) custom-call(s32[1]{0:T(128)} %bitcast.rep, bf16[128,1280]{1,0:T(8,128)(2,1)} %copy-done, bf16[128,1280]{1,0:T(8,128)(2,1)} %copy-done.4, bf16[128,1280]{1,0:T(8,128)(2,1)} %copy-done.6, bf16[128,1280]{1,0:T(8,128)(2,1)} %copy-done.8, ...), custom_call_target="tpu_custom_call" | custom-call | flops 629145600 | bytes 2457600 | tf_op jit(solution)/shard_map/gradient_step/pallas_call | solution.py:261
  81.9 0.5 collective-permute-start.22
  82.4 0.5 apply_step.14
  82.9 0.5 apply_step.10
  83.4 0.5 apply_step.11
  83.9 0.0 copy-start.11
  84.0 4.2 %collective-permute-start.12 = (bf16[128,640]{1,0:T(8,128)(2,1)S(1)}, bf16[128,640]{1,0:T(8,128)(2,1)S(1)}, u32[]{:S(2)}, u32[]{:S(2)}) collective-permute-start(bf16[128,640]{1,0:T(8,128)(2,1)S(1)} %apply_step.11), channel_id=1, source_target_pairs={{0,4},{4,8},{8,12},{12,0},{1,5},{5,9},{9,13},{13,1},{2,6},{6,10},{... | collective-permute-start | bytes 491528 | tf_op jit(solution)/shard_map/ppermute | solution.py:24
  88.2 0.5 apply_step.13
  88.7 0.0 collective-permute-done.11.query
  88.7 0.5 apply_step.9
  89.3 0.1 collective-permute-start.19
  89.4 3.4 %collective-permute-done.12 = bf16[128,640]{1,0:T(8,128)(2,1)S(1)} collective-permute-done((bf16[128,640]{1,0:T(8,128)(2,1)S(1)}, bf16[128,640]{1,0:T(8,128)(2,1)S(1)}, u32[]{:S(2)}, u32[]{:S(2)}) %collective-permute-start.12) | collective-permute-done | bytes 163872 | tf_op jit(solution)/shard_map/ppermute | solution.py:24
  92.8 2.5 %collective-permute-start.13 = (bf16[128,640]{1,0:T(8,128)(2,1)S(1)}, bf16[128,640]{1,0:T(8,128)(2,1)S(1)}, u32[]{:S(2)}, u32[]{:S(2)}) collective-permute-start(bf16[128,640]{1,0:T(8,128)(2,1)S(1)} %add_convert_fusion.3), channel_id=1, source_target_pairs={{0,4},{4,8},{8,12},{12,0},{1,5},{5,9},{9,13},{13,1},{2,6},{6,10},{... | collective-permute-start | bytes 491528 | tf_op jit(solution)/shard_map/ppermute | solution.py:24
  95.4 2.9 %collective-permute-done.19 = bf16[128,640]{1,0:T(8,128)(2,1)S(1)} collective-permute-done((bf16[128,640]{1,0:T(8,128)(2,1)S(1)}, bf16[128,640]{1,0:T(8,128)(2,1)S(1)}, u32[]{:S(2)}, u32[]{:S(2)}) %collective-permute-start.19) | collective-permute-done | bytes 163872 | tf_op jit(solution)/shard_map/ppermute | solution.py:24
  98.3 0.6 collective-permute-start.20
  98.9 1.8 %collective-permute-done.13 = bf16[128,640]{1,0:T(8,128)(2,1)S(1)} collective-permute-done((bf16[128,640]{1,0:T(8,128)(2,1)S(1)}, bf16[128,640]{1,0:T(8,128)(2,1)S(1)}, u32[]{:S(2)}, u32[]{:S(2)}) %collective-permute-start.13) | collective-permute-done | bytes 163872 | tf_op jit(solution)/shard_map/ppermute | solution.py:24
  100.7 1.8 %collective-permute-start.14 = (bf16[128,640]{1,0:T(8,128)(2,1)S(1)}, bf16[128,640]{1,0:T(8,128)(2,1)S(1)}, u32[]{:S(2)}, u32[]{:S(2)}) collective-permute-start(bf16[128,640]{1,0:T(8,128)(2,1)S(1)} %add_convert_fusion.2), channel_id=1, source_target_pairs={{0,4},{4,8},{8,12},{12,0},{1,5},{5,9},{9,13},{13,1},{2,6},{6,10},{... | collective-permute-start | bytes 491528 | tf_op jit(solution)/shard_map/ppermute | solution.py:24
  102.5 0.1 collective-permute-start.8
  102.7 6.3 %collective-permute-done.8.rate_prior = f32[2,1,128]{2,1,0:T(1,128)S(1)} collective-permute-done((f32[2,1,128]{2,1,0:T(1,128)S(1)}, f32[2,1,128]{2,1,0:T(1,128)S(1)}, u32[]{:S(2)}, u32[]{:S(2)}) %collective-permute-start.8) | collective-permute-done | bytes 1056 | tf_op jit(solution)/shard_map/ppermute | solution.py:24
  109.0 2.4 %attend_step.1 = (f32[128,640]{1,0:T(8,128)S(1)}, f32[128,640]{1,0:T(8,128)S(1)}) custom-call(s32[1]{0:T(128)} %bitcast.1.first, bf16[128,1280]{1,0:T(8,128)(2,1)} %copy-done, bf16[128,1280]{1,0:T(8,128)(2,1)} %copy-done.4, bf16[128,1280]{1,0:T(8,128)(2,1)} %copy-done.2, bf16[128,1280]{1,0:T(8,128)(2,1)} %copy-done.3, ...), custom_call_target="tpu_custom_call" | custom-call | flops 167772160 | bytes 2293760 | tf_op jit(solution)/shard_map/attend_step/pallas_call | solution.py:370
  111.4 0.0 copy-start.10
  111.4 0.5 apply_step.12.kept
  112.0 0.5 apply_step.8.kept
  112.5 0.7 output_step.2.refs_0_
  113.2 0.0 collective-permute-done.14.moved
  113.2 0.7 output_step.3
  113.9 0.0 collective-permute-done.21
  113.9 3.4 %maximum_select_fusion = f32[4,3,80,640]{3,2,1,0:T(8,128)} fusion(f32[1,3,80,640]{3,2,1,0:T(8,128)} %collective-permute-done.22, f32[1,3,80,640]{3,2,1,0:T(8,128)} %collective-permute-done.21, f32[1,3,80,640]{3,2,1,0:T(8,128)S(1)} %copy-done.10, f32[1,3,80,640]{3,2,1,0:T(8,128)S(1)} %copy-done.9, pred[]{:T(512)S(6)} %eq.7), kind=kLoop, calls=%fused_computation | loop fusion | flops 4300800 | bytes 4915201 | tf_op jit(solution)/shard_map/jit(_where)/select_n | solution.py:431
  (29 shorter events, 0.2 us)
Async XLA Ops:
  3.3 68.3 %collective-permute-start.7 = (f32[2,3,80,640]{3,2,1,0:T(8,128)}, f32[2,3,80,640]{3,2,1,0:T(8,128)S(1)}, u32[]{:S(2)}, u32[]{:S(2)}) collective-permute-start(f32[2,3,80,640]{3,2,1,0:T(8,128)} %get-tuple-element.16), channel_id=1, source_target_pairs={{0,1},{1,0},{2,3},{3,2},{4,5},{5,4},{6,7},{7,6},{8,9},{9,8},{10,11... | collective-permute-start | bytes 3686408 | tf_op jit(solution)/shard_map/ppermute | solution.py:24
  5.0 5.3 %copy-start.2 = (bf16[128,1280]{1,0:T(8,128)(2,1)}, bf16[128,1280]{1,0:T(8,128)(2,1)S(1)}, u32[]{:S(2)}) copy-start(bf16[128,1280]{1,0:T(8,128)(2,1)S(1)} %get-tuple-element.18.value_own) | copy-start | bytes 983044
  5.0 66.6 %copy-start.1 = (bf16[128,1280]{1,0:T(8,128)(2,1)}, bf16[128,1280]{1,0:T(8,128)(2,1)S(1)}, u32[]{:S(2)}) copy-start(bf16[128,1280]{1,0:T(8,128)(2,1)S(1)} %get-tuple-element.14.refs_4_) | copy-start | bytes 983044
  5.0 13.2 %collective-permute-start.3 = (bf16[128,1280]{1,0:T(8,128)(2,1)S(1)}, bf16[128,1280]{1,0:T(8,128)(2,1)S(1)}, u32[]{:S(2)}, u32[]{:S(2)}) collective-permute-start(bf16[128,1280]{1,0:T(8,128)(2,1)S(1)} %get-tuple-element.14.refs_4_), channel_id=1, source_target_pairs={{0,4},{4,8},{8,12},{12,0},{1,5},{5,9},{9,13},{13,1},{2,6},{6,10},{... | collective-permute-start | bytes 983048 | tf_op jit(solution)/shard_map/ppermute | solution.py:24
  8.6 63.0 %copy-start = (bf16[128,1280]{1,0:T(8,128)(2,1)}, bf16[128,1280]{1,0:T(8,128)(2,1)S(1)}, u32[]{:S(2)}) copy-start(bf16[128,1280]{1,0:T(8,128)(2,1)S(1)} %columns_step.1.refs_0_.key_own) | copy-start | bytes 983044
  8.6 16.6 %collective-permute-start = (bf16[128,1280]{1,0:T(8,128)(2,1)S(1)}, bf16[128,1280]{1,0:T(8,128)(2,1)S(1)}, u32[]{:S(2)}, u32[]{:S(2)}) collective-permute-start(bf16[128,1280]{1,0:T(8,128)(2,1)S(1)} %columns_step.1.refs_0_.key_own), channel_id=1, source_target_pairs={{0,4},{4,8},{8,12},{12,0},{1,5},{5,9},{9,13},{13,1},{2,6},{6,10},{... | collective-permute-start | bytes 983048 | tf_op jit(solution)/shard_map/ppermute | solution.py:24
  11.3 17.5 %collective-permute-start.15 = (bf16[128,640]{1,0:T(8,128)(2,1)S(1)}, bf16[128,640]{1,0:T(8,128)(2,1)S(1)}, u32[]{:S(2)}, u32[]{:S(2)}) collective-permute-start(bf16[128,640]{1,0:T(8,128)(2,1)S(1)} %get-tuple-element.26.refs_0_.query), channel_id=1, source_target_pairs={{0,4},{4,8},{8,12},{12,0},{1,5},{5,9},{9,13},{13,1},{2,6},{6,10},{... | collective-permute-start | bytes 491528 | tf_op jit(solution)/shard_map/ppermute | solution.py:24
  18.2 53.4 %copy-start.3 = (bf16[128,1280]{1,0:T(8,128)(2,1)}, bf16[128,1280]{1,0:T(8,128)(2,1)S(1)}, u32[]{:S(2)}) copy-start(bf16[128,1280]{1,0:T(8,128)(2,1)S(1)} %collective-permute-done.3.refs_5_.cot_prior) | copy-start | bytes 983044
  18.2 27.9 %collective-permute-start.4 = (bf16[128,1280]{1,0:T(8,128)(2,1)S(1)}, bf16[128,1280]{1,0:T(8,128)(2,1)S(1)}, u32[]{:S(2)}, u32[]{:S(2)}) collective-permute-start(bf16[128,1280]{1,0:T(8,128)(2,1)S(1)} %collective-permute-done.3.refs_5_.cot_prior), channel_id=1, source_target_pairs={{0,4},{4,8},{8,12},{12,0},{1,5},{5,9},{9,13},{13,1},{2,6},{6,10},{... | collective-permute-start | bytes 983048 | tf_op jit(solution)/shard_map/ppermute | solution.py:24
  25.2 46.3 %copy-start.4 = (bf16[128,1280]{1,0:T(8,128)(2,1)}, bf16[128,1280]{1,0:T(8,128)(2,1)S(1)}, u32[]{:S(2)}) copy-start(bf16[128,1280]{1,0:T(8,128)(2,1)S(1)} %collective-permute-done.refs_1_.key_prior) | copy-start | bytes 983044
  25.2 22.2 %collective-permute-start.1 = (bf16[128,1280]{1,0:T(8,128)(2,1)S(1)}, bf16[128,1280]{1,0:T(8,128)(2,1)S(1)}, u32[]{:S(2)}, u32[]{:S(2)}) collective-permute-start(bf16[128,1280]{1,0:T(8,128)(2,1)S(1)} %collective-permute-done.refs_1_.key_prior), channel_id=1, source_target_pairs={{0,4},{4,8},{8,12},{12,0},{1,5},{5,9},{9,13},{13,1},{2,6},{6,10},{... | collective-permute-start | bytes 983048 | tf_op jit(solution)/shard_map/ppermute | solution.py:24
  25.2 46.3 %collective-permute-start.6 = (bf16[2,3,80,640]{3,2,1,0:T(8,128)(2,1)}, bf16[2,3,80,640]{3,2,1,0:T(8,128)(2,1)S(1)}, u32[]{:S(2)}, u32[]{:S(2)}) collective-permute-start(bf16[2,3,80,640]{3,2,1,0:T(8,128)(2,1)} %get-tuple-element.15), channel_id=1, source_target_pairs={{0,1},{1,0},{2,3},{3,2},{4,5},{5,4},{6,7},{7,6},{8,9},{9,8},{10,11... | collective-permute-start | bytes 1843208 | tf_op jit(solution)/shard_map/ppermute | solution.py:24
  28.7 17.4 %collective-permute-start.9 = (bf16[128,640]{1,0:T(8,128)(2,1)S(1)}, bf16[128,640]{1,0:T(8,128)(2,1)S(1)}, u32[]{:S(2)}, u32[]{:S(2)}) collective-permute-start(bf16[128,640]{1,0:T(8,128)(2,1)S(1)} %get-tuple-element.27.refs_1_.query), channel_id=1, source_target_pairs={{0,4},{4,8},{8,12},{12,0},{1,5},{5,9},{9,13},{13,1},{2,6},{6,10},{... | collective-permute-start | bytes 491528 | tf_op jit(solution)/shard_map/ppermute | solution.py:24
  46.1 8.9 %collective-permute-start.16 = (bf16[128,640]{1,0:T(8,128)(2,1)S(1)}, bf16[128,640]{1,0:T(8,128)(2,1)S(1)}, u32[]{:S(2)}, u32[]{:S(2)}) collective-permute-start(bf16[128,640]{1,0:T(8,128)(2,1)S(1)} %collective-permute-done.15.query), channel_id=1, source_target_pairs={{0,4},{4,8},{8,12},{12,0},{1,5},{5,9},{9,13},{13,1},{2,6},{6,10},{... | collective-permute-start | bytes 491528 | tf_op jit(solution)/shard_map/ppermute | solution.py:24
  46.1 25.5 %copy-start.5 = (bf16[128,1280]{1,0:T(8,128)(2,1)}, bf16[128,1280]{1,0:T(8,128)(2,1)S(1)}, u32[]{:S(2)}) copy-start(bf16[128,1280]{1,0:T(8,128)(2,1)S(1)} %collective-permute-done.4.refs_6_) | copy-start | bytes 983044
  46.1 25.4 %collective-permute-start.5 = (bf16[128,1280]{1,0:T(8,128)(2,1)S(1)}, bf16[128,1280]{1,0:T(8,128)(2,1)S(1)}, u32[]{:S(2)}, u32[]{:S(2)}) collective-permute-start(bf16[128,1280]{1,0:T(8,128)(2,1)S(1)} %collective-permute-done.4.refs_6_), channel_id=1, source_target_pairs={{0,4},{4,8},{8,12},{12,0},{1,5},{5,9},{9,13},{13,1},{2,6},{6,10},{... | collective-permute-start | bytes 983048 | tf_op jit(solution)/shard_map/ppermute | solution.py:24
  47.4 24.2 %copy-start.6 = (bf16[128,1280]{1,0:T(8,128)(2,1)}, bf16[128,1280]{1,0:T(8,128)(2,1)S(1)}, u32[]{:S(2)}) copy-start(bf16[128,1280]{1,0:T(8,128)(2,1)S(1)} %collective-permute-done.1.refs_2_) | copy-start | bytes 983044
  47.4 24.1 %collective-permute-start.2 = (bf16[128,1280]{1,0:T(8,128)(2,1)S(1)}, bf16[128,1280]{1,0:T(8,128)(2,1)S(1)}, u32[]{:S(2)}, u32[]{:S(2)}) collective-permute-start(bf16[128,1280]{1,0:T(8,128)(2,1)S(1)} %collective-permute-done.1.refs_2_), channel_id=1, source_target_pairs={{0,4},{4,8},{8,12},{12,0},{1,5},{5,9},{9,13},{13,1},{2,6},{6,10},{... | collective-permute-start | bytes 983048 | tf_op jit(solution)/shard_map/ppermute | solution.py:24
  55.0 16.5 %collective-permute-start.10 = (bf16[128,640]{1,0:T(8,128)(2,1)S(1)}, bf16[128,640]{1,0:T(8,128)(2,1)S(1)}, u32[]{:S(2)}, u32[]{:S(2)}) collective-permute-start(bf16[128,640]{1,0:T(8,128)(2,1)S(1)} %collective-permute-done.9.query), channel_id=1, source_target_pairs={{0,4},{4,8},{8,12},{12,0},{1,5},{5,9},{9,13},{13,1},{2,6},{6,10},{... | collective-permute-start | bytes 491528 | tf_op jit(solution)/shard_map/ppermute | solution.py:24
  71.5 12.4 %collective-permute-start.17 = (bf16[128,640]{1,0:T(8,128)(2,1)S(1)}, bf16[128,640]{1,0:T(8,128)(2,1)S(1)}, u32[]{:S(2)}, u32[]{:S(2)}) collective-permute-start(bf16[128,640]{1,0:T(8,128)(2,1)S(1)} %collective-permute-done.16.query), channel_id=1, source_target_pairs={{0,4},{4,8},{8,12},{12,0},{1,5},{5,9},{9,13},{13,1},{2,6},{6,10},{... | collective-permute-start | bytes 491528 | tf_op jit(solution)/shard_map/ppermute | solution.py:24
  71.5 17.2 %collective-permute-start.11 = (bf16[128,640]{1,0:T(8,128)(2,1)S(1)}, bf16[128,640]{1,0:T(8,128)(2,1)S(1)}, u32[]{:S(2)}, u32[]{:S(2)}) collective-permute-start(bf16[128,640]{1,0:T(8,128)(2,1)S(1)} %collective-permute-done.10.query), channel_id=1, source_target_pairs={{0,4},{4,8},{8,12},{12,0},{1,5},{5,9},{9,13},{13,1},{2,6},{6,10},{... | collective-permute-start | bytes 491528 | tf_op jit(solution)/shard_map/ppermute | solution.py:24
  71.5 0.8 copy-start.7
  71.6 0.8 copy-start.8
  77.0 12.3 %collective-permute-start.18 = (bf16[128,640]{1,0:T(8,128)(2,1)S(1)}, bf16[128,640]{1,0:T(8,128)(2,1)S(1)}, u32[]{:S(2)}, u32[]{:S(2)}) collective-permute-start(bf16[128,640]{1,0:T(8,128)(2,1)S(1)} %apply_step.15), channel_id=1, source_target_pairs={{0,4},{4,8},{8,12},{12,0},{1,5},{5,9},{9,13},{13,1},{2,6},{6,10},{... | collective-permute-start | bytes 491528 | tf_op jit(solution)/shard_map/ppermute | solution.py:24
  77.8 36.1 %collective-permute-start.21 = (f32[1,3,80,640]{3,2,1,0:T(8,128)}, f32[1,3,80,640]{3,2,1,0:T(8,128)}, u32[]{:S(2)}, u32[]{:S(2)}) collective-permute-start(f32[1,3,80,640]{3,2,1,0:T(8,128)} %get-tuple-element.24), channel_id=1, source_target_pairs={{0,1},{1,0},{2,3},{3,2},{4,5},{5,4},{6,7},{7,6},{8,9},{9,8},{10,11... | collective-permute-start | bytes 1843208 | tf_op jit(solution)/shard_map/ppermute | solution.py:24
  81.9 32.0 %collective-permute-start.22 = (f32[1,3,80,640]{3,2,1,0:T(8,128)}, f32[1,3,80,640]{3,2,1,0:T(8,128)}, u32[]{:S(2)}, u32[]{:S(2)}) collective-permute-start(f32[1,3,80,640]{3,2,1,0:T(8,128)} %get-tuple-element.25), channel_id=1, source_target_pairs={{0,1},{1,0},{2,3},{3,2},{4,5},{5,4},{6,7},{7,6},{8,9},{9,8},{10,11... | collective-permute-start | bytes 1843208 | tf_op jit(solution)/shard_map/ppermute | solution.py:24
  83.9 18.6 %copy-start.11 = (f32[4,128]{1,0:T(4,128)S(1)}, f32[4,128]{1,0:T(4,128)}, u32[]{:S(2)}) copy-start(f32[4,128]{1,0:T(4,128)} %rates.1) | copy-start | bytes 6148
  84.0 8.8 %collective-permute-start.12 = (bf16[128,640]{1,0:T(8,128)(2,1)S(1)}, bf16[128,640]{1,0:T(8,128)(2,1)S(1)}, u32[]{:S(2)}, u32[]{:S(2)}) collective-permute-start(bf16[128,640]{1,0:T(8,128)(2,1)S(1)} %apply_step.11), channel_id=1, source_target_pairs={{0,4},{4,8},{8,12},{12,0},{1,5},{5,9},{9,13},{13,1},{2,6},{6,10},{... | collective-permute-start | bytes 491528 | tf_op jit(solution)/shard_map/ppermute | solution.py:24
  89.3 8.9 %collective-permute-start.19 = (bf16[128,640]{1,0:T(8,128)(2,1)S(1)}, bf16[128,640]{1,0:T(8,128)(2,1)S(1)}, u32[]{:S(2)}, u32[]{:S(2)}) collective-permute-start(bf16[128,640]{1,0:T(8,128)(2,1)S(1)} %add_convert_fusion.1), channel_id=1, source_target_pairs={{0,4},{4,8},{8,12},{12,0},{1,5},{5,9},{9,13},{13,1},{2,6},{6,10},{... | collective-permute-start | bytes 491528 | tf_op jit(solution)/shard_map/ppermute | solution.py:24
  92.8 7.8 %collective-permute-start.13 = (bf16[128,640]{1,0:T(8,128)(2,1)S(1)}, bf16[128,640]{1,0:T(8,128)(2,1)S(1)}, u32[]{:S(2)}, u32[]{:S(2)}) collective-permute-start(bf16[128,640]{1,0:T(8,128)(2,1)S(1)} %add_convert_fusion.3), channel_id=1, source_target_pairs={{0,4},{4,8},{8,12},{12,0},{1,5},{5,9},{9,13},{13,1},{2,6},{6,10},{... | collective-permute-start | bytes 491528 | tf_op jit(solution)/shard_map/ppermute | solution.py:24
  98.3 14.2 %collective-permute-start.20 = (bf16[128,640]{1,0:T(8,128)(2,1)S(1)}, bf16[128,640]{1,0:T(8,128)(2,1)S(1)}, u32[]{:S(2)}, u32[]{:S(2)}) collective-permute-start(bf16[128,640]{1,0:T(8,128)(2,1)S(1)} %add_convert_fusion), channel_id=1, source_target_pairs={{0,4},{4,8},{8,12},{12,0},{1,5},{5,9},{9,13},{13,1},{2,6},{6,10},{... | collective-permute-start | bytes 491528 | tf_op jit(solution)/shard_map/ppermute | solution.py:24
  100.7 12.5 %collective-permute-start.14 = (bf16[128,640]{1,0:T(8,128)(2,1)S(1)}, bf16[128,640]{1,0:T(8,128)(2,1)S(1)}, u32[]{:S(2)}, u32[]{:S(2)}) collective-permute-start(bf16[128,640]{1,0:T(8,128)(2,1)S(1)} %add_convert_fusion.2), channel_id=1, source_target_pairs={{0,4},{4,8},{8,12},{12,0},{1,5},{5,9},{9,13},{13,1},{2,6},{6,10},{... | collective-permute-start | bytes 491528 | tf_op jit(solution)/shard_map/ppermute | solution.py:24
  102.5 6.5 %collective-permute-start.8 = (f32[2,1,128]{2,1,0:T(1,128)S(1)}, f32[2,1,128]{2,1,0:T(1,128)S(1)}, u32[]{:S(2)}, u32[]{:S(2)}) collective-permute-start(f32[2,1,128]{2,1,0:T(1,128)S(1)} %bitcast.3), channel_id=1, source_target_pairs={{0,4},{4,8},{8,12},{12,0},{1,5},{5,9},{9,13},{13,1},{2,6},{6,10},{... | collective-permute-start | bytes 3080 | tf_op jit(solution)/shard_map/ppermute | solution.py:24
  111.4 2.5 %copy-start.9 = (f32[1,3,80,640]{3,2,1,0:T(8,128)S(1)}, f32[1,3,80,640]{3,2,1,0:T(8,128)}, u32[]{:S(2)}) copy-start(f32[1,3,80,640]{3,2,1,0:T(8,128)} %get-tuple-element.22) | copy-start | bytes 1843204
  111.4 2.5 %copy-start.10 = (f32[1,3,80,640]{3,2,1,0:T(8,128)S(1)}, f32[1,3,80,640]{3,2,1,0:T(8,128)}, u32[]{:S(2)}) copy-start(f32[1,3,80,640]{3,2,1,0:T(8,128)} %get-tuple-element.23) | copy-start | bytes 1843204

commit v3 on v2

--- a/solution.py
+++ b/solution.py
@@ -217,9 +217,22 @@
     )(rep, in_hbm(weights), in_hbm(momentum))
 
 
-def gradient_body(slots, rep, *refs):
+def gradient_products(unit, cot, low, hid):
+    fed = lax.dot_general(low[: 4 * hid, :], unit[...], NT, preferred_element_type=jnp.float32)
+    gate, upward = fed[: 2 * hid], fed[2 * hid :]
+    back = lax.dot_general(low[4 * hid :, :], cot[...], NT, preferred_element_type=jnp.float32)
+    sigma = jax.nn.sigmoid(gate)
+    activated = gate * sigma
+    hidden = (activated * upward).astype(jnp.bfloat16)
+    gate_back = (back * upward * sigma * (1.0 + gate * (1.0 - sigma))).astype(jnp.bfloat16)
+    up_back = (back * activated).astype(jnp.bfloat16)
+    pairs = ((gate_back, unit), (up_back, unit), (hidden, cot))
+    return [jnp.dot(left, right[...], preferred_element_type=jnp.float32) for left, right in pairs]
+
+
+def early_body(slots, rep, *refs):
     keys, cots = refs[:slots], refs[slots : 2 * slots]
-    weights, momentum, low_par, base_par, new_own, new_par, new_low, unit, cot, low = refs[2 * slots :]
+    weights, momentum, low_par, base_par, so_far, low, unit, cot = refs[2 * slots :]
     rows = keys[0].shape[0]
     hid = weights.shape[2]
     for s in range(slots):
@@ -229,25 +242,13 @@
     for m in range(3):
         low[pl.ds(2 * m * hid, hid), :] = weights[0, m].astype(jnp.bfloat16)
         low[pl.ds((2 * m + 1) * hid, hid), :] = low_par[0, m]
-    fed = lax.dot_general(low[: 4 * hid, :], unit[...], NT, preferred_element_type=jnp.float32)
-    gate, upward = fed[: 2 * hid], fed[2 * hid :]
-    back = lax.dot_general(low[4 * hid :, :], cot[...], NT, preferred_element_type=jnp.float32)
-    sigma = jax.nn.sigmoid(gate)
-    activated = gate * sigma
-    hidden = (activated * upward).astype(jnp.bfloat16)
-    gate_back = (back * upward * sigma * (1.0 + gate * (1.0 - sigma))).astype(jnp.bfloat16)
-    up_back = (back * activated).astype(jnp.bfloat16)
-    for m, (left, right) in enumerate(((gate_back, unit), (up_back, unit), (hidden, cot))):
-        grad = jnp.dot(left, right[...], preferred_element_type=jnp.float32)
-        fresh_own = weights[0, m] - (momentum_decay * momentum[0, m] + grad[:hid])
-        fresh_par = base_par[0, m] - grad[hid:]
-        new_own[0, m] = fresh_own
-        new_par[0, m] = fresh_par
-        new_low[0, pl.ds(2 * m * hid, hid), :] = fresh_own.astype(jnp.bfloat16)
-        new_low[0, pl.ds((2 * m + 1) * hid, hid), :] = fresh_par.astype(jnp.bfloat16)
-
-
-def gradient_step(head, rep, keys, cots, weights, momentum, low_par, base_par):
+    for m, grad in enumerate(gradient_products(unit, cot, low, hid)):
+        own, par = pl.ds(2 * m * hid, hid), pl.ds((2 * m + 1) * hid, hid)
+        so_far[own, :] = weights[0, m] - (momentum_decay * momentum[0, m] + grad[:hid])
+        so_far[par, :] = base_par[0, m] - grad[hid:]
+
+
+def early_step(head, rep, keys, cots, weights, momentum, low_par, base_par):
     slots = len(keys)
     rows = keys[0].shape[0]
     heads, _, hid, width = low_par.shape
@@ -255,42 +256,78 @@
     token_spec = pl.BlockSpec((rows, width), lambda i, rep: (0, head))
     own_spec = pl.BlockSpec(block, lambda i, rep: (rep[0] * heads + head, 0, 0, 0))
     par_spec = pl.BlockSpec(block, lambda i, rep: (head, 0, 0, 0))
-    new_spec = pl.BlockSpec(block, lambda i, rep: (0, 0, 0, 0))
-    low_spec = pl.BlockSpec((1, 6 * hid, width), lambda i, rep: (0, 0, 0))
-    fresh = pltpu.HBM(block, jnp.float32)
-    return pl.pallas_call(
-        functools.partial(gradient_body, slots),
-        out_shape=(fresh, fresh, jax.ShapeDtypeStruct((1, 6 * hid, width), jnp.bfloat16)),
+    made_spec = pl.BlockSpec((6 * hid, width), lambda i, rep: (0, 0))
+    return pl.pallas_call(
+        functools.partial(early_body, slots),
+        out_shape=(
+            jax.ShapeDtypeStruct((6 * hid, width), jnp.float32),
+            jax.ShapeDtypeStruct((6 * hid, width), jnp.bfloat16),
+        ),
         grid_spec=pltpu.PrefetchScalarGridSpec(
             num_scalar_prefetch=1,
             grid=(1,),
             in_specs=[token_spec] * (2 * slots) + [own_spec] * 2 + [par_spec] * 2,
-            out_specs=(new_spec, new_spec, low_spec),
+            out_specs=(made_spec, made_spec),
             scratch_shapes=[
                 pltpu.VMEM((slots * rows, width), jnp.bfloat16),
                 pltpu.VMEM((slots * rows, width), jnp.bfloat16),
-                pltpu.VMEM((6 * hid, width), jnp.bfloat16),
             ],
         ),
-        compiler_params=pltpu.CompilerParams(vmem_limit_bytes=24 << 20),
+        compiler_params=pltpu.CompilerParams(vmem_limit_bytes=20 << 20),
         cost_estimate=pl.CostEstimate(
             flops=24 * slots * rows * hid * width,
-            bytes_accessed=48 * hid * width,
+            bytes_accessed=60 * hid * width,
             transcendentals=0,
         ),
-        name="gradient_step",
+        name="early_step",
     )(rep, *map(in_hbm, (*keys, *cots, weights, momentum)), low_par, base_par)
 
 
+def last_body(key, cotangent, so_far, low, new_own, new_par, new_low, unit):
+    hid = so_far.shape[0] // 6
+    unit[...] = unit_rows(key[...])
+    for m, grad in enumerate(gradient_products(unit, cotangent, low, hid)):
+        fresh_own = so_far[pl.ds(2 * m * hid, hid), :] - grad[:hid]
+        fresh_par = so_far[pl.ds((2 * m + 1) * hid, hid), :] - grad[hid:]
+        new_own[0, m] = fresh_own
+        new_par[0, m] = fresh_par
+        new_low[pl.ds(2 * m * hid, hid), :] = fresh_own.astype(jnp.bfloat16)
+        new_low[pl.ds((2 * m + 1) * hid, hid), :] = fresh_par.astype(jnp.bfloat16)
+
+
+def last_step(head, key, cotangent, so_far, low):
+    rows = key.shape[0]
+    total, width = low.shape
+    hid = total // 6
+    token_spec = pl.BlockSpec((rows, width), lambda i: (0, head))
+    made_spec = pl.BlockSpec((total, width), lambda i: (0, 0))
+    block = (1, 3, hid, width)
+    new_spec = pl.BlockSpec(block, lambda i: (0, 0, 0, 0))
+    fresh = pltpu.HBM(block, jnp.float32)
+    return pl.pallas_call(
+        last_body,
+        out_shape=(fresh, fresh, jax.ShapeDtypeStruct((total, width), jnp.bfloat16)),
+        grid=(1,),
+        in_specs=[token_spec, token_spec, made_spec, made_spec],
+        out_specs=(new_spec, new_spec, made_spec),
+        scratch_shapes=[pltpu.VMEM((rows, width), jnp.bfloat16)],
+        compiler_params=pltpu.CompilerParams(vmem_limit_bytes=16 << 20),
+        cost_estimate=pl.CostEstimate(
+            flops=4 * rows * total * width, bytes_accessed=12 * total * width, transcendentals=0
+        ),
+        name="last_step",
+    )(key, cotangent, so_far, low)
+
+
 def apply_body(query, low, *refs):
-    hid = low.shape[1] // 6
+    hid = low.shape[0] // 6
     unit = unit_rows(query[...])
-    gate = lax.dot_general(unit, low[0, : 2 * hid, :], NT, preferred_element_type=jnp.float32)
+    gate = lax.dot_general(unit, low[: 2 * hid, :], NT, preferred_element_type=jnp.float32)
     upward = lax.dot_general(
-        unit, low[0, 2 * hid : 4 * hid, :], NT, preferred_element_type=jnp.float32
+        unit, low[2 * hid : 4 * hid, :], NT, preferred_element_type=jnp.float32
     )
     hidden = (gate * jax.nn.sigmoid(gate) * upward).astype(jnp.bfloat16)
-    made = jnp.dot(hidden, low[0, 4 * hid :, :], preferred_element_type=jnp.float32)
+    made = jnp.dot(hidden, low[4 * hid :, :], preferred_element_type=jnp.float32)
     if len(refs) > 1:
         made = made + refs[0][...]
     refs[-1][...] = made.astype(refs[-1].dtype)
@@ -298,13 +335,13 @@
 
 def apply_step(query, low, dtype, *more):
     rows, width = query.shape
-    total = low.shape[1]
+    total = low.shape[0]
     whole = pl.BlockSpec((rows, width), lambda i: (0, 0))
     return pl.pallas_call(
         apply_body,
         out_shape=jax.ShapeDtypeStruct((rows, width), dtype),
         grid=(1,),
-        in_specs=[whole, pl.BlockSpec((1, total, width), lambda i: (0, 0, 0))]
+        in_specs=[whole, pl.BlockSpec((total, width), lambda i: (0, 0))]
         + [whole] * len(more),
         out_specs=whole,
         compiler_params=pltpu.CompilerParams(vmem_limit_bytes=8 << 20),
@@ -408,9 +445,16 @@
     attended = attend_step(
         token_scale, first, keys[0], keys[1], value_own, cots[1], rate_prior, asked[0]
     )
+    early = []
+    for h in heads:
+        early.append(
+            early_step(
+                h, rep, keys[:-1], cots[:-1], fast_weights, momentum, low_par, base_par
+            )
+        )
     fresh = []
     for h in heads:
-        fresh.append(gradient_step(h, rep, keys, cots, fast_weights, momentum, low_par, base_par))
+        fresh.append(last_step(h, keys[-1], cots[-1], *early[h]))
     lows = [new[2] for new in fresh]
     moving = []
     for step in range(1, slots):

time: 118 us -> 118 us (level)
  local copies, waits for them, and re-layouts: 1.83 us -> 0.09 us
    pallas_call x2 -> x4, Pallas kernels: 8.15 us -> 9.11 us  [the longest x2 5.65 us: early_step(): pl.pallas_call(functools.partial(early_body, slots), out_shape=(jax.Shape...]
  transfers between devices with their start and end apart: 23 -> 23, of which waited for: 10 -> 10; matrix products, arithmetic and copies ran while one was open for 1% -> 0% of each run, Pallas kernels for 15% -> 16%
where the time goes in v3:
time: 118 us
  waiting for transfers between devices  71 us (60%)
  Pallas kernels  21.9 us (19%)
  starting transfers between devices  20.1 us (17%)
  other arithmetic  3.59 us (3%)
    ppermute x23, waiting for transfers between devices, ring(): lax.ppermute(value, axis, [(source, (source + steps) % count) for source...  71 us
    ppermute x23, starting transfers between devices, ring(): lax.ppermute(value, axis, [(source, (source + steps) % count) for source...  20.1 us
    pallas_call x2, Pallas kernels, early_step(): pl.pallas_call(functools.partial(early_body, slots), out_shape=(jax.Shape...  5.65 us
    pallas_call x8, Pallas kernels, apply_step(): pl.pallas_call(apply_body, out_shape=jax.ShapeDtypeStruct((rows, width),...  4.05 us
    pallas_call x2, Pallas kernels, last_step(): pl.pallas_call(last_body, out_shape=(fresh, fresh, jax.ShapeDtypeStruct((...  3.46 us
    select_n x1, other arithmetic, tokens_travel(): jnp.where(rep_index == 0, jnp.concatenate([*owned, *returned], axis=0), j...  3.43 us
    pallas_call x1, Pallas kernels, other_step(): pl.pallas_call(other_body, out_shape=(pltpu.HBM(made, jnp.bfloat16), pltp...  2.74 us
    pallas_call x1, Pallas kernels, attend_step(): pl.pallas_call(functools.partial(attend_body, token_scale), out_shape=mad...  2.42 us
  transfers between devices with their start and end apart: 23, of which 10 were waited for; matrix products, arithmetic and copies ran while one was open for 0% of the time, Pallas kernels for 16%

profile of v3, /device:TPU:0, one launch (start us, length us, event | category | flops | bytes accessed | tf_op | source)
XLA Modules:
  0.0 117.5 jit_solution(12643042539243069663)
XLA Ops:
  0.6 2.7 %other_step.1 = (bf16[2,3,80,640]{3,2,1,0:T(8,128)(2,1)}, f32[2,3,80,640]{3,2,1,0:T(8,128)}) custom-call(s32[1]{0:T(128)} %bitcast.rep, f32[4,3,80,640]{3,2,1,0:T(8,128)} %refs_6_.3, f32[4,3,80,640]{3,2,1,0:T(8,128)} %refs_7_.3), custom_call_target="tpu_custom_call" | custom-call | flops 614400 | bytes 4300800 | tf_op jit(solution)/shard_map/other_step/pallas_call | solution.py:203
  3.4 0.5 collective-permute-start.7
  3.9 1.2 cotangent_step.1
  5.1 2.6 %collective-permute-start.3 = (bf16[128,1280]{1,0:T(8,128)(2,1)S(1)}, bf16[128,1280]{1,0:T(8,128)(2,1)S(1)}, u32[]{:S(2)}, u32[]{:S(2)}) collective-permute-start(bf16[128,1280]{1,0:T(8,128)(2,1)S(1)} %get-tuple-element.18.refs_3_), channel_id=1, source_target_pairs={{0,4},{4,8},{8,12},{12,0},{1,5},{5,9},{9,13},{13,1},{2,6},{6,10},{... | collective-permute-start | bytes 983048 | tf_op jit(solution)/shard_map/ppermute | solution.py:24
  7.7 1.0 columns_step.1.refs_0_.key_own
  8.7 0.0 copy-start
  8.7 1.6 %collective-permute-start = (bf16[128,1280]{1,0:T(8,128)(2,1)S(1)}, bf16[128,1280]{1,0:T(8,128)(2,1)}, u32[]{:S(2)}, u32[]{:S(2)}) collective-permute-start(bf16[128,1280]{1,0:T(8,128)(2,1)S(1)} %columns_step.1.refs_0_.key_own), channel_id=1, source_target_pairs={{0,4},{4,8},{8,12},{12,0},{1,5},{5,9},{9,13},{13,1},{2,6},{6,10},{... | collective-permute-start | bytes 983048 | tf_op jit(solution)/shard_map/ppermute | solution.py:24
  10.4 1.6 %collective-permute-start.15 = (bf16[128,640]{1,0:T(8,128)(2,1)S(1)}, bf16[128,640]{1,0:T(8,128)(2,1)S(1)}, u32[]{:S(2)}, u32[]{:S(2)}) collective-permute-start(bf16[128,640]{1,0:T(8,128)(2,1)S(1)} %get-tuple-element.34.refs_0_.query), channel_id=1, source_target_pairs={{0,4},{4,8},{8,12},{12,0},{1,5},{5,9},{9,13},{13,1},{2,6},{6,10},{... | collective-permute-start | bytes 491528 | tf_op jit(solution)/shard_map/ppermute | solution.py:24
  12.0 0.0 collective-permute-start.6
  12.0 6.3 %collective-permute-done.3.refs_4_.cot_prior = bf16[128,1280]{1,0:T(8,128)(2,1)S(1)} collective-permute-done((bf16[128,1280]{1,0:T(8,128)(2,1)S(1)}, bf16[128,1280]{1,0:T(8,128)(2,1)S(1)}, u32[]{:S(2)}, u32[]{:S(2)}) %collective-permute-start.3) | collective-permute-done | bytes 327712 | tf_op jit(solution)/shard_map/ppermute | solution.py:24
  18.3 0.0 collective-permute-start.4
  18.3 7.1 %collective-permute-done.refs_1_.key_prior = bf16[128,1280]{1,0:T(8,128)(2,1)} collective-permute-done((bf16[128,1280]{1,0:T(8,128)(2,1)S(1)}, bf16[128,1280]{1,0:T(8,128)(2,1)}, u32[]{:S(2)}, u32[]{:S(2)}) %collective-permute-start) | collective-permute-done | bytes 327712 | tf_op jit(solution)/shard_map/ppermute | solution.py:24
  25.4 0.0 collective-permute-start.1
  25.4 3.4 %collective-permute-done.15.query = bf16[128,640]{1,0:T(8,128)(2,1)S(1)} collective-permute-done((bf16[128,640]{1,0:T(8,128)(2,1)S(1)}, bf16[128,640]{1,0:T(8,128)(2,1)S(1)}, u32[]{:S(2)}, u32[]{:S(2)}) %collective-permute-start.15) | collective-permute-done | bytes 163872 | tf_op jit(solution)/shard_map/ppermute | solution.py:24
  28.8 0.0 collective-permute-start.9
  28.8 17.4 %collective-permute-done.9.query = bf16[128,640]{1,0:T(8,128)(2,1)S(1)} collective-permute-done((bf16[128,640]{1,0:T(8,128)(2,1)S(1)}, bf16[128,640]{1,0:T(8,128)(2,1)S(1)}, u32[]{:S(2)}, u32[]{:S(2)}) %collective-permute-start.9) | collective-permute-done | bytes 163872 | tf_op jit(solution)/shard_map/ppermute | solution.py:24
  46.2 0.0 collective-permute-start.16
  46.2 0.0 collective-permute-done.4.refs_5_
  46.2 1.3 %collective-permute-start.5 = (bf16[128,1280]{1,0:T(8,128)(2,1)S(1)}, bf16[128,1280]{1,0:T(8,128)(2,1)S(1)}, u32[]{:S(2)}, u32[]{:S(2)}) collective-permute-start(bf16[128,1280]{1,0:T(8,128)(2,1)S(1)} %collective-permute-done.4.refs_5_), channel_id=1, source_target_pairs={{0,4},{4,8},{8,12},{12,0},{1,5},{5,9},{9,13},{13,1},{2,6},{6,10},{... | collective-permute-start | bytes 983048 | tf_op jit(solution)/shard_map/ppermute | solution.py:24
  47.5 0.0 collective-permute-done.1.refs_2_
  47.5 1.6 %collective-permute-start.2 = (bf16[128,1280]{1,0:T(8,128)(2,1)S(1)}, bf16[128,1280]{1,0:T(8,128)(2,1)S(1)}, u32[]{:S(2)}, u32[]{:S(2)}) collective-permute-start(bf16[128,1280]{1,0:T(8,128)(2,1)S(1)} %collective-permute-done.1.refs_2_), channel_id=1, source_target_pairs={{0,4},{4,8},{8,12},{12,0},{1,5},{5,9},{9,13},{13,1},{2,6},{6,10},{... | collective-permute-start | bytes 983048 | tf_op jit(solution)/shard_map/ppermute | solution.py:24
  49.1 6.0 %collective-permute-done.16.query = bf16[128,640]{1,0:T(8,128)(2,1)S(1)} collective-permute-done((bf16[128,640]{1,0:T(8,128)(2,1)S(1)}, bf16[128,640]{1,0:T(8,128)(2,1)S(1)}, u32[]{:S(2)}, u32[]{:S(2)}) %collective-permute-start.16) | collective-permute-done | bytes 163872 | tf_op jit(solution)/shard_map/ppermute | solution.py:24
  55.1 0.0 collective-permute-start.10
  55.1 16.5 %collective-permute-done.10.query = bf16[128,640]{1,0:T(8,128)(2,1)S(1)} collective-permute-done((bf16[128,640]{1,0:T(8,128)(2,1)S(1)}, bf16[128,640]{1,0:T(8,128)(2,1)S(1)}, u32[]{:S(2)}, u32[]{:S(2)}) %collective-permute-start.10) | collective-permute-done | bytes 163872 | tf_op jit(solution)/shard_map/ppermute | solution.py:24
  71.6 0.0 collective-permute-start.17
  71.6 0.0 collective-permute-done.7.refs_9_
  71.6 2.8 %early_step.3 = (f32[480,640]{1,0:T(8,128)S(1)}, bf16[480,640]{1,0:T(8,128)(2,1)S(1)}) custom-call(s32[1]{0:T(128)} %bitcast.rep, bf16[128,1280]{1,0:T(8,128)(2,1)} %copy-done, bf16[128,1280]{1,0:T(8,128)(2,1)} %collective-permute-done.refs_1_.key_prior, bf16[128,1280]{1,0:T(8,128)(2,1)} %copy-done.5, bf16[128,1280]{1,0:T(8,128)(2,1)} %copy-done.1, ...), custom_call_target="tpu_custom_call" | custom-call | flops 471859200 | bytes 3072000 | tf_op jit(solution)/shard_map/early_step/pallas_call | solution.py:260
  74.5 0.0 collective-permute-done.2.key
  74.5 1.7 %last_step.3 = (f32[1,3,80,640]{3,2,1,0:T(8,128)}, f32[1,3,80,640]{3,2,1,0:T(8,128)}, bf16[480,640]{1,0:T(8,128)(2,1)S(1)}) custom-call(bf16[128,1280]{1,0:T(8,128)(2,1)S(1)} %collective-permute-done.2.key, bf16[128,1280]{1,0:T(8,128)(2,1)S(1)} %collective-permute-done.5.cotangent, f32[480,640]{1,0:T(8,128)S(1)} %get-tuple-element.26.so_far, ...), custom_call_target="tpu_custom_call" | custom-call | flops 157286400 | bytes 3686400 | tf_op jit(solution)/shard_map/last_step/pallas_call | solution.py:307
  76.2 0.5 apply_step.15
  76.8 0.8 collective-permute-start.18
  77.6 0.0 collective-permute-start.21
  77.6 2.8 %early_step.2 = (f32[480,640]{1,0:T(8,128)S(1)}, bf16[480,640]{1,0:T(8,128)(2,1)S(1)}) custom-call(s32[1]{0:T(128)} %bitcast.rep, bf16[128,1280]{1,0:T(8,128)(2,1)} %copy-done, bf16[128,1280]{1,0:T(8,128)(2,1)} %collective-permute-done.refs_1_.key_prior, bf16[128,1280]{1,0:T(8,128)(2,1)} %copy-done.5, bf16[128,1280]{1,0:T(8,128)(2,1)} %copy-done.1, ...), custom_call_target="tpu_custom_call" | custom-call | flops 471859200 | bytes 3072000 | tf_op jit(solution)/shard_map/early_step/pallas_call | solution.py:260
  80.4 1.7 %last_step.2 = (f32[1,3,80,640]{3,2,1,0:T(8,128)}, f32[1,3,80,640]{3,2,1,0:T(8,128)}, bf16[480,640]{1,0:T(8,128)(2,1)S(1)}) custom-call(bf16[128,1280]{1,0:T(8,128)(2,1)S(1)} %collective-permute-done.2.key, bf16[128,1280]{1,0:T(8,128)(2,1)S(1)} %collective-permute-done.5.cotangent, f32[480,640]{1,0:T(8,128)S(1)} %get-tuple-element.21.so_far, ...), custom_call_target="tpu_custom_call" | custom-call | flops 157286400 | bytes 3686400 | tf_op jit(solution)/shard_map/last_step/pallas_call | solution.py:307
  82.1 0.5 collective-permute-start.22
  82.6 0.5 apply_step.14
  83.2 0.5 apply_step.10
  83.7 0.5 apply_step.11
  84.2 0.0 copy-start.9
  84.2 0.0 collective-permute-done.17.query
  84.2 4.2 %collective-permute-start.12 = (bf16[128,640]{1,0:T(8,128)(2,1)S(1)}, bf16[128,640]{1,0:T(8,128)(2,1)S(1)}, u32[]{:S(2)}, u32[]{:S(2)}) collective-permute-start(bf16[128,640]{1,0:T(8,128)(2,1)S(1)} %apply_step.11), channel_id=1, source_target_pairs={{0,4},{4,8},{8,12},{12,0},{1,5},{5,9},{9,13},{13,1},{2,6},{6,10},{... | collective-permute-start | bytes 491528 | tf_op jit(solution)/shard_map/ppermute | solution.py:24
  88.4 0.5 apply_step.13
  88.9 0.0 collective-permute-done.11.query
  88.9 0.5 apply_step.9
  89.4 0.0 collective-permute-done.18
  89.5 0.1 collective-permute-start.19
  89.6 3.4 %collective-permute-done.12 = bf16[128,640]{1,0:T(8,128)(2,1)S(1)} collective-permute-done((bf16[128,640]{1,0:T(8,128)(2,1)S(1)}, bf16[128,640]{1,0:T(8,128)(2,1)S(1)}, u32[]{:S(2)}, u32[]{:S(2)}) %collective-permute-start.12) | collective-permute-done | bytes 163872 | tf_op jit(solution)/shard_map/ppermute | solution.py:24
  93.0 2.5 %collective-permute-start.13 = (bf16[128,640]{1,0:T(8,128)(2,1)S(1)}, bf16[128,640]{1,0:T(8,128)(2,1)S(1)}, u32[]{:S(2)}, u32[]{:S(2)}) collective-permute-start(bf16[128,640]{1,0:T(8,128)(2,1)S(1)} %add_convert_fusion.3), channel_id=1, source_target_pairs={{0,4},{4,8},{8,12},{12,0},{1,5},{5,9},{9,13},{13,1},{2,6},{6,10},{... | collective-permute-start | bytes 491528 | tf_op jit(solution)/shard_map/ppermute | solution.py:24
  95.6 2.8 %collective-permute-done.19 = bf16[128,640]{1,0:T(8,128)(2,1)S(1)} collective-permute-done((bf16[128,640]{1,0:T(8,128)(2,1)S(1)}, bf16[128,640]{1,0:T(8,128)(2,1)S(1)}, u32[]{:S(2)}, u32[]{:S(2)}) %collective-permute-start.19) | collective-permute-done | bytes 163872 | tf_op jit(solution)/shard_map/ppermute | solution.py:24
  98.5 0.6 collective-permute-start.20
  99.1 1.7 %collective-permute-done.13 = bf16[128,640]{1,0:T(8,128)(2,1)S(1)} collective-permute-done((bf16[128,640]{1,0:T(8,128)(2,1)S(1)}, bf16[128,640]{1,0:T(8,128)(2,1)S(1)}, u32[]{:S(2)}, u32[]{:S(2)}) %collective-permute-start.13) | collective-permute-done | bytes 163872 | tf_op jit(solution)/shard_map/ppermute | solution.py:24
  100.9 1.9 %collective-permute-start.14 = (bf16[128,640]{1,0:T(8,128)(2,1)S(1)}, bf16[128,640]{1,0:T(8,128)(2,1)S(1)}, u32[]{:S(2)}, u32[]{:S(2)}) collective-permute-start(bf16[128,640]{1,0:T(8,128)(2,1)S(1)} %add_convert_fusion.2), channel_id=1, source_target_pairs={{0,4},{4,8},{8,12},{12,0},{1,5},{5,9},{9,13},{13,1},{2,6},{6,10},{... | collective-permute-start | bytes 491528 | tf_op jit(solution)/shard_map/ppermute | solution.py:24
  102.8 0.1 collective-permute-start.8
  102.9 6.3 %collective-permute-done.8.rate_prior = f32[2,1,128]{2,1,0:T(1,128)S(1)} collective-permute-done((f32[2,1,128]{2,1,0:T(1,128)S(1)}, f32[2,1,128]{2,1,0:T(1,128)S(1)}, u32[]{:S(2)}, u32[]{:S(2)}) %collective-permute-start.8) | collective-permute-done | bytes 1056 | tf_op jit(solution)/shard_map/ppermute | solution.py:24
  109.2 2.4 %attend_step.1 = (f32[128,640]{1,0:T(8,128)S(1)}, f32[128,640]{1,0:T(8,128)S(1)}) custom-call(s32[1]{0:T(128)} %bitcast.1.first, bf16[128,1280]{1,0:T(8,128)(2,1)} %copy-done, bf16[128,1280]{1,0:T(8,128)(2,1)} %collective-permute-done.refs_1_.key_prior, bf16[128,1280]{1,0:T(8,128)(2,1)} %copy-done.2, bf16[128,1280]{1,0:T(8,128)(2,1)} %copy-done.3, ...), custom_call_target="tpu_custom_call" | custom-call | flops 167772160 | bytes 2293760 | tf_op jit(solution)/shard_map/attend_step/pallas_call | solution.py:407
  111.6 0.0 copy-start.7
  111.6 0.5 apply_step.12.kept
  112.2 0.5 apply_step.8.kept
  112.7 0.0 collective-permute-done.20.moved
  112.7 0.7 output_step.2.refs_0_
  113.4 0.7 output_step.3
  114.1 0.0 collective-permute-done.21
  114.1 0.0 collective-permute-done.22
  114.1 3.4 %maximum_select_fusion = f32[4,3,80,640]{3,2,1,0:T(8,128)} fusion(f32[1,3,80,640]{3,2,1,0:T(8,128)} %collective-permute-done.22, f32[1,3,80,640]{3,2,1,0:T(8,128)} %collective-permute-done.21, f32[1,3,80,640]{3,2,1,0:T(8,128)S(1)} %copy-done.7, f32[1,3,80,640]{3,2,1,0:T(8,128)S(1)} %copy-done.6, pred[]{:T(512)S(6)} %eq.7), kind=kLoop, calls=%fused_computation | loop fusion | flops 4300800 | bytes 4915201 | tf_op jit(solution)/shard_map/jit(_where)/select_n | solution.py:475
  (27 shorter events, 0.2 us)
Async XLA Ops:
  0.6 9.7 %copy-start.8 = (bf16[128,2560]{1,0:T(8,128)(2,1)S(1)}, bf16[128,2560]{1,0:T(8,128)(2,1)}, u32[]{:S(2)}) copy-start(bf16[128,2560]{1,0:T(8,128)(2,1)} %param.6) | copy-start | bytes 1966084
  3.4 68.2 %collective-permute-start.7 = (f32[2,3,80,640]{3,2,1,0:T(8,128)}, f32[2,3,80,640]{3,2,1,0:T(8,128)S(1)}, u32[]{:S(2)}, u32[]{:S(2)}) collective-permute-start(f32[2,3,80,640]{3,2,1,0:T(8,128)} %get-tuple-element.20), channel_id=1, source_target_pairs={{0,1},{1,0},{2,3},{3,2},{4,5},{5,4},{6,7},{7,6},{8,9},{9,8},{10,11... | collective-permute-start | bytes 3686408 | tf_op jit(solution)/shard_map/ppermute | solution.py:24
  5.1 5.3 %copy-start.2 = (bf16[128,1280]{1,0:T(8,128)(2,1)}, bf16[128,1280]{1,0:T(8,128)(2,1)S(1)}, u32[]{:S(2)}) copy-start(bf16[128,1280]{1,0:T(8,128)(2,1)S(1)} %get-tuple-element.24.value_own) | copy-start | bytes 983044
  5.1 66.5 %copy-start.1 = (bf16[128,1280]{1,0:T(8,128)(2,1)}, bf16[128,1280]{1,0:T(8,128)(2,1)S(1)}, u32[]{:S(2)}) copy-start(bf16[128,1280]{1,0:T(8,128)(2,1)S(1)} %get-tuple-element.18.refs_3_) | copy-start | bytes 983044
  5.1 13.2 %collective-permute-start.3 = (bf16[128,1280]{1,0:T(8,128)(2,1)S(1)}, bf16[128,1280]{1,0:T(8,128)(2,1)S(1)}, u32[]{:S(2)}, u32[]{:S(2)}) collective-permute-start(bf16[128,1280]{1,0:T(8,128)(2,1)S(1)} %get-tuple-element.18.refs_3_), channel_id=1, source_target_pairs={{0,4},{4,8},{8,12},{12,0},{1,5},{5,9},{9,13},{13,1},{2,6},{6,10},{... | collective-permute-start | bytes 983048 | tf_op jit(solution)/shard_map/ppermute | solution.py:24
  8.7 62.9 %copy-start = (bf16[128,1280]{1,0:T(8,128)(2,1)}, bf16[128,1280]{1,0:T(8,128)(2,1)S(1)}, u32[]{:S(2)}) copy-start(bf16[128,1280]{1,0:T(8,128)(2,1)S(1)} %columns_step.1.refs_0_.key_own) | copy-start | bytes 983044
  8.7 16.7 %collective-permute-start = (bf16[128,1280]{1,0:T(8,128)(2,1)S(1)}, bf16[128,1280]{1,0:T(8,128)(2,1)}, u32[]{:S(2)}, u32[]{:S(2)}) collective-permute-start(bf16[128,1280]{1,0:T(8,128)(2,1)S(1)} %columns_step.1.refs_0_.key_own), channel_id=1, source_target_pairs={{0,4},{4,8},{8,12},{12,0},{1,5},{5,9},{9,13},{13,1},{2,6},{6,10},{... | collective-permute-start | bytes 983048 | tf_op jit(solution)/shard_map/ppermute | solution.py:24
  10.4 18.4 %collective-permute-start.15 = (bf16[128,640]{1,0:T(8,128)(2,1)S(1)}, bf16[128,640]{1,0:T(8,128)(2,1)S(1)}, u32[]{:S(2)}, u32[]{:S(2)}) collective-permute-start(bf16[128,640]{1,0:T(8,128)(2,1)S(1)} %get-tuple-element.34.refs_0_.query), channel_id=1, source_target_pairs={{0,4},{4,8},{8,12},{12,0},{1,5},{5,9},{9,13},{13,1},{2,6},{6,10},{... | collective-permute-start | bytes 491528 | tf_op jit(solution)/shard_map/ppermute | solution.py:24
  12.0 59.6 %collective-permute-start.6 = (bf16[2,3,80,640]{3,2,1,0:T(8,128)(2,1)}, bf16[2,3,80,640]{3,2,1,0:T(8,128)(2,1)S(1)}, u32[]{:S(2)}, u32[]{:S(2)}) collective-permute-start(bf16[2,3,80,640]{3,2,1,0:T(8,128)(2,1)} %get-tuple-element.19), channel_id=1, source_target_pairs={{0,1},{1,0},{2,3},{3,2},{4,5},{5,4},{6,7},{7,6},{8,9},{9,8},{10,11... | collective-permute-start | bytes 1843208 | tf_op jit(solution)/shard_map/ppermute | solution.py:24
  18.3 53.3 %copy-start.3 = (bf16[128,1280]{1,0:T(8,128)(2,1)}, bf16[128,1280]{1,0:T(8,128)(2,1)S(1)}, u32[]{:S(2)}) copy-start(bf16[128,1280]{1,0:T(8,128)(2,1)S(1)} %collective-permute-done.3.refs_4_.cot_prior) | copy-start | bytes 983044
  18.3 27.9 %collective-permute-start.4 = (bf16[128,1280]{1,0:T(8,128)(2,1)S(1)}, bf16[128,1280]{1,0:T(8,128)(2,1)S(1)}, u32[]{:S(2)}, u32[]{:S(2)}) collective-permute-start(bf16[128,1280]{1,0:T(8,128)(2,1)S(1)} %collective-permute-done.3.refs_4_.cot_prior), channel_id=1, source_target_pairs={{0,4},{4,8},{8,12},{12,0},{1,5},{5,9},{9,13},{13,1},{2,6},{6,10},{... | collective-permute-start | bytes 983048 | tf_op jit(solution)/shard_map/ppermute | solution.py:24
  25.4 22.1 %collective-permute-start.1 = (bf16[128,1280]{1,0:T(8,128)(2,1)}, bf16[128,1280]{1,0:T(8,128)(2,1)S(1)}, u32[]{:S(2)}, u32[]{:S(2)}) collective-permute-start(bf16[128,1280]{1,0:T(8,128)(2,1)} %collective-permute-done.refs_1_.key_prior), channel_id=1, source_target_pairs={{0,4},{4,8},{8,12},{12,0},{1,5},{5,9},{9,13},{13,1},{2,6},{6,10},{... | collective-permute-start | bytes 983048 | tf_op jit(solution)/shard_map/ppermute | solution.py:24
  28.8 17.4 %collective-permute-start.9 = (bf16[128,640]{1,0:T(8,128)(2,1)S(1)}, bf16[128,640]{1,0:T(8,128)(2,1)S(1)}, u32[]{:S(2)}, u32[]{:S(2)}) collective-permute-start(bf16[128,640]{1,0:T(8,128)(2,1)S(1)} %get-tuple-element.35.refs_1_.query), channel_id=1, source_target_pairs={{0,4},{4,8},{8,12},{12,0},{1,5},{5,9},{9,13},{13,1},{2,6},{6,10},{... | collective-permute-start | bytes 491528 | tf_op jit(solution)/shard_map/ppermute | solution.py:24
  46.2 8.9 %collective-permute-start.16 = (bf16[128,640]{1,0:T(8,128)(2,1)S(1)}, bf16[128,640]{1,0:T(8,128)(2,1)S(1)}, u32[]{:S(2)}, u32[]{:S(2)}) collective-permute-start(bf16[128,640]{1,0:T(8,128)(2,1)S(1)} %collective-permute-done.15.query), channel_id=1, source_target_pairs={{0,4},{4,8},{8,12},{12,0},{1,5},{5,9},{9,13},{13,1},{2,6},{6,10},{... | collective-permute-start | bytes 491528 | tf_op jit(solution)/shard_map/ppermute | solution.py:24
  46.2 25.4 %copy-start.4 = (bf16[128,1280]{1,0:T(8,128)(2,1)}, bf16[128,1280]{1,0:T(8,128)(2,1)S(1)}, u32[]{:S(2)}) copy-start(bf16[128,1280]{1,0:T(8,128)(2,1)S(1)} %collective-permute-done.4.refs_5_) | copy-start | bytes 983044
  46.2 28.3 %collective-permute-start.5 = (bf16[128,1280]{1,0:T(8,128)(2,1)S(1)}, bf16[128,1280]{1,0:T(8,128)(2,1)S(1)}, u32[]{:S(2)}, u32[]{:S(2)}) collective-permute-start(bf16[128,1280]{1,0:T(8,128)(2,1)S(1)} %collective-permute-done.4.refs_5_), channel_id=1, source_target_pairs={{0,4},{4,8},{8,12},{12,0},{1,5},{5,9},{9,13},{13,1},{2,6},{6,10},{... | collective-permute-start | bytes 983048 | tf_op jit(solution)/shard_map/ppermute | solution.py:24
  47.5 24.2 %copy-start.5 = (bf16[128,1280]{1,0:T(8,128)(2,1)}, bf16[128,1280]{1,0:T(8,128)(2,1)S(1)}, u32[]{:S(2)}) copy-start(bf16[128,1280]{1,0:T(8,128)(2,1)S(1)} %collective-permute-done.1.refs_2_) | copy-start | bytes 983044
  47.5 27.0 %collective-permute-start.2 = (bf16[128,1280]{1,0:T(8,128)(2,1)S(1)}, bf16[128,1280]{1,0:T(8,128)(2,1)S(1)}, u32[]{:S(2)}, u32[]{:S(2)}) collective-permute-start(bf16[128,1280]{1,0:T(8,128)(2,1)S(1)} %collective-permute-done.1.refs_2_), channel_id=1, source_target_pairs={{0,4},{4,8},{8,12},{12,0},{1,5},{5,9},{9,13},{13,1},{2,6},{6,10},{... | collective-permute-start | bytes 983048 | tf_op jit(solution)/shard_map/ppermute | solution.py:24
  55.1 16.5 %collective-permute-start.10 = (bf16[128,640]{1,0:T(8,128)(2,1)S(1)}, bf16[128,640]{1,0:T(8,128)(2,1)S(1)}, u32[]{:S(2)}, u32[]{:S(2)}) collective-permute-start(bf16[128,640]{1,0:T(8,128)(2,1)S(1)} %collective-permute-done.9.query), channel_id=1, source_target_pairs={{0,4},{4,8},{8,12},{12,0},{1,5},{5,9},{9,13},{13,1},{2,6},{6,10},{... | collective-permute-start | bytes 491528 | tf_op jit(solution)/shard_map/ppermute | solution.py:24
  71.6 12.6 %collective-permute-start.17 = (bf16[128,640]{1,0:T(8,128)(2,1)S(1)}, bf16[128,640]{1,0:T(8,128)(2,1)S(1)}, u32[]{:S(2)}, u32[]{:S(2)}) collective-permute-start(bf16[128,640]{1,0:T(8,128)(2,1)S(1)} %collective-permute-done.16.query), channel_id=1, source_target_pairs={{0,4},{4,8},{8,12},{12,0},{1,5},{5,9},{9,13},{13,1},{2,6},{6,10},{... | collective-permute-start | bytes 491528 | tf_op jit(solution)/shard_map/ppermute | solution.py:24
  71.6 17.3 %collective-permute-start.11 = (bf16[128,640]{1,0:T(8,128)(2,1)S(1)}, bf16[128,640]{1,0:T(8,128)(2,1)S(1)}, u32[]{:S(2)}, u32[]{:S(2)}) collective-permute-start(bf16[128,640]{1,0:T(8,128)(2,1)S(1)} %collective-permute-done.10.query), channel_id=1, source_target_pairs={{0,4},{4,8},{8,12},{12,0},{1,5},{5,9},{9,13},{13,1},{2,6},{6,10},{... | collective-permute-start | bytes 491528 | tf_op jit(solution)/shard_map/ppermute | solution.py:24
  76.8 12.7 %collective-permute-start.18 = (bf16[128,640]{1,0:T(8,128)(2,1)S(1)}, bf16[128,640]{1,0:T(8,128)(2,1)S(1)}, u32[]{:S(2)}, u32[]{:S(2)}) collective-permute-start(bf16[128,640]{1,0:T(8,128)(2,1)S(1)} %apply_step.15), channel_id=1, source_target_pairs={{0,4},{4,8},{8,12},{12,0},{1,5},{5,9},{9,13},{13,1},{2,6},{6,10},{... | collective-permute-start | bytes 491528 | tf_op jit(solution)/shard_map/ppermute | solution.py:24
  77.6 36.5 %collective-permute-start.21 = (f32[1,3,80,640]{3,2,1,0:T(8,128)}, f32[1,3,80,640]{3,2,1,0:T(8,128)}, u32[]{:S(2)}, u32[]{:S(2)}) collective-permute-start(f32[1,3,80,640]{3,2,1,0:T(8,128)} %get-tuple-element.32), channel_id=1, source_target_pairs={{0,1},{1,0},{2,3},{3,2},{4,5},{5,4},{6,7},{7,6},{8,9},{9,8},{10,11... | collective-permute-start | bytes 1843208 | tf_op jit(solution)/shard_map/ppermute | solution.py:24
  82.1 32.0 %collective-permute-start.22 = (f32[1,3,80,640]{3,2,1,0:T(8,128)}, f32[1,3,80,640]{3,2,1,0:T(8,128)}, u32[]{:S(2)}, u32[]{:S(2)}) collective-permute-start(f32[1,3,80,640]{3,2,1,0:T(8,128)} %get-tuple-element.33), channel_id=1, source_target_pairs={{0,1},{1,0},{2,3},{3,2},{4,5},{5,4},{6,7},{7,6},{8,9},{9,8},{10,11... | collective-permute-start | bytes 1843208 | tf_op jit(solution)/shard_map/ppermute | solution.py:24
  84.2 18.6 %copy-start.9 = (f32[4,128]{1,0:T(4,128)S(1)}, f32[4,128]{1,0:T(4,128)}, u32[]{:S(2)}) copy-start(f32[4,128]{1,0:T(4,128)} %rates.1) | copy-start | bytes 6148
  84.2 8.8 %collective-permute-start.12 = (bf16[128,640]{1,0:T(8,128)(2,1)S(1)}, bf16[128,640]{1,0:T(8,128)(2,1)S(1)}, u32[]{:S(2)}, u32[]{:S(2)}) collective-permute-start(bf16[128,640]{1,0:T(8,128)(2,1)S(1)} %apply_step.11), channel_id=1, source_target_pairs={{0,4},{4,8},{8,12},{12,0},{1,5},{5,9},{9,13},{13,1},{2,6},{6,10},{... | collective-permute-start | bytes 491528 | tf_op jit(solution)/shard_map/ppermute | solution.py:24
  89.5 8.9 %collective-permute-start.19 = (bf16[128,640]{1,0:T(8,128)(2,1)S(1)}, bf16[128,640]{1,0:T(8,128)(2,1)S(1)}, u32[]{:S(2)}, u32[]{:S(2)}) collective-permute-start(bf16[128,640]{1,0:T(8,128)(2,1)S(1)} %add_convert_fusion.1), channel_id=1, source_target_pairs={{0,4},{4,8},{8,12},{12,0},{1,5},{5,9},{9,13},{13,1},{2,6},{6,10},{... | collective-permute-start | bytes 491528 | tf_op jit(solution)/shard_map/ppermute | solution.py:24
  93.0 7.8 %collective-permute-start.13 = (bf16[128,640]{1,0:T(8,128)(2,1)S(1)}, bf16[128,640]{1,0:T(8,128)(2,1)S(1)}, u32[]{:S(2)}, u32[]{:S(2)}) collective-permute-start(bf16[128,640]{1,0:T(8,128)(2,1)S(1)} %add_convert_fusion.3), channel_id=1, source_target_pairs={{0,4},{4,8},{8,12},{12,0},{1,5},{5,9},{9,13},{13,1},{2,6},{6,10},{... | collective-permute-start | bytes 491528 | tf_op jit(solution)/shard_map/ppermute | solution.py:24
  98.5 14.2 %collective-permute-start.20 = (bf16[128,640]{1,0:T(8,128)(2,1)S(1)}, bf16[128,640]{1,0:T(8,128)(2,1)S(1)}, u32[]{:S(2)}, u32[]{:S(2)}) collective-permute-start(bf16[128,640]{1,0:T(8,128)(2,1)S(1)} %add_convert_fusion), channel_id=1, source_target_pairs={{0,4},{4,8},{8,12},{12,0},{1,5},{5,9},{9,13},{13,1},{2,6},{6,10},{... | collective-permute-start | bytes 491528 | tf_op jit(solution)/shard_map/ppermute | solution.py:24
  100.9 12.5 %collective-permute-start.14 = (bf16[128,640]{1,0:T(8,128)(2,1)S(1)}, bf16[128,640]{1,0:T(8,128)(2,1)S(1)}, u32[]{:S(2)}, u32[]{:S(2)}) collective-permute-start(bf16[128,640]{1,0:T(8,128)(2,1)S(1)} %add_convert_fusion.2), channel_id=1, source_target_pairs={{0,4},{4,8},{8,12},{12,0},{1,5},{5,9},{9,13},{13,1},{2,6},{6,10},{... | collective-permute-start | bytes 491528 | tf_op jit(solution)/shard_map/ppermute | solution.py:24
  102.8 6.4 %collective-permute-start.8 = (f32[2,1,128]{2,1,0:T(1,128)S(1)}, f32[2,1,128]{2,1,0:T(1,128)S(1)}, u32[]{:S(2)}, u32[]{:S(2)}) collective-permute-start(f32[2,1,128]{2,1,0:T(1,128)S(1)} %bitcast.3), channel_id=1, source_target_pairs={{0,4},{4,8},{8,12},{12,0},{1,5},{5,9},{9,13},{13,1},{2,6},{6,10},{... | collective-permute-start | bytes 3080 | tf_op jit(solution)/shard_map/ppermute | solution.py:24
  111.6 2.5 %copy-start.6 = (f32[1,3,80,640]{3,2,1,0:T(8,128)S(1)}, f32[1,3,80,640]{3,2,1,0:T(8,128)}, u32[]{:S(2)}) copy-start(f32[1,3,80,640]{3,2,1,0:T(8,128)} %get-tuple-element.30) | copy-start | bytes 1843204
  111.6 2.5 %copy-start.7 = (f32[1,3,80,640]{3,2,1,0:T(8,128)S(1)}, f32[1,3,80,640]{3,2,1,0:T(8,128)}, u32[]{:S(2)}) copy-start(f32[1,3,80,640]{3,2,1,0:T(8,128)} %get-tuple-element.31) | copy-start | bytes 1843204

commit v4 on v3

--- a/solution.py
+++ b/solution.py
@@ -358,13 +358,13 @@
 
 def output_step(head, heads, kept, moved, before):
     rows, width = kept.shape
-    whole = pl.BlockSpec((rows, width), lambda i: (0, 0))
     more = () if before is None else (before,)
     return pl.pallas_call(
         output_body,
         out_shape=pltpu.HBM((rows, heads * width), jnp.bfloat16),
         grid=(1,),
-        in_specs=[whole, whole] + [pl.BlockSpec(memory_space=pl.ANY)] * len(more),
+        in_specs=[pl.BlockSpec(memory_space=pltpu.VMEM)] * 2
+        + [pl.BlockSpec(memory_space=pl.ANY)] * len(more),
         out_specs=pl.BlockSpec((rows, width), lambda i: (0, head)),
         input_output_aliases={2: 0} if more else {},
         compiler_params=pltpu.CompilerParams(vmem_limit_bytes=4 << 20),
@@ -424,8 +424,8 @@
     start = rep_index * per_rep
     token_scale = float(slots * queries.shape[0]) ** (-0.5)
 
-    def hop(value, axis="ctx"):
-        return ring(value, axis)
+    def hop(value, axis="ctx", steps=-1):
+        return ring(value, axis, steps)
 
     rep = rep_index.reshape(1)
     value_own, cot = cotangent_step(token_scale, rep, values, learn_rates)
@@ -435,7 +435,7 @@
     for _ in range(1, slots):
         keys.append(hop(keys[-1]))
         cots.append(hop(cots[-1]))
-    rate_prior = hop(lax.dynamic_slice_in_dim(learn_rates, start, per_rep, 0)[:, None, :])
+    rate_prior = hop(lax.dynamic_slice_in_dim(learn_rates, start, per_rep, 0)[:, None, :], steps=1)
     low_other, base_other = other_step(rep, fast_weights, momentum)
     low_par = hop(low_other, "rep")
     base_par = hop(base_other, "rep")
@@ -443,7 +443,7 @@
         asked.append([hop(asked[-1][h]) for h in heads])
     first = (lax.axis_index("ctx") == 0).astype(jnp.int32).reshape(1)
     attended = attend_step(
-        token_scale, first, keys[0], keys[1], value_own, cots[1], rate_prior, asked[0]
+        token_scale, first, keys[0], keys[-1], value_own, cots[-1], rate_prior, asked[0]
     )
     early = []
     for h in heads:
@@ -458,14 +458,15 @@
     lows = [new[2] for new in fresh]
     moving = []
     for step in range(1, slots):
-        if step == 1:
-            sent = [apply_step(asked[step][h], lows[h], jnp.bfloat16) for h in heads]
-        else:
-            made = [apply_step(asked[step][h], lows[h], jnp.float32) for h in heads]
-            sent = [
+        made = []
+        for h in heads:
+            kind = jnp.bfloat16 if step == 1 else jnp.float32
+            made.append(apply_step(asked[step][h], lows[h], kind))
+        if step > 1:
+            made = [
                 (made[h] + moving[h].astype(jnp.float32)).astype(jnp.bfloat16) for h in heads
             ]
-        moving = [hop(sent[h]) for h in heads]
+        moving = [hop(made[h]) for h in heads]
     layer_output = None
     for h in heads:
         kept = apply_step(asked[0][h], lows[h], jnp.float32, attended[h])

time: 118 us -> 118 us (level)
  waiting for transfers between devices: 71 us -> 44.4 us
  starting transfers between devices: 20.1 us -> 45.9 us
  local copies, waits for them, and re-layouts: 0.09 us -> 1.43 us
    ppermute x23, waiting for transfers between devices: 71 us -> 44.4 us  [ring(): lax.ppermute(value, axis, [(source, (source + steps) % count) for source...]
    ppermute x23, starting transfers between devices: 20.1 us -> 45.9 us  [ring(): lax.ppermute(value, axis, [(source, (source + steps) % count) for source...]
    unnamed x20 -> x34, local copies, waits for them, and re-layouts: 0.05 us -> 1.39 us
  transfers between devices with their start and end apart: 23 -> 23, of which waited for: 10 -> 8; matrix products, arithmetic and copies ran while one was open for 0% -> 0% of each run, Pallas kernels for 16% -> 16%
where the time goes in v4:
time: 118 us
  starting transfers between devices  45.9 us (39%)
  waiting for transfers between devices  44.4 us (38%)
  Pallas kernels  22 us (19%)
  other arithmetic  3.07 us (3%)
  local copies, waits for them, and re-layouts  1.43 us (1%)
    ppermute x23, starting transfers between devices, ring(): lax.ppermute(value, axis, [(source, (source + steps) % count) for source...  45.9 us
    ppermute x23, waiting for transfers between devices, ring(): lax.ppermute(value, axis, [(source, (source + steps) % count) for source...  44.4 us
    pallas_call x2, Pallas kernels, early_step(): pl.pallas_call(functools.partial(early_body, slots), out_shape=(jax.Shape...  5.66 us
    pallas_call x8, Pallas kernels, apply_step(): pl.pallas_call(apply_body, out_shape=jax.ShapeDtypeStruct((rows, width),...  4.09 us
    pallas_call x2, Pallas kernels, last_step(): pl.pallas_call(last_body, out_shape=(fresh, fresh, jax.ShapeDtypeStruct((...  3.49 us
    select_n x1, other arithmetic, tokens_travel(): jnp.where(rep_index == 0, jnp.concatenate([*owned, *returned], axis=0), j...  2.91 us
    pallas_call x1, Pallas kernels, other_step(): pl.pallas_call(other_body, out_shape=(pltpu.HBM(made, jnp.bfloat16), pltp...  2.74 us
    pallas_call x1, Pallas kernels, attend_step(): pl.pallas_call(functools.partial(attend_body, token_scale), out_shape=mad...  2.43 us
  transfers between devices with their start and end apart: 23, of which 8 were waited for; matrix products, arithmetic and copies ran while one was open for 0% of the time, Pallas kernels for 16%

profile of v4, /device:TPU:0, one launch (start us, length us, event | category | flops | bytes accessed | tf_op | source)
XLA Modules:
  0.0 117.8 jit_solution(16652245606699911356)
XLA Ops:
  0.6 2.7 %other_step.1 = (bf16[2,3,80,640]{3,2,1,0:T(8,128)(2,1)}, f32[2,3,80,640]{3,2,1,0:T(8,128)}) custom-call(s32[1]{0:T(128)} %bitcast.rep, f32[4,3,80,640]{3,2,1,0:T(8,128)} %refs_6_.3, f32[4,3,80,640]{3,2,1,0:T(8,128)} %refs_7_.3), custom_call_target="tpu_custom_call" | custom-call | flops 614400 | bytes 4300800 | tf_op jit(solution)/shard_map/other_step/pallas_call | solution.py:203
  3.4 0.5 collective-permute-start.7
  3.9 1.2 cotangent_step.1
  5.1 4.6 %collective-permute-start.3 = (bf16[128,1280]{1,0:T(8,128)(2,1)S(1)}, bf16[128,1280]{1,0:T(8,128)(2,1)S(1)}, u32[]{:S(2)}, u32[]{:S(2)}) collective-permute-start(bf16[128,1280]{1,0:T(8,128)(2,1)S(1)} %get-tuple-element.18.refs_3_), channel_id=1, source_target_pairs={{0,12},{4,0},{8,4},{12,8},{1,13},{5,1},{9,5},{13,9},{2,14},{6,2},{... | collective-permute-start | bytes 983048 | tf_op jit(solution)/shard_map/ppermute | solution.py:24
  9.7 1.0 columns_step.1.refs_0_.key_own
  10.7 0.0 copy-start
  10.7 0.5 collective-permute-start
  11.3 0.5 collective-permute-start.15
  11.8 0.7 copy-done.5
  12.4 5.4 %collective-permute-done.3.refs_4_ = bf16[128,1280]{1,0:T(8,128)(2,1)S(1)} collective-permute-done((bf16[128,1280]{1,0:T(8,128)(2,1)S(1)}, bf16[128,1280]{1,0:T(8,128)(2,1)S(1)}, u32[]{:S(2)}, u32[]{:S(2)}) %collective-permute-start.3) | collective-permute-done | bytes 327712 | tf_op jit(solution)/shard_map/ppermute | solution.py:24
  17.8 4.3 %collective-permute-start.4 = (bf16[128,1280]{1,0:T(8,128)(2,1)S(1)}, bf16[128,1280]{1,0:T(8,128)(2,1)S(1)}, u32[]{:S(2)}, u32[]{:S(2)}) collective-permute-start(bf16[128,1280]{1,0:T(8,128)(2,1)S(1)} %collective-permute-done.3.refs_4_), channel_id=1, source_target_pairs={{0,12},{4,0},{8,4},{12,8},{1,13},{5,1},{9,5},{13,9},{2,14},{6,2},{... | collective-permute-start | bytes 983048 | tf_op jit(solution)/shard_map/ppermute | solution.py:24
  22.1 2.7 %collective-permute-done.refs_1_ = bf16[128,1280]{1,0:T(8,128)(2,1)S(1)} collective-permute-done((bf16[128,1280]{1,0:T(8,128)(2,1)S(1)}, bf16[128,1280]{1,0:T(8,128)(2,1)S(1)}, u32[]{:S(2)}, u32[]{:S(2)}) %collective-permute-start) | collective-permute-done | bytes 327712 | tf_op jit(solution)/shard_map/ppermute | solution.py:24
  24.8 4.3 %collective-permute-start.1 = (bf16[128,1280]{1,0:T(8,128)(2,1)S(1)}, bf16[128,1280]{1,0:T(8,128)(2,1)S(1)}, u32[]{:S(2)}, u32[]{:S(2)}) collective-permute-start(bf16[128,1280]{1,0:T(8,128)(2,1)S(1)} %collective-permute-done.refs_1_), channel_id=1, source_target_pairs={{0,12},{4,0},{8,4},{12,8},{1,13},{5,1},{9,5},{13,9},{2,14},{6,2},{... | collective-permute-start | bytes 983048 | tf_op jit(solution)/shard_map/ppermute | solution.py:24
  29.1 3.5 %collective-permute-start.9 = (bf16[128,640]{1,0:T(8,128)(2,1)S(1)}, bf16[128,640]{1,0:T(8,128)(2,1)S(1)}, u32[]{:S(2)}, u32[]{:S(2)}) collective-permute-start(bf16[128,640]{1,0:T(8,128)(2,1)S(1)} %get-tuple-element.35.refs_1_.query), channel_id=1, source_target_pairs={{0,12},{4,0},{8,4},{12,8},{1,13},{5,1},{9,5},{13,9},{2,14},{6,2},{... | collective-permute-start | bytes 491528 | tf_op jit(solution)/shard_map/ppermute | solution.py:24
  32.6 0.7 copy-done.3
  33.3 12.2 %collective-permute-done.9.query = bf16[128,640]{1,0:T(8,128)(2,1)S(1)} collective-permute-done((bf16[128,640]{1,0:T(8,128)(2,1)S(1)}, bf16[128,640]{1,0:T(8,128)(2,1)S(1)}, u32[]{:S(2)}, u32[]{:S(2)}) %collective-permute-start.9) | collective-permute-done | bytes 163872 | tf_op jit(solution)/shard_map/ppermute | solution.py:24
  45.4 4.3 %collective-permute-start.16 = (bf16[128,640]{1,0:T(8,128)(2,1)S(1)}, bf16[128,640]{1,0:T(8,128)(2,1)S(1)}, u32[]{:S(2)}, u32[]{:S(2)}) collective-permute-start(bf16[128,640]{1,0:T(8,128)(2,1)S(1)} %collective-permute-done.15.query), channel_id=1, source_target_pairs={{0,12},{4,0},{8,4},{12,8},{1,13},{5,1},{9,5},{13,9},{2,14},{6,2},{... | collective-permute-start | bytes 491528 | tf_op jit(solution)/shard_map/ppermute | solution.py:24
  49.7 0.0 collective-permute-done.4.refs_5_
  49.7 0.1 collective-permute-start.5
  49.8 0.0 collective-permute-done.1.refs_2_
  49.8 0.1 collective-permute-start.2
  49.9 4.4 %collective-permute-done.16.query = bf16[128,640]{1,0:T(8,128)(2,1)S(1)} collective-permute-done((bf16[128,640]{1,0:T(8,128)(2,1)S(1)}, bf16[128,640]{1,0:T(8,128)(2,1)S(1)}, u32[]{:S(2)}, u32[]{:S(2)}) %collective-permute-start.16) | collective-permute-done | bytes 163872 | tf_op jit(solution)/shard_map/ppermute | solution.py:24
  54.3 4.3 %collective-permute-start.10 = (bf16[128,640]{1,0:T(8,128)(2,1)S(1)}, bf16[128,640]{1,0:T(8,128)(2,1)S(1)}, u32[]{:S(2)}, u32[]{:S(2)}) collective-permute-start(bf16[128,640]{1,0:T(8,128)(2,1)S(1)} %collective-permute-done.9.query), channel_id=1, source_target_pairs={{0,12},{4,0},{8,4},{12,8},{1,13},{5,1},{9,5},{13,9},{2,14},{6,2},{... | collective-permute-start | bytes 491528 | tf_op jit(solution)/shard_map/ppermute | solution.py:24
  58.6 12.0 %collective-permute-done.10.query = bf16[128,640]{1,0:T(8,128)(2,1)S(1)} collective-permute-done((bf16[128,640]{1,0:T(8,128)(2,1)S(1)}, bf16[128,640]{1,0:T(8,128)(2,1)S(1)}, u32[]{:S(2)}, u32[]{:S(2)}) %collective-permute-start.10) | collective-permute-done | bytes 163872 | tf_op jit(solution)/shard_map/ppermute | solution.py:24
  70.6 4.3 %collective-permute-start.17 = (bf16[128,640]{1,0:T(8,128)(2,1)S(1)}, bf16[128,640]{1,0:T(8,128)(2,1)S(1)}, u32[]{:S(2)}, u32[]{:S(2)}) collective-permute-start(bf16[128,640]{1,0:T(8,128)(2,1)S(1)} %collective-permute-done.16.query), channel_id=1, source_target_pairs={{0,12},{4,0},{8,4},{12,8},{1,13},{5,1},{9,5},{13,9},{2,14},{6,2},{... | collective-permute-start | bytes 491528 | tf_op jit(solution)/shard_map/ppermute | solution.py:24
  74.8 0.0 collective-permute-done.6.refs_8_
  74.8 0.0 collective-permute-start.11
  74.9 0.0 collective-permute-done.7.refs_9_
  74.9 2.8 %early_step.3 = (f32[480,640]{1,0:T(8,128)S(1)}, bf16[480,640]{1,0:T(8,128)(2,1)S(1)}) custom-call(s32[1]{0:T(128)} %bitcast.rep, bf16[128,1280]{1,0:T(8,128)(2,1)} %copy-done, bf16[128,1280]{1,0:T(8,128)(2,1)} %copy-done.10, bf16[128,1280]{1,0:T(8,128)(2,1)} %copy-done.12, bf16[128,1280]{1,0:T(8,128)(2,1)} %copy-done.7, bf16[128,1280]{1,0:T(8,128)(2,1)} %copy-done.9, ...), custom_call_target="tpu_custom_call" | custom-call | flops 471859200 | bytes 3072000 | tf_op jit(solution)/shard_map/early_step/pallas_call | solution.py:260
  77.7 0.0 collective-permute-done.5.cotangent.cot_prior
  77.8 1.8 %last_step.3 = (f32[1,3,80,640]{3,2,1,0:T(8,128)}, f32[1,3,80,640]{3,2,1,0:T(8,128)}, bf16[480,640]{1,0:T(8,128)(2,1)S(1)}) custom-call(bf16[128,1280]{1,0:T(8,128)(2,1)S(1)} %collective-permute-done.2.key.key_prior, bf16[128,1280]{1,0:T(8,128)(2,1)S(1)} %collective-permute-done.5.cotangent.cot_prior, f32[480,640]{1,0:T(8,128)S(1)} %get-tuple-element.26.so_far, ...), custom_call_target="tpu_custom_call" | custom-call | flops 157286400 | bytes 3686400 | tf_op jit(solution)/shard_map/last_step/pallas_call | solution.py:307
  79.5 0.5 apply_step.15
  80.0 0.1 collective-permute-start.18
  80.1 0.1 collective-permute-start.21
  80.2 2.8 %early_step.2 = (f32[480,640]{1,0:T(8,128)S(1)}, bf16[480,640]{1,0:T(8,128)(2,1)S(1)}) custom-call(s32[1]{0:T(128)} %bitcast.rep, bf16[128,1280]{1,0:T(8,128)(2,1)} %copy-done, bf16[128,1280]{1,0:T(8,128)(2,1)} %copy-done.10, bf16[128,1280]{1,0:T(8,128)(2,1)} %copy-done.12, bf16[128,1280]{1,0:T(8,128)(2,1)} %copy-done.7, bf16[128,1280]{1,0:T(8,128)(2,1)} %copy-done.9, ...), custom_call_target="tpu_custom_call" | custom-call | flops 471859200 | bytes 3072000 | tf_op jit(solution)/shard_map/early_step/pallas_call | solution.py:260
  83.0 1.7 %last_step.2 = (f32[1,3,80,640]{3,2,1,0:T(8,128)}, f32[1,3,80,640]{3,2,1,0:T(8,128)}, bf16[480,640]{1,0:T(8,128)(2,1)S(1)}) custom-call(bf16[128,1280]{1,0:T(8,128)(2,1)S(1)} %collective-permute-done.2.key.key_prior, bf16[128,1280]{1,0:T(8,128)(2,1)S(1)} %collective-permute-done.5.cotangent.cot_prior, f32[480,640]{1,0:T(8,128)S(1)} %get-tuple-element.21.so_far, ...), custom_call_target="tpu_custom_call" | custom-call | flops 157286400 | bytes 3686400 | tf_op jit(solution)/shard_map/last_step/pallas_call | solution.py:307
  84.8 0.5 collective-permute-start.22
  85.3 0.5 apply_step.14
  85.8 0.5 apply_step.10
  86.3 0.5 apply_step.11
  86.8 0.0 copy-start.16
  86.9 0.6 collective-permute-start.12
  87.5 0.5 apply_step.13
  88.0 0.0 collective-permute-done.11.query
  88.0 0.5 apply_step.9
  88.6 4.3 %collective-permute-start.19 = (bf16[128,640]{1,0:T(8,128)(2,1)S(1)}, bf16[128,640]{1,0:T(8,128)(2,1)S(1)}, u32[]{:S(2)}, u32[]{:S(2)}) collective-permute-start(bf16[128,640]{1,0:T(8,128)(2,1)S(1)} %add_convert_fusion.1), channel_id=1, source_target_pairs={{0,12},{4,0},{8,4},{12,8},{1,13},{5,1},{9,5},{13,9},{2,14},{6,2},{... | collective-permute-start | bytes 491528 | tf_op jit(solution)/shard_map/ppermute | solution.py:24
  92.9 1.1 collective-permute-done.12
  94.0 2.4 %collective-permute-start.13 = (bf16[128,640]{1,0:T(8,128)(2,1)S(1)}, bf16[128,640]{1,0:T(8,128)(2,1)S(1)}, u32[]{:S(2)}, u32[]{:S(2)}) collective-permute-start(bf16[128,640]{1,0:T(8,128)(2,1)S(1)} %add_convert_fusion.3), channel_id=1, source_target_pairs={{0,12},{4,0},{8,4},{12,8},{1,13},{5,1},{9,5},{13,9},{2,14},{6,2},{... | collective-permute-start | bytes 491528 | tf_op jit(solution)/shard_map/ppermute | solution.py:24
  96.5 1.1 collective-permute-done.19
  97.5 4.3 %collective-permute-start.20 = (bf16[128,640]{1,0:T(8,128)(2,1)S(1)}, bf16[128,640]{1,0:T(8,128)(2,1)S(1)}, u32[]{:S(2)}, u32[]{:S(2)}) collective-permute-start(bf16[128,640]{1,0:T(8,128)(2,1)S(1)} %add_convert_fusion), channel_id=1, source_target_pairs={{0,12},{4,0},{8,4},{12,8},{1,13},{5,1},{9,5},{13,9},{2,14},{6,2},{... | collective-permute-start | bytes 491528 | tf_op jit(solution)/shard_map/ppermute | solution.py:24
  101.9 0.0 collective-permute-done.13
  101.9 2.4 %collective-permute-start.14 = (bf16[128,640]{1,0:T(8,128)(2,1)S(1)}, bf16[128,640]{1,0:T(8,128)(2,1)S(1)}, u32[]{:S(2)}, u32[]{:S(2)}) collective-permute-start(bf16[128,640]{1,0:T(8,128)(2,1)S(1)} %add_convert_fusion.2), channel_id=1, source_target_pairs={{0,12},{4,0},{8,4},{12,8},{1,13},{5,1},{9,5},{13,9},{2,14},{6,2},{... | collective-permute-start | bytes 491528 | tf_op jit(solution)/shard_map/ppermute | solution.py:24
  104.3 0.1 collective-permute-start.8
  104.4 5.5 %collective-permute-done.8.rate_prior = f32[2,1,128]{2,1,0:T(1,128)S(1)} collective-permute-done((f32[2,1,128]{2,1,0:T(1,128)S(1)}, f32[2,1,128]{2,1,0:T(1,128)S(1)}, u32[]{:S(2)}, u32[]{:S(2)}) %collective-permute-start.8) | collective-permute-done | bytes 1056 | tf_op jit(solution)/shard_map/ppermute | solution.py:24
  109.9 2.4 %attend_step.1 = (f32[128,640]{1,0:T(8,128)S(1)}, f32[128,640]{1,0:T(8,128)S(1)}) custom-call(s32[1]{0:T(128)} %bitcast.1.first, bf16[128,1280]{1,0:T(8,128)(2,1)} %copy-done, bf16[128,1280]{1,0:T(8,128)(2,1)} %copy-done.2, bf16[128,1280]{1,0:T(8,128)(2,1)} %copy-done.8, bf16[128,1280]{1,0:T(8,128)(2,1)} %copy-done.1, ...), custom_call_target="tpu_custom_call" | custom-call | flops 167772160 | bytes 2293760 | tf_op jit(solution)/shard_map/attend_step/pallas_call | solution.py:407
  112.4 0.0 copy-start.14
  112.4 0.5 apply_step.12.kept
  112.9 0.5 apply_step.8.kept
  113.4 0.0 collective-permute-done.20.moved
  113.4 0.7 output_step.2.refs_0_
  114.1 0.0 collective-permute-done.14.moved
  114.1 0.7 output_step.3
  114.8 0.0 collective-permute-done.22
  114.9 2.9 %maximum_select_fusion = f32[4,3,80,640]{3,2,1,0:T(8,128)} fusion(f32[1,3,80,640]{3,2,1,0:T(8,128)S(1)} %collective-permute-done.22, f32[1,3,80,640]{3,2,1,0:T(8,128)} %collective-permute-done.21, f32[1,3,80,640]{3,2,1,0:T(8,128)S(1)} %copy-done.14, f32[1,3,80,640]{3,2,1,0:T(8,128)S(1)} %copy-done.13, pred[]{:T(512)S(6)} %eq.7), kind=kLoop, calls=%fused_computation | loop fusion | flops 4300800 | bytes 4915201 | tf_op jit(solution)/shard_map/jit(_where)/select_n | solution.py:476
  (41 shorter events, 0.3 us)
Async XLA Ops:
  0.6 10.6 %copy-start.15 = (bf16[128,2560]{1,0:T(8,128)(2,1)S(1)}, bf16[128,2560]{1,0:T(8,128)(2,1)}, u32[]{:S(2)}) copy-start(bf16[128,2560]{1,0:T(8,128)(2,1)} %param.6) | copy-start | bytes 1966084
  3.4 71.5 %collective-permute-start.7 = (f32[2,3,80,640]{3,2,1,0:T(8,128)}, f32[2,3,80,640]{3,2,1,0:T(8,128)S(1)}, u32[]{:S(2)}, u32[]{:S(2)}) collective-permute-start(f32[2,3,80,640]{3,2,1,0:T(8,128)} %get-tuple-element.20), channel_id=1, source_target_pairs={{0,1},{1,0},{2,3},{3,2},{4,5},{5,4},{6,7},{7,6},{8,9},{9,8},{10,11... | collective-permute-start | bytes 3686408 | tf_op jit(solution)/shard_map/ppermute | solution.py:24
  5.1 6.7 %copy-start.8 = (bf16[128,1280]{1,0:T(8,128)(2,1)}, bf16[128,1280]{1,0:T(8,128)(2,1)S(1)}, u32[]{:S(2)}) copy-start(bf16[128,1280]{1,0:T(8,128)(2,1)S(1)} %get-tuple-element.24.value_own) | copy-start | bytes 983044
  5.1 69.8 %copy-start.7 = (bf16[128,1280]{1,0:T(8,128)(2,1)}, bf16[128,1280]{1,0:T(8,128)(2,1)S(1)}, u32[]{:S(2)}) copy-start(bf16[128,1280]{1,0:T(8,128)(2,1)S(1)} %get-tuple-element.18.refs_3_) | copy-start | bytes 983044
  5.1 12.7 %collective-permute-start.3 = (bf16[128,1280]{1,0:T(8,128)(2,1)S(1)}, bf16[128,1280]{1,0:T(8,128)(2,1)S(1)}, u32[]{:S(2)}, u32[]{:S(2)}) collective-permute-start(bf16[128,1280]{1,0:T(8,128)(2,1)S(1)} %get-tuple-element.18.refs_3_), channel_id=1, source_target_pairs={{0,12},{4,0},{8,4},{12,8},{1,13},{5,1},{9,5},{13,9},{2,14},{6,2},{... | collective-permute-start | bytes 983048 | tf_op jit(solution)/shard_map/ppermute | solution.py:24
  10.7 64.2 %copy-start = (bf16[128,1280]{1,0:T(8,128)(2,1)}, bf16[128,1280]{1,0:T(8,128)(2,1)S(1)}, u32[]{:S(2)}) copy-start(bf16[128,1280]{1,0:T(8,128)(2,1)S(1)} %columns_step.1.refs_0_.key_own) | copy-start | bytes 983044
  10.7 14.1 %collective-permute-start = (bf16[128,1280]{1,0:T(8,128)(2,1)S(1)}, bf16[128,1280]{1,0:T(8,128)(2,1)S(1)}, u32[]{:S(2)}, u32[]{:S(2)}) collective-permute-start(bf16[128,1280]{1,0:T(8,128)(2,1)S(1)} %columns_step.1.refs_0_.key_own), channel_id=1, source_target_pairs={{0,12},{4,0},{8,4},{12,8},{1,13},{5,1},{9,5},{13,9},{2,14},{6,2},{... | collective-permute-start | bytes 983048 | tf_op jit(solution)/shard_map/ppermute | solution.py:24
  11.3 17.9 %collective-permute-start.15 = (bf16[128,640]{1,0:T(8,128)(2,1)S(1)}, bf16[128,640]{1,0:T(8,128)(2,1)S(1)}, u32[]{:S(2)}, u32[]{:S(2)}) collective-permute-start(bf16[128,640]{1,0:T(8,128)(2,1)S(1)} %get-tuple-element.34.refs_0_.query), channel_id=1, source_target_pairs={{0,12},{4,0},{8,4},{12,8},{1,13},{5,1},{9,5},{13,9},{2,14},{6,2},{... | collective-permute-start | bytes 491528 | tf_op jit(solution)/shard_map/ppermute | solution.py:24
  11.8 0.7 copy-start.5
  12.4 62.4 %collective-permute-start.6 = (bf16[2,3,80,640]{3,2,1,0:T(8,128)(2,1)}, bf16[2,3,80,640]{3,2,1,0:T(8,128)(2,1)S(1)}, u32[]{:S(2)}, u32[]{:S(2)}) collective-permute-start(bf16[2,3,80,640]{3,2,1,0:T(8,128)(2,1)} %get-tuple-element.19), channel_id=1, source_target_pairs={{0,1},{1,0},{2,3},{3,2},{4,5},{5,4},{6,7},{7,6},{8,9},{9,8},{10,11... | collective-permute-start | bytes 1843208 | tf_op jit(solution)/shard_map/ppermute | solution.py:24
  17.8 31.9 %copy-start.9 = (bf16[128,1280]{1,0:T(8,128)(2,1)}, bf16[128,1280]{1,0:T(8,128)(2,1)S(1)}, u32[]{:S(2)}) copy-start(bf16[128,1280]{1,0:T(8,128)(2,1)S(1)} %collective-permute-done.3.refs_4_) | copy-start | bytes 983044
  17.8 31.9 %collective-permute-start.4 = (bf16[128,1280]{1,0:T(8,128)(2,1)S(1)}, bf16[128,1280]{1,0:T(8,128)(2,1)S(1)}, u32[]{:S(2)}, u32[]{:S(2)}) collective-permute-start(bf16[128,1280]{1,0:T(8,128)(2,1)S(1)} %collective-permute-done.3.refs_4_), channel_id=1, source_target_pairs={{0,12},{4,0},{8,4},{12,8},{1,13},{5,1},{9,5},{13,9},{2,14},{6,2},{... | collective-permute-start | bytes 983048 | tf_op jit(solution)/shard_map/ppermute | solution.py:24
  24.8 25.0 %copy-start.10 = (bf16[128,1280]{1,0:T(8,128)(2,1)}, bf16[128,1280]{1,0:T(8,128)(2,1)S(1)}, u32[]{:S(2)}) copy-start(bf16[128,1280]{1,0:T(8,128)(2,1)S(1)} %collective-permute-done.refs_1_) | copy-start | bytes 983044
  24.8 25.0 %collective-permute-start.1 = (bf16[128,1280]{1,0:T(8,128)(2,1)S(1)}, bf16[128,1280]{1,0:T(8,128)(2,1)S(1)}, u32[]{:S(2)}, u32[]{:S(2)}) collective-permute-start(bf16[128,1280]{1,0:T(8,128)(2,1)S(1)} %collective-permute-done.refs_1_), channel_id=1, source_target_pairs={{0,12},{4,0},{8,4},{12,8},{1,13},{5,1},{9,5},{13,9},{2,14},{6,2},{... | collective-permute-start | bytes 983048 | tf_op jit(solution)/shard_map/ppermute | solution.py:24
  29.1 16.3 %collective-permute-start.9 = (bf16[128,640]{1,0:T(8,128)(2,1)S(1)}, bf16[128,640]{1,0:T(8,128)(2,1)S(1)}, u32[]{:S(2)}, u32[]{:S(2)}) collective-permute-start(bf16[128,640]{1,0:T(8,128)(2,1)S(1)} %get-tuple-element.35.refs_1_.query), channel_id=1, source_target_pairs={{0,12},{4,0},{8,4},{12,8},{1,13},{5,1},{9,5},{13,9},{2,14},{6,2},{... | collective-permute-start | bytes 491528 | tf_op jit(solution)/shard_map/ppermute | solution.py:24
  32.6 0.7 copy-start.3
  45.4 8.9 %collective-permute-start.16 = (bf16[128,640]{1,0:T(8,128)(2,1)S(1)}, bf16[128,640]{1,0:T(8,128)(2,1)S(1)}, u32[]{:S(2)}, u32[]{:S(2)}) collective-permute-start(bf16[128,640]{1,0:T(8,128)(2,1)S(1)} %collective-permute-done.15.query), channel_id=1, source_target_pairs={{0,12},{4,0},{8,4},{12,8},{1,13},{5,1},{9,5},{13,9},{2,14},{6,2},{... | collective-permute-start | bytes 491528 | tf_op jit(solution)/shard_map/ppermute | solution.py:24
  49.7 25.1 %copy-start.11 = (bf16[128,1280]{1,0:T(8,128)(2,1)}, bf16[128,1280]{1,0:T(8,128)(2,1)S(1)}, u32[]{:S(2)}) copy-start(bf16[128,1280]{1,0:T(8,128)(2,1)S(1)} %collective-permute-done.4.refs_5_) | copy-start | bytes 983044
  49.7 28.0 %collective-permute-start.5 = (bf16[128,1280]{1,0:T(8,128)(2,1)S(1)}, bf16[128,1280]{1,0:T(8,128)(2,1)S(1)}, u32[]{:S(2)}, u32[]{:S(2)}) collective-permute-start(bf16[128,1280]{1,0:T(8,128)(2,1)S(1)} %collective-permute-done.4.refs_5_), channel_id=1, source_target_pairs={{0,12},{4,0},{8,4},{12,8},{1,13},{5,1},{9,5},{13,9},{2,14},{6,2},{... | collective-permute-start | bytes 983048 | tf_op jit(solution)/shard_map/ppermute | solution.py:24
  49.8 25.1 %copy-start.12 = (bf16[128,1280]{1,0:T(8,128)(2,1)}, bf16[128,1280]{1,0:T(8,128)(2,1)S(1)}, u32[]{:S(2)}) copy-start(bf16[128,1280]{1,0:T(8,128)(2,1)S(1)} %collective-permute-done.1.refs_2_) | copy-start | bytes 983044
  49.8 27.9 %collective-permute-start.2 = (bf16[128,1280]{1,0:T(8,128)(2,1)S(1)}, bf16[128,1280]{1,0:T(8,128)(2,1)S(1)}, u32[]{:S(2)}, u32[]{:S(2)}) collective-permute-start(bf16[128,1280]{1,0:T(8,128)(2,1)S(1)} %collective-permute-done.1.refs_2_), channel_id=1, source_target_pairs={{0,12},{4,0},{8,4},{12,8},{1,13},{5,1},{9,5},{13,9},{2,14},{6,2},{... | collective-permute-start | bytes 983048 | tf_op jit(solution)/shard_map/ppermute | solution.py:24
  54.3 16.2 %collective-permute-start.10 = (bf16[128,640]{1,0:T(8,128)(2,1)S(1)}, bf16[128,640]{1,0:T(8,128)(2,1)S(1)}, u32[]{:S(2)}, u32[]{:S(2)}) collective-permute-start(bf16[128,640]{1,0:T(8,128)(2,1)S(1)} %collective-permute-done.9.query), channel_id=1, source_target_pairs={{0,12},{4,0},{8,4},{12,8},{1,13},{5,1},{9,5},{13,9},{2,14},{6,2},{... | collective-permute-start | bytes 491528 | tf_op jit(solution)/shard_map/ppermute | solution.py:24
  70.6 16.3 %collective-permute-start.17 = (bf16[128,640]{1,0:T(8,128)(2,1)S(1)}, bf16[128,640]{1,0:T(8,128)(2,1)S(1)}, u32[]{:S(2)}, u32[]{:S(2)}) collective-permute-start(bf16[128,640]{1,0:T(8,128)(2,1)S(1)} %collective-permute-done.16.query), channel_id=1, source_target_pairs={{0,12},{4,0},{8,4},{12,8},{1,13},{5,1},{9,5},{13,9},{2,14},{6,2},{... | collective-permute-start | bytes 491528 | tf_op jit(solution)/shard_map/ppermute | solution.py:24
  74.8 13.2 %collective-permute-start.11 = (bf16[128,640]{1,0:T(8,128)(2,1)S(1)}, bf16[128,640]{1,0:T(8,128)(2,1)S(1)}, u32[]{:S(2)}, u32[]{:S(2)}) collective-permute-start(bf16[128,640]{1,0:T(8,128)(2,1)S(1)} %collective-permute-done.10.query), channel_id=1, source_target_pairs={{0,12},{4,0},{8,4},{12,8},{1,13},{5,1},{9,5},{13,9},{2,14},{6,2},{... | collective-permute-start | bytes 491528 | tf_op jit(solution)/shard_map/ppermute | solution.py:24
  77.7 5.3 %copy-start.1 = (bf16[128,1280]{1,0:T(8,128)(2,1)}, bf16[128,1280]{1,0:T(8,128)(2,1)S(1)}, u32[]{:S(2)}) copy-start(bf16[128,1280]{1,0:T(8,128)(2,1)S(1)} %collective-permute-done.5.cotangent.cot_prior) | copy-start | bytes 983044
  77.8 5.3 %copy-start.2 = (bf16[128,1280]{1,0:T(8,128)(2,1)}, bf16[128,1280]{1,0:T(8,128)(2,1)S(1)}, u32[]{:S(2)}) copy-start(bf16[128,1280]{1,0:T(8,128)(2,1)S(1)} %collective-permute-done.2.key.key_prior) | copy-start | bytes 983044
  80.0 8.5 %collective-permute-start.18 = (bf16[128,640]{1,0:T(8,128)(2,1)S(1)}, bf16[128,640]{1,0:T(8,128)(2,1)S(1)}, u32[]{:S(2)}, u32[]{:S(2)}) collective-permute-start(bf16[128,640]{1,0:T(8,128)(2,1)S(1)} %apply_step.15), channel_id=1, source_target_pairs={{0,12},{4,0},{8,4},{12,8},{1,13},{5,1},{9,5},{13,9},{2,14},{6,2},{... | collective-permute-start | bytes 491528 | tf_op jit(solution)/shard_map/ppermute | solution.py:24
  80.1 34.7 %collective-permute-start.21 = (f32[1,3,80,640]{3,2,1,0:T(8,128)}, f32[1,3,80,640]{3,2,1,0:T(8,128)}, u32[]{:S(2)}, u32[]{:S(2)}) collective-permute-start(f32[1,3,80,640]{3,2,1,0:T(8,128)} %get-tuple-element.32), channel_id=1, source_target_pairs={{0,1},{1,0},{2,3},{3,2},{4,5},{5,4},{6,7},{7,6},{8,9},{9,8},{10,11... | collective-permute-start | bytes 1843208 | tf_op jit(solution)/shard_map/ppermute | solution.py:24
  84.8 30.1 %collective-permute-start.22 = (f32[1,3,80,640]{3,2,1,0:T(8,128)}, f32[1,3,80,640]{3,2,1,0:T(8,128)S(1)}, u32[]{:S(2)}, u32[]{:S(2)}) collective-permute-start(f32[1,3,80,640]{3,2,1,0:T(8,128)} %get-tuple-element.33), channel_id=1, source_target_pairs={{0,1},{1,0},{2,3},{3,2},{4,5},{5,4},{6,7},{7,6},{8,9},{9,8},{10,11... | collective-permute-start | bytes 1843208 | tf_op jit(solution)/shard_map/ppermute | solution.py:24
  86.8 17.5 %copy-start.16 = (f32[4,128]{1,0:T(4,128)S(1)}, f32[4,128]{1,0:T(4,128)}, u32[]{:S(2)}) copy-start(f32[4,128]{1,0:T(4,128)} %rates.1) | copy-start | bytes 6148
  86.8 23.1 %copy-start.4 = (bf16[128,640]{1,0:T(8,128)(2,1)S(1)}, bf16[128,640]{1,0:T(8,128)(2,1)}, u32[]{:S(2)}) copy-start(bf16[128,640]{1,0:T(8,128)(2,1)} %copy-done.3) | copy-start | bytes 491524
  86.8 23.1 %copy-start.6 = (bf16[128,640]{1,0:T(8,128)(2,1)S(1)}, bf16[128,640]{1,0:T(8,128)(2,1)}, u32[]{:S(2)}) copy-start(bf16[128,640]{1,0:T(8,128)(2,1)} %copy-done.5) | copy-start | bytes 491524
  86.9 7.1 %collective-permute-start.12 = (bf16[128,640]{1,0:T(8,128)(2,1)S(1)}, bf16[128,640]{1,0:T(8,128)(2,1)S(1)}, u32[]{:S(2)}, u32[]{:S(2)}) collective-permute-start(bf16[128,640]{1,0:T(8,128)(2,1)S(1)} %apply_step.11), channel_id=1, source_target_pairs={{0,12},{4,0},{8,4},{12,8},{1,13},{5,1},{9,5},{13,9},{2,14},{6,2},{... | collective-permute-start | bytes 491528 | tf_op jit(solution)/shard_map/ppermute | solution.py:24
  88.6 8.9 %collective-permute-start.19 = (bf16[128,640]{1,0:T(8,128)(2,1)S(1)}, bf16[128,640]{1,0:T(8,128)(2,1)S(1)}, u32[]{:S(2)}, u32[]{:S(2)}) collective-permute-start(bf16[128,640]{1,0:T(8,128)(2,1)S(1)} %add_convert_fusion.1), channel_id=1, source_target_pairs={{0,12},{4,0},{8,4},{12,8},{1,13},{5,1},{9,5},{13,9},{2,14},{6,2},{... | collective-permute-start | bytes 491528 | tf_op jit(solution)/shard_map/ppermute | solution.py:24
  94.0 7.8 %collective-permute-start.13 = (bf16[128,640]{1,0:T(8,128)(2,1)S(1)}, bf16[128,640]{1,0:T(8,128)(2,1)S(1)}, u32[]{:S(2)}, u32[]{:S(2)}) collective-permute-start(bf16[128,640]{1,0:T(8,128)(2,1)S(1)} %add_convert_fusion.3), channel_id=1, source_target_pairs={{0,12},{4,0},{8,4},{12,8},{1,13},{5,1},{9,5},{13,9},{2,14},{6,2},{... | collective-permute-start | bytes 491528 | tf_op jit(solution)/shard_map/ppermute | solution.py:24
  97.5 15.9 %collective-permute-start.20 = (bf16[128,640]{1,0:T(8,128)(2,1)S(1)}, bf16[128,640]{1,0:T(8,128)(2,1)S(1)}, u32[]{:S(2)}, u32[]{:S(2)}) collective-permute-start(bf16[128,640]{1,0:T(8,128)(2,1)S(1)} %add_convert_fusion), channel_id=1, source_target_pairs={{0,12},{4,0},{8,4},{12,8},{1,13},{5,1},{9,5},{13,9},{2,14},{6,2},{... | collective-permute-start | bytes 491528 | tf_op jit(solution)/shard_map/ppermute | solution.py:24
  101.9 12.2 %collective-permute-start.14 = (bf16[128,640]{1,0:T(8,128)(2,1)S(1)}, bf16[128,640]{1,0:T(8,128)(2,1)S(1)}, u32[]{:S(2)}, u32[]{:S(2)}) collective-permute-start(bf16[128,640]{1,0:T(8,128)(2,1)S(1)} %add_convert_fusion.2), channel_id=1, source_target_pairs={{0,12},{4,0},{8,4},{12,8},{1,13},{5,1},{9,5},{13,9},{2,14},{6,2},{... | collective-permute-start | bytes 491528 | tf_op jit(solution)/shard_map/ppermute | solution.py:24
  104.3 5.6 %collective-permute-start.8 = (f32[2,1,128]{2,1,0:T(1,128)S(1)}, f32[2,1,128]{2,1,0:T(1,128)S(1)}, u32[]{:S(2)}, u32[]{:S(2)}) collective-permute-start(f32[2,1,128]{2,1,0:T(1,128)S(1)} %bitcast.3), channel_id=1, source_target_pairs={{0,4},{4,8},{8,12},{12,0},{1,5},{5,9},{9,13},{13,1},{2,6},{6,10},{... | collective-permute-start | bytes 3080 | tf_op jit(solution)/shard_map/ppermute | solution.py:24
  112.3 2.5 %copy-start.13 = (f32[1,3,80,640]{3,2,1,0:T(8,128)S(1)}, f32[1,3,80,640]{3,2,1,0:T(8,128)}, u32[]{:S(2)}) copy-start(f32[1,3,80,640]{3,2,1,0:T(8,128)} %get-tuple-element.30) | copy-start | bytes 1843204
  112.4 2.5 %copy-start.14 = (f32[1,3,80,640]{3,2,1,0:T(8,128)S(1)}, f32[1,3,80,640]{3,2,1,0:T(8,128)}, u32[]{:S(2)}) copy-start(f32[1,3,80,640]{3,2,1,0:T(8,128)} %get-tuple-element.31) | copy-start | bytes 1843204

commit v5 on v4

--- a/solution.py
+++ b/solution.py
@@ -19,9 +19,9 @@
     return lax.ppermute(value, axis, [(source, source + steps) for source in range(initial, last)])
 
 
-def ring(value, axis, steps=1):
-    count = lax.axis_size(axis)
-    return lax.ppermute(value, axis, [(source, (source + steps) % count) for source in range(count)])
+def ring(value, axis, order=None):
+    order = order or range(lax.axis_size(axis))
+    return lax.ppermute(value, axis, list(zip(order, (*order[1:], order[0]))))
 
 
 def unit_rows(tensor):
@@ -260,7 +260,7 @@
     return pl.pallas_call(
         functools.partial(early_body, slots),
         out_shape=(
-            jax.ShapeDtypeStruct((6 * hid, width), jnp.float32),
+            (pltpu.HBM if head else jax.ShapeDtypeStruct)((6 * hid, width), jnp.float32),
             jax.ShapeDtypeStruct((6 * hid, width), jnp.bfloat16),
         ),
         grid_spec=pltpu.PrefetchScalarGridSpec(
@@ -316,7 +316,7 @@
             flops=4 * rows * total * width, bytes_accessed=12 * total * width, transcendentals=0
         ),
         name="last_step",
-    )(key, cotangent, so_far, low)
+    )(key, cotangent, in_hbm(so_far) if head else so_far, low)
 
 
 def apply_body(query, low, *refs):
@@ -375,16 +375,27 @@
     )(kept, moved, *more)
 
 
-def attend_body(token_scale, first, key_own, key_prior, value_own, cot_prior, rate_prior, *refs):
-    heads = len(refs) // 2
-    asked, outs = refs[:heads], refs[heads:]
+def attend_body(token_scale, block_index, *refs):
+    key_own, value_own, rate_prior = refs[:3]
+    key_slots, cot_slots = refs[3:6], refs[6:9]
+    heads = (len(refs) - 9) // 2
+    asked, outs = refs[9 : 9 + heads], refs[9 + heads :]
     width = asked[0].shape[1]
-    allowed = jnp.where(first[0] != 0, -jnp.inf, 0.0).astype(jnp.float32)
+    index = block_index[0]
+    allowed = jnp.where(index == 0, -jnp.inf, 0.0).astype(jnp.float32)
     for h in range(heads):
         columns = slice(h * width, (h + 1) * width)
+        key_prior, cot_prior = (
+            jnp.where(
+                index == 3,
+                one[:, columns],
+                jnp.where(index == 2, two[:, columns], three[:, columns]),
+            )
+            for one, two, three in (key_slots, cot_slots)
+        )
         part = asked[h][...]
         near = lax.dot_general(part, key_own[:, columns], NT, preferred_element_type=jnp.float32)
-        far = lax.dot_general(part, key_prior[:, columns], NT, preferred_element_type=jnp.float32)
+        far = lax.dot_general(part, key_prior, NT, preferred_element_type=jnp.float32)
         near = near * width ** (-0.5)
         far = far * width ** (-0.5) + allowed
         peak = jnp.maximum(
@@ -398,22 +409,29 @@
         far = (far / total / rate).astype(jnp.bfloat16)
         outs[h][...] = jnp.dot(
             near, value_own[:, columns], preferred_element_type=jnp.float32
-        ) + jnp.dot(far, cot_prior[:, columns], preferred_element_type=jnp.float32)
-
-
-def attend_step(token_scale, first, key_own, key_prior, value_own, cot_prior, rate_prior, asked):
-    rows, columns = key_own.shape
+        ) + jnp.dot(far, cot_prior, preferred_element_type=jnp.float32)
+
+
+def attend_step(token_scale, block_index, keys, value_own, cots, rate_prior, asked):
+    rows, columns = value_own.shape
     made = tuple(jax.ShapeDtypeStruct(query.shape, jnp.float32) for query in asked)
     return pl.pallas_call(
         functools.partial(attend_body, token_scale),
         out_shape=made,
-        in_specs=[pl.BlockSpec(memory_space=pltpu.SMEM)] + [pl.BlockSpec()] * (5 + len(asked)),
-        compiler_params=pltpu.CompilerParams(vmem_limit_bytes=8 << 20),
-        cost_estimate=pl.CostEstimate(
-            flops=8 * rows * rows * columns, bytes_accessed=14 * rows * columns, transcendentals=0
+        in_specs=[pl.BlockSpec(memory_space=pltpu.SMEM)] + [pl.BlockSpec()] * (9 + len(asked)),
+        compiler_params=pltpu.CompilerParams(vmem_limit_bytes=10 << 20),
+        cost_estimate=pl.CostEstimate(
+            flops=8 * rows * rows * columns, bytes_accessed=20 * rows * columns, transcendentals=0
         ),
         name="attend_step",
-    )(first, *map(in_hbm, (key_own, key_prior, value_own, cot_prior)), rate_prior, *asked)
+    )(
+        block_index,
+        in_hbm(keys[0]),
+        in_hbm(value_own),
+        rate_prior,
+        *map(in_hbm, (*keys[1:], *cots)),
+        *asked,
+    )
 
 
 def tokens_travel(queries, key_vectors, values, learn_rates, fast_weights, momentum):
@@ -424,8 +442,10 @@
     start = rep_index * per_rep
     token_scale = float(slots * queries.shape[0]) ** (-0.5)
 
-    def hop(value, axis="ctx", steps=-1):
-        return ring(value, axis, steps)
+    cycle = (0, 2, 3, 1)
+
+    def hop(value, axis="ctx", order=cycle):
+        return ring(value, axis, order if axis == "ctx" else None)
 
     rep = rep_index.reshape(1)
     value_own, cot = cotangent_step(token_scale, rep, values, learn_rates)
@@ -435,15 +455,17 @@
     for _ in range(1, slots):
         keys.append(hop(keys[-1]))
         cots.append(hop(cots[-1]))
-    rate_prior = hop(lax.dynamic_slice_in_dim(learn_rates, start, per_rep, 0)[:, None, :], steps=1)
+    rate_prior = hop(
+        lax.dynamic_slice_in_dim(learn_rates, start, per_rep, 0)[:, None, :], order=None
+    )
     low_other, base_other = other_step(rep, fast_weights, momentum)
     low_par = hop(low_other, "rep")
     base_par = hop(base_other, "rep")
     for _ in range(1, slots):
         asked.append([hop(asked[-1][h]) for h in heads])
-    first = (lax.axis_index("ctx") == 0).astype(jnp.int32).reshape(1)
+    block_index = lax.axis_index("ctx").reshape(1)
     attended = attend_step(
-        token_scale, first, keys[0], keys[-1], value_own, cots[-1], rate_prior, asked[0]
+        token_scale, block_index, keys, value_own, cots[1:], rate_prior, asked[0]
     )
     early = []
     for h in heads:
@@ -485,8 +507,8 @@
     slots = lax.axis_size("ctx")
     fits = (
         lax.axis_size("rep") == 2
-        and 2 <= slots <= 8
-        and fast_weights.shape[0] % 2 == 0
+        and slots == 4
+        and fast_weights.shape[0] == 4
         and fast_weights.shape[2] % 16 == 0
         and queries.shape[0] == 128
     )

time: 118 us -> 118 us (level)
  starting transfers between devices: 45.9 us -> 37.8 us
  waiting for transfers between devices: 44.4 us -> 49.5 us
  Pallas kernels: 22 us -> 24.7 us
    ppermute x23, starting transfers between devices: 45.9 us -> 37.8 us  [ring(): return lax.ppermute(value, axis, list(zip(order, (*order[1:], order[0]))))]
    ppermute x23, waiting for transfers between devices: 44.4 us -> 49.5 us  [ring(): return lax.ppermute(value, axis, list(zip(order, (*order[1:], order[0]))))]
    pallas_call x2, Pallas kernels: 3.49 us -> 4.82 us  [last_step(): pl.pallas_call(last_body, out_shape=(fresh, fresh, jax.ShapeDtypeStruct((...]
  transfers between devices with their start and end apart: 23 -> 23, of which waited for: 8 -> 10; matrix products, arithmetic and copies ran while one was open for 0% -> 0% of each run, Pallas kernels for 16% -> 19%
where the time goes in v5:
time: 118 us
  waiting for transfers between devices  49.5 us (42%)
  starting transfers between devices  37.8 us (32%)
  Pallas kernels  24.7 us (21%)
  other arithmetic  3.07 us (3%)
  local copies, waits for them, and re-layouts  1.44 us (1%)
    ppermute x23, waiting for transfers between devices, ring(): return lax.ppermute(value, axis, list(zip(order, (*order[1:], order[0]))))  49.5 us
    ppermute x23, starting transfers between devices, ring(): return lax.ppermute(value, axis, list(zip(order, (*order[1:], order[0]))))  37.8 us
    pallas_call x2, Pallas kernels, early_step(): pl.pallas_call(functools.partial(early_body, slots), out_shape=((pltpu.HB...  6.69 us
    pallas_call x2, Pallas kernels, last_step(): pl.pallas_call(last_body, out_shape=(fresh, fresh, jax.ShapeDtypeStruct((...  4.82 us
    pallas_call x8, Pallas kernels, apply_step(): pl.pallas_call(apply_body, out_shape=jax.ShapeDtypeStruct((rows, width),...  4.1 us
    select_n x1, other arithmetic, tokens_travel(): jnp.where(rep_index == 0, jnp.concatenate([*owned, *returned], axis=0), j...  2.91 us
    pallas_call x1, Pallas kernels, attend_step(): pl.pallas_call(functools.partial(attend_body, token_scale), out_shape=mad...  2.81 us
    pallas_call x1, Pallas kernels, other_step(): pl.pallas_call(other_body, out_shape=(pltpu.HBM(made, jnp.bfloat16), pltp...  2.74 us
  transfers between devices with their start and end apart: 23, of which 10 were waited for; matrix products, arithmetic and copies ran while one was open for 0% of the time, Pallas kernels for 19%

profile of v5, /device:TPU:0, one launch (start us, length us, event | category | flops | bytes accessed | tf_op | source)
XLA Modules:
  0.0 117.5 jit_solution(10970605617832201708)
XLA Ops:
  0.6 2.7 %other_step.1 = (bf16[2,3,80,640]{3,2,1,0:T(8,128)(2,1)}, f32[2,3,80,640]{3,2,1,0:T(8,128)}) custom-call(s32[1]{0:T(128)} %bitcast.rep, f32[4,3,80,640]{3,2,1,0:T(8,128)} %refs_6_.3, f32[4,3,80,640]{3,2,1,0:T(8,128)} %refs_7_.3), custom_call_target="tpu_custom_call" | custom-call | flops 614400 | bytes 4300800 | tf_op jit(solution)/shard_map/other_step/pallas_call | solution.py:203
  3.4 0.5 collective-permute-start.7
  3.9 1.2 cotangent_step.1
  5.1 3.6 %collective-permute-start.3 = (bf16[128,1280]{1,0:T(8,128)(2,1)S(1)}, bf16[128,1280]{1,0:T(8,128)(2,1)S(1)}, u32[]{:S(2)}, u32[]{:S(2)}) collective-permute-start(bf16[128,1280]{1,0:T(8,128)(2,1)S(1)} %get-tuple-element.18.refs_3_), channel_id=1, source_target_pairs={{0,8},{8,12},{12,4},{4,0},{1,9},{9,13},{13,5},{5,1},{2,10},{10,14}... | collective-permute-start | bytes 983048 | tf_op jit(solution)/shard_map/ppermute | solution.py:24
  8.7 1.0 columns_step.1.refs_0_
  9.7 0.0 copy-start
  9.7 1.6 %collective-permute-start = (bf16[128,1280]{1,0:T(8,128)(2,1)S(1)}, bf16[128,1280]{1,0:T(8,128)(2,1)S(1)}, u32[]{:S(2)}, u32[]{:S(2)}) collective-permute-start(bf16[128,1280]{1,0:T(8,128)(2,1)S(1)} %columns_step.1.refs_0_), channel_id=1, source_target_pairs={{0,8},{8,12},{12,4},{4,0},{1,9},{9,13},{13,5},{5,1},{2,10},{10,14}... | collective-permute-start | bytes 983048 | tf_op jit(solution)/shard_map/ppermute | solution.py:24
  11.4 0.4 collective-permute-start.15
  11.8 0.7 copy-done.5
  12.4 0.0 collective-permute-start.6
  12.4 4.4 %collective-permute-done.3.refs_4_.refs_6_ = bf16[128,1280]{1,0:T(8,128)(2,1)S(1)} collective-permute-done((bf16[128,1280]{1,0:T(8,128)(2,1)S(1)}, bf16[128,1280]{1,0:T(8,128)(2,1)S(1)}, u32[]{:S(2)}, u32[]{:S(2)}) %collective-permute-start.3) | collective-permute-done | bytes 327712 | tf_op jit(solution)/shard_map/ppermute | solution.py:24
  16.8 3.4 %collective-permute-start.4 = (bf16[128,1280]{1,0:T(8,128)(2,1)S(1)}, bf16[128,1280]{1,0:T(8,128)(2,1)S(1)}, u32[]{:S(2)}, u32[]{:S(2)}) collective-permute-start(bf16[128,1280]{1,0:T(8,128)(2,1)S(1)} %collective-permute-done.3.refs_4_.refs_6_), channel_id=1, source_target_pairs={{0,8},{8,12},{12,4},{4,0},{1,9},{9,13},{13,5},{5,1},{2,10},{10,14}... | collective-permute-start | bytes 983048 | tf_op jit(solution)/shard_map/ppermute | solution.py:24
  20.2 3.6 %collective-permute-done.refs_1_.refs_3_ = bf16[128,1280]{1,0:T(8,128)(2,1)S(1)} collective-permute-done((bf16[128,1280]{1,0:T(8,128)(2,1)S(1)}, bf16[128,1280]{1,0:T(8,128)(2,1)S(1)}, u32[]{:S(2)}, u32[]{:S(2)}) %collective-permute-start) | collective-permute-done | bytes 327712 | tf_op jit(solution)/shard_map/ppermute | solution.py:24
  23.8 3.4 %collective-permute-start.1 = (bf16[128,1280]{1,0:T(8,128)(2,1)S(1)}, bf16[128,1280]{1,0:T(8,128)(2,1)S(1)}, u32[]{:S(2)}, u32[]{:S(2)}) collective-permute-start(bf16[128,1280]{1,0:T(8,128)(2,1)S(1)} %collective-permute-done.refs_1_.refs_3_), channel_id=1, source_target_pairs={{0,8},{8,12},{12,4},{4,0},{1,9},{9,13},{13,5},{5,1},{2,10},{10,14}... | collective-permute-start | bytes 983048 | tf_op jit(solution)/shard_map/ppermute | solution.py:24
  27.2 0.1 collective-permute-done.15.query
  27.3 3.4 %collective-permute-start.9 = (bf16[128,640]{1,0:T(8,128)(2,1)S(1)}, bf16[128,640]{1,0:T(8,128)(2,1)S(1)}, u32[]{:S(2)}, u32[]{:S(2)}) collective-permute-start(bf16[128,640]{1,0:T(8,128)(2,1)S(1)} %get-tuple-element.35.refs_10_.query), channel_id=1, source_target_pairs={{0,8},{8,12},{12,4},{4,0},{1,9},{9,13},{13,5},{5,1},{2,10},{10,14}... | collective-permute-start | bytes 491528 | tf_op jit(solution)/shard_map/ppermute | solution.py:24
  30.7 0.7 copy-done.3
  31.4 13.0 %collective-permute-done.9.query = bf16[128,640]{1,0:T(8,128)(2,1)S(1)} collective-permute-done((bf16[128,640]{1,0:T(8,128)(2,1)S(1)}, bf16[128,640]{1,0:T(8,128)(2,1)S(1)}, u32[]{:S(2)}, u32[]{:S(2)}) %collective-permute-start.9) | collective-permute-done | bytes 163872 | tf_op jit(solution)/shard_map/ppermute | solution.py:24
  44.4 3.4 %collective-permute-start.16 = (bf16[128,640]{1,0:T(8,128)(2,1)S(1)}, bf16[128,640]{1,0:T(8,128)(2,1)S(1)}, u32[]{:S(2)}, u32[]{:S(2)}) collective-permute-start(bf16[128,640]{1,0:T(8,128)(2,1)S(1)} %collective-permute-done.15.query), channel_id=1, source_target_pairs={{0,8},{8,12},{12,4},{4,0},{1,9},{9,13},{13,5},{5,1},{2,10},{10,14}... | collective-permute-start | bytes 491528 | tf_op jit(solution)/shard_map/ppermute | solution.py:24
  47.8 0.0 collective-permute-done.4.refs_5_.refs_7_
  47.8 0.7 collective-permute-start.5
  48.6 1.3 %collective-permute-start.2 = (bf16[128,1280]{1,0:T(8,128)(2,1)S(1)}, bf16[128,1280]{1,0:T(8,128)(2,1)S(1)}, u32[]{:S(2)}, u32[]{:S(2)}) collective-permute-start(bf16[128,1280]{1,0:T(8,128)(2,1)S(1)} %collective-permute-done.1.refs_2_.refs_4_), channel_id=1, source_target_pairs={{0,8},{8,12},{12,4},{4,0},{1,9},{9,13},{13,5},{5,1},{2,10},{10,14}... | collective-permute-start | bytes 983048 | tf_op jit(solution)/shard_map/ppermute | solution.py:24
  49.8 2.6 %collective-permute-done.16.query = bf16[128,640]{1,0:T(8,128)(2,1)S(1)} collective-permute-done((bf16[128,640]{1,0:T(8,128)(2,1)S(1)}, bf16[128,640]{1,0:T(8,128)(2,1)S(1)}, u32[]{:S(2)}, u32[]{:S(2)}) %collective-permute-start.16) | collective-permute-done | bytes 163872 | tf_op jit(solution)/shard_map/ppermute | solution.py:24
  52.4 3.4 %collective-permute-start.10 = (bf16[128,640]{1,0:T(8,128)(2,1)S(1)}, bf16[128,640]{1,0:T(8,128)(2,1)S(1)}, u32[]{:S(2)}, u32[]{:S(2)}) collective-permute-start(bf16[128,640]{1,0:T(8,128)(2,1)S(1)} %collective-permute-done.9.query), channel_id=1, source_target_pairs={{0,8},{8,12},{12,4},{4,0},{1,9},{9,13},{13,5},{5,1},{2,10},{10,14}... | collective-permute-start | bytes 491528 | tf_op jit(solution)/shard_map/ppermute | solution.py:24
  55.8 12.9 %collective-permute-done.10.query = bf16[128,640]{1,0:T(8,128)(2,1)S(1)} collective-permute-done((bf16[128,640]{1,0:T(8,128)(2,1)S(1)}, bf16[128,640]{1,0:T(8,128)(2,1)S(1)}, u32[]{:S(2)}, u32[]{:S(2)}) %collective-permute-start.10) | collective-permute-done | bytes 163872 | tf_op jit(solution)/shard_map/ppermute | solution.py:24
  68.6 3.4 %collective-permute-start.17 = (bf16[128,640]{1,0:T(8,128)(2,1)S(1)}, bf16[128,640]{1,0:T(8,128)(2,1)S(1)}, u32[]{:S(2)}, u32[]{:S(2)}) collective-permute-start(bf16[128,640]{1,0:T(8,128)(2,1)S(1)} %collective-permute-done.16.query), channel_id=1, source_target_pairs={{0,8},{8,12},{12,4},{4,0},{1,9},{9,13},{13,5},{5,1},{2,10},{10,14}... | collective-permute-start | bytes 491528 | tf_op jit(solution)/shard_map/ppermute | solution.py:24
  72.0 0.0 collective-permute-start.11
  72.0 0.0 collective-permute-done.7.refs_9_
  72.1 2.8 %early_step.3 = (f32[480,640]{1,0:T(8,128)S(1)}, bf16[480,640]{1,0:T(8,128)(2,1)S(1)}) custom-call(s32[1]{0:T(128)} %bitcast.rep, bf16[128,1280]{1,0:T(8,128)(2,1)} %copy-done, bf16[128,1280]{1,0:T(8,128)(2,1)} %copy-done.10, bf16[128,1280]{1,0:T(8,128)(2,1)} %copy-done.12, bf16[128,1280]{1,0:T(8,128)(2,1)} %copy-done.7, bf16[128,1280]{1,0:T(8,128)(2,1)} %copy-done.9, ...), custom_call_target="tpu_custom_call" | custom-call | flops 471859200 | bytes 3072000 | tf_op jit(solution)/shard_map/early_step/pallas_call | solution.py:260
  74.9 0.0 collective-permute-done.5.cotangent.refs_8_
  74.9 0.0 collective-permute-done.2.key.refs_5_
  75.0 1.8 %last_step.3 = (f32[1,3,80,640]{3,2,1,0:T(8,128)}, f32[1,3,80,640]{3,2,1,0:T(8,128)}, bf16[480,640]{1,0:T(8,128)(2,1)S(1)}) custom-call(bf16[128,1280]{1,0:T(8,128)(2,1)S(1)} %collective-permute-done.2.key.refs_5_, bf16[128,1280]{1,0:T(8,128)(2,1)S(1)} %collective-permute-done.5.cotangent.refs_8_, f32[480,640]{1,0:T(8,128)S(1)} %get-tuple-element.26.so_far, ...), custom_call_target="tpu_custom_call" | custom-call | flops 157286400 | bytes 3686400 | tf_op jit(solution)/shard_map/last_step/pallas_call | solution.py:307
  76.7 0.5 apply_step.15
  77.2 1.9 %collective-permute-start.18 = (bf16[128,640]{1,0:T(8,128)(2,1)S(1)}, bf16[128,640]{1,0:T(8,128)(2,1)S(1)}, u32[]{:S(2)}, u32[]{:S(2)}) collective-permute-start(bf16[128,640]{1,0:T(8,128)(2,1)S(1)} %apply_step.15), channel_id=1, source_target_pairs={{0,8},{8,12},{12,4},{4,0},{1,9},{9,13},{13,5},{5,1},{2,10},{10,14}... | collective-permute-start | bytes 491528 | tf_op jit(solution)/shard_map/ppermute | solution.py:24
  79.2 0.0 collective-permute-start.21
  79.2 3.9 %early_step.2 = (f32[480,640]{1,0:T(8,128)}, bf16[480,640]{1,0:T(8,128)(2,1)S(1)}) custom-call(s32[1]{0:T(128)} %bitcast.rep, bf16[128,1280]{1,0:T(8,128)(2,1)} %copy-done, bf16[128,1280]{1,0:T(8,128)(2,1)} %copy-done.10, bf16[128,1280]{1,0:T(8,128)(2,1)} %copy-done.12, bf16[128,1280]{1,0:T(8,128)(2,1)} %copy-done.7, bf16[128,1280]{1,0:T(8,128)(2,1)} %copy-done.9, ...), custom_call_target="tpu_custom_call" | custom-call | flops 471859200 | bytes 3072000 | tf_op jit(solution)/shard_map/early_step/pallas_call | solution.py:260
  83.0 3.1 %last_step.2 = (f32[1,3,80,640]{3,2,1,0:T(8,128)}, f32[1,3,80,640]{3,2,1,0:T(8,128)}, bf16[480,640]{1,0:T(8,128)(2,1)S(1)}) custom-call(bf16[128,1280]{1,0:T(8,128)(2,1)S(1)} %collective-permute-done.2.key.refs_5_, bf16[128,1280]{1,0:T(8,128)(2,1)S(1)} %collective-permute-done.5.cotangent.refs_8_, f32[480,640]{1,0:T(8,128)} %get-tuple-element.21.so_far, ...), custom_call_target="tpu_custom_call" | custom-call | flops 157286400 | bytes 3686400 | tf_op jit(solution)/shard_map/last_step/pallas_call | solution.py:307
  86.1 0.5 collective-permute-start.22
  86.6 0.5 apply_step.14
  87.1 0.5 apply_step.10
  87.7 0.5 apply_step.11
  88.2 0.0 copy-start.16
  88.2 0.0 collective-permute-done.17.query
  88.2 0.1 collective-permute-start.12
  88.3 0.5 apply_step.13
  88.8 0.5 apply_step.9
  89.4 0.0 collective-permute-done.18
  89.4 3.0 %collective-permute-start.19 = (bf16[128,640]{1,0:T(8,128)(2,1)S(1)}, bf16[128,640]{1,0:T(8,128)(2,1)S(1)}, u32[]{:S(2)}, u32[]{:S(2)}) collective-permute-start(bf16[128,640]{1,0:T(8,128)(2,1)S(1)} %add_convert_fusion.1), channel_id=1, source_target_pairs={{0,8},{8,12},{12,4},{4,0},{1,9},{9,13},{13,5},{5,1},{2,10},{10,14}... | collective-permute-start | bytes 491528 | tf_op jit(solution)/shard_map/ppermute | solution.py:24
  92.5 2.9 %collective-permute-done.12 = bf16[128,640]{1,0:T(8,128)(2,1)S(1)} collective-permute-done((bf16[128,640]{1,0:T(8,128)(2,1)S(1)}, bf16[128,640]{1,0:T(8,128)(2,1)S(1)}, u32[]{:S(2)}, u32[]{:S(2)}) %collective-permute-start.12) | collective-permute-done | bytes 163872 | tf_op jit(solution)/shard_map/ppermute | solution.py:24
  95.4 0.6 collective-permute-start.13
  96.0 2.9 %collective-permute-done.19 = bf16[128,640]{1,0:T(8,128)(2,1)S(1)} collective-permute-done((bf16[128,640]{1,0:T(8,128)(2,1)S(1)}, bf16[128,640]{1,0:T(8,128)(2,1)S(1)}, u32[]{:S(2)}, u32[]{:S(2)}) %collective-permute-start.19) | collective-permute-done | bytes 163872 | tf_op jit(solution)/shard_map/ppermute | solution.py:24
  98.9 1.1 collective-permute-start.20
  100.0 2.6 %collective-permute-done.13 = bf16[128,640]{1,0:T(8,128)(2,1)S(1)} collective-permute-done((bf16[128,640]{1,0:T(8,128)(2,1)S(1)}, bf16[128,640]{1,0:T(8,128)(2,1)S(1)}, u32[]{:S(2)}, u32[]{:S(2)}) %collective-permute-start.13) | collective-permute-done | bytes 163872 | tf_op jit(solution)/shard_map/ppermute | solution.py:24
  102.6 1.3 %collective-permute-start.14 = (bf16[128,640]{1,0:T(8,128)(2,1)S(1)}, bf16[128,640]{1,0:T(8,128)(2,1)S(1)}, u32[]{:S(2)}, u32[]{:S(2)}) collective-permute-start(bf16[128,640]{1,0:T(8,128)(2,1)S(1)} %add_convert_fusion.2), channel_id=1, source_target_pairs={{0,8},{8,12},{12,4},{4,0},{1,9},{9,13},{13,5},{5,1},{2,10},{10,14}... | collective-permute-start | bytes 491528 | tf_op jit(solution)/shard_map/ppermute | solution.py:24
  103.9 0.8 collective-permute-start.8
  104.7 4.6 %collective-permute-done.8.refs_2_ = f32[2,1,128]{2,1,0:T(1,128)S(1)} collective-permute-done((f32[2,1,128]{2,1,0:T(1,128)S(1)}, f32[2,1,128]{2,1,0:T(1,128)S(1)}, u32[]{:S(2)}, u32[]{:S(2)}) %collective-permute-start.8) | collective-permute-done | bytes 1056 | tf_op jit(solution)/shard_map/ppermute | solution.py:24
  109.3 2.8 %attend_step.1 = (f32[128,640]{1,0:T(8,128)S(1)}, f32[128,640]{1,0:T(8,128)S(1)}) custom-call(s32[1]{0:T(128)} %bitcast.1.block_index, bf16[128,1280]{1,0:T(8,128)(2,1)} %copy-done, bf16[128,1280]{1,0:T(8,128)(2,1)} %copy-done.8, f32[2,1,128]{2,1,0:T(1,128)S(1)} %collective-permute-done.8.refs_2_, bf16[128,1280]{1,0:T(8,128)(2,1)} %copy-done.10, ...), custom_call_target="tpu_custom_call" | custom-call | flops 167772160 | bytes 3276800 | tf_op jit(solution)/shard_map/attend_step/pallas_call | solution.py:418
  112.1 0.5 apply_step.12.kept
  112.6 0.5 apply_step.8.kept
  113.2 0.7 output_step.2.refs_0_
  113.9 0.0 collective-permute-done.14.moved
  113.9 0.7 output_step.3
  114.6 0.0 collective-permute-done.21
  114.6 2.9 %maximum_select_fusion = f32[4,3,80,640]{3,2,1,0:T(8,128)} fusion(f32[1,3,80,640]{3,2,1,0:T(8,128)S(1)} %collective-permute-done.22, f32[1,3,80,640]{3,2,1,0:T(8,128)} %collective-permute-done.21, f32[1,3,80,640]{3,2,1,0:T(8,128)S(1)} %copy-done.14, f32[1,3,80,640]{3,2,1,0:T(8,128)S(1)} %copy-done.13, pred[]{:T(512)S(6)} %eq.3), kind=kLoop, calls=%fused_computation | loop fusion | flops 4300800 | bytes 4915201 | tf_op jit(solution)/shard_map/jit(_where)/select_n | solution.py:498
  (41 shorter events, 0.3 us)
Async XLA Ops:
  0.6 10.7 %copy-start.15 = (bf16[128,2560]{1,0:T(8,128)(2,1)S(1)}, bf16[128,2560]{1,0:T(8,128)(2,1)}, u32[]{:S(2)}) copy-start(bf16[128,2560]{1,0:T(8,128)(2,1)} %param.6) | copy-start | bytes 1966084
  3.4 68.7 %collective-permute-start.7 = (f32[2,3,80,640]{3,2,1,0:T(8,128)}, f32[2,3,80,640]{3,2,1,0:T(8,128)S(1)}, u32[]{:S(2)}, u32[]{:S(2)}) collective-permute-start(f32[2,3,80,640]{3,2,1,0:T(8,128)} %get-tuple-element.20), channel_id=1, source_target_pairs={{0,1},{1,0},{2,3},{3,2},{4,5},{5,4},{6,7},{7,6},{8,9},{9,8},{10,11... | collective-permute-start | bytes 3686408 | tf_op jit(solution)/shard_map/ppermute | solution.py:24
  5.1 6.7 %copy-start.8 = (bf16[128,1280]{1,0:T(8,128)(2,1)}, bf16[128,1280]{1,0:T(8,128)(2,1)S(1)}, u32[]{:S(2)}) copy-start(bf16[128,1280]{1,0:T(8,128)(2,1)S(1)} %get-tuple-element.24.refs_1_) | copy-start | bytes 983044
  5.1 67.0 %copy-start.7 = (bf16[128,1280]{1,0:T(8,128)(2,1)}, bf16[128,1280]{1,0:T(8,128)(2,1)S(1)}, u32[]{:S(2)}) copy-start(bf16[128,1280]{1,0:T(8,128)(2,1)S(1)} %get-tuple-element.18.refs_3_) | copy-start | bytes 983044
  5.1 11.7 %collective-permute-start.3 = (bf16[128,1280]{1,0:T(8,128)(2,1)S(1)}, bf16[128,1280]{1,0:T(8,128)(2,1)S(1)}, u32[]{:S(2)}, u32[]{:S(2)}) collective-permute-start(bf16[128,1280]{1,0:T(8,128)(2,1)S(1)} %get-tuple-element.18.refs_3_), channel_id=1, source_target_pairs={{0,8},{8,12},{12,4},{4,0},{1,9},{9,13},{13,5},{5,1},{2,10},{10,14}... | collective-permute-start | bytes 983048 | tf_op jit(solution)/shard_map/ppermute | solution.py:24
  9.7 62.4 %copy-start = (bf16[128,1280]{1,0:T(8,128)(2,1)}, bf16[128,1280]{1,0:T(8,128)(2,1)S(1)}, u32[]{:S(2)}) copy-start(bf16[128,1280]{1,0:T(8,128)(2,1)S(1)} %columns_step.1.refs_0_) | copy-start | bytes 983044
  9.7 14.1 %collective-permute-start = (bf16[128,1280]{1,0:T(8,128)(2,1)S(1)}, bf16[128,1280]{1,0:T(8,128)(2,1)S(1)}, u32[]{:S(2)}, u32[]{:S(2)}) collective-permute-start(bf16[128,1280]{1,0:T(8,128)(2,1)S(1)} %columns_step.1.refs_0_), channel_id=1, source_target_pairs={{0,8},{8,12},{12,4},{4,0},{1,9},{9,13},{13,5},{5,1},{2,10},{10,14}... | collective-permute-start | bytes 983048 | tf_op jit(solution)/shard_map/ppermute | solution.py:24
  11.4 16.0 %collective-permute-start.15 = (bf16[128,640]{1,0:T(8,128)(2,1)S(1)}, bf16[128,640]{1,0:T(8,128)(2,1)S(1)}, u32[]{:S(2)}, u32[]{:S(2)}) collective-permute-start(bf16[128,640]{1,0:T(8,128)(2,1)S(1)} %get-tuple-element.34.refs_9_.query), channel_id=1, source_target_pairs={{0,8},{8,12},{12,4},{4,0},{1,9},{9,13},{13,5},{5,1},{2,10},{10,14}... | collective-permute-start | bytes 491528 | tf_op jit(solution)/shard_map/ppermute | solution.py:24
  11.8 0.7 copy-start.5
  12.4 59.6 %collective-permute-start.6 = (bf16[2,3,80,640]{3,2,1,0:T(8,128)(2,1)}, bf16[2,3,80,640]{3,2,1,0:T(8,128)(2,1)S(1)}, u32[]{:S(2)}, u32[]{:S(2)}) collective-permute-start(bf16[2,3,80,640]{3,2,1,0:T(8,128)(2,1)} %get-tuple-element.19), channel_id=1, source_target_pairs={{0,1},{1,0},{2,3},{3,2},{4,5},{5,4},{6,7},{7,6},{8,9},{9,8},{10,11... | collective-permute-start | bytes 1843208 | tf_op jit(solution)/shard_map/ppermute | solution.py:24
  16.8 31.0 %copy-start.9 = (bf16[128,1280]{1,0:T(8,128)(2,1)}, bf16[128,1280]{1,0:T(8,128)(2,1)S(1)}, u32[]{:S(2)}) copy-start(bf16[128,1280]{1,0:T(8,128)(2,1)S(1)} %collective-permute-done.3.refs_4_.refs_6_) | copy-start | bytes 983044
  16.8 31.0 %collective-permute-start.4 = (bf16[128,1280]{1,0:T(8,128)(2,1)S(1)}, bf16[128,1280]{1,0:T(8,128)(2,1)S(1)}, u32[]{:S(2)}, u32[]{:S(2)}) collective-permute-start(bf16[128,1280]{1,0:T(8,128)(2,1)S(1)} %collective-permute-done.3.refs_4_.refs_6_), channel_id=1, source_target_pairs={{0,8},{8,12},{12,4},{4,0},{1,9},{9,13},{13,5},{5,1},{2,10},{10,14}... | collective-permute-start | bytes 983048 | tf_op jit(solution)/shard_map/ppermute | solution.py:24
  23.8 24.7 %copy-start.10 = (bf16[128,1280]{1,0:T(8,128)(2,1)}, bf16[128,1280]{1,0:T(8,128)(2,1)S(1)}, u32[]{:S(2)}) copy-start(bf16[128,1280]{1,0:T(8,128)(2,1)S(1)} %collective-permute-done.refs_1_.refs_3_) | copy-start | bytes 983044
  23.8 24.7 %collective-permute-start.1 = (bf16[128,1280]{1,0:T(8,128)(2,1)S(1)}, bf16[128,1280]{1,0:T(8,128)(2,1)S(1)}, u32[]{:S(2)}, u32[]{:S(2)}) collective-permute-start(bf16[128,1280]{1,0:T(8,128)(2,1)S(1)} %collective-permute-done.refs_1_.refs_3_), channel_id=1, source_target_pairs={{0,8},{8,12},{12,4},{4,0},{1,9},{9,13},{13,5},{5,1},{2,10},{10,14}... | collective-permute-start | bytes 983048 | tf_op jit(solution)/shard_map/ppermute | solution.py:24
  27.3 17.1 %collective-permute-start.9 = (bf16[128,640]{1,0:T(8,128)(2,1)S(1)}, bf16[128,640]{1,0:T(8,128)(2,1)S(1)}, u32[]{:S(2)}, u32[]{:S(2)}) collective-permute-start(bf16[128,640]{1,0:T(8,128)(2,1)S(1)} %get-tuple-element.35.refs_10_.query), channel_id=1, source_target_pairs={{0,8},{8,12},{12,4},{4,0},{1,9},{9,13},{13,5},{5,1},{2,10},{10,14}... | collective-permute-start | bytes 491528 | tf_op jit(solution)/shard_map/ppermute | solution.py:24
  30.7 0.7 copy-start.3
  44.4 8.0 %collective-permute-start.16 = (bf16[128,640]{1,0:T(8,128)(2,1)S(1)}, bf16[128,640]{1,0:T(8,128)(2,1)S(1)}, u32[]{:S(2)}, u32[]{:S(2)}) collective-permute-start(bf16[128,640]{1,0:T(8,128)(2,1)S(1)} %collective-permute-done.15.query), channel_id=1, source_target_pairs={{0,8},{8,12},{12,4},{4,0},{1,9},{9,13},{13,5},{5,1},{2,10},{10,14}... | collective-permute-start | bytes 491528 | tf_op jit(solution)/shard_map/ppermute | solution.py:24
  47.8 24.2 %copy-start.11 = (bf16[128,1280]{1,0:T(8,128)(2,1)}, bf16[128,1280]{1,0:T(8,128)(2,1)S(1)}, u32[]{:S(2)}) copy-start(bf16[128,1280]{1,0:T(8,128)(2,1)S(1)} %collective-permute-done.4.refs_5_.refs_7_) | copy-start | bytes 983044
  47.8 27.1 %collective-permute-start.5 = (bf16[128,1280]{1,0:T(8,128)(2,1)S(1)}, bf16[128,1280]{1,0:T(8,128)(2,1)S(1)}, u32[]{:S(2)}, u32[]{:S(2)}) collective-permute-start(bf16[128,1280]{1,0:T(8,128)(2,1)S(1)} %collective-permute-done.4.refs_5_.refs_7_), channel_id=1, source_target_pairs={{0,8},{8,12},{12,4},{4,0},{1,9},{9,13},{13,5},{5,1},{2,10},{10,14}... | collective-permute-start | bytes 983048 | tf_op jit(solution)/shard_map/ppermute | solution.py:24
  48.6 23.5 %copy-start.12 = (bf16[128,1280]{1,0:T(8,128)(2,1)}, bf16[128,1280]{1,0:T(8,128)(2,1)S(1)}, u32[]{:S(2)}) copy-start(bf16[128,1280]{1,0:T(8,128)(2,1)S(1)} %collective-permute-done.1.refs_2_.refs_4_) | copy-start | bytes 983044
  48.6 26.4 %collective-permute-start.2 = (bf16[128,1280]{1,0:T(8,128)(2,1)S(1)}, bf16[128,1280]{1,0:T(8,128)(2,1)S(1)}, u32[]{:S(2)}, u32[]{:S(2)}) collective-permute-start(bf16[128,1280]{1,0:T(8,128)(2,1)S(1)} %collective-permute-done.1.refs_2_.refs_4_), channel_id=1, source_target_pairs={{0,8},{8,12},{12,4},{4,0},{1,9},{9,13},{13,5},{5,1},{2,10},{10,14}... | collective-permute-start | bytes 983048 | tf_op jit(solution)/shard_map/ppermute | solution.py:24
  52.4 16.2 %collective-permute-start.10 = (bf16[128,640]{1,0:T(8,128)(2,1)S(1)}, bf16[128,640]{1,0:T(8,128)(2,1)S(1)}, u32[]{:S(2)}, u32[]{:S(2)}) collective-permute-start(bf16[128,640]{1,0:T(8,128)(2,1)S(1)} %collective-permute-done.9.query), channel_id=1, source_target_pairs={{0,8},{8,12},{12,4},{4,0},{1,9},{9,13},{13,5},{5,1},{2,10},{10,14}... | collective-permute-start | bytes 491528 | tf_op jit(solution)/shard_map/ppermute | solution.py:24
  68.6 19.6 %collective-permute-start.17 = (bf16[128,640]{1,0:T(8,128)(2,1)S(1)}, bf16[128,640]{1,0:T(8,128)(2,1)S(1)}, u32[]{:S(2)}, u32[]{:S(2)}) collective-permute-start(bf16[128,640]{1,0:T(8,128)(2,1)S(1)} %collective-permute-done.16.query), channel_id=1, source_target_pairs={{0,8},{8,12},{12,4},{4,0},{1,9},{9,13},{13,5},{5,1},{2,10},{10,14}... | collective-permute-start | bytes 491528 | tf_op jit(solution)/shard_map/ppermute | solution.py:24
  72.0 16.8 %collective-permute-start.11 = (bf16[128,640]{1,0:T(8,128)(2,1)S(1)}, bf16[128,640]{1,0:T(8,128)(2,1)S(1)}, u32[]{:S(2)}, u32[]{:S(2)}) collective-permute-start(bf16[128,640]{1,0:T(8,128)(2,1)S(1)} %collective-permute-done.10.query), channel_id=1, source_target_pairs={{0,8},{8,12},{12,4},{4,0},{1,9},{9,13},{13,5},{5,1},{2,10},{10,14}... | collective-permute-start | bytes 491528 | tf_op jit(solution)/shard_map/ppermute | solution.py:24
  74.9 8.1 %copy-start.1 = (bf16[128,1280]{1,0:T(8,128)(2,1)}, bf16[128,1280]{1,0:T(8,128)(2,1)S(1)}, u32[]{:S(2)}) copy-start(bf16[128,1280]{1,0:T(8,128)(2,1)S(1)} %collective-permute-done.5.cotangent.refs_8_) | copy-start | bytes 983044
  74.9 8.1 %copy-start.2 = (bf16[128,1280]{1,0:T(8,128)(2,1)}, bf16[128,1280]{1,0:T(8,128)(2,1)S(1)}, u32[]{:S(2)}) copy-start(bf16[128,1280]{1,0:T(8,128)(2,1)S(1)} %collective-permute-done.2.key.refs_5_) | copy-start | bytes 983044
  77.2 12.2 %collective-permute-start.18 = (bf16[128,640]{1,0:T(8,128)(2,1)S(1)}, bf16[128,640]{1,0:T(8,128)(2,1)S(1)}, u32[]{:S(2)}, u32[]{:S(2)}) collective-permute-start(bf16[128,640]{1,0:T(8,128)(2,1)S(1)} %apply_step.15), channel_id=1, source_target_pairs={{0,8},{8,12},{12,4},{4,0},{1,9},{9,13},{13,5},{5,1},{2,10},{10,14}... | collective-permute-start | bytes 491528 | tf_op jit(solution)/shard_map/ppermute | solution.py:24
  79.2 35.4 %collective-permute-start.21 = (f32[1,3,80,640]{3,2,1,0:T(8,128)}, f32[1,3,80,640]{3,2,1,0:T(8,128)}, u32[]{:S(2)}, u32[]{:S(2)}) collective-permute-start(f32[1,3,80,640]{3,2,1,0:T(8,128)} %get-tuple-element.32), channel_id=1, source_target_pairs={{0,1},{1,0},{2,3},{3,2},{4,5},{5,4},{6,7},{7,6},{8,9},{9,8},{10,11... | collective-permute-start | bytes 1843208 | tf_op jit(solution)/shard_map/ppermute | solution.py:24
  86.1 28.5 %collective-permute-start.22 = (f32[1,3,80,640]{3,2,1,0:T(8,128)}, f32[1,3,80,640]{3,2,1,0:T(8,128)S(1)}, u32[]{:S(2)}, u32[]{:S(2)}) collective-permute-start(f32[1,3,80,640]{3,2,1,0:T(8,128)} %get-tuple-element.33), channel_id=1, source_target_pairs={{0,1},{1,0},{2,3},{3,2},{4,5},{5,4},{6,7},{7,6},{8,9},{9,8},{10,11... | collective-permute-start | bytes 1843208 | tf_op jit(solution)/shard_map/ppermute | solution.py:24
  88.2 15.7 %copy-start.16 = (f32[4,128]{1,0:T(4,128)S(1)}, f32[4,128]{1,0:T(4,128)}, u32[]{:S(2)}) copy-start(f32[4,128]{1,0:T(4,128)} %rates.1) | copy-start | bytes 6148
  88.2 21.1 %copy-start.4 = (bf16[128,640]{1,0:T(8,128)(2,1)S(1)}, bf16[128,640]{1,0:T(8,128)(2,1)}, u32[]{:S(2)}) copy-start(bf16[128,640]{1,0:T(8,128)(2,1)} %copy-done.3) | copy-start | bytes 491524
  88.2 21.1 %copy-start.6 = (bf16[128,640]{1,0:T(8,128)(2,1)S(1)}, bf16[128,640]{1,0:T(8,128)(2,1)}, u32[]{:S(2)}) copy-start(bf16[128,640]{1,0:T(8,128)(2,1)} %copy-done.5) | copy-start | bytes 491524
  88.2 7.1 %collective-permute-start.12 = (bf16[128,640]{1,0:T(8,128)(2,1)S(1)}, bf16[128,640]{1,0:T(8,128)(2,1)S(1)}, u32[]{:S(2)}, u32[]{:S(2)}) collective-permute-start(bf16[128,640]{1,0:T(8,128)(2,1)S(1)} %apply_step.11), channel_id=1, source_target_pairs={{0,8},{8,12},{12,4},{4,0},{1,9},{9,13},{13,5},{5,1},{2,10},{10,14}... | collective-permute-start | bytes 491528 | tf_op jit(solution)/shard_map/ppermute | solution.py:24
  89.4 9.4 %collective-permute-start.19 = (bf16[128,640]{1,0:T(8,128)(2,1)S(1)}, bf16[128,640]{1,0:T(8,128)(2,1)S(1)}, u32[]{:S(2)}, u32[]{:S(2)}) collective-permute-start(bf16[128,640]{1,0:T(8,128)(2,1)S(1)} %add_convert_fusion.1), channel_id=1, source_target_pairs={{0,8},{8,12},{12,4},{4,0},{1,9},{9,13},{13,5},{5,1},{2,10},{10,14}... | collective-permute-start | bytes 491528 | tf_op jit(solution)/shard_map/ppermute | solution.py:24
  95.4 7.1 %collective-permute-start.13 = (bf16[128,640]{1,0:T(8,128)(2,1)S(1)}, bf16[128,640]{1,0:T(8,128)(2,1)S(1)}, u32[]{:S(2)}, u32[]{:S(2)}) collective-permute-start(bf16[128,640]{1,0:T(8,128)(2,1)S(1)} %add_convert_fusion.3), channel_id=1, source_target_pairs={{0,8},{8,12},{12,4},{4,0},{1,9},{9,13},{13,5},{5,1},{2,10},{10,14}... | collective-permute-start | bytes 491528 | tf_op jit(solution)/shard_map/ppermute | solution.py:24
  98.9 14.3 %collective-permute-start.20 = (bf16[128,640]{1,0:T(8,128)(2,1)S(1)}, bf16[128,640]{1,0:T(8,128)(2,1)S(1)}, u32[]{:S(2)}, u32[]{:S(2)}) collective-permute-start(bf16[128,640]{1,0:T(8,128)(2,1)S(1)} %add_convert_fusion), channel_id=1, source_target_pairs={{0,8},{8,12},{12,4},{4,0},{1,9},{9,13},{13,5},{5,1},{2,10},{10,14}... | collective-permute-start | bytes 491528 | tf_op jit(solution)/shard_map/ppermute | solution.py:24
  102.6 11.3 %collective-permute-start.14 = (bf16[128,640]{1,0:T(8,128)(2,1)S(1)}, bf16[128,640]{1,0:T(8,128)(2,1)S(1)}, u32[]{:S(2)}, u32[]{:S(2)}) collective-permute-start(bf16[128,640]{1,0:T(8,128)(2,1)S(1)} %add_convert_fusion.2), channel_id=1, source_target_pairs={{0,8},{8,12},{12,4},{4,0},{1,9},{9,13},{13,5},{5,1},{2,10},{10,14}... | collective-permute-start | bytes 491528 | tf_op jit(solution)/shard_map/ppermute | solution.py:24
  103.9 5.4 %collective-permute-start.8 = (f32[2,1,128]{2,1,0:T(1,128)S(1)}, f32[2,1,128]{2,1,0:T(1,128)S(1)}, u32[]{:S(2)}, u32[]{:S(2)}) collective-permute-start(f32[2,1,128]{2,1,0:T(1,128)S(1)} %bitcast.3), channel_id=1, source_target_pairs={{0,4},{4,8},{8,12},{12,0},{1,5},{5,9},{9,13},{13,1},{2,6},{6,10},{... | collective-permute-start | bytes 3080 | tf_op jit(solution)/shard_map/ppermute | solution.py:24
  112.1 2.5 %copy-start.13 = (f32[1,3,80,640]{3,2,1,0:T(8,128)S(1)}, f32[1,3,80,640]{3,2,1,0:T(8,128)}, u32[]{:S(2)}) copy-start(f32[1,3,80,640]{3,2,1,0:T(8,128)} %get-tuple-element.30) | copy-start | bytes 1843204
  112.1 2.5 %copy-start.14 = (f32[1,3,80,640]{3,2,1,0:T(8,128)S(1)}, f32[1,3,80,640]{3,2,1,0:T(8,128)}, u32[]{:S(2)}) copy-start(f32[1,3,80,640]{3,2,1,0:T(8,128)} %get-tuple-element.31) | copy-start | bytes 1843204

commit v6 on v5

--- a/solution.py
+++ b/solution.py
@@ -319,7 +319,7 @@
     )(key, cotangent, in_hbm(so_far) if head else so_far, low)
 
 
-def apply_body(query, low, *refs):
+def apply_body(query, low, out):
     hid = low.shape[0] // 6
     unit = unit_rows(query[...])
     gate = lax.dot_general(unit, low[: 2 * hid, :], NT, preferred_element_type=jnp.float32)
@@ -328,12 +328,10 @@
     )
     hidden = (gate * jax.nn.sigmoid(gate) * upward).astype(jnp.bfloat16)
     made = jnp.dot(hidden, low[4 * hid :, :], preferred_element_type=jnp.float32)
-    if len(refs) > 1:
-        made = made + refs[0][...]
-    refs[-1][...] = made.astype(refs[-1].dtype)
-
-
-def apply_step(query, low, dtype, *more):
+    out[...] = made.astype(out.dtype)
+
+
+def apply_step(query, low, dtype):
     rows, width = query.shape
     total = low.shape[0]
     whole = pl.BlockSpec((rows, width), lambda i: (0, 0))
@@ -341,38 +339,38 @@
         apply_body,
         out_shape=jax.ShapeDtypeStruct((rows, width), dtype),
         grid=(1,),
-        in_specs=[whole, pl.BlockSpec((total, width), lambda i: (0, 0))]
-        + [whole] * len(more),
+        in_specs=[whole, pl.BlockSpec((total, width), lambda i: (0, 0))],
         out_specs=whole,
         compiler_params=pltpu.CompilerParams(vmem_limit_bytes=8 << 20),
         cost_estimate=pl.CostEstimate(
             flops=2 * rows * total * width, bytes_accessed=2 * total * width, transcendentals=0
         ),
         name="apply_step",
-    )(query, low, *more)
-
-
-def output_body(kept, moved, *refs):
-    refs[-1][...] = (kept[...] + moved[...].astype(jnp.float32)).astype(jnp.bfloat16)
-
-
-def output_step(head, heads, kept, moved, before):
+    )(query, low)
+
+
+def output_body(kept, attended, moved, *refs):
+    total = attended[...] + (kept[...] + moved[...].astype(jnp.float32))
+    refs[-1][...] = total.astype(jnp.bfloat16)
+
+
+def output_step(head, heads, kept, attended, moved, before):
     rows, width = kept.shape
     more = () if before is None else (before,)
     return pl.pallas_call(
         output_body,
         out_shape=pltpu.HBM((rows, heads * width), jnp.bfloat16),
         grid=(1,),
-        in_specs=[pl.BlockSpec(memory_space=pltpu.VMEM)] * 2
+        in_specs=[pl.BlockSpec(memory_space=pltpu.VMEM)] * 3
         + [pl.BlockSpec(memory_space=pl.ANY)] * len(more),
         out_specs=pl.BlockSpec((rows, width), lambda i: (0, head)),
-        input_output_aliases={2: 0} if more else {},
+        input_output_aliases={3: 0} if more else {},
         compiler_params=pltpu.CompilerParams(vmem_limit_bytes=4 << 20),
         cost_estimate=pl.CostEstimate(
             flops=rows * width, bytes_accessed=8 * rows * width, transcendentals=0
         ),
         name="output_step",
-    )(kept, moved, *more)
+    )(kept, attended, moved, *more)
 
 
 def attend_body(token_scale, block_index, *refs):
@@ -491,8 +489,8 @@
         moving = [hop(made[h]) for h in heads]
     layer_output = None
     for h in heads:
-        kept = apply_step(asked[0][h], lows[h], jnp.float32, attended[h])
-        layer_output = output_step(h, per_rep, kept, moving[h], layer_output)
+        kept = apply_step(asked[0][h], lows[h], jnp.float32)
+        layer_output = output_step(h, per_rep, kept, attended[h], moving[h], layer_output)
     returned = [hop(fresh[h][1], "rep") for h in heads]
     owned = [new[0] for new in fresh]
     fast_updated = jnp.where(

time: 118 us -> 118 us (level)
  no operation moved by 1% of the time
where the time goes in v6:
time: 118 us
  waiting for transfers between devices  49.5 us (42%)
  starting transfers between devices  37.8 us (32%)
  Pallas kernels  24.7 us (21%)
  other arithmetic  3.07 us (3%)
  local copies, waits for them, and re-layouts  1.44 us (1%)
    ppermute x23, waiting for transfers between devices, ring(): return lax.ppermute(value, axis, list(zip(order, (*order[1:], order[0]))))  49.5 us
    ppermute x23, starting transfers between devices, ring(): return lax.ppermute(value, axis, list(zip(order, (*order[1:], order[0]))))  37.8 us
    pallas_call x2, Pallas kernels, early_step(): pl.pallas_call(functools.partial(early_body, slots), out_shape=((pltpu.HB...  6.69 us
    pallas_call x2, Pallas kernels, last_step(): pl.pallas_call(last_body, out_shape=(fresh, fresh, jax.ShapeDtypeStruct((...  4.82 us
    pallas_call x8, Pallas kernels, apply_step(): pl.pallas_call(apply_body, out_shape=jax.ShapeDtypeStruct((rows, width),...  4.09 us
    select_n x1, other arithmetic, tokens_travel(): jnp.where(rep_index == 0, jnp.concatenate([*owned, *returned], axis=0), j...  2.91 us
    pallas_call x1, Pallas kernels, attend_step(): pl.pallas_call(functools.partial(attend_body, token_scale), out_shape=mad...  2.81 us
    pallas_call x1, Pallas kernels, other_step(): pl.pallas_call(other_body, out_shape=(pltpu.HBM(made, jnp.bfloat16), pltp...  2.74 us
  transfers between devices with their start and end apart: 23, of which 10 were waited for; matrix products, arithmetic and copies ran while one was open for 0% of the time, Pallas kernels for 19%

profile of v6, /device:TPU:0, one launch (start us, length us, event | category | flops | bytes accessed | tf_op | source)
XLA Modules:
  0.0 117.5 jit_solution(15477267250955942900)
XLA Ops:
  0.6 2.7 %other_step.1 = (bf16[2,3,80,640]{3,2,1,0:T(8,128)(2,1)}, f32[2,3,80,640]{3,2,1,0:T(8,128)}) custom-call(s32[1]{0:T(128)} %bitcast.rep, f32[4,3,80,640]{3,2,1,0:T(8,128)} %refs_6_.3, f32[4,3,80,640]{3,2,1,0:T(8,128)} %refs_7_.3), custom_call_target="tpu_custom_call" | custom-call | flops 614400 | bytes 4300800 | tf_op jit(solution)/shard_map/other_step/pallas_call | solution.py:203
  3.4 0.5 collective-permute-start.7
  3.9 1.2 cotangent_step.1
  5.1 3.6 %collective-permute-start.3 = (bf16[128,1280]{1,0:T(8,128)(2,1)S(1)}, bf16[128,1280]{1,0:T(8,128)(2,1)S(1)}, u32[]{:S(2)}, u32[]{:S(2)}) collective-permute-start(bf16[128,1280]{1,0:T(8,128)(2,1)S(1)} %get-tuple-element.18.refs_3_), channel_id=1, source_target_pairs={{0,8},{8,12},{12,4},{4,0},{1,9},{9,13},{13,5},{5,1},{2,10},{10,14}... | collective-permute-start | bytes 983048 | tf_op jit(solution)/shard_map/ppermute | solution.py:24
  8.7 1.0 columns_step.1.refs_0_
  9.7 0.0 copy-start
  9.7 1.6 %collective-permute-start = (bf16[128,1280]{1,0:T(8,128)(2,1)S(1)}, bf16[128,1280]{1,0:T(8,128)(2,1)S(1)}, u32[]{:S(2)}, u32[]{:S(2)}) collective-permute-start(bf16[128,1280]{1,0:T(8,128)(2,1)S(1)} %columns_step.1.refs_0_), channel_id=1, source_target_pairs={{0,8},{8,12},{12,4},{4,0},{1,9},{9,13},{13,5},{5,1},{2,10},{10,14}... | collective-permute-start | bytes 983048 | tf_op jit(solution)/shard_map/ppermute | solution.py:24
  11.4 0.4 collective-permute-start.15
  11.8 0.7 copy-done.5
  12.4 0.0 collective-permute-start.6
  12.4 4.4 %collective-permute-done.3.refs_4_.refs_6_ = bf16[128,1280]{1,0:T(8,128)(2,1)S(1)} collective-permute-done((bf16[128,1280]{1,0:T(8,128)(2,1)S(1)}, bf16[128,1280]{1,0:T(8,128)(2,1)S(1)}, u32[]{:S(2)}, u32[]{:S(2)}) %collective-permute-start.3) | collective-permute-done | bytes 327712 | tf_op jit(solution)/shard_map/ppermute | solution.py:24
  16.8 3.4 %collective-permute-start.4 = (bf16[128,1280]{1,0:T(8,128)(2,1)S(1)}, bf16[128,1280]{1,0:T(8,128)(2,1)S(1)}, u32[]{:S(2)}, u32[]{:S(2)}) collective-permute-start(bf16[128,1280]{1,0:T(8,128)(2,1)S(1)} %collective-permute-done.3.refs_4_.refs_6_), channel_id=1, source_target_pairs={{0,8},{8,12},{12,4},{4,0},{1,9},{9,13},{13,5},{5,1},{2,10},{10,14}... | collective-permute-start | bytes 983048 | tf_op jit(solution)/shard_map/ppermute | solution.py:24
  20.2 3.6 %collective-permute-done.refs_1_.refs_3_ = bf16[128,1280]{1,0:T(8,128)(2,1)S(1)} collective-permute-done((bf16[128,1280]{1,0:T(8,128)(2,1)S(1)}, bf16[128,1280]{1,0:T(8,128)(2,1)S(1)}, u32[]{:S(2)}, u32[]{:S(2)}) %collective-permute-start) | collective-permute-done | bytes 327712 | tf_op jit(solution)/shard_map/ppermute | solution.py:24
  23.8 3.4 %collective-permute-start.1 = (bf16[128,1280]{1,0:T(8,128)(2,1)S(1)}, bf16[128,1280]{1,0:T(8,128)(2,1)S(1)}, u32[]{:S(2)}, u32[]{:S(2)}) collective-permute-start(bf16[128,1280]{1,0:T(8,128)(2,1)S(1)} %collective-permute-done.refs_1_.refs_3_), channel_id=1, source_target_pairs={{0,8},{8,12},{12,4},{4,0},{1,9},{9,13},{13,5},{5,1},{2,10},{10,14}... | collective-permute-start | bytes 983048 | tf_op jit(solution)/shard_map/ppermute | solution.py:24
  27.2 0.1 collective-permute-done.15.query
  27.3 3.4 %collective-permute-start.9 = (bf16[128,640]{1,0:T(8,128)(2,1)S(1)}, bf16[128,640]{1,0:T(8,128)(2,1)S(1)}, u32[]{:S(2)}, u32[]{:S(2)}) collective-permute-start(bf16[128,640]{1,0:T(8,128)(2,1)S(1)} %get-tuple-element.35.query.refs_10_), channel_id=1, source_target_pairs={{0,8},{8,12},{12,4},{4,0},{1,9},{9,13},{13,5},{5,1},{2,10},{10,14}... | collective-permute-start | bytes 491528 | tf_op jit(solution)/shard_map/ppermute | solution.py:24
  30.7 0.7 copy-done.3
  31.4 13.0 %collective-permute-done.9.query = bf16[128,640]{1,0:T(8,128)(2,1)S(1)} collective-permute-done((bf16[128,640]{1,0:T(8,128)(2,1)S(1)}, bf16[128,640]{1,0:T(8,128)(2,1)S(1)}, u32[]{:S(2)}, u32[]{:S(2)}) %collective-permute-start.9) | collective-permute-done | bytes 163872 | tf_op jit(solution)/shard_map/ppermute | solution.py:24
  44.4 3.4 %collective-permute-start.16 = (bf16[128,640]{1,0:T(8,128)(2,1)S(1)}, bf16[128,640]{1,0:T(8,128)(2,1)S(1)}, u32[]{:S(2)}, u32[]{:S(2)}) collective-permute-start(bf16[128,640]{1,0:T(8,128)(2,1)S(1)} %collective-permute-done.15.query), channel_id=1, source_target_pairs={{0,8},{8,12},{12,4},{4,0},{1,9},{9,13},{13,5},{5,1},{2,10},{10,14}... | collective-permute-start | bytes 491528 | tf_op jit(solution)/shard_map/ppermute | solution.py:24
  47.8 0.0 collective-permute-done.4.refs_5_.refs_7_
  47.8 0.7 collective-permute-start.5
  48.6 1.3 %collective-permute-start.2 = (bf16[128,1280]{1,0:T(8,128)(2,1)S(1)}, bf16[128,1280]{1,0:T(8,128)(2,1)S(1)}, u32[]{:S(2)}, u32[]{:S(2)}) collective-permute-start(bf16[128,1280]{1,0:T(8,128)(2,1)S(1)} %collective-permute-done.1.refs_2_.refs_4_), channel_id=1, source_target_pairs={{0,8},{8,12},{12,4},{4,0},{1,9},{9,13},{13,5},{5,1},{2,10},{10,14}... | collective-permute-start | bytes 983048 | tf_op jit(solution)/shard_map/ppermute | solution.py:24
  49.8 2.6 %collective-permute-done.16.query = bf16[128,640]{1,0:T(8,128)(2,1)S(1)} collective-permute-done((bf16[128,640]{1,0:T(8,128)(2,1)S(1)}, bf16[128,640]{1,0:T(8,128)(2,1)S(1)}, u32[]{:S(2)}, u32[]{:S(2)}) %collective-permute-start.16) | collective-permute-done | bytes 163872 | tf_op jit(solution)/shard_map/ppermute | solution.py:24
  52.4 3.4 %collective-permute-start.10 = (bf16[128,640]{1,0:T(8,128)(2,1)S(1)}, bf16[128,640]{1,0:T(8,128)(2,1)S(1)}, u32[]{:S(2)}, u32[]{:S(2)}) collective-permute-start(bf16[128,640]{1,0:T(8,128)(2,1)S(1)} %collective-permute-done.9.query), channel_id=1, source_target_pairs={{0,8},{8,12},{12,4},{4,0},{1,9},{9,13},{13,5},{5,1},{2,10},{10,14}... | collective-permute-start | bytes 491528 | tf_op jit(solution)/shard_map/ppermute | solution.py:24
  55.8 12.9 %collective-permute-done.10.query = bf16[128,640]{1,0:T(8,128)(2,1)S(1)} collective-permute-done((bf16[128,640]{1,0:T(8,128)(2,1)S(1)}, bf16[128,640]{1,0:T(8,128)(2,1)S(1)}, u32[]{:S(2)}, u32[]{:S(2)}) %collective-permute-start.10) | collective-permute-done | bytes 163872 | tf_op jit(solution)/shard_map/ppermute | solution.py:24
  68.6 3.4 %collective-permute-start.17 = (bf16[128,640]{1,0:T(8,128)(2,1)S(1)}, bf16[128,640]{1,0:T(8,128)(2,1)S(1)}, u32[]{:S(2)}, u32[]{:S(2)}) collective-permute-start(bf16[128,640]{1,0:T(8,128)(2,1)S(1)} %collective-permute-done.16.query), channel_id=1, source_target_pairs={{0,8},{8,12},{12,4},{4,0},{1,9},{9,13},{13,5},{5,1},{2,10},{10,14}... | collective-permute-start | bytes 491528 | tf_op jit(solution)/shard_map/ppermute | solution.py:24
  72.0 0.0 collective-permute-start.11
  72.0 0.0 collective-permute-done.7.refs_9_
  72.1 2.8 %early_step.3 = (f32[480,640]{1,0:T(8,128)S(1)}, bf16[480,640]{1,0:T(8,128)(2,1)S(1)}) custom-call(s32[1]{0:T(128)} %bitcast.rep, bf16[128,1280]{1,0:T(8,128)(2,1)} %copy-done, bf16[128,1280]{1,0:T(8,128)(2,1)} %copy-done.10, bf16[128,1280]{1,0:T(8,128)(2,1)} %copy-done.12, bf16[128,1280]{1,0:T(8,128)(2,1)} %copy-done.7, bf16[128,1280]{1,0:T(8,128)(2,1)} %copy-done.9, ...), custom_call_target="tpu_custom_call" | custom-call | flops 471859200 | bytes 3072000 | tf_op jit(solution)/shard_map/early_step/pallas_call | solution.py:260
  74.9 0.0 collective-permute-done.5.cotangent.refs_8_
  74.9 0.0 collective-permute-done.2.key.refs_5_
  75.0 1.8 %last_step.3 = (f32[1,3,80,640]{3,2,1,0:T(8,128)}, f32[1,3,80,640]{3,2,1,0:T(8,128)}, bf16[480,640]{1,0:T(8,128)(2,1)S(1)}) custom-call(bf16[128,1280]{1,0:T(8,128)(2,1)S(1)} %collective-permute-done.2.key.refs_5_, bf16[128,1280]{1,0:T(8,128)(2,1)S(1)} %collective-permute-done.5.cotangent.refs_8_, f32[480,640]{1,0:T(8,128)S(1)} %get-tuple-element.26.so_far, ...), custom_call_target="tpu_custom_call" | custom-call | flops 157286400 | bytes 3686400 | tf_op jit(solution)/shard_map/last_step/pallas_call | solution.py:307
  76.7 0.5 apply_step.15
  77.2 1.9 %collective-permute-start.18 = (bf16[128,640]{1,0:T(8,128)(2,1)S(1)}, bf16[128,640]{1,0:T(8,128)(2,1)S(1)}, u32[]{:S(2)}, u32[]{:S(2)}) collective-permute-start(bf16[128,640]{1,0:T(8,128)(2,1)S(1)} %apply_step.15), channel_id=1, source_target_pairs={{0,8},{8,12},{12,4},{4,0},{1,9},{9,13},{13,5},{5,1},{2,10},{10,14}... | collective-permute-start | bytes 491528 | tf_op jit(solution)/shard_map/ppermute | solution.py:24
  79.2 0.0 collective-permute-start.21
  79.2 3.9 %early_step.2 = (f32[480,640]{1,0:T(8,128)}, bf16[480,640]{1,0:T(8,128)(2,1)S(1)}) custom-call(s32[1]{0:T(128)} %bitcast.rep, bf16[128,1280]{1,0:T(8,128)(2,1)} %copy-done, bf16[128,1280]{1,0:T(8,128)(2,1)} %copy-done.10, bf16[128,1280]{1,0:T(8,128)(2,1)} %copy-done.12, bf16[128,1280]{1,0:T(8,128)(2,1)} %copy-done.7, bf16[128,1280]{1,0:T(8,128)(2,1)} %copy-done.9, ...), custom_call_target="tpu_custom_call" | custom-call | flops 471859200 | bytes 3072000 | tf_op jit(solution)/shard_map/early_step/pallas_call | solution.py:260
  83.0 3.1 %last_step.2 = (f32[1,3,80,640]{3,2,1,0:T(8,128)}, f32[1,3,80,640]{3,2,1,0:T(8,128)}, bf16[480,640]{1,0:T(8,128)(2,1)S(1)}) custom-call(bf16[128,1280]{1,0:T(8,128)(2,1)S(1)} %collective-permute-done.2.key.refs_5_, bf16[128,1280]{1,0:T(8,128)(2,1)S(1)} %collective-permute-done.5.cotangent.refs_8_, f32[480,640]{1,0:T(8,128)} %get-tuple-element.21.so_far, ...), custom_call_target="tpu_custom_call" | custom-call | flops 157286400 | bytes 3686400 | tf_op jit(solution)/shard_map/last_step/pallas_call | solution.py:307
  86.1 0.5 collective-permute-start.22
  86.6 0.5 apply_step.14
  87.1 0.5 apply_step.10
  87.7 0.5 apply_step.11
  88.2 0.0 copy-start.16
  88.2 0.0 collective-permute-done.17.query
  88.2 0.1 collective-permute-start.12
  88.3 0.5 apply_step.13
  88.8 0.5 apply_step.9
  89.4 0.0 collective-permute-done.18
  89.4 3.0 %collective-permute-start.19 = (bf16[128,640]{1,0:T(8,128)(2,1)S(1)}, bf16[128,640]{1,0:T(8,128)(2,1)S(1)}, u32[]{:S(2)}, u32[]{:S(2)}) collective-permute-start(bf16[128,640]{1,0:T(8,128)(2,1)S(1)} %add_convert_fusion.1), channel_id=1, source_target_pairs={{0,8},{8,12},{12,4},{4,0},{1,9},{9,13},{13,5},{5,1},{2,10},{10,14}... | collective-permute-start | bytes 491528 | tf_op jit(solution)/shard_map/ppermute | solution.py:24
  92.5 2.9 %collective-permute-done.12 = bf16[128,640]{1,0:T(8,128)(2,1)S(1)} collective-permute-done((bf16[128,640]{1,0:T(8,128)(2,1)S(1)}, bf16[128,640]{1,0:T(8,128)(2,1)S(1)}, u32[]{:S(2)}, u32[]{:S(2)}) %collective-permute-start.12) | collective-permute-done | bytes 163872 | tf_op jit(solution)/shard_map/ppermute | solution.py:24
  95.4 0.6 collective-permute-start.13
  96.0 2.9 %collective-permute-done.19 = bf16[128,640]{1,0:T(8,128)(2,1)S(1)} collective-permute-done((bf16[128,640]{1,0:T(8,128)(2,1)S(1)}, bf16[128,640]{1,0:T(8,128)(2,1)S(1)}, u32[]{:S(2)}, u32[]{:S(2)}) %collective-permute-start.19) | collective-permute-done | bytes 163872 | tf_op jit(solution)/shard_map/ppermute | solution.py:24
  98.9 1.1 collective-permute-start.20
  100.0 2.6 %collective-permute-done.13 = bf16[128,640]{1,0:T(8,128)(2,1)S(1)} collective-permute-done((bf16[128,640]{1,0:T(8,128)(2,1)S(1)}, bf16[128,640]{1,0:T(8,128)(2,1)S(1)}, u32[]{:S(2)}, u32[]{:S(2)}) %collective-permute-start.13) | collective-permute-done | bytes 163872 | tf_op jit(solution)/shard_map/ppermute | solution.py:24
  102.6 1.3 %collective-permute-start.14 = (bf16[128,640]{1,0:T(8,128)(2,1)S(1)}, bf16[128,640]{1,0:T(8,128)(2,1)S(1)}, u32[]{:S(2)}, u32[]{:S(2)}) collective-permute-start(bf16[128,640]{1,0:T(8,128)(2,1)S(1)} %add_convert_fusion.2), channel_id=1, source_target_pairs={{0,8},{8,12},{12,4},{4,0},{1,9},{9,13},{13,5},{5,1},{2,10},{10,14}... | collective-permute-start | bytes 491528 | tf_op jit(solution)/shard_map/ppermute | solution.py:24
  103.9 0.8 collective-permute-start.8
  104.7 4.6 %collective-permute-done.8.refs_2_ = f32[2,1,128]{2,1,0:T(1,128)S(1)} collective-permute-done((f32[2,1,128]{2,1,0:T(1,128)S(1)}, f32[2,1,128]{2,1,0:T(1,128)S(1)}, u32[]{:S(2)}, u32[]{:S(2)}) %collective-permute-start.8) | collective-permute-done | bytes 1056 | tf_op jit(solution)/shard_map/ppermute | solution.py:24
  109.3 2.8 %attend_step.1 = (f32[128,640]{1,0:T(8,128)S(1)}, f32[128,640]{1,0:T(8,128)S(1)}) custom-call(s32[1]{0:T(128)} %bitcast.1.block_index, bf16[128,1280]{1,0:T(8,128)(2,1)} %copy-done, bf16[128,1280]{1,0:T(8,128)(2,1)} %copy-done.8, f32[2,1,128]{2,1,0:T(1,128)S(1)} %collective-permute-done.8.refs_2_, bf16[128,1280]{1,0:T(8,128)(2,1)} %copy-done.10, ...), custom_call_target="tpu_custom_call" | custom-call | flops 167772160 | bytes 3276800 | tf_op jit(solution)/shard_map/attend_step/pallas_call | solution.py:416
  112.1 0.5 apply_step.12.kept
  112.6 0.5 apply_step.8.kept
  113.2 0.7 output_step.2.refs_0_
  113.9 0.7 output_step.3
  114.6 0.0 collective-permute-done.21
  114.6 0.0 collective-permute-done.22
  114.6 2.9 %maximum_select_fusion = f32[4,3,80,640]{3,2,1,0:T(8,128)} fusion(f32[1,3,80,640]{3,2,1,0:T(8,128)S(1)} %collective-permute-done.22, f32[1,3,80,640]{3,2,1,0:T(8,128)} %collective-permute-done.21, f32[1,3,80,640]{3,2,1,0:T(8,128)S(1)} %copy-done.14, f32[1,3,80,640]{3,2,1,0:T(8,128)S(1)} %copy-done.13, pred[]{:T(512)S(6)} %eq.3), kind=kLoop, calls=%fused_computation | loop fusion | flops 4300800 | bytes 4915201 | tf_op jit(solution)/shard_map/jit(_where)/select_n | solution.py:496
  (41 shorter events, 0.3 us)
Async XLA Ops:
  0.6 10.7 %copy-start.15 = (bf16[128,2560]{1,0:T(8,128)(2,1)S(1)}, bf16[128,2560]{1,0:T(8,128)(2,1)}, u32[]{:S(2)}) copy-start(bf16[128,2560]{1,0:T(8,128)(2,1)} %param.6) | copy-start | bytes 1966084
  3.4 68.7 %collective-permute-start.7 = (f32[2,3,80,640]{3,2,1,0:T(8,128)}, f32[2,3,80,640]{3,2,1,0:T(8,128)S(1)}, u32[]{:S(2)}, u32[]{:S(2)}) collective-permute-start(f32[2,3,80,640]{3,2,1,0:T(8,128)} %get-tuple-element.20), channel_id=1, source_target_pairs={{0,1},{1,0},{2,3},{3,2},{4,5},{5,4},{6,7},{7,6},{8,9},{9,8},{10,11... | collective-permute-start | bytes 3686408 | tf_op jit(solution)/shard_map/ppermute | solution.py:24
  5.1 6.7 %copy-start.8 = (bf16[128,1280]{1,0:T(8,128)(2,1)}, bf16[128,1280]{1,0:T(8,128)(2,1)S(1)}, u32[]{:S(2)}) copy-start(bf16[128,1280]{1,0:T(8,128)(2,1)S(1)} %get-tuple-element.24.refs_1_) | copy-start | bytes 983044
  5.1 67.0 %copy-start.7 = (bf16[128,1280]{1,0:T(8,128)(2,1)}, bf16[128,1280]{1,0:T(8,128)(2,1)S(1)}, u32[]{:S(2)}) copy-start(bf16[128,1280]{1,0:T(8,128)(2,1)S(1)} %get-tuple-element.18.refs_3_) | copy-start | bytes 983044
  5.1 11.7 %collective-permute-start.3 = (bf16[128,1280]{1,0:T(8,128)(2,1)S(1)}, bf16[128,1280]{1,0:T(8,128)(2,1)S(1)}, u32[]{:S(2)}, u32[]{:S(2)}) collective-permute-start(bf16[128,1280]{1,0:T(8,128)(2,1)S(1)} %get-tuple-element.18.refs_3_), channel_id=1, source_target_pairs={{0,8},{8,12},{12,4},{4,0},{1,9},{9,13},{13,5},{5,1},{2,10},{10,14}... | collective-permute-start | bytes 983048 | tf_op jit(solution)/shard_map/ppermute | solution.py:24
  9.7 62.4 %copy-start = (bf16[128,1280]{1,0:T(8,128)(2,1)}, bf16[128,1280]{1,0:T(8,128)(2,1)S(1)}, u32[]{:S(2)}) copy-start(bf16[128,1280]{1,0:T(8,128)(2,1)S(1)} %columns_step.1.refs_0_) | copy-start | bytes 983044
  9.7 14.1 %collective-permute-start = (bf16[128,1280]{1,0:T(8,128)(2,1)S(1)}, bf16[128,1280]{1,0:T(8,128)(2,1)S(1)}, u32[]{:S(2)}, u32[]{:S(2)}) collective-permute-start(bf16[128,1280]{1,0:T(8,128)(2,1)S(1)} %columns_step.1.refs_0_), channel_id=1, source_target_pairs={{0,8},{8,12},{12,4},{4,0},{1,9},{9,13},{13,5},{5,1},{2,10},{10,14}... | collective-permute-start | bytes 983048 | tf_op jit(solution)/shard_map/ppermute | solution.py:24
  11.4 16.0 %collective-permute-start.15 = (bf16[128,640]{1,0:T(8,128)(2,1)S(1)}, bf16[128,640]{1,0:T(8,128)(2,1)S(1)}, u32[]{:S(2)}, u32[]{:S(2)}) collective-permute-start(bf16[128,640]{1,0:T(8,128)(2,1)S(1)} %get-tuple-element.34.refs_9_.query), channel_id=1, source_target_pairs={{0,8},{8,12},{12,4},{4,0},{1,9},{9,13},{13,5},{5,1},{2,10},{10,14}... | collective-permute-start | bytes 491528 | tf_op jit(solution)/shard_map/ppermute | solution.py:24
  11.8 0.7 copy-start.5
  12.4 59.6 %collective-permute-start.6 = (bf16[2,3,80,640]{3,2,1,0:T(8,128)(2,1)}, bf16[2,3,80,640]{3,2,1,0:T(8,128)(2,1)S(1)}, u32[]{:S(2)}, u32[]{:S(2)}) collective-permute-start(bf16[2,3,80,640]{3,2,1,0:T(8,128)(2,1)} %get-tuple-element.19), channel_id=1, source_target_pairs={{0,1},{1,0},{2,3},{3,2},{4,5},{5,4},{6,7},{7,6},{8,9},{9,8},{10,11... | collective-permute-start | bytes 1843208 | tf_op jit(solution)/shard_map/ppermute | solution.py:24
  16.8 31.0 %copy-start.9 = (bf16[128,1280]{1,0:T(8,128)(2,1)}, bf16[128,1280]{1,0:T(8,128)(2,1)S(1)}, u32[]{:S(2)}) copy-start(bf16[128,1280]{1,0:T(8,128)(2,1)S(1)} %collective-permute-done.3.refs_4_.refs_6_) | copy-start | bytes 983044
  16.8 31.0 %collective-permute-start.4 = (bf16[128,1280]{1,0:T(8,128)(2,1)S(1)}, bf16[128,1280]{1,0:T(8,128)(2,1)S(1)}, u32[]{:S(2)}, u32[]{:S(2)}) collective-permute-start(bf16[128,1280]{1,0:T(8,128)(2,1)S(1)} %collective-permute-done.3.refs_4_.refs_6_), channel_id=1, source_target_pairs={{0,8},{8,12},{12,4},{4,0},{1,9},{9,13},{13,5},{5,1},{2,10},{10,14}... | collective-permute-start | bytes 983048 | tf_op jit(solution)/shard_map/ppermute | solution.py:24
  23.8 24.7 %copy-start.10 = (bf16[128,1280]{1,0:T(8,128)(2,1)}, bf16[128,1280]{1,0:T(8,128)(2,1)S(1)}, u32[]{:S(2)}) copy-start(bf16[128,1280]{1,0:T(8,128)(2,1)S(1)} %collective-permute-done.refs_1_.refs_3_) | copy-start | bytes 983044
  23.8 24.7 %collective-permute-start.1 = (bf16[128,1280]{1,0:T(8,128)(2,1)S(1)}, bf16[128,1280]{1,0:T(8,128)(2,1)S(1)}, u32[]{:S(2)}, u32[]{:S(2)}) collective-permute-start(bf16[128,1280]{1,0:T(8,128)(2,1)S(1)} %collective-permute-done.refs_1_.refs_3_), channel_id=1, source_target_pairs={{0,8},{8,12},{12,4},{4,0},{1,9},{9,13},{13,5},{5,1},{2,10},{10,14}... | collective-permute-start | bytes 983048 | tf_op jit(solution)/shard_map/ppermute | solution.py:24
  27.3 17.1 %collective-permute-start.9 = (bf16[128,640]{1,0:T(8,128)(2,1)S(1)}, bf16[128,640]{1,0:T(8,128)(2,1)S(1)}, u32[]{:S(2)}, u32[]{:S(2)}) collective-permute-start(bf16[128,640]{1,0:T(8,128)(2,1)S(1)} %get-tuple-element.35.query.refs_10_), channel_id=1, source_target_pairs={{0,8},{8,12},{12,4},{4,0},{1,9},{9,13},{13,5},{5,1},{2,10},{10,14}... | collective-permute-start | bytes 491528 | tf_op jit(solution)/shard_map/ppermute | solution.py:24
  30.7 0.7 copy-start.3
  44.4 8.0 %collective-permute-start.16 = (bf16[128,640]{1,0:T(8,128)(2,1)S(1)}, bf16[128,640]{1,0:T(8,128)(2,1)S(1)}, u32[]{:S(2)}, u32[]{:S(2)}) collective-permute-start(bf16[128,640]{1,0:T(8,128)(2,1)S(1)} %collective-permute-done.15.query), channel_id=1, source_target_pairs={{0,8},{8,12},{12,4},{4,0},{1,9},{9,13},{13,5},{5,1},{2,10},{10,14}... | collective-permute-start | bytes 491528 | tf_op jit(solution)/shard_map/ppermute | solution.py:24
  47.8 24.2 %copy-start.11 = (bf16[128,1280]{1,0:T(8,128)(2,1)}, bf16[128,1280]{1,0:T(8,128)(2,1)S(1)}, u32[]{:S(2)}) copy-start(bf16[128,1280]{1,0:T(8,128)(2,1)S(1)} %collective-permute-done.4.refs_5_.refs_7_) | copy-start | bytes 983044
  47.8 27.1 %collective-permute-start.5 = (bf16[128,1280]{1,0:T(8,128)(2,1)S(1)}, bf16[128,1280]{1,0:T(8,128)(2,1)S(1)}, u32[]{:S(2)}, u32[]{:S(2)}) collective-permute-start(bf16[128,1280]{1,0:T(8,128)(2,1)S(1)} %collective-permute-done.4.refs_5_.refs_7_), channel_id=1, source_target_pairs={{0,8},{8,12},{12,4},{4,0},{1,9},{9,13},{13,5},{5,1},{2,10},{10,14}... | collective-permute-start | bytes 983048 | tf_op jit(solution)/shard_map/ppermute | solution.py:24
  48.6 23.5 %copy-start.12 = (bf16[128,1280]{1,0:T(8,128)(2,1)}, bf16[128,1280]{1,0:T(8,128)(2,1)S(1)}, u32[]{:S(2)}) copy-start(bf16[128,1280]{1,0:T(8,128)(2,1)S(1)} %collective-permute-done.1.refs_2_.refs_4_) | copy-start | bytes 983044
  48.6 26.4 %collective-permute-start.2 = (bf16[128,1280]{1,0:T(8,128)(2,1)S(1)}, bf16[128,1280]{1,0:T(8,128)(2,1)S(1)}, u32[]{:S(2)}, u32[]{:S(2)}) collective-permute-start(bf16[128,1280]{1,0:T(8,128)(2,1)S(1)} %collective-permute-done.1.refs_2_.refs_4_), channel_id=1, source_target_pairs={{0,8},{8,12},{12,4},{4,0},{1,9},{9,13},{13,5},{5,1},{2,10},{10,14}... | collective-permute-start | bytes 983048 | tf_op jit(solution)/shard_map/ppermute | solution.py:24
  52.4 16.2 %collective-permute-start.10 = (bf16[128,640]{1,0:T(8,128)(2,1)S(1)}, bf16[128,640]{1,0:T(8,128)(2,1)S(1)}, u32[]{:S(2)}, u32[]{:S(2)}) collective-permute-start(bf16[128,640]{1,0:T(8,128)(2,1)S(1)} %collective-permute-done.9.query), channel_id=1, source_target_pairs={{0,8},{8,12},{12,4},{4,0},{1,9},{9,13},{13,5},{5,1},{2,10},{10,14}... | collective-permute-start | bytes 491528 | tf_op jit(solution)/shard_map/ppermute | solution.py:24
  68.6 19.6 %collective-permute-start.17 = (bf16[128,640]{1,0:T(8,128)(2,1)S(1)}, bf16[128,640]{1,0:T(8,128)(2,1)S(1)}, u32[]{:S(2)}, u32[]{:S(2)}) collective-permute-start(bf16[128,640]{1,0:T(8,128)(2,1)S(1)} %collective-permute-done.16.query), channel_id=1, source_target_pairs={{0,8},{8,12},{12,4},{4,0},{1,9},{9,13},{13,5},{5,1},{2,10},{10,14}... | collective-permute-start | bytes 491528 | tf_op jit(solution)/shard_map/ppermute | solution.py:24
  72.0 16.8 %collective-permute-start.11 = (bf16[128,640]{1,0:T(8,128)(2,1)S(1)}, bf16[128,640]{1,0:T(8,128)(2,1)S(1)}, u32[]{:S(2)}, u32[]{:S(2)}) collective-permute-start(bf16[128,640]{1,0:T(8,128)(2,1)S(1)} %collective-permute-done.10.query), channel_id=1, source_target_pairs={{0,8},{8,12},{12,4},{4,0},{1,9},{9,13},{13,5},{5,1},{2,10},{10,14}... | collective-permute-start | bytes 491528 | tf_op jit(solution)/shard_map/ppermute | solution.py:24
  74.9 8.1 %copy-start.1 = (bf16[128,1280]{1,0:T(8,128)(2,1)}, bf16[128,1280]{1,0:T(8,128)(2,1)S(1)}, u32[]{:S(2)}) copy-start(bf16[128,1280]{1,0:T(8,128)(2,1)S(1)} %collective-permute-done.5.cotangent.refs_8_) | copy-start | bytes 983044
  74.9 8.1 %copy-start.2 = (bf16[128,1280]{1,0:T(8,128)(2,1)}, bf16[128,1280]{1,0:T(8,128)(2,1)S(1)}, u32[]{:S(2)}) copy-start(bf16[128,1280]{1,0:T(8,128)(2,1)S(1)} %collective-permute-done.2.key.refs_5_) | copy-start | bytes 983044
  77.2 12.2 %collective-permute-start.18 = (bf16[128,640]{1,0:T(8,128)(2,1)S(1)}, bf16[128,640]{1,0:T(8,128)(2,1)S(1)}, u32[]{:S(2)}, u32[]{:S(2)}) collective-permute-start(bf16[128,640]{1,0:T(8,128)(2,1)S(1)} %apply_step.15), channel_id=1, source_target_pairs={{0,8},{8,12},{12,4},{4,0},{1,9},{9,13},{13,5},{5,1},{2,10},{10,14}... | collective-permute-start | bytes 491528 | tf_op jit(solution)/shard_map/ppermute | solution.py:24
  79.2 35.4 %collective-permute-start.21 = (f32[1,3,80,640]{3,2,1,0:T(8,128)}, f32[1,3,80,640]{3,2,1,0:T(8,128)}, u32[]{:S(2)}, u32[]{:S(2)}) collective-permute-start(f32[1,3,80,640]{3,2,1,0:T(8,128)} %get-tuple-element.32), channel_id=1, source_target_pairs={{0,1},{1,0},{2,3},{3,2},{4,5},{5,4},{6,7},{7,6},{8,9},{9,8},{10,11... | collective-permute-start | bytes 1843208 | tf_op jit(solution)/shard_map/ppermute | solution.py:24
  86.1 28.5 %collective-permute-start.22 = (f32[1,3,80,640]{3,2,1,0:T(8,128)}, f32[1,3,80,640]{3,2,1,0:T(8,128)S(1)}, u32[]{:S(2)}, u32[]{:S(2)}) collective-permute-start(f32[1,3,80,640]{3,2,1,0:T(8,128)} %get-tuple-element.33), channel_id=1, source_target_pairs={{0,1},{1,0},{2,3},{3,2},{4,5},{5,4},{6,7},{7,6},{8,9},{9,8},{10,11... | collective-permute-start | bytes 1843208 | tf_op jit(solution)/shard_map/ppermute | solution.py:24
  88.2 15.7 %copy-start.16 = (f32[4,128]{1,0:T(4,128)S(1)}, f32[4,128]{1,0:T(4,128)}, u32[]{:S(2)}) copy-start(f32[4,128]{1,0:T(4,128)} %rates.1) | copy-start | bytes 6148
  88.2 21.1 %copy-start.4 = (bf16[128,640]{1,0:T(8,128)(2,1)S(1)}, bf16[128,640]{1,0:T(8,128)(2,1)}, u32[]{:S(2)}) copy-start(bf16[128,640]{1,0:T(8,128)(2,1)} %copy-done.3) | copy-start | bytes 491524
  88.2 21.1 %copy-start.6 = (bf16[128,640]{1,0:T(8,128)(2,1)S(1)}, bf16[128,640]{1,0:T(8,128)(2,1)}, u32[]{:S(2)}) copy-start(bf16[128,640]{1,0:T(8,128)(2,1)} %copy-done.5) | copy-start | bytes 491524
  88.2 7.1 %collective-permute-start.12 = (bf16[128,640]{1,0:T(8,128)(2,1)S(1)}, bf16[128,640]{1,0:T(8,128)(2,1)S(1)}, u32[]{:S(2)}, u32[]{:S(2)}) collective-permute-start(bf16[128,640]{1,0:T(8,128)(2,1)S(1)} %apply_step.11), channel_id=1, source_target_pairs={{0,8},{8,12},{12,4},{4,0},{1,9},{9,13},{13,5},{5,1},{2,10},{10,14}... | collective-permute-start | bytes 491528 | tf_op jit(solution)/shard_map/ppermute | solution.py:24
  89.4 9.4 %collective-permute-start.19 = (bf16[128,640]{1,0:T(8,128)(2,1)S(1)}, bf16[128,640]{1,0:T(8,128)(2,1)S(1)}, u32[]{:S(2)}, u32[]{:S(2)}) collective-permute-start(bf16[128,640]{1,0:T(8,128)(2,1)S(1)} %add_convert_fusion.1), channel_id=1, source_target_pairs={{0,8},{8,12},{12,4},{4,0},{1,9},{9,13},{13,5},{5,1},{2,10},{10,14}... | collective-permute-start | bytes 491528 | tf_op jit(solution)/shard_map/ppermute | solution.py:24
  95.4 7.1 %collective-permute-start.13 = (bf16[128,640]{1,0:T(8,128)(2,1)S(1)}, bf16[128,640]{1,0:T(8,128)(2,1)S(1)}, u32[]{:S(2)}, u32[]{:S(2)}) collective-permute-start(bf16[128,640]{1,0:T(8,128)(2,1)S(1)} %add_convert_fusion.3), channel_id=1, source_target_pairs={{0,8},{8,12},{12,4},{4,0},{1,9},{9,13},{13,5},{5,1},{2,10},{10,14}... | collective-permute-start | bytes 491528 | tf_op jit(solution)/shard_map/ppermute | solution.py:24
  98.9 14.3 %collective-permute-start.20 = (bf16[128,640]{1,0:T(8,128)(2,1)S(1)}, bf16[128,640]{1,0:T(8,128)(2,1)S(1)}, u32[]{:S(2)}, u32[]{:S(2)}) collective-permute-start(bf16[128,640]{1,0:T(8,128)(2,1)S(1)} %add_convert_fusion), channel_id=1, source_target_pairs={{0,8},{8,12},{12,4},{4,0},{1,9},{9,13},{13,5},{5,1},{2,10},{10,14}... | collective-permute-start | bytes 491528 | tf_op jit(solution)/shard_map/ppermute | solution.py:24
  102.6 11.3 %collective-permute-start.14 = (bf16[128,640]{1,0:T(8,128)(2,1)S(1)}, bf16[128,640]{1,0:T(8,128)(2,1)S(1)}, u32[]{:S(2)}, u32[]{:S(2)}) collective-permute-start(bf16[128,640]{1,0:T(8,128)(2,1)S(1)} %add_convert_fusion.2), channel_id=1, source_target_pairs={{0,8},{8,12},{12,4},{4,0},{1,9},{9,13},{13,5},{5,1},{2,10},{10,14}... | collective-permute-start | bytes 491528 | tf_op jit(solution)/shard_map/ppermute | solution.py:24
  103.9 5.4 %collective-permute-start.8 = (f32[2,1,128]{2,1,0:T(1,128)S(1)}, f32[2,1,128]{2,1,0:T(1,128)S(1)}, u32[]{:S(2)}, u32[]{:S(2)}) collective-permute-start(f32[2,1,128]{2,1,0:T(1,128)S(1)} %bitcast.3), channel_id=1, source_target_pairs={{0,4},{4,8},{8,12},{12,0},{1,5},{5,9},{9,13},{13,1},{2,6},{6,10},{... | collective-permute-start | bytes 3080 | tf_op jit(solution)/shard_map/ppermute | solution.py:24
  112.1 2.5 %copy-start.13 = (f32[1,3,80,640]{3,2,1,0:T(8,128)S(1)}, f32[1,3,80,640]{3,2,1,0:T(8,128)}, u32[]{:S(2)}) copy-start(f32[1,3,80,640]{3,2,1,0:T(8,128)} %get-tuple-element.30) | copy-start | bytes 1843204
  112.1 2.5 %copy-start.14 = (f32[1,3,80,640]{3,2,1,0:T(8,128)S(1)}, f32[1,3,80,640]{3,2,1,0:T(8,128)}, u32[]{:S(2)}) copy-start(f32[1,3,80,640]{3,2,1,0:T(8,128)} %get-tuple-element.31) | copy-start | bytes 1843204

commit v7 on v6

--- a/solution.py
+++ b/solution.py
@@ -283,7 +283,8 @@
     )(rep, *map(in_hbm, (*keys, *cots, weights, momentum)), low_par, base_par)
 
 
-def last_body(key, cotangent, so_far, low, new_own, new_par, new_low, unit):
+def last_body(rep, key, cotangent, so_far, low, *refs):
+    new_own, new_par, new_low, unit = refs[-4:]
     hid = so_far.shape[0] // 6
     unit[...] = unit_rows(key[...])
     for m, grad in enumerate(gradient_products(unit, cotangent, low, hid)):
@@ -295,28 +296,82 @@
         new_low[pl.ds((2 * m + 1) * hid, hid), :] = fresh_par.astype(jnp.bfloat16)
 
 
-def last_step(head, key, cotangent, so_far, low):
+def last_step(head, heads, rep, key, cotangent, so_far, low, before):
     rows = key.shape[0]
     total, width = low.shape
     hid = total // 6
-    token_spec = pl.BlockSpec((rows, width), lambda i: (0, head))
-    made_spec = pl.BlockSpec((total, width), lambda i: (0, 0))
+    token_spec = pl.BlockSpec((rows, width), lambda i, rep: (0, head))
+    made_spec = pl.BlockSpec((total, width), lambda i, rep: (0, 0))
     block = (1, 3, hid, width)
-    new_spec = pl.BlockSpec(block, lambda i: (0, 0, 0, 0))
-    fresh = pltpu.HBM(block, jnp.float32)
+    own_spec = pl.BlockSpec(block, lambda i, rep: (rep[0] * heads + head, 0, 0, 0))
+    par_spec = pl.BlockSpec(block, lambda i, rep: (0, 0, 0, 0))
+    more = () if before is None else (before,)
     return pl.pallas_call(
         last_body,
-        out_shape=(fresh, fresh, jax.ShapeDtypeStruct((total, width), jnp.bfloat16)),
-        grid=(1,),
-        in_specs=[token_spec, token_spec, made_spec, made_spec],
-        out_specs=(new_spec, new_spec, made_spec),
-        scratch_shapes=[pltpu.VMEM((rows, width), jnp.bfloat16)],
+        out_shape=(
+            pltpu.HBM((2 * heads, 3, hid, width), jnp.float32),
+            pltpu.HBM(block, jnp.float32),
+            jax.ShapeDtypeStruct((total, width), jnp.bfloat16),
+        ),
+        grid_spec=pltpu.PrefetchScalarGridSpec(
+            num_scalar_prefetch=1,
+            grid=(1,),
+            in_specs=[token_spec, token_spec, made_spec, made_spec]
+            + [pl.BlockSpec(memory_space=pl.ANY)] * len(more),
+            out_specs=(own_spec, par_spec, made_spec),
+            scratch_shapes=[pltpu.VMEM((rows, width), jnp.bfloat16)],
+        ),
+        input_output_aliases={5: 0} if more else {},
         compiler_params=pltpu.CompilerParams(vmem_limit_bytes=16 << 20),
         cost_estimate=pl.CostEstimate(
             flops=4 * rows * total * width, bytes_accessed=12 * total * width, transcendentals=0
         ),
         name="last_step",
-    )(key, cotangent, in_hbm(so_far) if head else so_far, low)
+    )(rep, key, cotangent, in_hbm(so_far) if head else so_far, low, *more)
+
+
+def place_body(rep, block, before, out):
+    out[...] = block[...]
+
+
+def place_step(head, heads, rep, block, before):
+    given = pl.BlockSpec(block.shape, lambda i, rep: (0, 0, 0, 0))
+    taken = pl.BlockSpec(block.shape, lambda i, rep: ((1 - rep[0]) * heads + head, 0, 0, 0))
+    return pl.pallas_call(
+        place_body,
+        out_shape=pltpu.HBM(before.shape, before.dtype),
+        grid_spec=pltpu.PrefetchScalarGridSpec(
+            num_scalar_prefetch=1,
+            grid=(1,),
+            in_specs=[given, pl.BlockSpec(memory_space=pl.ANY)],
+            out_specs=taken,
+        ),
+        input_output_aliases={2: 0},
+        compiler_params=pltpu.CompilerParams(vmem_limit_bytes=6 << 20),
+        cost_estimate=pl.CostEstimate(
+            flops=0, bytes_accessed=8 * block.size, transcendentals=0
+        ),
+        name="place_step",
+    )(rep, block, before)
+
+
+def join_body(made, moved, out):
+    out[...] = (made[...] + moved[...].astype(jnp.float32)).astype(jnp.bfloat16)
+
+
+def join_step(made, moved):
+    in_vmem = pl.BlockSpec(memory_space=pltpu.VMEM)
+    return pl.pallas_call(
+        join_body,
+        out_shape=jax.ShapeDtypeStruct(made.shape, jnp.bfloat16),
+        in_specs=[in_vmem, in_vmem],
+        out_specs=in_vmem,
+        compiler_params=pltpu.CompilerParams(vmem_limit_bytes=2 << 20),
+        cost_estimate=pl.CostEstimate(
+            flops=made.size, bytes_accessed=8 * made.size, transcendentals=0
+        ),
+        name="join_step",
+    )(made, moved)
 
 
 def apply_body(query, low, out):
@@ -472,10 +527,13 @@
                 h, rep, keys[:-1], cots[:-1], fast_weights, momentum, low_par, base_par
             )
         )
-    fresh = []
+    fast_updated, sent_back, lows = None, [], []
     for h in heads:
-        fresh.append(last_step(h, keys[-1], cots[-1], *early[h]))
-    lows = [new[2] for new in fresh]
+        fast_updated, for_other, low = last_step(
+            h, per_rep, rep, keys[-1], cots[-1], *early[h], fast_updated
+        )
+        sent_back.append(for_other)
+        lows.append(low)
     moving = []
     for step in range(1, slots):
         made = []
@@ -483,21 +541,15 @@
             kind = jnp.bfloat16 if step == 1 else jnp.float32
             made.append(apply_step(asked[step][h], lows[h], kind))
         if step > 1:
-            made = [
-                (made[h] + moving[h].astype(jnp.float32)).astype(jnp.bfloat16) for h in heads
-            ]
+            made = [join_step(made[h], moving[h]) for h in heads]
         moving = [hop(made[h]) for h in heads]
     layer_output = None
     for h in heads:
         kept = apply_step(asked[0][h], lows[h], jnp.float32)
         layer_output = output_step(h, per_rep, kept, attended[h], moving[h], layer_output)
-    returned = [hop(fresh[h][1], "rep") for h in heads]
-    owned = [new[0] for new in fresh]
-    fast_updated = jnp.where(
-        rep_index == 0,
-        jnp.concatenate([*owned, *returned], axis=0),
-        jnp.concatenate([*returned, *owned], axis=0),
-    )
+    for h in heads:
+        returned = hop(sent_back[h], "rep")
+        fast_updated = place_step(h, per_rep, rep, returned, fast_updated)
     return (layer_output, fast_updated)
 
 

time: 118 us -> 116 us (0.983)
  waiting for transfers between devices: 49.5 us -> 40.9 us
  starting transfers between devices: 37.8 us -> 43.3 us
  other arithmetic: 3.07 us -> 0 us
  Pallas kernels: 24.7 us -> 27.6 us
  local copies, waits for them, and re-layouts: 1.44 us -> 3.12 us
    ppermute x23, waiting for transfers between devices: 49.5 us -> 40.9 us  [ring(): return lax.ppermute(value, axis, list(zip(order, (*order[1:], order[0]))))]
    ppermute x23, starting transfers between devices: 37.8 us -> 43.3 us  [ring(): return lax.ppermute(value, axis, list(zip(order, (*order[1:], order[0]))))]
    pallas_call x2 -> x8, Pallas kernels: 4.82 us -> 7.78 us  [the longest x2 4.84 us: last_step(): pl.pallas_call(last_body, out_shape=(pltpu.HBM((2 * heads, 3, hid, width)...]
    select_n x1 -> x0, other arithmetic: 2.91 us -> none  [tokens_travel(): jnp.where(rep_index == 0, jnp.concatenate([*owned, *returned], axis=0), j...]
  transfers between devices with their start and end apart: 23 -> 23, of which waited for: 10 -> 12; matrix products, arithmetic and copies ran while one was open for 0% -> 1% of each run, Pallas kernels for 19% -> 21%
where the time goes in v7:
time: 116 us
  starting transfers between devices  43.3 us (37%)
  waiting for transfers between devices  40.9 us (35%)
  Pallas kernels  27.6 us (24%)
  local copies, waits for them, and re-layouts  3.12 us (3%)
    ppermute x23, starting transfers between devices, ring(): return lax.ppermute(value, axis, list(zip(order, (*order[1:], order[0]))))  43.3 us
    ppermute x23, waiting for transfers between devices, ring(): return lax.ppermute(value, axis, list(zip(order, (*order[1:], order[0]))))  40.9 us
    pallas_call x2, Pallas kernels, early_step(): pl.pallas_call(functools.partial(early_body, slots), out_shape=((pltpu.HB...  6.71 us
    pallas_call x2, Pallas kernels, last_step(): pl.pallas_call(last_body, out_shape=(pltpu.HBM((2 * heads, 3, hid, width)...  4.84 us
    pallas_call x8, Pallas kernels, apply_step(): pl.pallas_call(apply_body, out_shape=jax.ShapeDtypeStruct((rows, width),...  4.04 us
    pallas_call x1, Pallas kernels, attend_step(): pl.pallas_call(functools.partial(attend_body, token_scale), out_shape=mad...  2.81 us
    pallas_call x2, Pallas kernels, place_step(): pl.pallas_call(place_body, out_shape=pltpu.HBM(before.shape, before.dtype...  2.8 us
    pallas_call x1, Pallas kernels, other_step(): pl.pallas_call(other_body, out_shape=(pltpu.HBM(made, jnp.bfloat16), pltp...  2.69 us
  transfers between devices with their start and end apart: 23, of which 12 were waited for; matrix products, arithmetic and copies ran while one was open for 1% of the time, Pallas kernels for 21%

profile of v7, /device:TPU:0, one launch (start us, length us, event | category | flops | bytes accessed | tf_op | source)
XLA Modules:
  0.0 115.7 jit_solution(11598282090326532448)
XLA Ops:
  0.6 2.7 %other_step.1 = (bf16[2,3,80,640]{3,2,1,0:T(8,128)(2,1)}, f32[2,3,80,640]{3,2,1,0:T(8,128)}) custom-call(s32[1]{0:T(128)} %bitcast.rep, f32[4,3,80,640]{3,2,1,0:T(8,128)} %refs_6_.3, f32[4,3,80,640]{3,2,1,0:T(8,128)} %refs_7_.3), custom_call_target="tpu_custom_call" | custom-call | flops 614400 | bytes 4300800 | tf_op jit(solution)/shard_map/other_step/pallas_call | solution.py:203
  3.3 0.5 collective-permute-start.7
  3.8 1.0 columns_step.1.refs_0_
  4.8 0.0 copy-start
  4.8 3.6 %collective-permute-start = (bf16[128,1280]{1,0:T(8,128)(2,1)S(1)}, bf16[128,1280]{1,0:T(8,128)(2,1)S(1)}, u32[]{:S(2)}, u32[]{:S(2)}) collective-permute-start(bf16[128,1280]{1,0:T(8,128)(2,1)S(1)} %columns_step.1.refs_0_), channel_id=1, source_target_pairs={{0,8},{8,12},{12,4},{4,0},{1,9},{9,13},{13,5},{5,1},{2,10},{10,14}... | collective-permute-start | bytes 983048 | tf_op jit(solution)/shard_map/ppermute | solution.py:24
  8.4 1.2 %cotangent_step.1 = (bf16[128,1280]{1,0:T(8,128)(2,1)S(1)}, bf16[128,1280]{1,0:T(8,128)(2,1)S(1)}) custom-call(s32[1]{0:T(128)} %bitcast.rep, bf16[128,2560]{1,0:T(8,128)(2,1)} %values.1, f32[4,128]{1,0:T(4,128)} %rates.1), custom_call_target="tpu_custom_call" | custom-call | flops 327680 | bytes 983040 | tf_op jit(solution)/shard_map/cotangent_step/pallas_call | solution.py:171
  9.6 0.7 copy-done.8
  10.3 1.6 %collective-permute-start.3 = (bf16[128,1280]{1,0:T(8,128)(2,1)S(1)}, bf16[128,1280]{1,0:T(8,128)(2,1)S(1)}, u32[]{:S(2)}, u32[]{:S(2)}) collective-permute-start(bf16[128,1280]{1,0:T(8,128)(2,1)S(1)} %get-tuple-element.18.refs_3_), channel_id=1, source_target_pairs={{0,8},{8,12},{12,4},{4,0},{1,9},{9,13},{13,5},{5,1},{2,10},{10,14}... | collective-permute-start | bytes 983048 | tf_op jit(solution)/shard_map/ppermute | solution.py:24
  11.9 0.0 collective-permute-start.6
  11.9 4.6 %collective-permute-done.refs_1_.refs_3_ = bf16[128,1280]{1,0:T(8,128)(2,1)S(1)} collective-permute-done((bf16[128,1280]{1,0:T(8,128)(2,1)S(1)}, bf16[128,1280]{1,0:T(8,128)(2,1)S(1)}, u32[]{:S(2)}, u32[]{:S(2)}) %collective-permute-start) | collective-permute-done | bytes 327712 | tf_op jit(solution)/shard_map/ppermute | solution.py:24
  16.6 3.4 %collective-permute-start.1 = (bf16[128,1280]{1,0:T(8,128)(2,1)S(1)}, bf16[128,1280]{1,0:T(8,128)(2,1)}, u32[]{:S(2)}, u32[]{:S(2)}) collective-permute-start(bf16[128,1280]{1,0:T(8,128)(2,1)S(1)} %collective-permute-done.refs_1_.refs_3_), channel_id=1, source_target_pairs={{0,8},{8,12},{12,4},{4,0},{1,9},{9,13},{13,5},{5,1},{2,10},{10,14}... | collective-permute-start | bytes 983048 | tf_op jit(solution)/shard_map/ppermute | solution.py:24
  19.9 3.6 %collective-permute-done.3.refs_4_.refs_6_ = bf16[128,1280]{1,0:T(8,128)(2,1)S(1)} collective-permute-done((bf16[128,1280]{1,0:T(8,128)(2,1)S(1)}, bf16[128,1280]{1,0:T(8,128)(2,1)S(1)}, u32[]{:S(2)}, u32[]{:S(2)}) %collective-permute-start.3) | collective-permute-done | bytes 327712 | tf_op jit(solution)/shard_map/ppermute | solution.py:24
  23.6 3.4 %collective-permute-start.4 = (bf16[128,1280]{1,0:T(8,128)(2,1)S(1)}, bf16[128,1280]{1,0:T(8,128)(2,1)}, u32[]{:S(2)}, u32[]{:S(2)}) collective-permute-start(bf16[128,1280]{1,0:T(8,128)(2,1)S(1)} %collective-permute-done.3.refs_4_.refs_6_), channel_id=1, source_target_pairs={{0,8},{8,12},{12,4},{4,0},{1,9},{9,13},{13,5},{5,1},{2,10},{10,14}... | collective-permute-start | bytes 983048 | tf_op jit(solution)/shard_map/ppermute | solution.py:24
  27.0 1.0 constant_dynamic-slice_fusion
  28.0 0.7 collective-permute-start.15
  28.7 0.7 copy-done.3
  29.4 1.2 %collective-permute-done.1.refs_2_.refs_4_ = bf16[128,1280]{1,0:T(8,128)(2,1)} collective-permute-done((bf16[128,1280]{1,0:T(8,128)(2,1)S(1)}, bf16[128,1280]{1,0:T(8,128)(2,1)}, u32[]{:S(2)}, u32[]{:S(2)}) %collective-permute-start.1) | collective-permute-done | bytes 327712 | tf_op jit(solution)/shard_map/ppermute | solution.py:24
  30.6 3.5 %collective-permute-start.2 = (bf16[128,1280]{1,0:T(8,128)(2,1)}, bf16[128,1280]{1,0:T(8,128)(2,1)S(1)}, u32[]{:S(2)}, u32[]{:S(2)}) collective-permute-start(bf16[128,1280]{1,0:T(8,128)(2,1)} %collective-permute-done.1.refs_2_.refs_4_), channel_id=1, source_target_pairs={{0,8},{8,12},{12,4},{4,0},{1,9},{9,13},{13,5},{5,1},{2,10},{10,14}... | collective-permute-start | bytes 983048 | tf_op jit(solution)/shard_map/ppermute | solution.py:24
  34.1 3.5 %collective-permute-done.4.refs_5_.refs_7_ = bf16[128,1280]{1,0:T(8,128)(2,1)} collective-permute-done((bf16[128,1280]{1,0:T(8,128)(2,1)S(1)}, bf16[128,1280]{1,0:T(8,128)(2,1)}, u32[]{:S(2)}, u32[]{:S(2)}) %collective-permute-start.4) | collective-permute-done | bytes 327712 | tf_op jit(solution)/shard_map/ppermute | solution.py:24
  37.6 3.5 %collective-permute-start.5 = (bf16[128,1280]{1,0:T(8,128)(2,1)}, bf16[128,1280]{1,0:T(8,128)(2,1)S(1)}, u32[]{:S(2)}, u32[]{:S(2)}) collective-permute-start(bf16[128,1280]{1,0:T(8,128)(2,1)} %collective-permute-done.4.refs_5_.refs_7_), channel_id=1, source_target_pairs={{0,8},{8,12},{12,4},{4,0},{1,9},{9,13},{13,5},{5,1},{2,10},{10,14}... | collective-permute-start | bytes 983048 | tf_op jit(solution)/shard_map/ppermute | solution.py:24
  41.1 0.0 collective-permute-done.15.query
  41.1 3.4 %collective-permute-start.9 = (bf16[128,640]{1,0:T(8,128)(2,1)S(1)}, bf16[128,640]{1,0:T(8,128)(2,1)S(1)}, u32[]{:S(2)}, u32[]{:S(2)}) collective-permute-start(bf16[128,640]{1,0:T(8,128)(2,1)S(1)} %get-tuple-element.35.query.refs_10_), channel_id=1, source_target_pairs={{0,8},{8,12},{12,4},{4,0},{1,9},{9,13},{13,5},{5,1},{2,10},{10,14}... | collective-permute-start | bytes 491528 | tf_op jit(solution)/shard_map/ppermute | solution.py:24
  44.5 0.7 copy-done.5
  45.2 13.0 %collective-permute-done.9.query = bf16[128,640]{1,0:T(8,128)(2,1)S(1)} collective-permute-done((bf16[128,640]{1,0:T(8,128)(2,1)S(1)}, bf16[128,640]{1,0:T(8,128)(2,1)S(1)}, u32[]{:S(2)}, u32[]{:S(2)}) %collective-permute-start.9) | collective-permute-done | bytes 163872 | tf_op jit(solution)/shard_map/ppermute | solution.py:24
  58.2 3.4 %collective-permute-start.16 = (bf16[128,640]{1,0:T(8,128)(2,1)S(1)}, bf16[128,640]{1,0:T(8,128)(2,1)S(1)}, u32[]{:S(2)}, u32[]{:S(2)}) collective-permute-start(bf16[128,640]{1,0:T(8,128)(2,1)S(1)} %collective-permute-done.15.query), channel_id=1, source_target_pairs={{0,8},{8,12},{12,4},{4,0},{1,9},{9,13},{13,5},{5,1},{2,10},{10,14}... | collective-permute-start | bytes 491528 | tf_op jit(solution)/shard_map/ppermute | solution.py:24
  61.6 0.0 collective-permute-done.6.refs_8_
  61.6 0.7 collective-permute-start.10
  62.3 0.0 collective-permute-done.7.refs_9_
  62.3 2.8 %early_step.3 = (f32[480,640]{1,0:T(8,128)S(1)}, bf16[480,640]{1,0:T(8,128)(2,1)S(1)}) custom-call(s32[1]{0:T(128)} %bitcast.rep, bf16[128,1280]{1,0:T(8,128)(2,1)} %copy-done, bf16[128,1280]{1,0:T(8,128)(2,1)} %copy-done.9, bf16[128,1280]{1,0:T(8,128)(2,1)} %collective-permute-done.1.refs_2_.refs_4_, bf16[128,1280]{1,0:T(8,128)(2,1)} %copy-done.7, ...), custom_call_target="tpu_custom_call" | custom-call | flops 471859200 | bytes 3072000 | tf_op jit(solution)/shard_map/early_step/pallas_call | solution.py:260
  65.1 0.0 collective-permute-done.5.cotangent.refs_8_
  65.2 1.8 %last_step.2 = (f32[4,3,80,640]{3,2,1,0:T(8,128)}, f32[1,3,80,640]{3,2,1,0:T(8,128)}, bf16[480,640]{1,0:T(8,128)(2,1)S(1)}) custom-call(s32[1]{0:T(128)} %bitcast.rep, bf16[128,1280]{1,0:T(8,128)(2,1)S(1)} %collective-permute-done.2.key.refs_5_, bf16[128,1280]{1,0:T(8,128)(2,1)S(1)} %collective-permute-done.5.cotangent.refs_8_, ...), custom_call_target="tpu_custom_call" | custom-call | flops 157286400 | bytes 3686400 | tf_op jit(solution)/shard_map/last_step/pallas_call | solution.py:309
  67.0 3.9 %early_step.2 = (f32[480,640]{1,0:T(8,128)}, bf16[480,640]{1,0:T(8,128)(2,1)S(1)}) custom-call(s32[1]{0:T(128)} %bitcast.rep, bf16[128,1280]{1,0:T(8,128)(2,1)} %copy-done, bf16[128,1280]{1,0:T(8,128)(2,1)} %copy-done.9, bf16[128,1280]{1,0:T(8,128)(2,1)} %collective-permute-done.1.refs_2_.refs_4_, bf16[128,1280]{1,0:T(8,128)(2,1)} %copy-done.7, ...), custom_call_target="tpu_custom_call" | custom-call | flops 471859200 | bytes 3072000 | tf_op jit(solution)/shard_map/early_step/pallas_call | solution.py:260
  70.9 3.0 %last_step.3 = (f32[4,3,80,640]{3,2,1,0:T(8,128)}, f32[1,3,80,640]{3,2,1,0:T(8,128)}, bf16[480,640]{1,0:T(8,128)(2,1)S(1)}) custom-call(s32[1]{0:T(128)} %bitcast.rep, bf16[128,1280]{1,0:T(8,128)(2,1)S(1)} %collective-permute-done.2.key.refs_5_, bf16[128,1280]{1,0:T(8,128)(2,1)S(1)} %collective-permute-done.5.cotangent.refs_8_, ...), custom_call_target="tpu_custom_call", output_to_operand_aliasing={{0}: (5, {})} | custom-call | flops 157286400 | bytes 3686400 | tf_op jit(solution)/shard_map/last_step/pallas_call | solution.py:309
  73.9 0.5 collective-permute-start.21
  74.4 0.5 apply_step.15
  74.9 1.3 %collective-permute-start.18 = (bf16[128,640]{1,0:T(8,128)(2,1)S(1)}, bf16[128,640]{1,0:T(8,128)(2,1)S(1)}, u32[]{:S(2)}, u32[]{:S(2)}) collective-permute-start(bf16[128,640]{1,0:T(8,128)(2,1)S(1)} %apply_step.15), channel_id=1, source_target_pairs={{0,8},{8,12},{12,4},{4,0},{1,9},{9,13},{13,5},{5,1},{2,10},{10,14}... | collective-permute-start | bytes 491528 | tf_op jit(solution)/shard_map/ppermute | solution.py:24
  76.2 0.5 apply_step.11
  76.7 0.1 collective-permute-start.12
  76.8 3.0 %collective-permute-start.11 = (bf16[128,640]{1,0:T(8,128)(2,1)S(1)}, bf16[128,640]{1,0:T(8,128)(2,1)S(1)}, u32[]{:S(2)}, u32[]{:S(2)}) collective-permute-start(bf16[128,640]{1,0:T(8,128)(2,1)S(1)} %collective-permute-done.10.query), channel_id=1, source_target_pairs={{0,8},{8,12},{12,4},{4,0},{1,9},{9,13},{13,5},{5,1},{2,10},{10,14}... | collective-permute-start | bytes 491528 | tf_op jit(solution)/shard_map/ppermute | solution.py:24
  79.8 0.5 apply_step.14.made
  80.3 1.7 %collective-permute-done.18.moved = bf16[128,640]{1,0:T(8,128)(2,1)S(1)} collective-permute-done((bf16[128,640]{1,0:T(8,128)(2,1)S(1)}, bf16[128,640]{1,0:T(8,128)(2,1)S(1)}, u32[]{:S(2)}, u32[]{:S(2)}) %collective-permute-start.18) | collective-permute-done | bytes 163872 | tf_op jit(solution)/shard_map/ppermute | solution.py:24
  82.0 2.1 %collective-permute-start.17 = (bf16[128,640]{1,0:T(8,128)(2,1)S(1)}, bf16[128,640]{1,0:T(8,128)(2,1)S(1)}, u32[]{:S(2)}, u32[]{:S(2)}) collective-permute-start(bf16[128,640]{1,0:T(8,128)(2,1)S(1)} %collective-permute-done.16.query), channel_id=1, source_target_pairs={{0,8},{8,12},{12,4},{4,0},{1,9},{9,13},{13,5},{5,1},{2,10},{10,14}... | collective-permute-start | bytes 491528 | tf_op jit(solution)/shard_map/ppermute | solution.py:24
  84.2 0.5 apply_step.10.made
  84.7 0.0 copy-start.11
  84.8 0.8 collective-permute-done.12.moved
  85.6 2.1 %collective-permute-start.19 = (bf16[128,640]{1,0:T(8,128)(2,1)S(1)}, bf16[128,640]{1,0:T(8,128)(2,1)S(1)}, u32[]{:S(2)}, u32[]{:S(2)}) collective-permute-start(bf16[128,640]{1,0:T(8,128)(2,1)S(1)} %join_step.6), channel_id=1, source_target_pairs={{0,8},{8,12},{12,4},{4,0},{1,9},{9,13},{13,5},{5,1},{2,10},{10,14}... | collective-permute-start | bytes 491528 | tf_op jit(solution)/shard_map/ppermute | solution.py:24
  87.7 1.3 %collective-permute-done.11.query = bf16[128,640]{1,0:T(8,128)(2,1)S(1)} collective-permute-done((bf16[128,640]{1,0:T(8,128)(2,1)S(1)}, bf16[128,640]{1,0:T(8,128)(2,1)S(1)}, u32[]{:S(2)}, u32[]{:S(2)}) %collective-permute-start.11) | collective-permute-done | bytes 163872 | tf_op jit(solution)/shard_map/ppermute | solution.py:24
  89.1 2.1 %collective-permute-start.13 = (bf16[128,640]{1,0:T(8,128)(2,1)S(1)}, bf16[128,640]{1,0:T(8,128)(2,1)S(1)}, u32[]{:S(2)}, u32[]{:S(2)}) collective-permute-start(bf16[128,640]{1,0:T(8,128)(2,1)S(1)} %join_step.4), channel_id=1, source_target_pairs={{0,8},{8,12},{12,4},{4,0},{1,9},{9,13},{13,5},{5,1},{2,10},{10,14}... | collective-permute-start | bytes 491528 | tf_op jit(solution)/shard_map/ppermute | solution.py:24
  91.2 0.5 apply_step.9.made
  91.7 0.9 collective-permute-done.17.query
  92.6 0.5 apply_step.13.made
  93.1 3.0 %collective-permute-done.19.moved = bf16[128,640]{1,0:T(8,128)(2,1)S(1)} collective-permute-done((bf16[128,640]{1,0:T(8,128)(2,1)S(1)}, bf16[128,640]{1,0:T(8,128)(2,1)S(1)}, u32[]{:S(2)}, u32[]{:S(2)}) %collective-permute-start.19) | collective-permute-done | bytes 163872 | tf_op jit(solution)/shard_map/ppermute | solution.py:24
  96.1 2.2 %collective-permute-start.20 = (bf16[128,640]{1,0:T(8,128)(2,1)S(1)}, bf16[128,640]{1,0:T(8,128)(2,1)S(1)}, u32[]{:S(2)}, u32[]{:S(2)}) collective-permute-start(bf16[128,640]{1,0:T(8,128)(2,1)S(1)} %join_step.7), channel_id=1, source_target_pairs={{0,8},{8,12},{12,4},{4,0},{1,9},{9,13},{13,5},{5,1},{2,10},{10,14}... | collective-permute-start | bytes 491528 | tf_op jit(solution)/shard_map/ppermute | solution.py:24
  98.3 1.3 %collective-permute-done.13.moved = bf16[128,640]{1,0:T(8,128)(2,1)S(1)} collective-permute-done((bf16[128,640]{1,0:T(8,128)(2,1)S(1)}, bf16[128,640]{1,0:T(8,128)(2,1)S(1)}, u32[]{:S(2)}, u32[]{:S(2)}) %collective-permute-start.13) | collective-permute-done | bytes 163872 | tf_op jit(solution)/shard_map/ppermute | solution.py:24
  99.6 2.0 %collective-permute-start.14 = (bf16[128,640]{1,0:T(8,128)(2,1)S(1)}, bf16[128,640]{1,0:T(8,128)(2,1)S(1)}, u32[]{:S(2)}, u32[]{:S(2)}) collective-permute-start(bf16[128,640]{1,0:T(8,128)(2,1)S(1)} %join_step.5), channel_id=1, source_target_pairs={{0,8},{8,12},{12,4},{4,0},{1,9},{9,13},{13,5},{5,1},{2,10},{10,14}... | collective-permute-start | bytes 491528 | tf_op jit(solution)/shard_map/ppermute | solution.py:24
  101.7 0.2 collective-permute-start.8
  101.8 5.8 %collective-permute-done.8.refs_2_ = f32[2,1,128]{2,1,0:T(1,128)S(1)} collective-permute-done((f32[2,1,128]{2,1,0:T(1,128)S(1)}, f32[2,1,128]{2,1,0:T(1,128)S(1)}, u32[]{:S(2)}, u32[]{:S(2)}) %collective-permute-start.8) | collective-permute-done | bytes 1056 | tf_op jit(solution)/shard_map/ppermute | solution.py:24
  107.6 2.8 %attend_step.1 = (f32[128,640]{1,0:T(8,128)S(1)}, f32[128,640]{1,0:T(8,128)S(1)}) custom-call(s32[1]{0:T(128)} %bitcast.1.block_index, bf16[128,1280]{1,0:T(8,128)(2,1)} %copy-done, bf16[128,1280]{1,0:T(8,128)(2,1)} %copy-done.8, f32[2,1,128]{2,1,0:T(1,128)S(1)} %collective-permute-done.8.refs_2_, bf16[128,1280]{1,0:T(8,128)(2,1)} %copy-done.9, ...), custom_call_target="tpu_custom_call" | custom-call | flops 167772160 | bytes 3276800 | tf_op jit(solution)/shard_map/attend_step/pallas_call | solution.py:471
  110.4 0.5 apply_step.8.kept
  110.9 0.5 apply_step.12.kept
  111.5 0.7 output_step.2.refs_0_
  112.2 0.7 output_step.3
  112.9 1.9 %place_step.2.before = f32[4,3,80,640]{3,2,1,0:T(8,128)} custom-call(s32[1]{0:T(128)} %bitcast.rep, f32[1,3,80,640]{3,2,1,0:T(8,128)} %collective-permute-done.22.block, f32[4,3,80,640]{3,2,1,0:T(8,128)} %get-tuple-element.33.before), custom_call_target="tpu_custom_call", output_to_operand_aliasing={{}: (2, {})} | custom-call | bytes 1228800 | tf_op jit(solution)/shard_map/place_step/pallas_call | solution.py:340
  114.9 0.9 place_step.3
  (32 shorter events, 0.2 us)
Async XLA Ops:
  3.3 59.0 %collective-permute-start.7 = (f32[2,3,80,640]{3,2,1,0:T(8,128)}, f32[2,3,80,640]{3,2,1,0:T(8,128)S(1)}, u32[]{:S(2)}, u32[]{:S(2)}) collective-permute-start(f32[2,3,80,640]{3,2,1,0:T(8,128)} %get-tuple-element.20), channel_id=1, source_target_pairs={{0,1},{1,0},{2,3},{3,2},{4,5},{5,4},{6,7},{7,6},{8,9},{9,8},{10,11... | collective-permute-start | bytes 3686408 | tf_op jit(solution)/shard_map/ppermute | solution.py:24
  4.8 57.5 %copy-start = (bf16[128,1280]{1,0:T(8,128)(2,1)}, bf16[128,1280]{1,0:T(8,128)(2,1)S(1)}, u32[]{:S(2)}) copy-start(bf16[128,1280]{1,0:T(8,128)(2,1)S(1)} %columns_step.1.refs_0_) | copy-start | bytes 983044
  4.8 11.7 %collective-permute-start = (bf16[128,1280]{1,0:T(8,128)(2,1)S(1)}, bf16[128,1280]{1,0:T(8,128)(2,1)S(1)}, u32[]{:S(2)}, u32[]{:S(2)}) collective-permute-start(bf16[128,1280]{1,0:T(8,128)(2,1)S(1)} %columns_step.1.refs_0_), channel_id=1, source_target_pairs={{0,8},{8,12},{12,4},{4,0},{1,9},{9,13},{13,5},{5,1},{2,10},{10,14}... | collective-permute-start | bytes 983048 | tf_op jit(solution)/shard_map/ppermute | solution.py:24
  9.6 0.7 copy-start.8
  10.3 51.9 %copy-start.7 = (bf16[128,1280]{1,0:T(8,128)(2,1)}, bf16[128,1280]{1,0:T(8,128)(2,1)S(1)}, u32[]{:S(2)}) copy-start(bf16[128,1280]{1,0:T(8,128)(2,1)S(1)} %get-tuple-element.18.refs_3_) | copy-start | bytes 983044
  10.3 13.2 %collective-permute-start.3 = (bf16[128,1280]{1,0:T(8,128)(2,1)S(1)}, bf16[128,1280]{1,0:T(8,128)(2,1)S(1)}, u32[]{:S(2)}, u32[]{:S(2)}) collective-permute-start(bf16[128,1280]{1,0:T(8,128)(2,1)S(1)} %get-tuple-element.18.refs_3_), channel_id=1, source_target_pairs={{0,8},{8,12},{12,4},{4,0},{1,9},{9,13},{13,5},{5,1},{2,10},{10,14}... | collective-permute-start | bytes 983048 | tf_op jit(solution)/shard_map/ppermute | solution.py:24
  11.9 49.7 %collective-permute-start.6 = (bf16[2,3,80,640]{3,2,1,0:T(8,128)(2,1)}, bf16[2,3,80,640]{3,2,1,0:T(8,128)(2,1)S(1)}, u32[]{:S(2)}, u32[]{:S(2)}) collective-permute-start(bf16[2,3,80,640]{3,2,1,0:T(8,128)(2,1)} %get-tuple-element.19), channel_id=1, source_target_pairs={{0,1},{1,0},{2,3},{3,2},{4,5},{5,4},{6,7},{7,6},{8,9},{9,8},{10,11... | collective-permute-start | bytes 1843208 | tf_op jit(solution)/shard_map/ppermute | solution.py:24
  16.5 12.2 %copy-start.9 = (bf16[128,1280]{1,0:T(8,128)(2,1)}, bf16[128,1280]{1,0:T(8,128)(2,1)S(1)}, u32[]{:S(2)}) copy-start(bf16[128,1280]{1,0:T(8,128)(2,1)S(1)} %collective-permute-done.refs_1_.refs_3_) | copy-start | bytes 983044
  16.6 14.0 %collective-permute-start.1 = (bf16[128,1280]{1,0:T(8,128)(2,1)S(1)}, bf16[128,1280]{1,0:T(8,128)(2,1)}, u32[]{:S(2)}, u32[]{:S(2)}) collective-permute-start(bf16[128,1280]{1,0:T(8,128)(2,1)S(1)} %collective-permute-done.refs_1_.refs_3_), channel_id=1, source_target_pairs={{0,8},{8,12},{12,4},{4,0},{1,9},{9,13},{13,5},{5,1},{2,10},{10,14}... | collective-permute-start | bytes 983048 | tf_op jit(solution)/shard_map/ppermute | solution.py:24
  23.6 10.5 %copy-start.10 = (bf16[128,1280]{1,0:T(8,128)(2,1)}, bf16[128,1280]{1,0:T(8,128)(2,1)S(1)}, u32[]{:S(2)}) copy-start(bf16[128,1280]{1,0:T(8,128)(2,1)S(1)} %collective-permute-done.3.refs_4_.refs_6_) | copy-start | bytes 983044
  23.6 14.0 %collective-permute-start.4 = (bf16[128,1280]{1,0:T(8,128)(2,1)S(1)}, bf16[128,1280]{1,0:T(8,128)(2,1)}, u32[]{:S(2)}, u32[]{:S(2)}) collective-permute-start(bf16[128,1280]{1,0:T(8,128)(2,1)S(1)} %collective-permute-done.3.refs_4_.refs_6_), channel_id=1, source_target_pairs={{0,8},{8,12},{12,4},{4,0},{1,9},{9,13},{13,5},{5,1},{2,10},{10,14}... | collective-permute-start | bytes 983048 | tf_op jit(solution)/shard_map/ppermute | solution.py:24
  28.0 13.1 %collective-permute-start.15 = (bf16[128,640]{1,0:T(8,128)(2,1)S(1)}, bf16[128,640]{1,0:T(8,128)(2,1)S(1)}, u32[]{:S(2)}, u32[]{:S(2)}) collective-permute-start(bf16[128,640]{1,0:T(8,128)(2,1)S(1)} %get-tuple-element.34.refs_9_.query), channel_id=1, source_target_pairs={{0,8},{8,12},{12,4},{4,0},{1,9},{9,13},{13,5},{5,1},{2,10},{10,14}... | collective-permute-start | bytes 491528 | tf_op jit(solution)/shard_map/ppermute | solution.py:24
  28.7 0.7 copy-start.3
  30.6 34.5 %collective-permute-start.2 = (bf16[128,1280]{1,0:T(8,128)(2,1)}, bf16[128,1280]{1,0:T(8,128)(2,1)S(1)}, u32[]{:S(2)}, u32[]{:S(2)}) collective-permute-start(bf16[128,1280]{1,0:T(8,128)(2,1)} %collective-permute-done.1.refs_2_.refs_4_), channel_id=1, source_target_pairs={{0,8},{8,12},{12,4},{4,0},{1,9},{9,13},{13,5},{5,1},{2,10},{10,14}... | collective-permute-start | bytes 983048 | tf_op jit(solution)/shard_map/ppermute | solution.py:24
  37.6 27.5 %collective-permute-start.5 = (bf16[128,1280]{1,0:T(8,128)(2,1)}, bf16[128,1280]{1,0:T(8,128)(2,1)S(1)}, u32[]{:S(2)}, u32[]{:S(2)}) collective-permute-start(bf16[128,1280]{1,0:T(8,128)(2,1)} %collective-permute-done.4.refs_5_.refs_7_), channel_id=1, source_target_pairs={{0,8},{8,12},{12,4},{4,0},{1,9},{9,13},{13,5},{5,1},{2,10},{10,14}... | collective-permute-start | bytes 983048 | tf_op jit(solution)/shard_map/ppermute | solution.py:24
  41.1 17.1 %collective-permute-start.9 = (bf16[128,640]{1,0:T(8,128)(2,1)S(1)}, bf16[128,640]{1,0:T(8,128)(2,1)S(1)}, u32[]{:S(2)}, u32[]{:S(2)}) collective-permute-start(bf16[128,640]{1,0:T(8,128)(2,1)S(1)} %get-tuple-element.35.query.refs_10_), channel_id=1, source_target_pairs={{0,8},{8,12},{12,4},{4,0},{1,9},{9,13},{13,5},{5,1},{2,10},{10,14}... | collective-permute-start | bytes 491528 | tf_op jit(solution)/shard_map/ppermute | solution.py:24
  44.5 0.7 copy-start.5
  58.2 18.5 %collective-permute-start.16 = (bf16[128,640]{1,0:T(8,128)(2,1)S(1)}, bf16[128,640]{1,0:T(8,128)(2,1)S(1)}, u32[]{:S(2)}, u32[]{:S(2)}) collective-permute-start(bf16[128,640]{1,0:T(8,128)(2,1)S(1)} %collective-permute-done.15.query), channel_id=1, source_target_pairs={{0,8},{8,12},{12,4},{4,0},{1,9},{9,13},{13,5},{5,1},{2,10},{10,14}... | collective-permute-start | bytes 491528 | tf_op jit(solution)/shard_map/ppermute | solution.py:24
  61.6 15.2 %collective-permute-start.10 = (bf16[128,640]{1,0:T(8,128)(2,1)S(1)}, bf16[128,640]{1,0:T(8,128)(2,1)S(1)}, u32[]{:S(2)}, u32[]{:S(2)}) collective-permute-start(bf16[128,640]{1,0:T(8,128)(2,1)S(1)} %collective-permute-done.9.query), channel_id=1, source_target_pairs={{0,8},{8,12},{12,4},{4,0},{1,9},{9,13},{13,5},{5,1},{2,10},{10,14}... | collective-permute-start | bytes 491528 | tf_op jit(solution)/shard_map/ppermute | solution.py:24
  65.1 5.7 %copy-start.1 = (bf16[128,1280]{1,0:T(8,128)(2,1)}, bf16[128,1280]{1,0:T(8,128)(2,1)S(1)}, u32[]{:S(2)}) copy-start(bf16[128,1280]{1,0:T(8,128)(2,1)S(1)} %collective-permute-done.2.key.refs_5_) | copy-start | bytes 983044
  65.2 5.7 %copy-start.2 = (bf16[128,1280]{1,0:T(8,128)(2,1)}, bf16[128,1280]{1,0:T(8,128)(2,1)S(1)}, u32[]{:S(2)}) copy-start(bf16[128,1280]{1,0:T(8,128)(2,1)S(1)} %collective-permute-done.5.cotangent.refs_8_) | copy-start | bytes 983044
  67.0 45.9 %collective-permute-start.22 = (f32[1,3,80,640]{3,2,1,0:T(8,128)}, f32[1,3,80,640]{3,2,1,0:T(8,128)}, u32[]{:S(2)}, u32[]{:S(2)}) collective-permute-start(f32[1,3,80,640]{3,2,1,0:T(8,128)} %get-tuple-element.32), channel_id=1, source_target_pairs={{0,1},{1,0},{2,3},{3,2},{4,5},{5,4},{6,7},{7,6},{8,9},{9,8},{10,11... | collective-permute-start | bytes 1843208 | tf_op jit(solution)/shard_map/ppermute | solution.py:24
  73.9 41.0 %collective-permute-start.21 = (f32[1,3,80,640]{3,2,1,0:T(8,128)}, f32[1,3,80,640]{3,2,1,0:T(8,128)S(1)}, u32[]{:S(2)}, u32[]{:S(2)}) collective-permute-start(f32[1,3,80,640]{3,2,1,0:T(8,128)} %get-tuple-element.31), channel_id=1, source_target_pairs={{0,1},{1,0},{2,3},{3,2},{4,5},{5,4},{6,7},{7,6},{8,9},{9,8},{10,11... | collective-permute-start | bytes 1843208 | tf_op jit(solution)/shard_map/ppermute | solution.py:24
  74.9 7.1 %collective-permute-start.18 = (bf16[128,640]{1,0:T(8,128)(2,1)S(1)}, bf16[128,640]{1,0:T(8,128)(2,1)S(1)}, u32[]{:S(2)}, u32[]{:S(2)}) collective-permute-start(bf16[128,640]{1,0:T(8,128)(2,1)S(1)} %apply_step.15), channel_id=1, source_target_pairs={{0,8},{8,12},{12,4},{4,0},{1,9},{9,13},{13,5},{5,1},{2,10},{10,14}... | collective-permute-start | bytes 491528 | tf_op jit(solution)/shard_map/ppermute | solution.py:24
  76.7 8.8 %collective-permute-start.12 = (bf16[128,640]{1,0:T(8,128)(2,1)S(1)}, bf16[128,640]{1,0:T(8,128)(2,1)S(1)}, u32[]{:S(2)}, u32[]{:S(2)}) collective-permute-start(bf16[128,640]{1,0:T(8,128)(2,1)S(1)} %apply_step.11), channel_id=1, source_target_pairs={{0,8},{8,12},{12,4},{4,0},{1,9},{9,13},{13,5},{5,1},{2,10},{10,14}... | collective-permute-start | bytes 491528 | tf_op jit(solution)/shard_map/ppermute | solution.py:24
  76.8 12.3 %collective-permute-start.11 = (bf16[128,640]{1,0:T(8,128)(2,1)S(1)}, bf16[128,640]{1,0:T(8,128)(2,1)S(1)}, u32[]{:S(2)}, u32[]{:S(2)}) collective-permute-start(bf16[128,640]{1,0:T(8,128)(2,1)S(1)} %collective-permute-done.10.query), channel_id=1, source_target_pairs={{0,8},{8,12},{12,4},{4,0},{1,9},{9,13},{13,5},{5,1},{2,10},{10,14}... | collective-permute-start | bytes 491528 | tf_op jit(solution)/shard_map/ppermute | solution.py:24
  82.0 10.5 %collective-permute-start.17 = (bf16[128,640]{1,0:T(8,128)(2,1)S(1)}, bf16[128,640]{1,0:T(8,128)(2,1)S(1)}, u32[]{:S(2)}, u32[]{:S(2)}) collective-permute-start(bf16[128,640]{1,0:T(8,128)(2,1)S(1)} %collective-permute-done.16.query), channel_id=1, source_target_pairs={{0,8},{8,12},{12,4},{4,0},{1,9},{9,13},{13,5},{5,1},{2,10},{10,14}... | collective-permute-start | bytes 491528 | tf_op jit(solution)/shard_map/ppermute | solution.py:24
  84.7 17.0 %copy-start.11 = (f32[4,128]{1,0:T(4,128)S(1)}, f32[4,128]{1,0:T(4,128)}, u32[]{:S(2)}) copy-start(f32[4,128]{1,0:T(4,128)} %rates.1) | copy-start | bytes 6148
  84.7 22.9 %copy-start.4 = (bf16[128,640]{1,0:T(8,128)(2,1)S(1)}, bf16[128,640]{1,0:T(8,128)(2,1)}, u32[]{:S(2)}) copy-start(bf16[128,640]{1,0:T(8,128)(2,1)} %copy-done.3) | copy-start | bytes 491524
  84.7 22.9 %copy-start.6 = (bf16[128,640]{1,0:T(8,128)(2,1)S(1)}, bf16[128,640]{1,0:T(8,128)(2,1)}, u32[]{:S(2)}) copy-start(bf16[128,640]{1,0:T(8,128)(2,1)} %copy-done.5) | copy-start | bytes 491524
  85.6 10.5 %collective-permute-start.19 = (bf16[128,640]{1,0:T(8,128)(2,1)S(1)}, bf16[128,640]{1,0:T(8,128)(2,1)S(1)}, u32[]{:S(2)}, u32[]{:S(2)}) collective-permute-start(bf16[128,640]{1,0:T(8,128)(2,1)S(1)} %join_step.6), channel_id=1, source_target_pairs={{0,8},{8,12},{12,4},{4,0},{1,9},{9,13},{13,5},{5,1},{2,10},{10,14}... | collective-permute-start | bytes 491528 | tf_op jit(solution)/shard_map/ppermute | solution.py:24
  89.1 10.5 %collective-permute-start.13 = (bf16[128,640]{1,0:T(8,128)(2,1)S(1)}, bf16[128,640]{1,0:T(8,128)(2,1)S(1)}, u32[]{:S(2)}, u32[]{:S(2)}) collective-permute-start(bf16[128,640]{1,0:T(8,128)(2,1)S(1)} %join_step.4), channel_id=1, source_target_pairs={{0,8},{8,12},{12,4},{4,0},{1,9},{9,13},{13,5},{5,1},{2,10},{10,14}... | collective-permute-start | bytes 491528 | tf_op jit(solution)/shard_map/ppermute | solution.py:24
  96.1 15.4 %collective-permute-start.20 = (bf16[128,640]{1,0:T(8,128)(2,1)S(1)}, bf16[128,640]{1,0:T(8,128)(2,1)S(1)}, u32[]{:S(2)}, u32[]{:S(2)}) collective-permute-start(bf16[128,640]{1,0:T(8,128)(2,1)S(1)} %join_step.7), channel_id=1, source_target_pairs={{0,8},{8,12},{12,4},{4,0},{1,9},{9,13},{13,5},{5,1},{2,10},{10,14}... | collective-permute-start | bytes 491528 | tf_op jit(solution)/shard_map/ppermute | solution.py:24
  99.6 12.6 %collective-permute-start.14 = (bf16[128,640]{1,0:T(8,128)(2,1)S(1)}, bf16[128,640]{1,0:T(8,128)(2,1)S(1)}, u32[]{:S(2)}, u32[]{:S(2)}) collective-permute-start(bf16[128,640]{1,0:T(8,128)(2,1)S(1)} %join_step.5), channel_id=1, source_target_pairs={{0,8},{8,12},{12,4},{4,0},{1,9},{9,13},{13,5},{5,1},{2,10},{10,14}... | collective-permute-start | bytes 491528 | tf_op jit(solution)/shard_map/ppermute | solution.py:24
  101.7 5.9 %collective-permute-start.8 = (f32[2,1,128]{2,1,0:T(1,128)S(1)}, f32[2,1,128]{2,1,0:T(1,128)S(1)}, u32[]{:S(2)}, u32[]{:S(2)}) collective-permute-start(f32[2,1,128]{2,1,0:T(1,128)S(1)} %bitcast.3), channel_id=1, source_target_pairs={{0,4},{4,8},{8,12},{12,0},{1,5},{5,9},{9,13},{13,1},{2,6},{6,10},{... | collective-permute-start | bytes 3080 | tf_op jit(solution)/shard_map/ppermute | solution.py:24

commit v8 on v7

--- a/solution.py
+++ b/solution.py
@@ -128,20 +128,21 @@
     return pltpu.with_memory_space_constraint(value, pltpu.HBM)
 
 
-def columns_body(rep, whole, out, semaphore):
+def columns_body(whole, out, semaphore):
     columns = out.shape[1]
-    taken = whole.at[:, pl.ds(pl.multiple_of(rep[0] * columns, columns), columns)]
+    first = pl.multiple_of(lax.axis_index("rep") * columns, columns)
+    taken = whole.at[:, pl.ds(first, columns)]
     copy = pltpu.make_async_copy(taken, out, semaphore)
     copy.start()
     copy.wait()
 
 
-def columns_step(rep, whole):
+def columns_step(whole):
     rows, columns = whole.shape[0], whole.shape[1] // 2
     return pl.pallas_call(
         columns_body,
         out_shape=jax.ShapeDtypeStruct((rows, columns), whole.dtype),
-        in_specs=[pl.BlockSpec(memory_space=pltpu.SMEM), pl.BlockSpec(memory_space=pl.ANY)],
+        in_specs=[pl.BlockSpec(memory_space=pl.ANY)],
         out_specs=pl.BlockSpec(memory_space=pltpu.VMEM),
         scratch_shapes=[pltpu.SemaphoreType.DMA],
         compiler_params=pltpu.CompilerParams(vmem_limit_bytes=4 << 20),
@@ -149,7 +150,7 @@
             flops=0, bytes_accessed=4 * rows * columns, transcendentals=0
         ),
         name="columns_step",
-    )(rep, in_hbm(whole))
+    )(in_hbm(whole))
 
 
 def cotangent_body(token_scale, rep, values, rates, out_raw, out):
@@ -355,17 +356,23 @@
     )(rep, block, before)
 
 
-def join_body(made, moved, out):
-    out[...] = (made[...] + moved[...].astype(jnp.float32)).astype(jnp.bfloat16)
-
-
-def join_step(made, moved):
+def join_body(first, made, moved, *outs):
+    for out in outs:
+        rows = out.shape[0]
+        here = moved[...] if moved.shape[0] == rows else moved[first : first + rows, :]
+        total = made[first : first + rows, :] + here.astype(jnp.float32)
+        out[...] = total.astype(jnp.bfloat16)
+        first += rows
+
+
+def join_step(made, moved, first=0, pieces=1):
+    rows, width = moved.shape
     in_vmem = pl.BlockSpec(memory_space=pltpu.VMEM)
     return pl.pallas_call(
-        join_body,
-        out_shape=jax.ShapeDtypeStruct(made.shape, jnp.bfloat16),
+        functools.partial(join_body, first),
+        out_shape=(jax.ShapeDtypeStruct((rows // pieces, width), jnp.bfloat16),) * pieces,
         in_specs=[in_vmem, in_vmem],
-        out_specs=in_vmem,
+        out_specs=(in_vmem,) * pieces,
         compiler_params=pltpu.CompilerParams(vmem_limit_bytes=2 << 20),
         cost_estimate=pl.CostEstimate(
             flops=made.size, bytes_accessed=8 * made.size, transcendentals=0
@@ -404,28 +411,32 @@
     )(query, low)
 
 
-def output_body(kept, attended, moved, *refs):
-    total = attended[...] + (kept[...] + moved[...].astype(jnp.float32))
-    refs[-1][...] = total.astype(jnp.bfloat16)
+def output_body(parts, kept, attended, *refs):
+    first = 0
+    for moved in refs[:parts]:
+        here = slice(first, first + moved.shape[0])
+        total = attended[here, :] + (kept[here, :] + moved[...].astype(jnp.float32))
+        refs[-1][here, :] = total.astype(jnp.bfloat16)
+        first += moved.shape[0]
 
 
 def output_step(head, heads, kept, attended, moved, before):
     rows, width = kept.shape
     more = () if before is None else (before,)
     return pl.pallas_call(
-        output_body,
+        functools.partial(output_body, len(moved)),
         out_shape=pltpu.HBM((rows, heads * width), jnp.bfloat16),
         grid=(1,),
-        in_specs=[pl.BlockSpec(memory_space=pltpu.VMEM)] * 3
+        in_specs=[pl.BlockSpec(memory_space=pltpu.VMEM)] * (2 + len(moved))
         + [pl.BlockSpec(memory_space=pl.ANY)] * len(more),
         out_specs=pl.BlockSpec((rows, width), lambda i: (0, head)),
-        input_output_aliases={3: 0} if more else {},
+        input_output_aliases={2 + len(moved): 0} if more else {},
         compiler_params=pltpu.CompilerParams(vmem_limit_bytes=4 << 20),
         cost_estimate=pl.CostEstimate(
             flops=rows * width, bytes_accessed=8 * rows * width, transcendentals=0
         ),
         name="output_step",
-    )(kept, attended, moved, *more)
+    )(kept, attended, *moved, *more)
 
 
 def attend_body(token_scale, block_index, *refs):
@@ -503,7 +514,7 @@
     rep = rep_index.reshape(1)
     value_own, cot = cotangent_step(token_scale, rep, values, learn_rates)
     heads = range(per_rep)
-    keys, cots = [columns_step(rep, key_vectors)], [cot]
+    keys, cots = [columns_step(key_vectors)], [cot]
     asked = [[lax.dynamic_slice_in_dim(queries, (start + h) * width, width, 1) for h in heads]]
     for _ in range(1, slots):
         keys.append(hop(keys[-1]))
@@ -540,9 +551,19 @@
         for h in heads:
             kind = jnp.bfloat16 if step == 1 else jnp.float32
             made.append(apply_step(asked[step][h], lows[h], kind))
-        if step > 1:
-            made = [join_step(made[h], moving[h]) for h in heads]
-        moving = [hop(made[h]) for h in heads]
+        if step == 1:
+            moving = [[hop(made[h])] for h in heads]
+            continue
+        sent = []
+        for h in heads:
+            if step == 2:
+                sent.append(join_step(made[h], moving[h][0], 0, 1 + h))
+            else:
+                rows = made[h].shape[0] // len(moving[h])
+                sent.append([])
+                for i, part in enumerate(moving[h]):
+                    sent[h].append(join_step(made[h], part, i * rows)[0])
+        moving = [[hop(part) for part in sent[h]] for h in heads]
     layer_output = None
     for h in heads:
         kept = apply_step(asked[0][h], lows[h], jnp.float32)

time: 116 us -> 114 us (0.983)
  waiting for transfers between devices: 40.9 us -> 37.1 us
  starting transfers between devices: 43.3 us -> 45.1 us
    ppermute x23 -> x25, waiting for transfers between devices: 40.9 us -> 37.1 us  [ring(): return lax.ppermute(value, axis, list(zip(order, (*order[1:], order[0]))))]
    ppermute x23 -> x25, starting transfers between devices: 43.3 us -> 45.1 us  [ring(): return lax.ppermute(value, axis, list(zip(order, (*order[1:], order[0]))))]
  transfers between devices with their start and end apart: 23 -> 25, of which waited for: 12 -> 12; matrix products, arithmetic and copies ran while one was open for 1% -> 1% of each run, Pallas kernels for 21% -> 21%
where the time goes in v8:
time: 114 us
  starting transfers between devices  45.1 us (40%)
  waiting for transfers between devices  37.1 us (33%)
  Pallas kernels  27.7 us (24%)
  local copies, waits for them, and re-layouts  3.14 us (3%)
    ppermute x25, starting transfers between devices, ring(): return lax.ppermute(value, axis, list(zip(order, (*order[1:], order[0]))))  45.1 us
    ppermute x25, waiting for transfers between devices, ring(): return lax.ppermute(value, axis, list(zip(order, (*order[1:], order[0]))))  37.1 us
    pallas_call x2, Pallas kernels, early_step(): pl.pallas_call(functools.partial(early_body, slots), out_shape=((pltpu.HB...  6.72 us
    pallas_call x2, Pallas kernels, last_step(): pl.pallas_call(last_body, out_shape=(pltpu.HBM((2 * heads, 3, hid, width)...  4.88 us
    pallas_call x8, Pallas kernels, apply_step(): pl.pallas_call(apply_body, out_shape=jax.ShapeDtypeStruct((rows, width),...  4.06 us
    pallas_call x1, Pallas kernels, attend_step(): pl.pallas_call(functools.partial(attend_body, token_scale), out_shape=mad...  2.82 us
    pallas_call x2, Pallas kernels, place_step(): pl.pallas_call(place_body, out_shape=pltpu.HBM(before.shape, before.dtype...  2.8 us
    pallas_call x1, Pallas kernels, other_step(): pl.pallas_call(other_body, out_shape=(pltpu.HBM(made, jnp.bfloat16), pltp...  2.69 us
  transfers between devices with their start and end apart: 25, of which 12 were waited for; matrix products, arithmetic and copies ran while one was open for 1% of the time, Pallas kernels for 21%

profile of v8, /device:TPU:0, one launch (start us, length us, event | category | flops | bytes accessed | tf_op | source)
XLA Modules:
  0.0 113.9 jit_solution(5619578044352038835)
XLA Ops:
  0.6 2.7 %other_step.1 = (bf16[2,3,80,640]{3,2,1,0:T(8,128)(2,1)}, f32[2,3,80,640]{3,2,1,0:T(8,128)}) custom-call(s32[1]{0:T(128)} %bitcast.rep, f32[4,3,80,640]{3,2,1,0:T(8,128)} %refs_6_.3, f32[4,3,80,640]{3,2,1,0:T(8,128)} %refs_7_.3), custom_call_target="tpu_custom_call" | custom-call | flops 614400 | bytes 4300800 | tf_op jit(solution)/shard_map/other_step/pallas_call | solution.py:204
  3.3 0.5 collective-permute-start.7
  3.8 1.0 columns_step.1.refs_0_
  4.8 0.0 copy-start
  4.8 3.6 %collective-permute-start = (bf16[128,1280]{1,0:T(8,128)(2,1)S(1)}, bf16[128,1280]{1,0:T(8,128)(2,1)S(1)}, u32[]{:S(2)}, u32[]{:S(2)}) collective-permute-start(bf16[128,1280]{1,0:T(8,128)(2,1)S(1)} %columns_step.1.refs_0_), channel_id=1, source_target_pairs={{0,8},{8,12},{12,4},{4,0},{1,9},{9,13},{13,5},{5,1},{2,10},{10,14}... | collective-permute-start | bytes 983048 | tf_op jit(solution)/shard_map/ppermute | solution.py:24
  8.4 1.2 %cotangent_step.1 = (bf16[128,1280]{1,0:T(8,128)(2,1)S(1)}, bf16[128,1280]{1,0:T(8,128)(2,1)S(1)}) custom-call(s32[1]{0:T(128)} %bitcast.rep, bf16[128,2560]{1,0:T(8,128)(2,1)} %values.1, f32[4,128]{1,0:T(4,128)} %rates.1), custom_call_target="tpu_custom_call" | custom-call | flops 327680 | bytes 983040 | tf_op jit(solution)/shard_map/cotangent_step/pallas_call | solution.py:172
  9.6 0.7 copy-done.8
  10.4 1.6 %collective-permute-start.3 = (bf16[128,1280]{1,0:T(8,128)(2,1)S(1)}, bf16[128,1280]{1,0:T(8,128)(2,1)S(1)}, u32[]{:S(2)}, u32[]{:S(2)}) collective-permute-start(bf16[128,1280]{1,0:T(8,128)(2,1)S(1)} %get-tuple-element.20.refs_3_), channel_id=1, source_target_pairs={{0,8},{8,12},{12,4},{4,0},{1,9},{9,13},{13,5},{5,1},{2,10},{10,14}... | collective-permute-start | bytes 983048 | tf_op jit(solution)/shard_map/ppermute | solution.py:24
  11.9 0.0 collective-permute-start.6
  12.0 4.6 %collective-permute-done.refs_1_.refs_3_ = bf16[128,1280]{1,0:T(8,128)(2,1)S(1)} collective-permute-done((bf16[128,1280]{1,0:T(8,128)(2,1)S(1)}, bf16[128,1280]{1,0:T(8,128)(2,1)S(1)}, u32[]{:S(2)}, u32[]{:S(2)}) %collective-permute-start) | collective-permute-done | bytes 327712 | tf_op jit(solution)/shard_map/ppermute | solution.py:24
  16.6 3.4 %collective-permute-start.1 = (bf16[128,1280]{1,0:T(8,128)(2,1)S(1)}, bf16[128,1280]{1,0:T(8,128)(2,1)}, u32[]{:S(2)}, u32[]{:S(2)}) collective-permute-start(bf16[128,1280]{1,0:T(8,128)(2,1)S(1)} %collective-permute-done.refs_1_.refs_3_), channel_id=1, source_target_pairs={{0,8},{8,12},{12,4},{4,0},{1,9},{9,13},{13,5},{5,1},{2,10},{10,14}... | collective-permute-start | bytes 983048 | tf_op jit(solution)/shard_map/ppermute | solution.py:24
  19.9 3.6 %collective-permute-done.3.refs_4_.refs_6_ = bf16[128,1280]{1,0:T(8,128)(2,1)S(1)} collective-permute-done((bf16[128,1280]{1,0:T(8,128)(2,1)S(1)}, bf16[128,1280]{1,0:T(8,128)(2,1)S(1)}, u32[]{:S(2)}, u32[]{:S(2)}) %collective-permute-start.3) | collective-permute-done | bytes 327712 | tf_op jit(solution)/shard_map/ppermute | solution.py:24
  23.6 3.4 %collective-permute-start.4 = (bf16[128,1280]{1,0:T(8,128)(2,1)S(1)}, bf16[128,1280]{1,0:T(8,128)(2,1)}, u32[]{:S(2)}, u32[]{:S(2)}) collective-permute-start(bf16[128,1280]{1,0:T(8,128)(2,1)S(1)} %collective-permute-done.3.refs_4_.refs_6_), channel_id=1, source_target_pairs={{0,8},{8,12},{12,4},{4,0},{1,9},{9,13},{13,5},{5,1},{2,10},{10,14}... | collective-permute-start | bytes 983048 | tf_op jit(solution)/shard_map/ppermute | solution.py:24
  27.0 3.6 %collective-permute-done.1.refs_2_.refs_4_ = bf16[128,1280]{1,0:T(8,128)(2,1)} collective-permute-done((bf16[128,1280]{1,0:T(8,128)(2,1)S(1)}, bf16[128,1280]{1,0:T(8,128)(2,1)}, u32[]{:S(2)}, u32[]{:S(2)}) %collective-permute-start.1) | collective-permute-done | bytes 327712 | tf_op jit(solution)/shard_map/ppermute | solution.py:24
  30.6 3.5 %collective-permute-start.2 = (bf16[128,1280]{1,0:T(8,128)(2,1)}, bf16[128,1280]{1,0:T(8,128)(2,1)S(1)}, u32[]{:S(2)}, u32[]{:S(2)}) collective-permute-start(bf16[128,1280]{1,0:T(8,128)(2,1)} %collective-permute-done.1.refs_2_.refs_4_), channel_id=1, source_target_pairs={{0,8},{8,12},{12,4},{4,0},{1,9},{9,13},{13,5},{5,1},{2,10},{10,14}... | collective-permute-start | bytes 983048 | tf_op jit(solution)/shard_map/ppermute | solution.py:24
  34.1 3.5 %collective-permute-done.4.refs_5_.refs_7_ = bf16[128,1280]{1,0:T(8,128)(2,1)} collective-permute-done((bf16[128,1280]{1,0:T(8,128)(2,1)S(1)}, bf16[128,1280]{1,0:T(8,128)(2,1)}, u32[]{:S(2)}, u32[]{:S(2)}) %collective-permute-start.4) | collective-permute-done | bytes 327712 | tf_op jit(solution)/shard_map/ppermute | solution.py:24
  37.6 3.5 %collective-permute-start.5 = (bf16[128,1280]{1,0:T(8,128)(2,1)}, bf16[128,1280]{1,0:T(8,128)(2,1)S(1)}, u32[]{:S(2)}, u32[]{:S(2)}) collective-permute-start(bf16[128,1280]{1,0:T(8,128)(2,1)} %collective-permute-done.4.refs_5_.refs_7_), channel_id=1, source_target_pairs={{0,8},{8,12},{12,4},{4,0},{1,9},{9,13},{13,5},{5,1},{2,10},{10,14}... | collective-permute-start | bytes 983048 | tf_op jit(solution)/shard_map/ppermute | solution.py:24
  41.1 1.0 constant_dynamic-slice_fusion
  42.1 0.7 collective-permute-start.17
  42.9 0.7 copy-done.3
  43.5 11.2 %collective-permute-done.17.query = bf16[128,640]{1,0:T(8,128)(2,1)S(1)} collective-permute-done((bf16[128,640]{1,0:T(8,128)(2,1)S(1)}, bf16[128,640]{1,0:T(8,128)(2,1)S(1)}, u32[]{:S(2)}, u32[]{:S(2)}) %collective-permute-start.17) | collective-permute-done | bytes 163872 | tf_op jit(solution)/shard_map/ppermute | solution.py:24
  54.7 3.4 %collective-permute-start.9 = (bf16[128,640]{1,0:T(8,128)(2,1)S(1)}, bf16[128,640]{1,0:T(8,128)(2,1)S(1)}, u32[]{:S(2)}, u32[]{:S(2)}) collective-permute-start(bf16[128,640]{1,0:T(8,128)(2,1)S(1)} %get-tuple-element.39.query.refs_10_), channel_id=1, source_target_pairs={{0,8},{8,12},{12,4},{4,0},{1,9},{9,13},{13,5},{5,1},{2,10},{10,14}... | collective-permute-start | bytes 491528 | tf_op jit(solution)/shard_map/ppermute | solution.py:24
  58.1 0.7 copy-done.5
  58.8 0.7 collective-permute-start.18
  59.4 0.0 collective-permute-done.7.refs_9_
  59.5 2.8 %early_step.3 = (f32[480,640]{1,0:T(8,128)S(1)}, bf16[480,640]{1,0:T(8,128)(2,1)S(1)}) custom-call(s32[1]{0:T(128)} %bitcast.rep, bf16[128,1280]{1,0:T(8,128)(2,1)} %copy-done, bf16[128,1280]{1,0:T(8,128)(2,1)} %copy-done.9, bf16[128,1280]{1,0:T(8,128)(2,1)} %collective-permute-done.1.refs_2_.refs_4_, bf16[128,1280]{1,0:T(8,128)(2,1)} %copy-done.7, ...), custom_call_target="tpu_custom_call" | custom-call | flops 471859200 | bytes 3072000 | tf_op jit(solution)/shard_map/early_step/pallas_call | solution.py:261
  62.3 0.0 collective-permute-done.5.cotangent.refs_8_
  62.3 1.8 %last_step.2 = (f32[4,3,80,640]{3,2,1,0:T(8,128)}, f32[1,3,80,640]{3,2,1,0:T(8,128)}, bf16[480,640]{1,0:T(8,128)(2,1)S(1)}) custom-call(s32[1]{0:T(128)} %bitcast.rep, bf16[128,1280]{1,0:T(8,128)(2,1)S(1)} %collective-permute-done.2.key.refs_5_, bf16[128,1280]{1,0:T(8,128)(2,1)S(1)} %collective-permute-done.5.cotangent.refs_8_, ...), custom_call_target="tpu_custom_call" | custom-call | flops 157286400 | bytes 3686400 | tf_op jit(solution)/shard_map/last_step/pallas_call | solution.py:310
  64.2 0.0 collective-permute-start.24
  64.2 3.9 %early_step.2 = (f32[480,640]{1,0:T(8,128)}, bf16[480,640]{1,0:T(8,128)(2,1)S(1)}) custom-call(s32[1]{0:T(128)} %bitcast.rep, bf16[128,1280]{1,0:T(8,128)(2,1)} %copy-done, bf16[128,1280]{1,0:T(8,128)(2,1)} %copy-done.9, bf16[128,1280]{1,0:T(8,128)(2,1)} %collective-permute-done.1.refs_2_.refs_4_, bf16[128,1280]{1,0:T(8,128)(2,1)} %copy-done.7, ...), custom_call_target="tpu_custom_call" | custom-call | flops 471859200 | bytes 3072000 | tf_op jit(solution)/shard_map/early_step/pallas_call | solution.py:261
  68.1 3.0 %last_step.3 = (f32[4,3,80,640]{3,2,1,0:T(8,128)}, f32[1,3,80,640]{3,2,1,0:T(8,128)}, bf16[480,640]{1,0:T(8,128)(2,1)S(1)}) custom-call(s32[1]{0:T(128)} %bitcast.rep, bf16[128,1280]{1,0:T(8,128)(2,1)S(1)} %collective-permute-done.2.key.refs_5_, bf16[128,1280]{1,0:T(8,128)(2,1)S(1)} %collective-permute-done.5.cotangent.refs_8_, ...), custom_call_target="tpu_custom_call", output_to_operand_aliasing={{0}: (5, {})} | custom-call | flops 157286400 | bytes 3686400 | tf_op jit(solution)/shard_map/last_step/pallas_call | solution.py:310
  71.1 0.5 collective-permute-start.23
  71.6 0.5 apply_step.15
  72.1 1.3 %collective-permute-start.20 = (bf16[128,640]{1,0:T(8,128)(2,1)S(1)}, bf16[128,640]{1,0:T(8,128)(2,1)S(1)}, u32[]{:S(2)}, u32[]{:S(2)}) collective-permute-start(bf16[128,640]{1,0:T(8,128)(2,1)S(1)} %apply_step.15), channel_id=1, source_target_pairs={{0,8},{8,12},{12,4},{4,0},{1,9},{9,13},{13,5},{5,1},{2,10},{10,14}... | collective-permute-start | bytes 491528 | tf_op jit(solution)/shard_map/ppermute | solution.py:24
  73.4 0.1 collective-permute-start.10
  73.5 3.0 %collective-permute-start.19 = (bf16[128,640]{1,0:T(8,128)(2,1)S(1)}, bf16[128,640]{1,0:T(8,128)(2,1)S(1)}, u32[]{:S(2)}, u32[]{:S(2)}) collective-permute-start(bf16[128,640]{1,0:T(8,128)(2,1)S(1)} %collective-permute-done.18.query), channel_id=1, source_target_pairs={{0,8},{8,12},{12,4},{4,0},{1,9},{9,13},{13,5},{5,1},{2,10},{10,14}... | collective-permute-start | bytes 491528 | tf_op jit(solution)/shard_map/ppermute | solution.py:24
  76.5 0.5 apply_step.11
  77.0 0.0 copy-start.11
  77.0 2.3 %collective-permute-done.20.moved = bf16[128,640]{1,0:T(8,128)(2,1)S(1)} collective-permute-done((bf16[128,640]{1,0:T(8,128)(2,1)S(1)}, bf16[128,640]{1,0:T(8,128)(2,1)S(1)}, u32[]{:S(2)}, u32[]{:S(2)}) %collective-permute-start.20) | collective-permute-done | bytes 163872 | tf_op jit(solution)/shard_map/ppermute | solution.py:24
  79.2 2.1 %collective-permute-start.12 = (bf16[128,640]{1,0:T(8,128)(2,1)S(1)}, bf16[128,640]{1,0:T(8,128)(2,1)S(1)}, u32[]{:S(2)}, u32[]{:S(2)}) collective-permute-start(bf16[128,640]{1,0:T(8,128)(2,1)S(1)} %apply_step.11), channel_id=1, source_target_pairs={{0,8},{8,12},{12,4},{4,0},{1,9},{9,13},{13,5},{5,1},{2,10},{10,14}... | collective-permute-start | bytes 491528 | tf_op jit(solution)/shard_map/ppermute | solution.py:24
  81.4 0.5 apply_step.14.made
  81.9 0.8 collective-permute-done.10.query
  82.8 2.1 %collective-permute-start.21 = (bf16[128,640]{1,0:T(8,128)(2,1)S(1)}, bf16[128,640]{1,0:T(8,128)(2,1)S(1)}, u32[]{:S(2)}, u32[]{:S(2)}) collective-permute-start(bf16[128,640]{1,0:T(8,128)(2,1)S(1)} %join_step.8), channel_id=1, source_target_pairs={{0,8},{8,12},{12,4},{4,0},{1,9},{9,13},{13,5},{5,1},{2,10},{10,14}... | collective-permute-start | bytes 491528 | tf_op jit(solution)/shard_map/ppermute | solution.py:24
  84.9 1.4 %collective-permute-done.19.query = bf16[128,640]{1,0:T(8,128)(2,1)S(1)} collective-permute-done((bf16[128,640]{1,0:T(8,128)(2,1)S(1)}, bf16[128,640]{1,0:T(8,128)(2,1)S(1)}, u32[]{:S(2)}, u32[]{:S(2)}) %collective-permute-start.19) | collective-permute-done | bytes 163872 | tf_op jit(solution)/shard_map/ppermute | solution.py:24
  86.3 2.1 %collective-permute-start.11 = (bf16[128,640]{1,0:T(8,128)(2,1)S(1)}, bf16[128,640]{1,0:T(8,128)(2,1)S(1)}, u32[]{:S(2)}, u32[]{:S(2)}) collective-permute-start(bf16[128,640]{1,0:T(8,128)(2,1)S(1)} %collective-permute-done.10.query), channel_id=1, source_target_pairs={{0,8},{8,12},{12,4},{4,0},{1,9},{9,13},{13,5},{5,1},{2,10},{10,14}... | collective-permute-start | bytes 491528 | tf_op jit(solution)/shard_map/ppermute | solution.py:24
  88.4 0.5 apply_step.10.made
  88.9 0.5 apply_step.13.made
  89.4 0.3 collective-permute-done.12.moved
  89.8 2.2 %collective-permute-start.13 = (bf16[64,640]{1,0:T(8,128)(2,1)S(1)}, bf16[64,640]{1,0:T(8,128)(2,1)S(1)}, u32[]{:S(2)}, u32[]{:S(2)}) collective-permute-start(bf16[64,640]{1,0:T(8,128)(2,1)S(1)} %get-tuple-element.31), channel_id=1, source_target_pairs={{0,8},{8,12},{12,4},{4,0},{1,9},{9,13},{13,5},{5,1},{2,10},{10,14}... | collective-permute-start | bytes 245768 | tf_op jit(solution)/shard_map/ppermute | solution.py:24
  92.0 1.3 %collective-permute-done.21.moved = bf16[128,640]{1,0:T(8,128)(2,1)S(1)} collective-permute-done((bf16[128,640]{1,0:T(8,128)(2,1)S(1)}, bf16[128,640]{1,0:T(8,128)(2,1)S(1)}, u32[]{:S(2)}, u32[]{:S(2)}) %collective-permute-start.21) | collective-permute-done | bytes 163872 | tf_op jit(solution)/shard_map/ppermute | solution.py:24
  93.3 2.1 %collective-permute-start.15 = (bf16[64,640]{1,0:T(8,128)(2,1)S(1)}, bf16[64,640]{1,0:T(8,128)(2,1)S(1)}, u32[]{:S(2)}, u32[]{:S(2)}) collective-permute-start(bf16[64,640]{1,0:T(8,128)(2,1)S(1)} %get-tuple-element.32), channel_id=1, source_target_pairs={{0,8},{8,12},{12,4},{4,0},{1,9},{9,13},{13,5},{5,1},{2,10},{10,14}... | collective-permute-start | bytes 245768 | tf_op jit(solution)/shard_map/ppermute | solution.py:24
  95.5 1.3 %collective-permute-done.11.query = bf16[128,640]{1,0:T(8,128)(2,1)S(1)} collective-permute-done((bf16[128,640]{1,0:T(8,128)(2,1)S(1)}, bf16[128,640]{1,0:T(8,128)(2,1)S(1)}, u32[]{:S(2)}, u32[]{:S(2)}) %collective-permute-start.11) | collective-permute-done | bytes 163872 | tf_op jit(solution)/shard_map/ppermute | solution.py:24
  96.8 2.1 %collective-permute-start.22 = (bf16[128,640]{1,0:T(8,128)(2,1)S(1)}, bf16[128,640]{1,0:T(8,128)(2,1)S(1)}, u32[]{:S(2)}, u32[]{:S(2)}) collective-permute-start(bf16[128,640]{1,0:T(8,128)(2,1)S(1)} %join_step.9), channel_id=1, source_target_pairs={{0,8},{8,12},{12,4},{4,0},{1,9},{9,13},{13,5},{5,1},{2,10},{10,14}... | collective-permute-start | bytes 491528 | tf_op jit(solution)/shard_map/ppermute | solution.py:24
  98.9 1.8 %collective-permute-start.8 = (f32[2,1,128]{2,1,0:T(1,128)S(1)}, f32[2,1,128]{2,1,0:T(1,128)S(1)}, u32[]{:S(2)}, u32[]{:S(2)}) collective-permute-start(f32[2,1,128]{2,1,0:T(1,128)S(1)} %bitcast.3), channel_id=1, source_target_pairs={{0,4},{4,8},{8,12},{12,0},{1,5},{5,9},{9,13},{13,1},{2,6},{6,10},{... | collective-permute-start | bytes 3080 | tf_op jit(solution)/shard_map/ppermute | solution.py:24
  100.7 0.5 apply_step.9.made
  101.3 1.4 %collective-permute-start.14 = (bf16[64,640]{1,0:T(8,128)(2,1)S(1)}, bf16[64,640]{1,0:T(8,128)(2,1)S(1)}, u32[]{:S(2)}, u32[]{:S(2)}) collective-permute-start(bf16[64,640]{1,0:T(8,128)(2,1)S(1)} %join_step.6), channel_id=1, source_target_pairs={{0,8},{8,12},{12,4},{4,0},{1,9},{9,13},{13,5},{5,1},{2,10},{10,14}... | collective-permute-start | bytes 245768 | tf_op jit(solution)/shard_map/ppermute | solution.py:24
  102.7 3.1 %collective-permute-done.8.refs_2_ = f32[2,1,128]{2,1,0:T(1,128)S(1)} collective-permute-done((f32[2,1,128]{2,1,0:T(1,128)S(1)}, f32[2,1,128]{2,1,0:T(1,128)S(1)}, u32[]{:S(2)}, u32[]{:S(2)}) %collective-permute-start.8) | collective-permute-done | bytes 1056 | tf_op jit(solution)/shard_map/ppermute | solution.py:24
  105.7 2.8 %attend_step.1 = (f32[128,640]{1,0:T(8,128)S(1)}, f32[128,640]{1,0:T(8,128)S(1)}) custom-call(s32[1]{0:T(128)} %bitcast.1.block_index, bf16[128,1280]{1,0:T(8,128)(2,1)} %copy-done, bf16[128,1280]{1,0:T(8,128)(2,1)} %copy-done.8, f32[2,1,128]{2,1,0:T(1,128)S(1)} %collective-permute-done.8.refs_2_, bf16[128,1280]{1,0:T(8,128)(2,1)} %copy-done.9, ...), custom_call_target="tpu_custom_call" | custom-call | flops 167772160 | bytes 3276800 | tf_op jit(solution)/shard_map/attend_step/pallas_call | solution.py:482
  108.6 0.5 apply_step.8.kept
  109.1 0.5 apply_step.12.kept
  109.6 0.7 output_step.2.refs_2_
  110.3 0.7 output_step.3
  111.1 1.9 %place_step.2.before = f32[4,3,80,640]{3,2,1,0:T(8,128)} custom-call(s32[1]{0:T(128)} %bitcast.rep, f32[1,3,80,640]{3,2,1,0:T(8,128)} %collective-permute-done.24.block, f32[4,3,80,640]{3,2,1,0:T(8,128)} %get-tuple-element.37.before), custom_call_target="tpu_custom_call", output_to_operand_aliasing={{}: (2, {})} | custom-call | bytes 1228800 | tf_op jit(solution)/shard_map/place_step/pallas_call | solution.py:341
  113.0 0.9 place_step.3
  (37 shorter events, 0.2 us)
Async XLA Ops:
  3.3 56.1 %collective-permute-start.7 = (f32[2,3,80,640]{3,2,1,0:T(8,128)}, f32[2,3,80,640]{3,2,1,0:T(8,128)S(1)}, u32[]{:S(2)}, u32[]{:S(2)}) collective-permute-start(f32[2,3,80,640]{3,2,1,0:T(8,128)} %get-tuple-element.22), channel_id=1, source_target_pairs={{0,1},{1,0},{2,3},{3,2},{4,5},{5,4},{6,7},{7,6},{8,9},{9,8},{10,11... | collective-permute-start | bytes 3686408 | tf_op jit(solution)/shard_map/ppermute | solution.py:24
  4.8 54.6 %copy-start = (bf16[128,1280]{1,0:T(8,128)(2,1)}, bf16[128,1280]{1,0:T(8,128)(2,1)S(1)}, u32[]{:S(2)}) copy-start(bf16[128,1280]{1,0:T(8,128)(2,1)S(1)} %columns_step.1.refs_0_) | copy-start | bytes 983044
  4.8 11.7 %collective-permute-start = (bf16[128,1280]{1,0:T(8,128)(2,1)S(1)}, bf16[128,1280]{1,0:T(8,128)(2,1)S(1)}, u32[]{:S(2)}, u32[]{:S(2)}) collective-permute-start(bf16[128,1280]{1,0:T(8,128)(2,1)S(1)} %columns_step.1.refs_0_), channel_id=1, source_target_pairs={{0,8},{8,12},{12,4},{4,0},{1,9},{9,13},{13,5},{5,1},{2,10},{10,14}... | collective-permute-start | bytes 983048 | tf_op jit(solution)/shard_map/ppermute | solution.py:24
  9.6 0.8 copy-start.8
  10.4 49.1 %copy-start.7 = (bf16[128,1280]{1,0:T(8,128)(2,1)}, bf16[128,1280]{1,0:T(8,128)(2,1)S(1)}, u32[]{:S(2)}) copy-start(bf16[128,1280]{1,0:T(8,128)(2,1)S(1)} %get-tuple-element.20.refs_3_) | copy-start | bytes 983044
  10.4 13.2 %collective-permute-start.3 = (bf16[128,1280]{1,0:T(8,128)(2,1)S(1)}, bf16[128,1280]{1,0:T(8,128)(2,1)S(1)}, u32[]{:S(2)}, u32[]{:S(2)}) collective-permute-start(bf16[128,1280]{1,0:T(8,128)(2,1)S(1)} %get-tuple-element.20.refs_3_), channel_id=1, source_target_pairs={{0,8},{8,12},{12,4},{4,0},{1,9},{9,13},{13,5},{5,1},{2,10},{10,14}... | collective-permute-start | bytes 983048 | tf_op jit(solution)/shard_map/ppermute | solution.py:24
  11.9 46.8 %collective-permute-start.6 = (bf16[2,3,80,640]{3,2,1,0:T(8,128)(2,1)}, bf16[2,3,80,640]{3,2,1,0:T(8,128)(2,1)S(1)}, u32[]{:S(2)}, u32[]{:S(2)}) collective-permute-start(bf16[2,3,80,640]{3,2,1,0:T(8,128)(2,1)} %get-tuple-element.21), channel_id=1, source_target_pairs={{0,1},{1,0},{2,3},{3,2},{4,5},{5,4},{6,7},{7,6},{8,9},{9,8},{10,11... | collective-permute-start | bytes 1843208 | tf_op jit(solution)/shard_map/ppermute | solution.py:24
  16.5 10.4 %copy-start.9 = (bf16[128,1280]{1,0:T(8,128)(2,1)}, bf16[128,1280]{1,0:T(8,128)(2,1)S(1)}, u32[]{:S(2)}) copy-start(bf16[128,1280]{1,0:T(8,128)(2,1)S(1)} %collective-permute-done.refs_1_.refs_3_) | copy-start | bytes 983044
  16.6 14.0 %collective-permute-start.1 = (bf16[128,1280]{1,0:T(8,128)(2,1)S(1)}, bf16[128,1280]{1,0:T(8,128)(2,1)}, u32[]{:S(2)}, u32[]{:S(2)}) collective-permute-start(bf16[128,1280]{1,0:T(8,128)(2,1)S(1)} %collective-permute-done.refs_1_.refs_3_), channel_id=1, source_target_pairs={{0,8},{8,12},{12,4},{4,0},{1,9},{9,13},{13,5},{5,1},{2,10},{10,14}... | collective-permute-start | bytes 983048 | tf_op jit(solution)/shard_map/ppermute | solution.py:24
  23.6 10.5 %copy-start.10 = (bf16[128,1280]{1,0:T(8,128)(2,1)}, bf16[128,1280]{1,0:T(8,128)(2,1)S(1)}, u32[]{:S(2)}) copy-start(bf16[128,1280]{1,0:T(8,128)(2,1)S(1)} %collective-permute-done.3.refs_4_.refs_6_) | copy-start | bytes 983044
  23.6 14.0 %collective-permute-start.4 = (bf16[128,1280]{1,0:T(8,128)(2,1)S(1)}, bf16[128,1280]{1,0:T(8,128)(2,1)}, u32[]{:S(2)}, u32[]{:S(2)}) collective-permute-start(bf16[128,1280]{1,0:T(8,128)(2,1)S(1)} %collective-permute-done.3.refs_4_.refs_6_), channel_id=1, source_target_pairs={{0,8},{8,12},{12,4},{4,0},{1,9},{9,13},{13,5},{5,1},{2,10},{10,14}... | collective-permute-start | bytes 983048 | tf_op jit(solution)/shard_map/ppermute | solution.py:24
  30.6 31.7 %collective-permute-start.2 = (bf16[128,1280]{1,0:T(8,128)(2,1)}, bf16[128,1280]{1,0:T(8,128)(2,1)S(1)}, u32[]{:S(2)}, u32[]{:S(2)}) collective-permute-start(bf16[128,1280]{1,0:T(8,128)(2,1)} %collective-permute-done.1.refs_2_.refs_4_), channel_id=1, source_target_pairs={{0,8},{8,12},{12,4},{4,0},{1,9},{9,13},{13,5},{5,1},{2,10},{10,14}... | collective-permute-start | bytes 983048 | tf_op jit(solution)/shard_map/ppermute | solution.py:24
  37.6 24.7 %collective-permute-start.5 = (bf16[128,1280]{1,0:T(8,128)(2,1)}, bf16[128,1280]{1,0:T(8,128)(2,1)S(1)}, u32[]{:S(2)}, u32[]{:S(2)}) collective-permute-start(bf16[128,1280]{1,0:T(8,128)(2,1)} %collective-permute-done.4.refs_5_.refs_7_), channel_id=1, source_target_pairs={{0,8},{8,12},{12,4},{4,0},{1,9},{9,13},{13,5},{5,1},{2,10},{10,14}... | collective-permute-start | bytes 983048 | tf_op jit(solution)/shard_map/ppermute | solution.py:24
  42.1 12.6 %collective-permute-start.17 = (bf16[128,640]{1,0:T(8,128)(2,1)S(1)}, bf16[128,640]{1,0:T(8,128)(2,1)S(1)}, u32[]{:S(2)}, u32[]{:S(2)}) collective-permute-start(bf16[128,640]{1,0:T(8,128)(2,1)S(1)} %get-tuple-element.38.refs_9_.query), channel_id=1, source_target_pairs={{0,8},{8,12},{12,4},{4,0},{1,9},{9,13},{13,5},{5,1},{2,10},{10,14}... | collective-permute-start | bytes 491528 | tf_op jit(solution)/shard_map/ppermute | solution.py:24
  42.9 0.7 copy-start.3
  54.7 18.7 %collective-permute-start.9 = (bf16[128,640]{1,0:T(8,128)(2,1)S(1)}, bf16[128,640]{1,0:T(8,128)(2,1)S(1)}, u32[]{:S(2)}, u32[]{:S(2)}) collective-permute-start(bf16[128,640]{1,0:T(8,128)(2,1)S(1)} %get-tuple-element.39.query.refs_10_), channel_id=1, source_target_pairs={{0,8},{8,12},{12,4},{4,0},{1,9},{9,13},{13,5},{5,1},{2,10},{10,14}... | collective-permute-start | bytes 491528 | tf_op jit(solution)/shard_map/ppermute | solution.py:24
  58.1 0.7 copy-start.5
  58.8 14.7 %collective-permute-start.18 = (bf16[128,640]{1,0:T(8,128)(2,1)S(1)}, bf16[128,640]{1,0:T(8,128)(2,1)S(1)}, u32[]{:S(2)}, u32[]{:S(2)}) collective-permute-start(bf16[128,640]{1,0:T(8,128)(2,1)S(1)} %collective-permute-done.17.query), channel_id=1, source_target_pairs={{0,8},{8,12},{12,4},{4,0},{1,9},{9,13},{13,5},{5,1},{2,10},{10,14}... | collective-permute-start | bytes 491528 | tf_op jit(solution)/shard_map/ppermute | solution.py:24
  62.3 5.8 %copy-start.1 = (bf16[128,1280]{1,0:T(8,128)(2,1)}, bf16[128,1280]{1,0:T(8,128)(2,1)S(1)}, u32[]{:S(2)}) copy-start(bf16[128,1280]{1,0:T(8,128)(2,1)S(1)} %collective-permute-done.2.key.refs_5_) | copy-start | bytes 983044
  62.3 5.7 %copy-start.2 = (bf16[128,1280]{1,0:T(8,128)(2,1)}, bf16[128,1280]{1,0:T(8,128)(2,1)S(1)}, u32[]{:S(2)}) copy-start(bf16[128,1280]{1,0:T(8,128)(2,1)S(1)} %collective-permute-done.5.cotangent.refs_8_) | copy-start | bytes 983044
  64.2 46.9 %collective-permute-start.24 = (f32[1,3,80,640]{3,2,1,0:T(8,128)}, f32[1,3,80,640]{3,2,1,0:T(8,128)}, u32[]{:S(2)}, u32[]{:S(2)}) collective-permute-start(f32[1,3,80,640]{3,2,1,0:T(8,128)} %get-tuple-element.36), channel_id=1, source_target_pairs={{0,1},{1,0},{2,3},{3,2},{4,5},{5,4},{6,7},{7,6},{8,9},{9,8},{10,11... | collective-permute-start | bytes 1843208 | tf_op jit(solution)/shard_map/ppermute | solution.py:24
  71.1 41.9 %collective-permute-start.23 = (f32[1,3,80,640]{3,2,1,0:T(8,128)}, f32[1,3,80,640]{3,2,1,0:T(8,128)S(1)}, u32[]{:S(2)}, u32[]{:S(2)}) collective-permute-start(f32[1,3,80,640]{3,2,1,0:T(8,128)} %get-tuple-element.35), channel_id=1, source_target_pairs={{0,1},{1,0},{2,3},{3,2},{4,5},{5,4},{6,7},{7,6},{8,9},{9,8},{10,11... | collective-permute-start | bytes 1843208 | tf_op jit(solution)/shard_map/ppermute | solution.py:24
  72.1 7.1 %collective-permute-start.20 = (bf16[128,640]{1,0:T(8,128)(2,1)S(1)}, bf16[128,640]{1,0:T(8,128)(2,1)S(1)}, u32[]{:S(2)}, u32[]{:S(2)}) collective-permute-start(bf16[128,640]{1,0:T(8,128)(2,1)S(1)} %apply_step.15), channel_id=1, source_target_pairs={{0,8},{8,12},{12,4},{4,0},{1,9},{9,13},{13,5},{5,1},{2,10},{10,14}... | collective-permute-start | bytes 491528 | tf_op jit(solution)/shard_map/ppermute | solution.py:24
  73.4 9.3 %collective-permute-start.10 = (bf16[128,640]{1,0:T(8,128)(2,1)S(1)}, bf16[128,640]{1,0:T(8,128)(2,1)S(1)}, u32[]{:S(2)}, u32[]{:S(2)}) collective-permute-start(bf16[128,640]{1,0:T(8,128)(2,1)S(1)} %collective-permute-done.9.query), channel_id=1, source_target_pairs={{0,8},{8,12},{12,4},{4,0},{1,9},{9,13},{13,5},{5,1},{2,10},{10,14}... | collective-permute-start | bytes 491528 | tf_op jit(solution)/shard_map/ppermute | solution.py:24
  73.5 12.8 %collective-permute-start.19 = (bf16[128,640]{1,0:T(8,128)(2,1)S(1)}, bf16[128,640]{1,0:T(8,128)(2,1)S(1)}, u32[]{:S(2)}, u32[]{:S(2)}) collective-permute-start(bf16[128,640]{1,0:T(8,128)(2,1)S(1)} %collective-permute-done.18.query), channel_id=1, source_target_pairs={{0,8},{8,12},{12,4},{4,0},{1,9},{9,13},{13,5},{5,1},{2,10},{10,14}... | collective-permute-start | bytes 491528 | tf_op jit(solution)/shard_map/ppermute | solution.py:24
  77.0 22.0 %copy-start.11 = (f32[4,128]{1,0:T(4,128)S(1)}, f32[4,128]{1,0:T(4,128)}, u32[]{:S(2)}) copy-start(f32[4,128]{1,0:T(4,128)} %rates.1) | copy-start | bytes 6148
  79.2 10.5 %collective-permute-start.12 = (bf16[128,640]{1,0:T(8,128)(2,1)S(1)}, bf16[128,640]{1,0:T(8,128)(2,1)S(1)}, u32[]{:S(2)}, u32[]{:S(2)}) collective-permute-start(bf16[128,640]{1,0:T(8,128)(2,1)S(1)} %apply_step.11), channel_id=1, source_target_pairs={{0,8},{8,12},{12,4},{4,0},{1,9},{9,13},{13,5},{5,1},{2,10},{10,14}... | collective-permute-start | bytes 491528 | tf_op jit(solution)/shard_map/ppermute | solution.py:24
  82.8 10.5 %collective-permute-start.21 = (bf16[128,640]{1,0:T(8,128)(2,1)S(1)}, bf16[128,640]{1,0:T(8,128)(2,1)S(1)}, u32[]{:S(2)}, u32[]{:S(2)}) collective-permute-start(bf16[128,640]{1,0:T(8,128)(2,1)S(1)} %join_step.8), channel_id=1, source_target_pairs={{0,8},{8,12},{12,4},{4,0},{1,9},{9,13},{13,5},{5,1},{2,10},{10,14}... | collective-permute-start | bytes 491528 | tf_op jit(solution)/shard_map/ppermute | solution.py:24
  86.3 10.5 %collective-permute-start.11 = (bf16[128,640]{1,0:T(8,128)(2,1)S(1)}, bf16[128,640]{1,0:T(8,128)(2,1)S(1)}, u32[]{:S(2)}, u32[]{:S(2)}) collective-permute-start(bf16[128,640]{1,0:T(8,128)(2,1)S(1)} %collective-permute-done.10.query), channel_id=1, source_target_pairs={{0,8},{8,12},{12,4},{4,0},{1,9},{9,13},{13,5},{5,1},{2,10},{10,14}... | collective-permute-start | bytes 491528 | tf_op jit(solution)/shard_map/ppermute | solution.py:24
  88.4 17.3 %copy-start.4 = (bf16[128,640]{1,0:T(8,128)(2,1)S(1)}, bf16[128,640]{1,0:T(8,128)(2,1)}, u32[]{:S(2)}) copy-start(bf16[128,640]{1,0:T(8,128)(2,1)} %copy-done.3) | copy-start | bytes 491524
  88.4 17.3 %copy-start.6 = (bf16[128,640]{1,0:T(8,128)(2,1)S(1)}, bf16[128,640]{1,0:T(8,128)(2,1)}, u32[]{:S(2)}) copy-start(bf16[128,640]{1,0:T(8,128)(2,1)} %copy-done.5) | copy-start | bytes 491524
  89.8 9.1 %collective-permute-start.13 = (bf16[64,640]{1,0:T(8,128)(2,1)S(1)}, bf16[64,640]{1,0:T(8,128)(2,1)S(1)}, u32[]{:S(2)}, u32[]{:S(2)}) collective-permute-start(bf16[64,640]{1,0:T(8,128)(2,1)S(1)} %get-tuple-element.31), channel_id=1, source_target_pairs={{0,8},{8,12},{12,4},{4,0},{1,9},{9,13},{13,5},{5,1},{2,10},{10,14}... | collective-permute-start | bytes 245768 | tf_op jit(solution)/shard_map/ppermute | solution.py:24
  93.3 8.0 %collective-permute-start.15 = (bf16[64,640]{1,0:T(8,128)(2,1)S(1)}, bf16[64,640]{1,0:T(8,128)(2,1)S(1)}, u32[]{:S(2)}, u32[]{:S(2)}) collective-permute-start(bf16[64,640]{1,0:T(8,128)(2,1)S(1)} %get-tuple-element.32), channel_id=1, source_target_pairs={{0,8},{8,12},{12,4},{4,0},{1,9},{9,13},{13,5},{5,1},{2,10},{10,14}... | collective-permute-start | bytes 245768 | tf_op jit(solution)/shard_map/ppermute | solution.py:24
  96.8 12.8 %collective-permute-start.22 = (bf16[128,640]{1,0:T(8,128)(2,1)S(1)}, bf16[128,640]{1,0:T(8,128)(2,1)S(1)}, u32[]{:S(2)}, u32[]{:S(2)}) collective-permute-start(bf16[128,640]{1,0:T(8,128)(2,1)S(1)} %join_step.9), channel_id=1, source_target_pairs={{0,8},{8,12},{12,4},{4,0},{1,9},{9,13},{13,5},{5,1},{2,10},{10,14}... | collective-permute-start | bytes 491528 | tf_op jit(solution)/shard_map/ppermute | solution.py:24
  98.9 6.8 %collective-permute-start.8 = (f32[2,1,128]{2,1,0:T(1,128)S(1)}, f32[2,1,128]{2,1,0:T(1,128)S(1)}, u32[]{:S(2)}, u32[]{:S(2)}) collective-permute-start(f32[2,1,128]{2,1,0:T(1,128)S(1)} %bitcast.3), channel_id=1, source_target_pairs={{0,4},{4,8},{8,12},{12,0},{1,5},{5,9},{9,13},{13,1},{2,6},{6,10},{... | collective-permute-start | bytes 3080 | tf_op jit(solution)/shard_map/ppermute | solution.py:24
  101.3 9.1 %collective-permute-start.14 = (bf16[64,640]{1,0:T(8,128)(2,1)S(1)}, bf16[64,640]{1,0:T(8,128)(2,1)S(1)}, u32[]{:S(2)}, u32[]{:S(2)}) collective-permute-start(bf16[64,640]{1,0:T(8,128)(2,1)S(1)} %join_step.6), channel_id=1, source_target_pairs={{0,8},{8,12},{12,4},{4,0},{1,9},{9,13},{13,5},{5,1},{2,10},{10,14}... | collective-permute-start | bytes 245768 | tf_op jit(solution)/shard_map/ppermute | solution.py:24
  105.7 4.6 %collective-permute-start.16 = (bf16[64,640]{1,0:T(8,128)(2,1)S(1)}, bf16[64,640]{1,0:T(8,128)(2,1)S(1)}, u32[]{:S(2)}, u32[]{:S(2)}) collective-permute-start(bf16[64,640]{1,0:T(8,128)(2,1)S(1)} %join_step.7), channel_id=1, source_target_pairs={{0,8},{8,12},{12,4},{4,0},{1,9},{9,13},{13,5},{5,1},{2,10},{10,14}... | collective-permute-start | bytes 245768 | tf_op jit(solution)/shard_map/ppermute | solution.py:24

commit v9 on v7

--- a/solution.py
+++ b/solution.py
@@ -128,20 +128,21 @@
     return pltpu.with_memory_space_constraint(value, pltpu.HBM)
 
 
-def columns_body(rep, whole, out, semaphore):
+def columns_body(whole, out, semaphore):
     columns = out.shape[1]
-    taken = whole.at[:, pl.ds(pl.multiple_of(rep[0] * columns, columns), columns)]
+    first = pl.multiple_of(lax.axis_index("rep") * columns, columns)
+    taken = whole.at[:, pl.ds(first, columns)]
     copy = pltpu.make_async_copy(taken, out, semaphore)
     copy.start()
     copy.wait()
 
 
-def columns_step(rep, whole):
+def columns_step(whole):
     rows, columns = whole.shape[0], whole.shape[1] // 2
     return pl.pallas_call(
         columns_body,
         out_shape=jax.ShapeDtypeStruct((rows, columns), whole.dtype),
-        in_specs=[pl.BlockSpec(memory_space=pltpu.SMEM), pl.BlockSpec(memory_space=pl.ANY)],
+        in_specs=[pl.BlockSpec(memory_space=pl.ANY)],
         out_specs=pl.BlockSpec(memory_space=pltpu.VMEM),
         scratch_shapes=[pltpu.SemaphoreType.DMA],
         compiler_params=pltpu.CompilerParams(vmem_limit_bytes=4 << 20),
@@ -149,7 +150,7 @@
             flops=0, bytes_accessed=4 * rows * columns, transcendentals=0
         ),
         name="columns_step",
-    )(rep, in_hbm(whole))
+    )(in_hbm(whole))
 
 
 def cotangent_body(token_scale, rep, values, rates, out_raw, out):
@@ -498,12 +499,17 @@
     cycle = (0, 2, 3, 1)
 
     def hop(value, axis="ctx", order=cycle):
-        return ring(value, axis, order if axis == "ctx" else None)
+        if order is None or axis != "ctx":
+            return ring(value, axis)
+        ahead = list(zip(order, (*order[1:], order[0])))
+        pairs = [(2 * source, 2 * target) for source, target in ahead]
+        pairs += [(2 * target + 1, 2 * source + 1) for source, target in ahead]
+        return lax.ppermute(value, ("ctx", "rep"), pairs)
 
     rep = rep_index.reshape(1)
     value_own, cot = cotangent_step(token_scale, rep, values, learn_rates)
     heads = range(per_rep)
-    keys, cots = [columns_step(rep, key_vectors)], [cot]
+    keys, cots = [columns_step(key_vectors)], [cot]
     asked = [[lax.dynamic_slice_in_dim(queries, (start + h) * width, width, 1) for h in heads]]
     for _ in range(1, slots):
         keys.append(hop(keys[-1]))
@@ -516,7 +522,8 @@
     base_par = hop(base_other, "rep")
     for _ in range(1, slots):
         asked.append([hop(asked[-1][h]) for h in heads])
-    block_index = lax.axis_index("ctx").reshape(1)
+    block_index = lax.axis_index("ctx")
+    block_index = jnp.where(rep_index == 0, block_index, (slots - block_index) % slots).reshape(1)
     attended = attend_step(
         token_scale, block_index, keys, value_own, cots[1:], rate_prior, asked[0]
     )

time: 116 us -> 115 us (level)
    ppermute x23 -> x5, starting transfers between devices: 43.3 us -> 1.82 us  [ring(): return lax.ppermute(value, axis, list(zip(order, (*order[1:], order[0]))))]
    ppermute x0 -> x18, starting transfers between devices: none -> 40.8 us  [hop(): return lax.ppermute(value, ('ctx', 'rep'), pairs)]
    ppermute x23 -> x5, waiting for transfers between devices: 40.9 us -> 5.02 us  [ring(): return lax.ppermute(value, axis, list(zip(order, (*order[1:], order[0]))))]
    ppermute x0 -> x18, waiting for transfers between devices: none -> 35.6 us  [hop(): return lax.ppermute(value, ('ctx', 'rep'), pairs)]
  transfers between devices with their start and end apart: 23 -> 23, of which waited for: 12 -> 13; matrix products, arithmetic and copies ran while one was open for 1% -> 1% of each run, Pallas kernels for 21% -> 21%
where the time goes in v9:
time: 115 us
  starting transfers between devices  42.6 us (37%)
  waiting for transfers between devices  40.6 us (35%)
  Pallas kernels  27.6 us (24%)
  local copies, waits for them, and re-layouts  3.12 us (3%)
    ppermute x18, starting transfers between devices, hop(): return lax.ppermute(value, ('ctx', 'rep'), pairs)  40.8 us
    ppermute x18, waiting for transfers between devices, hop(): return lax.ppermute(value, ('ctx', 'rep'), pairs)  35.6 us
    pallas_call x2, Pallas kernels, early_step(): pl.pallas_call(functools.partial(early_body, slots), out_shape=((pltpu.HB...  6.7 us
    ppermute x5, waiting for transfers between devices, ring(): return lax.ppermute(value, axis, list(zip(order, (*order[1:], order[0]))))  5.02 us
    pallas_call x2, Pallas kernels, last_step(): pl.pallas_call(last_body, out_shape=(pltpu.HBM((2 * heads, 3, hid, width)...  4.84 us
    pallas_call x8, Pallas kernels, apply_step(): pl.pallas_call(apply_body, out_shape=jax.ShapeDtypeStruct((rows, width),...  4.04 us
    pallas_call x1, Pallas kernels, attend_step(): pl.pallas_call(functools.partial(attend_body, token_scale), out_shape=mad...  2.81 us
    pallas_call x2, Pallas kernels, place_step(): pl.pallas_call(place_body, out_shape=pltpu.HBM(before.shape, before.dtype...  2.8 us
  transfers between devices with their start and end apart: 23, of which 13 were waited for; matrix products, arithmetic and copies ran while one was open for 1% of the time, Pallas kernels for 21%

profile of v9, /device:TPU:0, one launch (start us, length us, event | category | flops | bytes accessed | tf_op | source)
XLA Modules:
  0.0 114.8 jit_solution(2990034537056936439)
XLA Ops:
  0.6 2.7 %other_step.1 = (bf16[2,3,80,640]{3,2,1,0:T(8,128)(2,1)}, f32[2,3,80,640]{3,2,1,0:T(8,128)}) custom-call(s32[1]{0:T(128)} %bitcast.rep, f32[4,3,80,640]{3,2,1,0:T(8,128)} %refs_6_.3, f32[4,3,80,640]{3,2,1,0:T(8,128)} %refs_7_.3), custom_call_target="tpu_custom_call" | custom-call | flops 614400 | bytes 4300800 | tf_op jit(solution)/shard_map/other_step/pallas_call | solution.py:204
  3.3 0.5 collective-permute-start.7
  3.8 1.0 columns_step.1.refs_0_
  4.8 0.0 copy-start
  4.8 3.6 %collective-permute-start = (bf16[128,1280]{1,0:T(8,128)(2,1)S(1)}, bf16[128,1280]{1,0:T(8,128)(2,1)S(1)}, u32[]{:S(2)}, u32[]{:S(2)}) collective-permute-start(bf16[128,1280]{1,0:T(8,128)(2,1)S(1)} %columns_step.1.refs_0_), channel_id=1, source_target_pairs={{0,8},{8,12},{12,4},{4,0},{9,1},{13,9},{5,13},{1,5},{2,10},{10,14}... | collective-permute-start | bytes 983048 | tf_op jit(solution)/shard_map/ppermute | solution.py:507
  8.4 1.2 %cotangent_step.1 = (bf16[128,1280]{1,0:T(8,128)(2,1)S(1)}, bf16[128,1280]{1,0:T(8,128)(2,1)S(1)}) custom-call(s32[1]{0:T(128)} %bitcast.rep, bf16[128,2560]{1,0:T(8,128)(2,1)} %values.1, f32[4,128]{1,0:T(4,128)} %rates.1), custom_call_target="tpu_custom_call" | custom-call | flops 327680 | bytes 983040 | tf_op jit(solution)/shard_map/cotangent_step/pallas_call | solution.py:172
  9.6 0.7 copy-done.8
  10.3 1.6 %collective-permute-start.3 = (bf16[128,1280]{1,0:T(8,128)(2,1)S(1)}, bf16[128,1280]{1,0:T(8,128)(2,1)S(1)}, u32[]{:S(2)}, u32[]{:S(2)}) collective-permute-start(bf16[128,1280]{1,0:T(8,128)(2,1)S(1)} %get-tuple-element.18.refs_3_), channel_id=1, source_target_pairs={{0,8},{8,12},{12,4},{4,0},{9,1},{13,9},{5,13},{1,5},{2,10},{10,14}... | collective-permute-start | bytes 983048 | tf_op jit(solution)/shard_map/ppermute | solution.py:507
  11.9 0.0 collective-permute-start.6
  11.9 4.7 %collective-permute-done.refs_1_.refs_3_ = bf16[128,1280]{1,0:T(8,128)(2,1)S(1)} collective-permute-done((bf16[128,1280]{1,0:T(8,128)(2,1)S(1)}, bf16[128,1280]{1,0:T(8,128)(2,1)S(1)}, u32[]{:S(2)}, u32[]{:S(2)}) %collective-permute-start) | collective-permute-done | bytes 327712 | tf_op jit(solution)/shard_map/ppermute | solution.py:507
  16.6 3.3 %collective-permute-start.1 = (bf16[128,1280]{1,0:T(8,128)(2,1)S(1)}, bf16[128,1280]{1,0:T(8,128)(2,1)}, u32[]{:S(2)}, u32[]{:S(2)}) collective-permute-start(bf16[128,1280]{1,0:T(8,128)(2,1)S(1)} %collective-permute-done.refs_1_.refs_3_), channel_id=1, source_target_pairs={{0,8},{8,12},{12,4},{4,0},{9,1},{13,9},{5,13},{1,5},{2,10},{10,14}... | collective-permute-start | bytes 983048 | tf_op jit(solution)/shard_map/ppermute | solution.py:507
  19.9 3.7 %collective-permute-done.3.refs_4_.refs_6_ = bf16[128,1280]{1,0:T(8,128)(2,1)S(1)} collective-permute-done((bf16[128,1280]{1,0:T(8,128)(2,1)S(1)}, bf16[128,1280]{1,0:T(8,128)(2,1)S(1)}, u32[]{:S(2)}, u32[]{:S(2)}) %collective-permute-start.3) | collective-permute-done | bytes 327712 | tf_op jit(solution)/shard_map/ppermute | solution.py:507
  23.6 3.3 %collective-permute-start.4 = (bf16[128,1280]{1,0:T(8,128)(2,1)S(1)}, bf16[128,1280]{1,0:T(8,128)(2,1)}, u32[]{:S(2)}, u32[]{:S(2)}) collective-permute-start(bf16[128,1280]{1,0:T(8,128)(2,1)S(1)} %collective-permute-done.3.refs_4_.refs_6_), channel_id=1, source_target_pairs={{0,8},{8,12},{12,4},{4,0},{9,1},{13,9},{5,13},{1,5},{2,10},{10,14}... | collective-permute-start | bytes 983048 | tf_op jit(solution)/shard_map/ppermute | solution.py:507
  27.0 1.0 constant_dynamic-slice_fusion
  28.0 0.6 collective-permute-start.15
  28.6 0.7 copy-done.3
  29.3 1.5 %collective-permute-done.1.refs_2_.refs_4_ = bf16[128,1280]{1,0:T(8,128)(2,1)} collective-permute-done((bf16[128,1280]{1,0:T(8,128)(2,1)S(1)}, bf16[128,1280]{1,0:T(8,128)(2,1)}, u32[]{:S(2)}, u32[]{:S(2)}) %collective-permute-start.1) | collective-permute-done | bytes 327712 | tf_op jit(solution)/shard_map/ppermute | solution.py:507
  30.7 3.3 %collective-permute-start.2 = (bf16[128,1280]{1,0:T(8,128)(2,1)}, bf16[128,1280]{1,0:T(8,128)(2,1)S(1)}, u32[]{:S(2)}, u32[]{:S(2)}) collective-permute-start(bf16[128,1280]{1,0:T(8,128)(2,1)} %collective-permute-done.1.refs_2_.refs_4_), channel_id=1, source_target_pairs={{0,8},{8,12},{12,4},{4,0},{9,1},{13,9},{5,13},{1,5},{2,10},{10,14}... | collective-permute-start | bytes 983048 | tf_op jit(solution)/shard_map/ppermute | solution.py:507
  34.1 3.7 %collective-permute-done.4.refs_5_.refs_7_ = bf16[128,1280]{1,0:T(8,128)(2,1)} collective-permute-done((bf16[128,1280]{1,0:T(8,128)(2,1)S(1)}, bf16[128,1280]{1,0:T(8,128)(2,1)}, u32[]{:S(2)}, u32[]{:S(2)}) %collective-permute-start.4) | collective-permute-done | bytes 327712 | tf_op jit(solution)/shard_map/ppermute | solution.py:507
  37.8 3.3 %collective-permute-start.5 = (bf16[128,1280]{1,0:T(8,128)(2,1)}, bf16[128,1280]{1,0:T(8,128)(2,1)S(1)}, u32[]{:S(2)}, u32[]{:S(2)}) collective-permute-start(bf16[128,1280]{1,0:T(8,128)(2,1)} %collective-permute-done.4.refs_5_.refs_7_), channel_id=1, source_target_pairs={{0,8},{8,12},{12,4},{4,0},{9,1},{13,9},{5,13},{1,5},{2,10},{10,14}... | collective-permute-start | bytes 983048 | tf_op jit(solution)/shard_map/ppermute | solution.py:507
  41.1 0.1 collective-permute-done.15.query
  41.2 3.3 %collective-permute-start.9 = (bf16[128,640]{1,0:T(8,128)(2,1)S(1)}, bf16[128,640]{1,0:T(8,128)(2,1)S(1)}, u32[]{:S(2)}, u32[]{:S(2)}) collective-permute-start(bf16[128,640]{1,0:T(8,128)(2,1)S(1)} %get-tuple-element.35.query.refs_10_), channel_id=1, source_target_pairs={{0,8},{8,12},{12,4},{4,0},{9,1},{13,9},{5,13},{1,5},{2,10},{10,14}... | collective-permute-start | bytes 491528 | tf_op jit(solution)/shard_map/ppermute | solution.py:507
  44.5 0.7 copy-done.5
  45.2 12.9 %collective-permute-done.9.query = bf16[128,640]{1,0:T(8,128)(2,1)S(1)} collective-permute-done((bf16[128,640]{1,0:T(8,128)(2,1)S(1)}, bf16[128,640]{1,0:T(8,128)(2,1)S(1)}, u32[]{:S(2)}, u32[]{:S(2)}) %collective-permute-start.9) | collective-permute-done | bytes 163872 | tf_op jit(solution)/shard_map/ppermute | solution.py:507
  58.1 2.6 %collective-permute-start.16 = (bf16[128,640]{1,0:T(8,128)(2,1)S(1)}, bf16[128,640]{1,0:T(8,128)(2,1)S(1)}, u32[]{:S(2)}, u32[]{:S(2)}) collective-permute-start(bf16[128,640]{1,0:T(8,128)(2,1)S(1)} %collective-permute-done.15.query), channel_id=1, source_target_pairs={{0,8},{8,12},{12,4},{4,0},{9,1},{13,9},{5,13},{1,5},{2,10},{10,14}... | collective-permute-start | bytes 491528 | tf_op jit(solution)/shard_map/ppermute | solution.py:507
  60.7 1.0 collective-permute-start.10
  61.7 2.8 %early_step.3 = (f32[480,640]{1,0:T(8,128)S(1)}, bf16[480,640]{1,0:T(8,128)(2,1)S(1)}) custom-call(s32[1]{0:T(128)} %bitcast.rep, bf16[128,1280]{1,0:T(8,128)(2,1)} %copy-done, bf16[128,1280]{1,0:T(8,128)(2,1)} %copy-done.9, bf16[128,1280]{1,0:T(8,128)(2,1)} %collective-permute-done.1.refs_2_.refs_4_, bf16[128,1280]{1,0:T(8,128)(2,1)} %copy-done.7, ...), custom_call_target="tpu_custom_call" | custom-call | flops 471859200 | bytes 3072000 | tf_op jit(solution)/shard_map/early_step/pallas_call | solution.py:261
  64.6 0.0 collective-permute-done.2.key.refs_5_
  64.6 0.0 collective-permute-done.5.cotangent.refs_8_
  64.6 1.8 %last_step.2 = (f32[4,3,80,640]{3,2,1,0:T(8,128)}, f32[1,3,80,640]{3,2,1,0:T(8,128)}, bf16[480,640]{1,0:T(8,128)(2,1)S(1)}) custom-call(s32[1]{0:T(128)} %bitcast.rep, bf16[128,1280]{1,0:T(8,128)(2,1)S(1)} %collective-permute-done.2.key.refs_5_, bf16[128,1280]{1,0:T(8,128)(2,1)S(1)} %collective-permute-done.5.cotangent.refs_8_, ...), custom_call_target="tpu_custom_call" | custom-call | flops 157286400 | bytes 3686400 | tf_op jit(solution)/shard_map/last_step/pallas_call | solution.py:310
  66.4 0.7 collective-permute-start.22
  67.1 3.9 %early_step.2 = (f32[480,640]{1,0:T(8,128)}, bf16[480,640]{1,0:T(8,128)(2,1)S(1)}) custom-call(s32[1]{0:T(128)} %bitcast.rep, bf16[128,1280]{1,0:T(8,128)(2,1)} %copy-done, bf16[128,1280]{1,0:T(8,128)(2,1)} %copy-done.9, bf16[128,1280]{1,0:T(8,128)(2,1)} %collective-permute-done.1.refs_2_.refs_4_, bf16[128,1280]{1,0:T(8,128)(2,1)} %copy-done.7, ...), custom_call_target="tpu_custom_call" | custom-call | flops 471859200 | bytes 3072000 | tf_op jit(solution)/shard_map/early_step/pallas_call | solution.py:261
  71.0 3.0 %last_step.3 = (f32[4,3,80,640]{3,2,1,0:T(8,128)}, f32[1,3,80,640]{3,2,1,0:T(8,128)}, bf16[480,640]{1,0:T(8,128)(2,1)S(1)}) custom-call(s32[1]{0:T(128)} %bitcast.rep, bf16[128,1280]{1,0:T(8,128)(2,1)S(1)} %collective-permute-done.2.key.refs_5_, bf16[128,1280]{1,0:T(8,128)(2,1)S(1)} %collective-permute-done.5.cotangent.refs_8_, ...), custom_call_target="tpu_custom_call", output_to_operand_aliasing={{0}: (5, {})} | custom-call | flops 157286400 | bytes 3686400 | tf_op jit(solution)/shard_map/last_step/pallas_call | solution.py:310
  74.0 0.0 collective-permute-start.21
  74.0 0.5 apply_step.15
  74.5 1.8 %collective-permute-start.18 = (bf16[128,640]{1,0:T(8,128)(2,1)S(1)}, bf16[128,640]{1,0:T(8,128)(2,1)S(1)}, u32[]{:S(2)}, u32[]{:S(2)}) collective-permute-start(bf16[128,640]{1,0:T(8,128)(2,1)S(1)} %apply_step.15), channel_id=1, source_target_pairs={{0,8},{8,12},{12,4},{4,0},{9,1},{13,9},{5,13},{1,5},{2,10},{10,14}... | collective-permute-start | bytes 491528 | tf_op jit(solution)/shard_map/ppermute | solution.py:507
  76.3 0.5 apply_step.11
  76.8 0.1 collective-permute-start.12
  76.9 2.0 %collective-permute-start.11 = (bf16[128,640]{1,0:T(8,128)(2,1)S(1)}, bf16[128,640]{1,0:T(8,128)(2,1)S(1)}, u32[]{:S(2)}, u32[]{:S(2)}) collective-permute-start(bf16[128,640]{1,0:T(8,128)(2,1)S(1)} %collective-permute-done.10.query), channel_id=1, source_target_pairs={{0,8},{8,12},{12,4},{4,0},{9,1},{13,9},{5,13},{1,5},{2,10},{10,14}... | collective-permute-start | bytes 491528 | tf_op jit(solution)/shard_map/ppermute | solution.py:507
  78.9 0.5 apply_step.14.made
  79.4 2.5 %collective-permute-done.18.moved = bf16[128,640]{1,0:T(8,128)(2,1)S(1)} collective-permute-done((bf16[128,640]{1,0:T(8,128)(2,1)S(1)}, bf16[128,640]{1,0:T(8,128)(2,1)S(1)}, u32[]{:S(2)}, u32[]{:S(2)}) %collective-permute-start.18) | collective-permute-done | bytes 163872 | tf_op jit(solution)/shard_map/ppermute | solution.py:507
  82.0 2.3 %collective-permute-start.17 = (bf16[128,640]{1,0:T(8,128)(2,1)S(1)}, bf16[128,640]{1,0:T(8,128)(2,1)S(1)}, u32[]{:S(2)}, u32[]{:S(2)}) collective-permute-start(bf16[128,640]{1,0:T(8,128)(2,1)S(1)} %collective-permute-done.16.query), channel_id=1, source_target_pairs={{0,8},{8,12},{12,4},{4,0},{9,1},{13,9},{5,13},{1,5},{2,10},{10,14}... | collective-permute-start | bytes 491528 | tf_op jit(solution)/shard_map/ppermute | solution.py:507
  84.3 0.5 apply_step.10.made
  84.8 0.0 copy-start.11
  84.9 0.6 collective-permute-done.12.moved
  85.5 2.3 %collective-permute-start.19 = (bf16[128,640]{1,0:T(8,128)(2,1)S(1)}, bf16[128,640]{1,0:T(8,128)(2,1)S(1)}, u32[]{:S(2)}, u32[]{:S(2)}) collective-permute-start(bf16[128,640]{1,0:T(8,128)(2,1)S(1)} %join_step.6), channel_id=1, source_target_pairs={{0,8},{8,12},{12,4},{4,0},{9,1},{13,9},{5,13},{1,5},{2,10},{10,14}... | collective-permute-start | bytes 491528 | tf_op jit(solution)/shard_map/ppermute | solution.py:507
  87.8 1.1 collective-permute-done.11.query
  89.0 2.3 %collective-permute-start.13 = (bf16[128,640]{1,0:T(8,128)(2,1)S(1)}, bf16[128,640]{1,0:T(8,128)(2,1)S(1)}, u32[]{:S(2)}, u32[]{:S(2)}) collective-permute-start(bf16[128,640]{1,0:T(8,128)(2,1)S(1)} %join_step.4), channel_id=1, source_target_pairs={{0,8},{8,12},{12,4},{4,0},{9,1},{13,9},{5,13},{1,5},{2,10},{10,14}... | collective-permute-start | bytes 491528 | tf_op jit(solution)/shard_map/ppermute | solution.py:507
  91.3 0.5 apply_step.9.made
  91.8 0.7 collective-permute-done.17.query
  92.5 0.5 apply_step.13.made
  93.0 3.0 %collective-permute-done.19.moved = bf16[128,640]{1,0:T(8,128)(2,1)S(1)} collective-permute-done((bf16[128,640]{1,0:T(8,128)(2,1)S(1)}, bf16[128,640]{1,0:T(8,128)(2,1)S(1)}, u32[]{:S(2)}, u32[]{:S(2)}) %collective-permute-start.19) | collective-permute-done | bytes 163872 | tf_op jit(solution)/shard_map/ppermute | solution.py:507
  96.0 2.4 %collective-permute-start.20 = (bf16[128,640]{1,0:T(8,128)(2,1)S(1)}, bf16[128,640]{1,0:T(8,128)(2,1)S(1)}, u32[]{:S(2)}, u32[]{:S(2)}) collective-permute-start(bf16[128,640]{1,0:T(8,128)(2,1)S(1)} %join_step.7), channel_id=1, source_target_pairs={{0,8},{8,12},{12,4},{4,0},{9,1},{13,9},{5,13},{1,5},{2,10},{10,14}... | collective-permute-start | bytes 491528 | tf_op jit(solution)/shard_map/ppermute | solution.py:507
  98.4 1.1 collective-permute-done.13.moved
  99.6 1.5 %collective-permute-start.14 = (bf16[128,640]{1,0:T(8,128)(2,1)S(1)}, bf16[128,640]{1,0:T(8,128)(2,1)S(1)}, u32[]{:S(2)}, u32[]{:S(2)}) collective-permute-start(bf16[128,640]{1,0:T(8,128)(2,1)S(1)} %join_step.5), channel_id=1, source_target_pairs={{0,8},{8,12},{12,4},{4,0},{9,1},{13,9},{5,13},{1,5},{2,10},{10,14}... | collective-permute-start | bytes 491528 | tf_op jit(solution)/shard_map/ppermute | solution.py:507
  101.0 0.7 collective-permute-start.8
  101.7 5.0 %collective-permute-done.8.refs_2_ = f32[2,1,128]{2,1,0:T(1,128)S(1)} collective-permute-done((f32[2,1,128]{2,1,0:T(1,128)S(1)}, f32[2,1,128]{2,1,0:T(1,128)S(1)}, u32[]{:S(2)}, u32[]{:S(2)}) %collective-permute-start.8) | collective-permute-done | bytes 1056 | tf_op jit(solution)/shard_map/ppermute | solution.py:24
  106.7 2.8 %attend_step.1 = (f32[128,640]{1,0:T(8,128)S(1)}, f32[128,640]{1,0:T(8,128)S(1)}) custom-call(s32[1]{0:T(128)} %bitcast.1.block_index, bf16[128,1280]{1,0:T(8,128)(2,1)} %copy-done, bf16[128,1280]{1,0:T(8,128)(2,1)} %copy-done.8, f32[2,1,128]{2,1,0:T(1,128)S(1)} %collective-permute-done.8.refs_2_, bf16[128,1280]{1,0:T(8,128)(2,1)} %copy-done.9, ...), custom_call_target="tpu_custom_call" | custom-call | flops 167772160 | bytes 3276800 | tf_op jit(solution)/shard_map/attend_step/pallas_call | solution.py:472
  109.5 0.5 apply_step.8.kept
  110.0 0.5 apply_step.12.kept
  110.6 0.7 output_step.2.refs_0_
  111.3 0.7 output_step.3
  112.0 1.9 %place_step.2.before = f32[4,3,80,640]{3,2,1,0:T(8,128)} custom-call(s32[1]{0:T(128)} %bitcast.rep, f32[1,3,80,640]{3,2,1,0:T(8,128)} %collective-permute-done.22.block, f32[4,3,80,640]{3,2,1,0:T(8,128)} %get-tuple-element.33.before), custom_call_target="tpu_custom_call", output_to_operand_aliasing={{}: (2, {})} | custom-call | bytes 1228800 | tf_op jit(solution)/shard_map/place_step/pallas_call | solution.py:341
  114.0 0.9 place_step.3
  (32 shorter events, 0.2 us)
Async XLA Ops:
  3.3 58.4 %collective-permute-start.7 = (f32[2,3,80,640]{3,2,1,0:T(8,128)}, f32[2,3,80,640]{3,2,1,0:T(8,128)S(1)}, u32[]{:S(2)}, u32[]{:S(2)}) collective-permute-start(f32[2,3,80,640]{3,2,1,0:T(8,128)} %get-tuple-element.20), channel_id=1, source_target_pairs={{0,1},{1,0},{2,3},{3,2},{4,5},{5,4},{6,7},{7,6},{8,9},{9,8},{10,11... | collective-permute-start | bytes 3686408 | tf_op jit(solution)/shard_map/ppermute | solution.py:24
  4.8 56.9 %copy-start = (bf16[128,1280]{1,0:T(8,128)(2,1)}, bf16[128,1280]{1,0:T(8,128)(2,1)S(1)}, u32[]{:S(2)}) copy-start(bf16[128,1280]{1,0:T(8,128)(2,1)S(1)} %columns_step.1.refs_0_) | copy-start | bytes 983044
  4.8 11.8 %collective-permute-start = (bf16[128,1280]{1,0:T(8,128)(2,1)S(1)}, bf16[128,1280]{1,0:T(8,128)(2,1)S(1)}, u32[]{:S(2)}, u32[]{:S(2)}) collective-permute-start(bf16[128,1280]{1,0:T(8,128)(2,1)S(1)} %columns_step.1.refs_0_), channel_id=1, source_target_pairs={{0,8},{8,12},{12,4},{4,0},{9,1},{13,9},{5,13},{1,5},{2,10},{10,14}... | collective-permute-start | bytes 983048 | tf_op jit(solution)/shard_map/ppermute | solution.py:507
  9.6 0.7 copy-start.8
  10.3 51.4 %copy-start.7 = (bf16[128,1280]{1,0:T(8,128)(2,1)}, bf16[128,1280]{1,0:T(8,128)(2,1)S(1)}, u32[]{:S(2)}) copy-start(bf16[128,1280]{1,0:T(8,128)(2,1)S(1)} %get-tuple-element.18.refs_3_) | copy-start | bytes 983044
  10.3 13.3 %collective-permute-start.3 = (bf16[128,1280]{1,0:T(8,128)(2,1)S(1)}, bf16[128,1280]{1,0:T(8,128)(2,1)S(1)}, u32[]{:S(2)}, u32[]{:S(2)}) collective-permute-start(bf16[128,1280]{1,0:T(8,128)(2,1)S(1)} %get-tuple-element.18.refs_3_), channel_id=1, source_target_pairs={{0,8},{8,12},{12,4},{4,0},{9,1},{13,9},{5,13},{1,5},{2,10},{10,14}... | collective-permute-start | bytes 983048 | tf_op jit(solution)/shard_map/ppermute | solution.py:507
  11.9 48.8 %collective-permute-start.6 = (bf16[2,3,80,640]{3,2,1,0:T(8,128)(2,1)}, bf16[2,3,80,640]{3,2,1,0:T(8,128)(2,1)S(1)}, u32[]{:S(2)}, u32[]{:S(2)}) collective-permute-start(bf16[2,3,80,640]{3,2,1,0:T(8,128)(2,1)} %get-tuple-element.19), channel_id=1, source_target_pairs={{0,1},{1,0},{2,3},{3,2},{4,5},{5,4},{6,7},{7,6},{8,9},{9,8},{10,11... | collective-permute-start | bytes 1843208 | tf_op jit(solution)/shard_map/ppermute | solution.py:24
  16.6 12.0 %copy-start.9 = (bf16[128,1280]{1,0:T(8,128)(2,1)}, bf16[128,1280]{1,0:T(8,128)(2,1)S(1)}, u32[]{:S(2)}) copy-start(bf16[128,1280]{1,0:T(8,128)(2,1)S(1)} %collective-permute-done.refs_1_.refs_3_) | copy-start | bytes 983044
  16.6 14.1 %collective-permute-start.1 = (bf16[128,1280]{1,0:T(8,128)(2,1)S(1)}, bf16[128,1280]{1,0:T(8,128)(2,1)}, u32[]{:S(2)}, u32[]{:S(2)}) collective-permute-start(bf16[128,1280]{1,0:T(8,128)(2,1)S(1)} %collective-permute-done.refs_1_.refs_3_), channel_id=1, source_target_pairs={{0,8},{8,12},{12,4},{4,0},{9,1},{13,9},{5,13},{1,5},{2,10},{10,14}... | collective-permute-start | bytes 983048 | tf_op jit(solution)/shard_map/ppermute | solution.py:507
  23.6 10.5 %copy-start.10 = (bf16[128,1280]{1,0:T(8,128)(2,1)}, bf16[128,1280]{1,0:T(8,128)(2,1)S(1)}, u32[]{:S(2)}) copy-start(bf16[128,1280]{1,0:T(8,128)(2,1)S(1)} %collective-permute-done.3.refs_4_.refs_6_) | copy-start | bytes 983044
  23.6 14.1 %collective-permute-start.4 = (bf16[128,1280]{1,0:T(8,128)(2,1)S(1)}, bf16[128,1280]{1,0:T(8,128)(2,1)}, u32[]{:S(2)}, u32[]{:S(2)}) collective-permute-start(bf16[128,1280]{1,0:T(8,128)(2,1)S(1)} %collective-permute-done.3.refs_4_.refs_6_), channel_id=1, source_target_pairs={{0,8},{8,12},{12,4},{4,0},{9,1},{13,9},{5,13},{1,5},{2,10},{10,14}... | collective-permute-start | bytes 983048 | tf_op jit(solution)/shard_map/ppermute | solution.py:507
  28.0 13.2 %collective-permute-start.15 = (bf16[128,640]{1,0:T(8,128)(2,1)S(1)}, bf16[128,640]{1,0:T(8,128)(2,1)S(1)}, u32[]{:S(2)}, u32[]{:S(2)}) collective-permute-start(bf16[128,640]{1,0:T(8,128)(2,1)S(1)} %get-tuple-element.34.refs_9_.query), channel_id=1, source_target_pairs={{0,8},{8,12},{12,4},{4,0},{9,1},{13,9},{5,13},{1,5},{2,10},{10,14}... | collective-permute-start | bytes 491528 | tf_op jit(solution)/shard_map/ppermute | solution.py:507
  28.6 0.7 copy-start.3
  30.7 33.8 %collective-permute-start.2 = (bf16[128,1280]{1,0:T(8,128)(2,1)}, bf16[128,1280]{1,0:T(8,128)(2,1)S(1)}, u32[]{:S(2)}, u32[]{:S(2)}) collective-permute-start(bf16[128,1280]{1,0:T(8,128)(2,1)} %collective-permute-done.1.refs_2_.refs_4_), channel_id=1, source_target_pairs={{0,8},{8,12},{12,4},{4,0},{9,1},{13,9},{5,13},{1,5},{2,10},{10,14}... | collective-permute-start | bytes 983048 | tf_op jit(solution)/shard_map/ppermute | solution.py:507
  37.8 26.8 %collective-permute-start.5 = (bf16[128,1280]{1,0:T(8,128)(2,1)}, bf16[128,1280]{1,0:T(8,128)(2,1)S(1)}, u32[]{:S(2)}, u32[]{:S(2)}) collective-permute-start(bf16[128,1280]{1,0:T(8,128)(2,1)} %collective-permute-done.4.refs_5_.refs_7_), channel_id=1, source_target_pairs={{0,8},{8,12},{12,4},{4,0},{9,1},{13,9},{5,13},{1,5},{2,10},{10,14}... | collective-permute-start | bytes 983048 | tf_op jit(solution)/shard_map/ppermute | solution.py:507
  41.2 17.0 %collective-permute-start.9 = (bf16[128,640]{1,0:T(8,128)(2,1)S(1)}, bf16[128,640]{1,0:T(8,128)(2,1)S(1)}, u32[]{:S(2)}, u32[]{:S(2)}) collective-permute-start(bf16[128,640]{1,0:T(8,128)(2,1)S(1)} %get-tuple-element.35.query.refs_10_), channel_id=1, source_target_pairs={{0,8},{8,12},{12,4},{4,0},{9,1},{13,9},{5,13},{1,5},{2,10},{10,14}... | collective-permute-start | bytes 491528 | tf_op jit(solution)/shard_map/ppermute | solution.py:507
  44.5 0.7 copy-start.5
  58.1 18.7 %collective-permute-start.16 = (bf16[128,640]{1,0:T(8,128)(2,1)S(1)}, bf16[128,640]{1,0:T(8,128)(2,1)S(1)}, u32[]{:S(2)}, u32[]{:S(2)}) collective-permute-start(bf16[128,640]{1,0:T(8,128)(2,1)S(1)} %collective-permute-done.15.query), channel_id=1, source_target_pairs={{0,8},{8,12},{12,4},{4,0},{9,1},{13,9},{5,13},{1,5},{2,10},{10,14}... | collective-permute-start | bytes 491528 | tf_op jit(solution)/shard_map/ppermute | solution.py:507
  60.7 16.2 %collective-permute-start.10 = (bf16[128,640]{1,0:T(8,128)(2,1)S(1)}, bf16[128,640]{1,0:T(8,128)(2,1)S(1)}, u32[]{:S(2)}, u32[]{:S(2)}) collective-permute-start(bf16[128,640]{1,0:T(8,128)(2,1)S(1)} %collective-permute-done.9.query), channel_id=1, source_target_pairs={{0,8},{8,12},{12,4},{4,0},{9,1},{13,9},{5,13},{1,5},{2,10},{10,14}... | collective-permute-start | bytes 491528 | tf_op jit(solution)/shard_map/ppermute | solution.py:507
  64.6 6.4 %copy-start.1 = (bf16[128,1280]{1,0:T(8,128)(2,1)}, bf16[128,1280]{1,0:T(8,128)(2,1)S(1)}, u32[]{:S(2)}) copy-start(bf16[128,1280]{1,0:T(8,128)(2,1)S(1)} %collective-permute-done.2.key.refs_5_) | copy-start | bytes 983044
  64.6 6.4 %copy-start.2 = (bf16[128,1280]{1,0:T(8,128)(2,1)}, bf16[128,1280]{1,0:T(8,128)(2,1)S(1)}, u32[]{:S(2)}) copy-start(bf16[128,1280]{1,0:T(8,128)(2,1)S(1)} %collective-permute-done.5.cotangent.refs_8_) | copy-start | bytes 983044
  66.4 45.6 %collective-permute-start.22 = (f32[1,3,80,640]{3,2,1,0:T(8,128)}, f32[1,3,80,640]{3,2,1,0:T(8,128)}, u32[]{:S(2)}, u32[]{:S(2)}) collective-permute-start(f32[1,3,80,640]{3,2,1,0:T(8,128)} %get-tuple-element.32), channel_id=1, source_target_pairs={{0,1},{1,0},{2,3},{3,2},{4,5},{5,4},{6,7},{7,6},{8,9},{9,8},{10,11... | collective-permute-start | bytes 1843208 | tf_op jit(solution)/shard_map/ppermute | solution.py:24
  74.0 40.0 %collective-permute-start.21 = (f32[1,3,80,640]{3,2,1,0:T(8,128)}, f32[1,3,80,640]{3,2,1,0:T(8,128)S(1)}, u32[]{:S(2)}, u32[]{:S(2)}) collective-permute-start(f32[1,3,80,640]{3,2,1,0:T(8,128)} %get-tuple-element.31), channel_id=1, source_target_pairs={{0,1},{1,0},{2,3},{3,2},{4,5},{5,4},{6,7},{7,6},{8,9},{9,8},{10,11... | collective-permute-start | bytes 1843208 | tf_op jit(solution)/shard_map/ppermute | solution.py:24
  74.5 7.4 %collective-permute-start.18 = (bf16[128,640]{1,0:T(8,128)(2,1)S(1)}, bf16[128,640]{1,0:T(8,128)(2,1)S(1)}, u32[]{:S(2)}, u32[]{:S(2)}) collective-permute-start(bf16[128,640]{1,0:T(8,128)(2,1)S(1)} %apply_step.15), channel_id=1, source_target_pairs={{0,8},{8,12},{12,4},{4,0},{9,1},{13,9},{5,13},{1,5},{2,10},{10,14}... | collective-permute-start | bytes 491528 | tf_op jit(solution)/shard_map/ppermute | solution.py:507
  76.8 8.6 %collective-permute-start.12 = (bf16[128,640]{1,0:T(8,128)(2,1)S(1)}, bf16[128,640]{1,0:T(8,128)(2,1)S(1)}, u32[]{:S(2)}, u32[]{:S(2)}) collective-permute-start(bf16[128,640]{1,0:T(8,128)(2,1)S(1)} %apply_step.11), channel_id=1, source_target_pairs={{0,8},{8,12},{12,4},{4,0},{9,1},{13,9},{5,13},{1,5},{2,10},{10,14}... | collective-permute-start | bytes 491528 | tf_op jit(solution)/shard_map/ppermute | solution.py:507
  76.9 12.1 %collective-permute-start.11 = (bf16[128,640]{1,0:T(8,128)(2,1)S(1)}, bf16[128,640]{1,0:T(8,128)(2,1)S(1)}, u32[]{:S(2)}, u32[]{:S(2)}) collective-permute-start(bf16[128,640]{1,0:T(8,128)(2,1)S(1)} %collective-permute-done.10.query), channel_id=1, source_target_pairs={{0,8},{8,12},{12,4},{4,0},{9,1},{13,9},{5,13},{1,5},{2,10},{10,14}... | collective-permute-start | bytes 491528 | tf_op jit(solution)/shard_map/ppermute | solution.py:507
  82.0 10.5 %collective-permute-start.17 = (bf16[128,640]{1,0:T(8,128)(2,1)S(1)}, bf16[128,640]{1,0:T(8,128)(2,1)S(1)}, u32[]{:S(2)}, u32[]{:S(2)}) collective-permute-start(bf16[128,640]{1,0:T(8,128)(2,1)S(1)} %collective-permute-done.16.query), channel_id=1, source_target_pairs={{0,8},{8,12},{12,4},{4,0},{9,1},{13,9},{5,13},{1,5},{2,10},{10,14}... | collective-permute-start | bytes 491528 | tf_op jit(solution)/shard_map/ppermute | solution.py:507
  84.8 16.2 %copy-start.11 = (f32[4,128]{1,0:T(4,128)S(1)}, f32[4,128]{1,0:T(4,128)}, u32[]{:S(2)}) copy-start(f32[4,128]{1,0:T(4,128)} %rates.1) | copy-start | bytes 6148
  84.8 21.9 %copy-start.4 = (bf16[128,640]{1,0:T(8,128)(2,1)S(1)}, bf16[128,640]{1,0:T(8,128)(2,1)}, u32[]{:S(2)}) copy-start(bf16[128,640]{1,0:T(8,128)(2,1)} %copy-done.3) | copy-start | bytes 491524
  84.8 21.9 %copy-start.6 = (bf16[128,640]{1,0:T(8,128)(2,1)S(1)}, bf16[128,640]{1,0:T(8,128)(2,1)}, u32[]{:S(2)}) copy-start(bf16[128,640]{1,0:T(8,128)(2,1)} %copy-done.5) | copy-start | bytes 491524
  85.5 10.5 %collective-permute-start.19 = (bf16[128,640]{1,0:T(8,128)(2,1)S(1)}, bf16[128,640]{1,0:T(8,128)(2,1)S(1)}, u32[]{:S(2)}, u32[]{:S(2)}) collective-permute-start(bf16[128,640]{1,0:T(8,128)(2,1)S(1)} %join_step.6), channel_id=1, source_target_pairs={{0,8},{8,12},{12,4},{4,0},{9,1},{13,9},{5,13},{1,5},{2,10},{10,14}... | collective-permute-start | bytes 491528 | tf_op jit(solution)/shard_map/ppermute | solution.py:507
  89.0 10.5 %collective-permute-start.13 = (bf16[128,640]{1,0:T(8,128)(2,1)S(1)}, bf16[128,640]{1,0:T(8,128)(2,1)S(1)}, u32[]{:S(2)}, u32[]{:S(2)}) collective-permute-start(bf16[128,640]{1,0:T(8,128)(2,1)S(1)} %join_step.4), channel_id=1, source_target_pairs={{0,8},{8,12},{12,4},{4,0},{9,1},{13,9},{5,13},{1,5},{2,10},{10,14}... | collective-permute-start | bytes 491528 | tf_op jit(solution)/shard_map/ppermute | solution.py:507
  96.0 14.5 %collective-permute-start.20 = (bf16[128,640]{1,0:T(8,128)(2,1)S(1)}, bf16[128,640]{1,0:T(8,128)(2,1)S(1)}, u32[]{:S(2)}, u32[]{:S(2)}) collective-permute-start(bf16[128,640]{1,0:T(8,128)(2,1)S(1)} %join_step.7), channel_id=1, source_target_pairs={{0,8},{8,12},{12,4},{4,0},{9,1},{13,9},{5,13},{1,5},{2,10},{10,14}... | collective-permute-start | bytes 491528 | tf_op jit(solution)/shard_map/ppermute | solution.py:507
  99.6 11.7 %collective-permute-start.14 = (bf16[128,640]{1,0:T(8,128)(2,1)S(1)}, bf16[128,640]{1,0:T(8,128)(2,1)S(1)}, u32[]{:S(2)}, u32[]{:S(2)}) collective-permute-start(bf16[128,640]{1,0:T(8,128)(2,1)S(1)} %join_step.5), channel_id=1, source_target_pairs={{0,8},{8,12},{12,4},{4,0},{9,1},{13,9},{5,13},{1,5},{2,10},{10,14}... | collective-permute-start | bytes 491528 | tf_op jit(solution)/shard_map/ppermute | solution.py:507
  101.0 5.7 %collective-permute-start.8 = (f32[2,1,128]{2,1,0:T(1,128)S(1)}, f32[2,1,128]{2,1,0:T(1,128)S(1)}, u32[]{:S(2)}, u32[]{:S(2)}) collective-permute-start(f32[2,1,128]{2,1,0:T(1,128)S(1)} %bitcast.3), channel_id=1, source_target_pairs={{0,4},{4,8},{8,12},{12,0},{1,5},{5,9},{9,13},{13,1},{2,6},{6,10},{... | collective-permute-start | bytes 3080 | tf_op jit(solution)/shard_map/ppermute | solution.py:24
